TPU v7x, 128 devices: a whole 4x4x4 slice. The times are simulated.
128 devices in a mesh: dir: 2 (over z_lo), row: 8 (over y, z_hi), col: 8 (over x, core).
Axes of the slice: x: 4, y: 4, z: 4 (z_hi: 2, z_lo: 2; z = z_hi * 2 + z_lo), core: 2. Of those that a mesh axis runs over, the one named last changes fastest.
Arguments:
- cotangent: bfloat16 [2048, 512], P('dir'), may hold values from -3 to 3
- radiation: bfloat16 [2, 32768, 2048], P(None, ('row', 'col'), 'dir'), may hold values from -0.125 to 0.125
- near_z: float32 [2, 1024, 512, 512], P(None, ('dir', 'row', 'col')), may hold values from -0.25 to 0.25
- near_pairs: int32 [1024, 2], P(('dir', 'row', 'col')), may hold values from 0 to 63, as said below
- far_ut: float32 [2, 512, 96, 512], P(None, ('dir', 'row', 'col')), may hold values from -0.25 to 0.25
- far_vt: float32 [2, 512, 96, 512], P(None, ('dir', 'row', 'col')), may hold values from -0.625 to 0.625
- far_pairs: int32 [512, 2], P(('dir', 'row', 'col')), may hold values from 0 to 63, as said below
- far_ranks: int32 [512], P(('dir', 'row', 'col')), may hold values from 32 to 96
- block_counts: int32 [128, 2], P(('dir', 'row', 'col')), may hold values from 1 to 8, as said below
Outputs:
- adjoint: float32 [32768, 512], P(('col', 'dir', 'row'))
Inputs may be any that keep to these rules, and one draw needn't show every extreme that they name: `near_pairs`: slot s belongs to the device at position g = s div 8 in the order dir, row, col, with row index r and column index c; its row cluster lies in r * 8 to (r + 1) * 8 - 1 and its column cluster in c * 8 to (c + 1) * 8 - 1. Pairs may repeat. `far_pairs`: slot s belongs to the device at position s div 4 in the order dir, row, col, with row index r and column index c; its row cluster lies in r * 8 to (r + 1) * 8 - 1 and its column cluster in c * 8 to (c + 1) * 8 - 1. Pairs may repeat. `block_counts`: column 0 is at most 8 and column 1 at most 4; the live slots of a device are its first ones.
All inputs are finite; a program needn't handle non-finite values.
Results may differ from a plain program's by a relative error of at most 0.0003.
Values sent between devices are 32-bit elements; how exact they have to be, the bound alone decides.
No kernel may reach another device: no remote copies, remote signals or barrier semaphores. Data moves between devices by JAX's collectives and lax.ppermute only.
A program may use at most 128 MiB of HBM per device.

v0:
```python
import jax
import jax.numpy as jnp
from jax import lax
from jax.sharding import Mesh
from jax.sharding import PartitionSpec as P

ROW = ("row_0", "row_1")
ROW_COL = ("row_0", "row_1", "col")
DIR_ROW_COL = ("dir", "row_0", "row_1", "col")
COL_DIR_ROW = ("col", "dir", "row_0", "row_1")


def from_everyone(shard, axis):
    copies = jnp.broadcast_to(shard, (lax.axis_size(axis), *shard.shape))
    return lax.all_to_all(copies, axis, split_axis=0, concat_axis=0, tiled=True)


def over_copies(shard, axis):
    everything = from_everyone(shard, axis)
    return jnp.sum(everything, axis=0)


def split_up(shard, dim, peers):
    shape = shard.shape
    parts = shard.reshape(*shape[:dim], peers, shape[dim] // peers, *shape[dim + 1 :])
    return jnp.moveaxis(parts, dim, 0)


def sum_at_owner(shard, axis, dim):
    parts = split_up(shard, dim, lax.axis_size(axis))
    arrived = lax.all_to_all(parts, axis, split_axis=0, concat_axis=0, tiled=True)
    return arrived.sum(axis=0)


def summed_rows(shard, axes, dim):
    for axis in axes:
        shard = lax.psum_scatter(shard, axis, scatter_dimension=dim, tiled=True)
    return shard


def swap_parts(values):
    half_width = values.shape[1] // 2
    return jnp.concatenate([-values[:, half_width:], values[:, :half_width]], axis=1)


def transposed_dot(left, right):
    return lax.dot_general(
        left,
        right,
        (((0,), (0,)), ((), ())),
        precision=lax.Precision.HIGHEST,
        preferred_element_type=jnp.float32,
    )


def plain_dot(left, right):
    return jnp.dot(left, right, precision=lax.Precision.HIGHEST, preferred_element_type=jnp.float32)


def add_rows(total, term, start):
    current = lax.dynamic_slice_in_dim(total, start, term.shape[0], 0)
    return lax.dynamic_update_slice_in_dim(total, current + term, start, 0)


def shards(
    cotangent, radiation, near_z, near_pairs, far_ut, far_vt, far_pairs, far_ranks, block_counts
):
    block_rows = near_z.shape[2]
    rank_most = far_ut.shape[2]
    partial_rhs = jnp.dot(radiation[0], cotangent, preferred_element_type=jnp.float32) + jnp.dot(
        radiation[1], swap_parts(cotangent), preferred_element_type=jnp.float32
    )
    summed = over_copies(partial_rhs, "dir")
    shard_rhs = lax.all_gather(summed, "col", axis=0, tiled=True)
    swapped_rhs = swap_parts(shard_rhs)
    row_base = lax.axis_index(ROW) * lax.axis_size("col")
    col_base = lax.axis_index("col") * lax.axis_size(ROW)
    column_rows = lax.axis_size(ROW) * block_rows

    def near_step(slot_index, total):
        row_start = (near_pairs[slot_index, 0] - row_base) * block_rows
        col_start = (near_pairs[slot_index, 1] - col_base) * block_rows
        source = lax.dynamic_slice_in_dim(shard_rhs, row_start, block_rows, 0)
        source_swap = lax.dynamic_slice_in_dim(swapped_rhs, row_start, block_rows, 0)
        blocks = near_z[:, slot_index]
        term = transposed_dot(blocks[0], source) + transposed_dot(blocks[1], source_swap)
        return add_rows(total, term, col_start)

    def far_step(slot_index, total):
        row_start = (far_pairs[slot_index, 0] - row_base) * block_rows
        col_start = (far_pairs[slot_index, 1] - col_base) * block_rows
        source = lax.dynamic_slice_in_dim(shard_rhs, row_start, block_rows, 0)
        source_swap = lax.dynamic_slice_in_dim(swapped_rhs, row_start, block_rows, 0)
        left_f = far_ut[:, slot_index]
        right_f = far_vt[:, slot_index]
        coeffs = plain_dot(left_f[0], source) + plain_dot(left_f[1], source_swap)
        keep_rows = (lax.iota(jnp.int32, rank_most) < far_ranks[slot_index])[:, None]
        coeffs = jnp.where(keep_rows, coeffs, jnp.zeros_like(coeffs))
        term = transposed_dot(right_f[0], coeffs) + transposed_dot(right_f[1], swap_parts(coeffs))
        return add_rows(total, term, col_start)

    partial_out = jnp.zeros((column_rows, shard_rhs.shape[1]), jnp.float32)
    partial_out = lax.fori_loop(0, block_counts[0, 0], near_step, partial_out)
    partial_out = lax.fori_loop(0, block_counts[0, 1], far_step, partial_out)
    first_section = sum_at_owner(partial_out, "dir", 0)
    result = summed_rows(first_section, ROW, 0)
    return result


def solution(mesh):
    finer = Mesh(
        mesh.devices.reshape(mesh.shape["dir"], 4, 2, mesh.shape["col"]),
        ("dir", "row_0", "row_1", "col"),
    )
    in_specs = (
        P("dir", None),
        P(None, ROW_COL, "dir"),
        P(None, DIR_ROW_COL, None, None),
        P(DIR_ROW_COL, None),
        P(None, DIR_ROW_COL, None, None),
        P(None, DIR_ROW_COL, None, None),
        P(DIR_ROW_COL, None),
        P(DIR_ROW_COL),
        P(DIR_ROW_COL, None),
    )
    out_specs = P(COL_DIR_ROW, None)
    return jax.shard_map(
        shards, mesh=finer, in_specs=in_specs, out_specs=out_specs, check_vma=False
    )
```

profile of v0, /device:TPU:0, one launch (start us, length us, event | category | flops | bytes accessed | tf_op | source)
XLA Modules:
  0.0 430.0 jit_solution(15735743187826674259)
XLA Ops:
  6.5 1.3 slice_negate_fusion.2
  7.8 2.2 fusion.27
  10.1 1.9 fusion.22
  12.0 0.3 broadcast_in_dim.16
  12.3 27.9 %all_to_all.10 = f32[2,512,512]{2,1,0:T(8,128)S(1)} all-to-all(f32[2,512,512]{2,1,0:T(8,128)S(1)} %broadcast_in_dim.16), channel_id=1, replica_groups=mesh['dir'=2,'row_0'=4,'row_1'=2,'col'=8] {'dir'}, dimensions={0} | all-to-all | bytes 4194304 | tf_op jit(solution)/shard_map/all_to_all | solution.py:15
  40.2 1.3 reduce_sum.18
  41.6 0.7 fusion.32
  42.3 51.1 %all-gather.2.cloned.1.call-done = f32[4096,512]{1,0:T(8,128)} async-done(((f32[512,512]{1,0:T(8,128)}), f32[4096,512]{1,0:T(8,128)}) %all-gather.2.cloned.1.call-update) | async-done | bytes 8388624 | tf_op jit(solution)/shard_map/all_gather | solution.py:74
  93.4 4.1 slice_negate_fusion.1
  97.6 4.6 %pad_maximum_fusion = f32[4096,512]{1,0:T(8,128)} fusion(f32[4096,256]{1,0:T(8,128)S(1)} %get-tuple-element.160, f32[4096,256]{1,0:T(8,128)S(1)} %get-tuple-element.159), kind=kLoop, calls=%fused_computation.37 | loop fusion | flops 2097152 | bytes 16777216 | tf_op jit(solution)/shard_map/concatenate | solution.py:43
  102.1 4.3 broadcast_in_dim.15
  106.4 85.5 %while.20 = (s32[]{:T(128)}, f32[4096,512]{1,0:T(8,128)}, s32[]{:T(128)}, s32[8,2]{0,1:T(2,128)S(1)}, s32[]{:T(128)}, /*index=5*/f32[2,8,512,512]{3,2,1,0:T(8,12...) while((s32[]{:T(128)}, f32[4096,512]{1,0:T(8,128)}, ...), condition=%wide.region_2.0_spmd, body=%wide.region_1.0_spmd.sunk | while | flops 3221749760 | bytes 8388963 | solution.py:103
  107.0 0.7 constant_dynamic-slice_fusion.6
  108.9 3.4 fusion.49
  112.3 4.8 %fusion.50 = f32[4096,512]{1,0:T(8,128)} fusion(f32[4096,512]{1,0:T(8,128)} %get-tuple-element.317, s32[]{:T(128)S(6)} %select_n.41, f32[512,512]{1,0:T(8,128)S(1)} %fusion.49, f32[2,8,512,512]{3,2,1,0:T(8,128)} %get-tuple-element.336, s32[]{:T(128)S(6)} %add.105, s32[]{:T(128)S(6)} %select_n.40, f32[4096,512]{1,0:T(8,128)} %get-tuple-element.339, ...), kind=kOutput, calls=%fused_computation.2.clone.1 | convolution fusion | flops 1611137024 | bytes 5242896 | tf_op jit(solution)/shard_map/while/body/dot_general | solution.py:47
  117.6 0.7 constant_dynamic-slice_fusion.6
  119.5 3.4 fusion.49
  122.9 4.8 %fusion.50 = f32[4096,512]{1,0:T(8,128)} fusion(f32[4096,512]{1,0:T(8,128)} %get-tuple-element.317, s32[]{:T(128)S(6)} %select_n.41, f32[512,512]{1,0:T(8,128)S(1)} %fusion.49, f32[2,8,512,512]{3,2,1,0:T(8,128)} %get-tuple-element.336, s32[]{:T(128)S(6)} %add.105, s32[]{:T(128)S(6)} %select_n.40, f32[4096,512]{1,0:T(8,128)} %get-tuple-element.339, ...), kind=kOutput, calls=%fused_computation.2.clone.1 | convolution fusion | flops 1611137024 | bytes 5242896 | tf_op jit(solution)/shard_map/while/body/dot_general | solution.py:47
  128.2 0.7 constant_dynamic-slice_fusion.6
  130.1 3.4 fusion.49
  133.5 4.8 %fusion.50 = f32[4096,512]{1,0:T(8,128)} fusion(f32[4096,512]{1,0:T(8,128)} %get-tuple-element.317, s32[]{:T(128)S(6)} %select_n.41, f32[512,512]{1,0:T(8,128)S(1)} %fusion.49, f32[2,8,512,512]{3,2,1,0:T(8,128)} %get-tuple-element.336, s32[]{:T(128)S(6)} %add.105, s32[]{:T(128)S(6)} %select_n.40, f32[4096,512]{1,0:T(8,128)} %get-tuple-element.339, ...), kind=kOutput, calls=%fused_computation.2.clone.1 | convolution fusion | flops 1611137024 | bytes 5242896 | tf_op jit(solution)/shard_map/while/body/dot_general | solution.py:47
  138.8 0.7 constant_dynamic-slice_fusion.6
  140.7 3.4 fusion.49
  144.1 4.8 %fusion.50 = f32[4096,512]{1,0:T(8,128)} fusion(f32[4096,512]{1,0:T(8,128)} %get-tuple-element.317, s32[]{:T(128)S(6)} %select_n.41, f32[512,512]{1,0:T(8,128)S(1)} %fusion.49, f32[2,8,512,512]{3,2,1,0:T(8,128)} %get-tuple-element.336, s32[]{:T(128)S(6)} %add.105, s32[]{:T(128)S(6)} %select_n.40, f32[4096,512]{1,0:T(8,128)} %get-tuple-element.339, ...), kind=kOutput, calls=%fused_computation.2.clone.1 | convolution fusion | flops 1611137024 | bytes 5242896 | tf_op jit(solution)/shard_map/while/body/dot_general | solution.py:47
  149.4 0.7 constant_dynamic-slice_fusion.6
  151.3 3.4 fusion.49
  154.7 4.8 %fusion.50 = f32[4096,512]{1,0:T(8,128)} fusion(f32[4096,512]{1,0:T(8,128)} %get-tuple-element.317, s32[]{:T(128)S(6)} %select_n.41, f32[512,512]{1,0:T(8,128)S(1)} %fusion.49, f32[2,8,512,512]{3,2,1,0:T(8,128)} %get-tuple-element.336, s32[]{:T(128)S(6)} %add.105, s32[]{:T(128)S(6)} %select_n.40, f32[4096,512]{1,0:T(8,128)} %get-tuple-element.339, ...), kind=kOutput, calls=%fused_computation.2.clone.1 | convolution fusion | flops 1611137024 | bytes 5242896 | tf_op jit(solution)/shard_map/while/body/dot_general | solution.py:47
  160.1 0.7 constant_dynamic-slice_fusion.6
  161.9 3.4 fusion.49
  165.3 4.8 %fusion.50 = f32[4096,512]{1,0:T(8,128)} fusion(f32[4096,512]{1,0:T(8,128)} %get-tuple-element.317, s32[]{:T(128)S(6)} %select_n.41, f32[512,512]{1,0:T(8,128)S(1)} %fusion.49, f32[2,8,512,512]{3,2,1,0:T(8,128)} %get-tuple-element.336, s32[]{:T(128)S(6)} %add.105, s32[]{:T(128)S(6)} %select_n.40, f32[4096,512]{1,0:T(8,128)} %get-tuple-element.339, ...), kind=kOutput, calls=%fused_computation.2.clone.1 | convolution fusion | flops 1611137024 | bytes 5242896 | tf_op jit(solution)/shard_map/while/body/dot_general | solution.py:47
  170.7 0.7 constant_dynamic-slice_fusion.6
  172.6 3.4 fusion.49
  176.0 4.8 %fusion.50 = f32[4096,512]{1,0:T(8,128)} fusion(f32[4096,512]{1,0:T(8,128)} %get-tuple-element.317, s32[]{:T(128)S(6)} %select_n.41, f32[512,512]{1,0:T(8,128)S(1)} %fusion.49, f32[2,8,512,512]{3,2,1,0:T(8,128)} %get-tuple-element.336, s32[]{:T(128)S(6)} %add.105, s32[]{:T(128)S(6)} %select_n.40, f32[4096,512]{1,0:T(8,128)} %get-tuple-element.339, ...), kind=kOutput, calls=%fused_computation.2.clone.1 | convolution fusion | flops 1611137024 | bytes 5242896 | tf_op jit(solution)/shard_map/while/body/dot_general | solution.py:47
  181.3 0.7 constant_dynamic-slice_fusion.6
  183.2 3.4 fusion.49
  186.6 4.8 %fusion.50 = f32[4096,512]{1,0:T(8,128)} fusion(f32[4096,512]{1,0:T(8,128)} %get-tuple-element.317, s32[]{:T(128)S(6)} %select_n.41, f32[512,512]{1,0:T(8,128)S(1)} %fusion.49, f32[2,8,512,512]{3,2,1,0:T(8,128)} %get-tuple-element.336, s32[]{:T(128)S(6)} %add.105, s32[]{:T(128)S(6)} %select_n.40, f32[4096,512]{1,0:T(8,128)} %get-tuple-element.339, ...), kind=kOutput, calls=%fused_computation.2.clone.1 | convolution fusion | flops 1611137024 | bytes 5242896 | tf_op jit(solution)/shard_map/while/body/dot_general | solution.py:47
  192.0 13.8 %while.21 = (s32[]{:T(128)}, f32[4096,512]{1,0:T(8,128)}, s32[]{:T(128)}, s32[4,2]{0,1:T(2,128)S(1)}, s32[]{:T(128)}, /*index=5*/f32[2,4,96,512]{3,2,1,0:T(8,128...) while((s32[]{:T(128)}, f32[4096,512]{1,0:T(8,128)}, ...), condition=%wide.region_4.5_spmd, body=%wide.region_3.4_spmd.sunk | while | flops 1208656000 | bytes 8454735 | solution.py:104
  192.7 0.6 dynamic_slice.73
  193.3 0.6 iota_compare_fusion.2
  193.8 0.6 constant_dynamic-slice_fusion.7
  195.6 2.1 fusion.55
  197.6 2.1 fusion.56
  199.8 2.0 fusion.57
  201.7 3.4 fusion.58
  205.8 103.8 %all_to_all.11 = f32[2,2048,512]{2,1,0:T(8,128)} all-to-all(f32[2,2048,512]{2,1,0:T(8,128)} %bitcast.62), channel_id=1, replica_groups=mesh['dir'=2,'row_0'=4,'row_1'=2,'col'=8] {'dir'}, dimensions={0} | all-to-all | bytes 16777216 | tf_op jit(solution)/shard_map/all_to_all | solution.py:31
  309.6 6.8 %reduce_sum.19 = f32[2048,512]{1,0:T(8,128)} reduce(f32[2,2048,512]{2,1,0:T(8,128)} %all_to_all.11, f32[]{:T(128)} %constant.20.clone.1), dimensions={0}, to_apply=%region_5.6 | reduce | flops 1048576 | bytes 12582916 | tf_op jit(solution)/shard_map/reduce_sum | solution.py:32
  316.5 80.3 %reduce-scatter.3.cloned.1.call-done = f32[512,512]{1,0:T(8,128)} async-done(((f32[2048,512]{1,0:T(8,128)}), f32[512,512]{1,0:T(8,128)}) %reduce-scatter.3.cloned.1.call-update) | async-done | bytes 1048592 | tf_op jit(solution)/shard_map/reduce_scatter | solution.py:37
  396.7 26.7 %reduce-scatter.5.cloned.1.call-done = f32[256,512]{1,0:T(8,128)} async-done(((f32[512,512]{1,0:T(8,128)}), f32[256,512]{1,0:T(8,128)}) %reduce-scatter.5.cloned.1.call-update) | async-done | bytes 524304 | tf_op jit(solution)/shard_map/reduce_scatter | solution.py:37
  (15 shorter events, 0.2 us)
Async XLA Ops:
  6.5 86.9 %all-gather.2.cloned.1.call-start = ((), (), s32[]{:S(2)}) async-start(), calls=%async_computation.4 | async-start | bytes 9437184 | tf_op jit(solution)/shard_map/all_gather | solution.py:74
  10.1 31.6 %copy-start.2 = (s32[1,2]{1,0:T(1,128)S(1)}, s32[1,2]{1,0:T(1,128)}, u32[]{:S(2)}) copy-start(s32[1,2]{1,0:T(1,128)} %param.21) | copy-start | bytes 28
  41.6 355.1 %reduce-scatter.3.cloned.1.call-start = ((), (), s32[]{:S(2)}) async-start(), calls=%async_computation.5 | async-start | bytes 5242880 | tf_op jit(solution)/shard_map/reduce_scatter | solution.py:37
  102.1 4.3 %copy-start = (s32[8,2]{0,1:T(2,128)S(1)}, s32[8,2]{0,1:T(2,128)}, u32[]{:S(2)}) copy-start(s32[8,2]{0,1:T(2,128)} %param.16) | copy-start | bytes 196
  106.4 85.5 %copy-start.1 = (s32[4,2]{0,1:T(2,128)S(1)}, s32[4,2]{0,1:T(2,128)}, u32[]{:S(2)}) copy-start(s32[4,2]{0,1:T(2,128)} %param.19) | copy-start | bytes 100
  106.4 85.5 %copy-start.3 = (s32[4]{0:T(128)S(1)}, s32[4]{0:T(128)}, u32[]{:S(2)}) copy-start(s32[4]{0:T(128)} %param.20) | copy-start | bytes 52
  316.4 107.0 %reduce-scatter.5.cloned.1.call-start = ((), (), s32[]{:S(2)}) async-start(), calls=%async_computation.6 | async-start | bytes 1572864 | tf_op jit(solution)/shard_map/reduce_scatter | solution.py:37
Sparse Core Ops, SparseCore 0:
  41.7 51.7 all-gather.1
  316.5 80.1 reduce-scatter.2
  399.2 24.1 reduce-scatter.4
where the time goes:
time: 435 us; the launch traced here: 430 us
  waiting for transfers between devices  158 us (36%)
  blocking collectives  132 us (30%)
  matrix products  79 us (18%)
  other arithmetic  18.6 us (4%)
  loops' own time  17.5 us (4%)
  between operations  13.2 us (3%)
  local copies, waits for them, and re-layouts  11.6 us (3%)
    reduce_scatter x2, waiting for transfers between devices, summed_rows(): shard = lax.psum_scatter(shard, axis, scatter_dimension=dim, tiled=True)  107 us
    all_to_all x1, blocking collectives, sum_at_owner(): lax.all_to_all(parts, axis, split_axis=0, concat_axis=0, tiled=True)  104 us
    dot_general x18, matrix products, transposed_dot(): lax.dot_general(left, right, (((0,), (0,)), ((), ())), precision=lax.Prec...  70.7 us
    all_gather x1, waiting for transfers between devices, shards(): shard_rhs = lax.all_gather(summed, 'col', axis=0, tiled=True)  51.1 us
    all_to_all x1, blocking collectives, from_everyone(): return lax.all_to_all(copies, axis, split_axis=0, concat_axis=0, tiled=True)  27.9 us
    another operation x1, loops' own time, shards(): partial_out = lax.fori_loop(0, block_counts[0, 0], near_step, partial_out)  15 us
  transfers between devices with their start and end apart: 3, of which 3 were waited for; matrix products, arithmetic and copies ran while one was open for 0% of the time, Pallas kernels for 0%

commit v1 on v0

v1 whole, which is shorter than its diff:
```python
import functools

import jax
import jax.numpy as jnp
from jax import lax
from jax.experimental import pallas as pl
from jax.experimental.pallas import tpu as pltpu
from jax.sharding import Mesh
from jax.sharding import PartitionSpec as P

AXES = ("dir", "y", "zhi", "x", "core")
ROW = ("y", "zhi")
COL = ("x", "core")
SIZES = (2, 4, 2, 4, 2)
CHUNKS = 2
CLUSTER = 512
HALF = 128
WIDE = 2 * HALF
PAD = 128
NEAR = 8
FAR = 4
VMEM_LIMIT = 48 << 20

ANY = pl.BlockSpec(memory_space=pl.ANY)
SMEM = pl.BlockSpec(memory_space=pltpu.SMEM)

N_NEAR, N_FAR, NEAR_A, NEAR_B, FAR_A, FAR_B, RANK, ORDER = 0, 1, 2, 10, 18, 22, 26, 30


def split(values):
    high = values.astype(jnp.bfloat16)
    low = (values - high.astype(jnp.float32)).astype(jnp.bfloat16)
    return high, low


def dot(left, right):
    return jnp.dot(left, right, preferred_element_type=jnp.float32)


def rotations():
    tables = []
    for first in (True, False):
        for shift in (1, 2, 3):
            pairs = []
            for lo in range(2):
                for y in range(4):
                    for hi in range(2):
                        for x in range(4):
                            for core in range(2):
                                z = hi * 2 + lo
                                if (core == 0) == first:
                                    to_y, to_z = (y + shift) % 4, z
                                else:
                                    to_y, to_z = y, (z + shift) % 4
                                here = (((lo * 4 + y) * 2 + hi) * 4 + x) * 2 + core
                                there = (((to_z % 2 * 4 + to_y) * 2 + to_z // 2) * 4 + x) * 2 + core
                                pairs.append((here, there))
            tables.append(pairs)
    return tables[:3], tables[3:]


def rhs_kernel(cot_ref, rad_ref, *out_refs):
    width = cot_ref.shape[1] // 2
    for chunk, out_ref in enumerate(out_refs):
        re = cot_ref[:, chunk * HALF : (chunk + 1) * HALF]
        im = cot_ref[:, width + chunk * HALF : width + (chunk + 1) * HALF]
        out_ref[...] = dot(rad_ref[0], jnp.concatenate([re, im], 1)) + dot(
            rad_ref[1], jnp.concatenate([-im, re], 1)
        )


def partial_rhs(cotangent, radiation):
    _, rows, dirs = radiation.shape
    tile = 128
    return pl.pallas_call(
        rhs_kernel,
        name="rhs",
        grid=(rows // tile,),
        in_specs=[
            pl.BlockSpec(cotangent.shape, lambda i: (0, 0)),
            pl.BlockSpec((2, tile, dirs), lambda i: (0, i, 0)),
        ],
        out_specs=[pl.BlockSpec((tile, WIDE), lambda i: (i, 0))] * CHUNKS,
        out_shape=[jax.ShapeDtypeStruct((rows, WIDE), jnp.float32)] * CHUNKS,
        compiler_params=pltpu.CompilerParams(vmem_limit_bytes=VMEM_LIMIT),
        cost_estimate=pl.CostEstimate(flops=1 << 30, bytes_accessed=4 << 20, transcendentals=0),
    )(cotangent, radiation)


def prepare_kernel(table, z_ref, u_ref, v_ref, z_out, u_out, v_out, z_in, z_buf, u_in, u_buf, v_in, v_buf, sem_in, sem_out, sem_u, sem_v, sem_uo, sem_vo):
    near, far = table[N_NEAR], table[N_FAR]

    def fetch(s, b):
        return pltpu.make_async_copy(z_ref.at[:, s], z_in.at[b], sem_in.at[b])

    def keep(s, b):
        return pltpu.make_async_copy(z_buf.at[b], z_out.at[s], sem_out.at[b])

    fetch(0, 0).start()

    def near_step(s, _):
        b = lax.rem(s, 2)
        fetch(s, b).wait()

        @pl.when(s + 1 < near)
        def _():
            fetch(s + 1, 1 - b).start()

        @pl.when(s >= 2)
        def _():
            keep(s - 2, b).wait()

        for part in range(2):
            high, low = split(z_in[b, part].T)
            z_buf[b, :, part * CLUSTER : (part + 1) * CLUSTER] = high
            z_buf[b, :, (part + 2) * CLUSTER : (part + 3) * CLUSTER] = low
        keep(s, b).start()
        return 0

    lax.fori_loop(0, near, near_step, 0)

    @pl.when(near >= 2)
    def _():
        keep(near - 2, lax.rem(near, 2)).wait()

    keep(near - 1, lax.rem(near - 1, 2)).wait()

    rank_most = u_in.shape[1]
    u_buf[...] = jnp.zeros_like(u_buf)
    v_buf[...] = jnp.zeros_like(v_buf)

    def far_step(s, _):
        copies = (
            pltpu.make_async_copy(u_ref.at[:, s], u_in, sem_u),
            pltpu.make_async_copy(v_ref.at[:, s], v_in, sem_v),
        )
        for copy in copies:
            copy.start()
        for copy in copies:
            copy.wait()
        live = lax.broadcasted_iota(jnp.int32, u_in.shape[1:], 0) < table[RANK + s]
        for part in range(2):
            high, low = split(jnp.where(live, u_in[part], 0.0))
            u_buf[:rank_most, part * CLUSTER : (part + 1) * CLUSTER] = high
            u_buf[:rank_most, (part + 2) * CLUSTER : (part + 3) * CLUSTER] = low
            padded = jnp.concatenate([v_in[part], jnp.zeros((PAD - rank_most, CLUSTER), jnp.float32)], 0)
            high, low = split(padded.T)
            v_buf[:, part * PAD : (part + 1) * PAD] = high
            v_buf[:, (part + 2) * PAD : (part + 3) * PAD] = low
        copies = (
            pltpu.make_async_copy(u_buf, u_out.at[s], sem_uo),
            pltpu.make_async_copy(v_buf, v_out.at[s], sem_vo),
        )
        for copy in copies:
            copy.start()
        for copy in copies:
            copy.wait()
        return 0

    lax.fori_loop(0, far, far_step, 0)


def prepare(table, near_z, far_ut, far_vt):
    bf16 = jnp.bfloat16
    rank_most = far_ut.shape[2]
    return pl.pallas_call(
        prepare_kernel,
        name="prepare",
        in_specs=[SMEM, ANY, ANY, ANY],
        out_specs=[ANY, ANY, ANY],
        out_shape=[
            jax.ShapeDtypeStruct((NEAR, CLUSTER, 4 * CLUSTER), bf16),
            jax.ShapeDtypeStruct((FAR, PAD, 4 * CLUSTER), bf16),
            jax.ShapeDtypeStruct((FAR, CLUSTER, 4 * PAD), bf16),
        ],
        scratch_shapes=[
            pltpu.VMEM((2, 2, CLUSTER, CLUSTER), jnp.float32),
            pltpu.VMEM((2, CLUSTER, 4 * CLUSTER), bf16),
            pltpu.VMEM((2, rank_most, CLUSTER), jnp.float32),
            pltpu.VMEM((PAD, 4 * CLUSTER), bf16),
            pltpu.VMEM((2, rank_most, CLUSTER), jnp.float32),
            pltpu.VMEM((CLUSTER, 4 * PAD), bf16),
            pltpu.SemaphoreType.DMA((2,)),
            pltpu.SemaphoreType.DMA((2,)),
            pltpu.SemaphoreType.DMA,
            pltpu.SemaphoreType.DMA,
            pltpu.SemaphoreType.DMA,
            pltpu.SemaphoreType.DMA,
        ],
        compiler_params=pltpu.CompilerParams(vmem_limit_bytes=VMEM_LIMIT),
        cost_estimate=pl.CostEstimate(flops=1 << 30, bytes_accessed=36 << 20, transcendentals=0),
    )(table, near_z, far_ut, far_vt)


def parts_of(values):
    high, low = split(values)
    high = jnp.concatenate([high, jnp.concatenate([-high[:, HALF:], high[:, :HALF]], 1)], 0)
    low = jnp.concatenate([low, jnp.concatenate([-low[:, HALF:], low[:, :HALF]], 1)], 0)
    return high, low


def product(left, values):
    high, low = parts_of(values)
    return dot(left, jnp.concatenate([high, high], 0)) + dot(left[:, : left.shape[1] // 2], low)


def apply_kernel(table, x_ref, z_ref, u_ref, v_ref, *rest):
    outs, (total, z_buf, x_buf, u_buf, v_buf, fx_buf, sem_z, sem_x, sem_u, sem_v, sem_fx, sem_out) = rest[:4], rest[4:]
    near, far = table[N_NEAR], table[N_FAR]

    def fetch(s, b):
        return (
            pltpu.make_async_copy(z_ref.at[s], z_buf.at[b], sem_z.at[b]),
            pltpu.make_async_copy(x_ref.at[table[NEAR_A + s]], x_buf.at[b], sem_x.at[b]),
        )

    def fetch_far(s):
        return (
            pltpu.make_async_copy(u_ref.at[s], u_buf.at[s], sem_u.at[s]),
            pltpu.make_async_copy(v_ref.at[s], v_buf.at[s], sem_v.at[s]),
            pltpu.make_async_copy(x_ref.at[table[FAR_A + s]], fx_buf.at[s], sem_fx.at[s]),
        )

    for copy in fetch(0, 0):
        copy.start()

    def far_start(s, _):
        for copy in fetch_far(s):
            copy.start()
        return 0

    lax.fori_loop(0, far, far_start, 0)
    total[...] = jnp.zeros_like(total)

    def near_step(s, _):
        b = lax.rem(s, 2)

        @pl.when(s + 1 < near)
        def _():
            for copy in fetch(s + 1, 1 - b):
                copy.start()

        for copy in fetch(s, b):
            copy.wait()
        total[table[NEAR_B + s]] += product(z_buf[b], x_buf[b])
        return 0

    lax.fori_loop(0, near, near_step, 0)

    def far_step(s, _):
        for copy in fetch_far(s):
            copy.wait()
        coeffs = product(u_buf[s], fx_buf[s])
        total[table[FAR_B + s]] += product(v_buf[s], coeffs)
        return 0

    lax.fori_loop(0, far, far_step, 0)

    copies = []
    for first in range(4):
        for second in range(4):
            place = table[ORDER + first * 4 + second]
            source = total.at[place // 2, pl.ds(pl.multiple_of(lax.rem(place, 2) * (CLUSTER // 2), CLUSTER // 2), CLUSTER // 2)]
            copies.append(pltpu.make_async_copy(source, outs[first].at[second], sem_out.at[first * 4 + second]))
    for copy in copies:
        copy.start()
    for copy in copies:
        copy.wait()


def apply_blocks(table, x, z, u, v, index):
    bf16 = jnp.bfloat16
    return pl.pallas_call(
        apply_kernel,
        name=f"apply_{index}",
        in_specs=[SMEM, ANY, ANY, ANY, ANY],
        out_specs=[ANY] * 4,
        out_shape=[jax.ShapeDtypeStruct((4, CLUSTER // 2, WIDE), jnp.float32)] * 4,
        scratch_shapes=[
            pltpu.VMEM((8, CLUSTER, WIDE), jnp.float32),
            pltpu.VMEM((2, CLUSTER, 4 * CLUSTER), bf16),
            pltpu.VMEM((2, CLUSTER, WIDE), jnp.float32),
            pltpu.VMEM((FAR, PAD, 4 * CLUSTER), bf16),
            pltpu.VMEM((FAR, CLUSTER, 4 * PAD), bf16),
            pltpu.VMEM((FAR, CLUSTER, WIDE), jnp.float32),
            pltpu.SemaphoreType.DMA((2,)),
            pltpu.SemaphoreType.DMA((2,)),
            pltpu.SemaphoreType.DMA((FAR,)),
            pltpu.SemaphoreType.DMA((FAR,)),
            pltpu.SemaphoreType.DMA((FAR,)),
            pltpu.SemaphoreType.DMA((16,)),
        ],
        compiler_params=pltpu.CompilerParams(vmem_limit_bytes=VMEM_LIMIT),
        cost_estimate=pl.CostEstimate(flops=12 << 30, bytes_accessed=32 << 20, transcendentals=0),
    )(table, x, z, u, v)


def scalars(near_pairs, far_pairs, far_ranks, block_counts):
    row_base = lax.axis_index(ROW) * 8
    col_base = lax.axis_index(COL) * 8
    core = lax.axis_index("core")
    index = lax.iota(jnp.int32, 16)
    first, second = index // 4, index % 4
    y = (lax.axis_index("y") + jnp.where(core == 0, first, second)) % 4
    z = (lax.axis_index("zhi") * 2 + lax.axis_index("dir") + jnp.where(core == 0, second, first)) % 4
    order = (z % 2 * 4 + y) * 2 + z // 2
    pieces = [
        block_counts[0],
        near_pairs[:, 0] - row_base,
        near_pairs[:, 1] - col_base,
        far_pairs[:, 0] - row_base,
        far_pairs[:, 1] - col_base,
        far_ranks,
        order,
    ]
    return jnp.concatenate(pieces).astype(jnp.int32)


def shards(cotangent, radiation, near_z, near_pairs, far_ut, far_vt, far_pairs, far_ranks, block_counts):
    first_turn, second_turn = rotations()
    table = scalars(near_pairs, far_pairs, far_ranks, block_counts)
    partial = partial_rhs(cotangent, radiation)
    swap_dir = [(0, 1), (1, 0)]

    gathered = []
    for chunk in range(CHUNKS):
        own = partial[chunk]
        if chunk > 0:
            own = lax.optimization_barrier((own, rhs))[0]
        rhs = own + lax.ppermute(own, "dir", swap_dir)
        gathered.append(lax.all_gather(rhs, COL, axis=0, tiled=False))
    blocks = prepare(table, near_z, far_ut, far_vt)

    results = []
    for chunk in range(CHUNKS):
        mine, *others = apply_blocks(table, gathered[chunk], *blocks, chunk)
        came = [lax.ppermute(part, AXES, turn) for part, turn in zip(others, first_turn)]
        sums = [mine[k] + came[0][k] + came[1][k] + came[2][k] for k in range(4)]
        came = [lax.ppermute(part, AXES, turn) for part, turn in zip(sums[1:], second_turn)]
        results.append(sums[0] + came[0] + came[1] + came[2])
    parts = [r[:, :HALF] for r in results] + [r[:, HALF:] for r in results]
    return jnp.concatenate(parts, axis=1)


def solution(mesh):
    finer = Mesh(mesh.devices.reshape(SIZES), AXES)
    blocks = P(None, AXES, None, None)
    in_specs = (
        P("dir", None),
        P(None, ("y", "zhi", "x", "core"), "dir"),
        blocks,
        P(AXES, None),
        blocks,
        blocks,
        P(AXES, None),
        P(AXES),
        P(AXES, None),
    )
    out_specs = P(("x", "core", "dir", "y", "zhi"), None)
    return jax.shard_map(shards, mesh=finer, in_specs=in_specs, out_specs=out_specs, check_vma=False)
```

time: 435 us -> 170 us (0.39); the launches traced: 430 us -> 170 us
  blocking collectives: 132 us -> 0 us
  waiting for transfers between devices: 158 us -> 72 us
  matrix products: 79 us -> 0 us
  starting transfers between devices: 0.09 us -> 49.3 us
  Pallas kernels: 0 us -> 23.1 us
  loops' own time: 17.5 us -> 0 us
  other arithmetic: 18.6 us -> 7.02 us
  local copies, waits for them, and re-layouts: 11.6 us -> 5.11 us
    all_to_all x2 -> x0, blocking collectives: 132 us -> none  [the longest x1 104 us: sum_at_owner(): lax.all_to_all(parts, axis, split_axis=0, concat_axis=0, tiled=True)]
    reduce_scatter x2 -> x0, waiting for transfers between devices: 107 us -> none  [summed_rows(): shard = lax.psum_scatter(shard, axis, scatter_dimension=dim, tiled=True)]
    dot_general x22 -> x0, matrix products: 79 us -> none  [the longest x18 70.7 us: transposed_dot(): lax.dot_general(left, right, (((0,), (0,)), ((), ())), precision=lax.Prec...]
    ppermute x0 -> x14, starting transfers between devices: none -> 49.3 us  [the longest x12 45.4 us: shards(): lax.ppermute(part, AXES, turn)]
    ppermute x0 -> x14, waiting for transfers between devices: none -> 47.4 us  [the longest x12 23.9 us: shards(): lax.ppermute(part, AXES, turn)]
    all_gather x1 -> x2, waiting for transfers between devices: 51.1 us -> 24.5 us  [shards(): gathered.append(lax.all_gather(rhs, COL, axis=0, tiled=False))]
    pallas_call x0 -> x4, Pallas kernels: none -> 23.1 us  [the longest x2 13.9 us: apply_blocks(): pl.pallas_call(apply_kernel, name=f'apply_{index}', in_specs=[SMEM, ANY,...]
    another operation x2 -> x0, loops' own time: 17.5 us -> none  [the longest x1 15 us: shards(): partial_out = lax.fori_loop(0, block_counts[0, 0], near_step, partial_out)]
  transfers between devices with their start and end apart: 3 -> 16, of which waited for: 3 -> 8; matrix products, arithmetic and copies ran while one was open for 0% -> 3% of each run, Pallas kernels for 0% -> 12%
where the time goes in v1:
time: 170 us
  waiting for transfers between devices  72 us (42%)
  starting transfers between devices  49.3 us (29%)
  Pallas kernels  23.1 us (14%)
  between operations  13.6 us (8%)
  other arithmetic  7.02 us (4%)
  local copies, waits for them, and re-layouts  5.11 us (3%)
    ppermute x12, starting transfers between devices, shards(): lax.ppermute(part, AXES, turn)  45.4 us
    all_gather x2, waiting for transfers between devices, shards(): gathered.append(lax.all_gather(rhs, COL, axis=0, tiled=False))  24.5 us
    ppermute x12, waiting for transfers between devices, shards(): lax.ppermute(part, AXES, turn)  23.9 us
    ppermute x2, waiting for transfers between devices, shards(): rhs = own + lax.ppermute(own, 'dir', swap_dir)  23.5 us
    pallas_call x2, Pallas kernels, apply_blocks(): pl.pallas_call(apply_kernel, name=f'apply_{index}', in_specs=[SMEM, ANY,...  13.9 us
    pallas_call x1, Pallas kernels, prepare(): pl.pallas_call(prepare_kernel, name='prepare', in_specs=[SMEM, ANY, ANY,...  7.29 us
    unnamed x20, local copies, waits for them, and re-layouts  4.99 us
    ppermute x2, starting transfers between devices, shards(): rhs = own + lax.ppermute(own, 'dir', swap_dir)  3.9 us
  transfers between devices with their start and end apart: 16, of which 8 were waited for; matrix products, arithmetic and copies ran while one was open for 3% of the time, Pallas kernels for 12%

profile of v1, /device:TPU:0, one launch (start us, length us, event | category | flops | bytes accessed | tf_op | source)
XLA Modules:
  0.0 170.2 jit_solution(10391677971104928747)
XLA Ops:
  6.5 1.6 copy-done.3
  8.1 1.2 copy-done.5
  9.4 2.0 %rhs.1 = (f32[512,256]{1,0:T(8,128)S(1)}, f32[512,256]{1,0:T(8,128)S(1)}) custom-call(bf16[1024,512]{1,0:T(8,128)(2,1)S(1)} %copy-done.5, bf16[2,512,1024]{2,1,0:T(8,128)(2,1)S(1)} %copy-done.3), custom_call_target="tpu_custom_call" | custom-call | flops 1073741824 | bytes 4194304 | tf_op jit(solution)/shard_map/rhs/pallas_call | solution.py:75
  11.4 0.0 copy-start.2
  11.4 0.8 copy-done.2
  12.2 0.0 copy-start
  12.2 0.0 copy-start.1
  12.2 2.1 %collective-permute-start = (f32[512,256]{1,0:T(8,128)S(1)}, f32[512,256]{1,0:T(8,128)S(1)}, u32[]{:S(2)}, u32[]{:S(2)}) collective-permute-start(f32[512,256]{1,0:T(8,128)S(1)} %get-tuple-element.19), channel_id=1, source_target_pairs={{0,64},{64,0},{1,65},{65,1},{2,66},{66,2},{3,67},{67,3},{4,68},{68... | collective-permute-start | bytes 1572872 | tf_op jit(solution)/shard_map/ppermute | solution.py:330
  14.3 11.9 %collective-permute-done = f32[512,256]{1,0:T(8,128)S(1)} collective-permute-done((f32[512,256]{1,0:T(8,128)S(1)}, f32[512,256]{1,0:T(8,128)S(1)}, u32[]{:S(2)}, u32[]{:S(2)}) %collective-permute-start) | collective-permute-done | bytes 524320 | tf_op jit(solution)/shard_map/ppermute | solution.py:330
  26.2 0.9 add.198
  27.1 0.0 all-gather.5.cloned.1.call-update
  27.1 0.0 all-gather.7.cloned.1.call-start
  27.1 1.8 %collective-permute-start.7 = (f32[512,256]{1,0:T(8,128)}, f32[512,256]{1,0:T(8,128)S(1)}, u32[]{:S(2)}, u32[]{:S(2)}) collective-permute-start(f32[512,256]{1,0:T(8,128)} %copy-done.2), channel_id=1, source_target_pairs={{0,64},{64,0},{1,65},{65,1},{2,66},{66,2},{3,67},{67,3},{4,68},{68... | collective-permute-start | bytes 1572872 | tf_op jit(solution)/shard_map/ppermute | solution.py:330
  29.0 11.5 %collective-permute-done.7 = f32[512,256]{1,0:T(8,128)S(1)} collective-permute-done((f32[512,256]{1,0:T(8,128)}, f32[512,256]{1,0:T(8,128)S(1)}, u32[]{:S(2)}, u32[]{:S(2)}) %collective-permute-start.7) | collective-permute-done | bytes 524320 | tf_op jit(solution)/shard_map/ppermute | solution.py:330
  40.5 1.9 %add.218 = f32[512,256]{1,0:T(8,128)} add(f32[512,256]{1,0:T(8,128)} %copy-done.2, f32[512,256]{1,0:T(8,128)S(1)} %collective-permute-done.7) | non-fusion elementwise | flops 131072 | bytes 1572864 | tf_op jit(solution)/shard_map/add | solution.py:330
  42.4 0.0 all-gather.7.cloned.1.call-update
  42.6 0.1 concatenate.6.table
  42.6 7.3 %prepare.1 = (bf16[8,512,2048]{2,1,0:T(8,128)(2,1)}, bf16[4,128,2048]{2,1,0:T(8,128)(2,1)S(1)}, bf16[4,512,512]{2,1,0:T(8,128)(2,1)}) custom-call(s32[46]{0:T(128)S(1)} %concatenate.6.table, f32[2,8,512,512]{3,2,1,0:T(8,128)} %z_ref.1, f32[2,4,96,512]{3,2,1,0:T(8,128)S(1)} %copy-done, f32[2,4,96,512]{3,2,1,0:T(8,128)S(1)} %copy-done.1), custom_call_target="tpu_custom_call" | custom-call | flops 1073741824 | bytes 37748736 | tf_op jit(solution)/shard_map/prepare/pallas_call | solution.py:166
  49.9 1.4 copy-done.4
  51.3 10.2 %all-gather.5.cloned.1.call-done = f32[4096,256]{1,0:T(8,128)} async-done(((f32[512,256]{1,0:T(8,128)}), f32[4096,256]{1,0:T(8,128)}) %all-gather.5.cloned.1.call-update) | async-done | bytes 4194320 | tf_op jit(solution)/shard_map/all_gather | solution.py:331
  61.5 7.4 %apply_0.1 = (f32[4,256,256]{2,1,0:T(8,128)S(1)}, f32[4,256,256]{2,1,0:T(8,128)S(1)}, f32[4,256,256]{2,1,0:T(8,128)S(1)}, f32[4,256,256]{2,1,0:T(8,128)}) custom-call(s32[46]{0:T(128)S(1)} %concatenate.6.table, f32[8,512,256]{2,1,0:T(8,128)} %bitcast.41, bf16[8,512,2048]{2,1,0:T(8,128)(2,1)} %get-tuple-element.20.z_ref, bf16[4,128,2048]{2,1,0:T(8,128)(2,1)} %copy-done.4, ...), custom_call_target="tpu_custom_call" | custom-call | flops 12884901888 | bytes 33554432 | tf_op jit(solution)/shard_map/apply_0/pallas_call | solution.py:273
  68.9 11.2 %collective-permute-start.3 = (f32[4,256,256]{2,1,0:T(8,128)}, f32[4,256,256]{2,1,0:T(8,128)}, u32[]{:S(2)}, u32[]{:S(2)}) collective-permute-start(f32[4,256,256]{2,1,0:T(8,128)} %get-tuple-element.26), channel_id=1, source_target_pairs={{0,48},{1,73},{2,50},{3,75},{4,52},{5,77},{6,54},{7,79},{8,56},{9,... | collective-permute-start | bytes 3145736 | tf_op jit(solution)/shard_map/ppermute | solution.py:337
  80.1 0.9 collective-permute-start.2
  80.9 0.1 collective-permute-start.1
  81.0 14.3 %all-gather.7.cloned.1.call-done = f32[4096,256]{1,0:T(8,128)} async-done(((f32[512,256]{1,0:T(8,128)}), f32[4096,256]{1,0:T(8,128)}) %all-gather.7.cloned.1.call-update) | async-done | bytes 4194320 | tf_op jit(solution)/shard_map/all_gather | solution.py:331
  95.3 6.5 %apply_1.1 = (f32[4,256,256]{2,1,0:T(8,128)S(1)}, f32[4,256,256]{2,1,0:T(8,128)S(1)}, f32[4,256,256]{2,1,0:T(8,128)S(1)}, f32[4,256,256]{2,1,0:T(8,128)S(1)}) custom-call(s32[46]{0:T(128)S(1)} %concatenate.6.table, f32[8,512,256]{2,1,0:T(8,128)} %bitcast.40, bf16[8,512,2048]{2,1,0:T(8,128)(2,1)} %get-tuple-element.20.z_ref, bf16[4,128,2048]{2,1,0:T(8,128)(2,1)} %copy-done.4, ...), custom_call_target="tpu_custom_call" | custom-call | flops 12884901888 | bytes 33554432 | tf_op jit(solution)/shard_map/apply_1/pallas_call | solution.py:273
  101.9 11.0 %collective-permute-start.10 = (f32[4,256,256]{2,1,0:T(8,128)S(1)}, f32[4,256,256]{2,1,0:T(8,128)S(1)}, u32[]{:S(2)}, u32[]{:S(2)}) collective-permute-start(f32[4,256,256]{2,1,0:T(8,128)S(1)} %get-tuple-element.32), channel_id=1, source_target_pairs={{0,48},{1,73},{2,50},{3,75},{4,52},{5,77},{6,54},{7,79},{8,56},{9,... | collective-permute-start | bytes 3145736 | tf_op jit(solution)/shard_map/ppermute | solution.py:337
  112.9 0.8 collective-permute-start.9
  113.7 0.0 collective-permute-done.3
  113.7 0.1 collective-permute-start.8
  113.8 0.0 collective-permute-done.2
  113.8 0.0 collective-permute-done.1
  113.8 1.8 %fusion.9 = (f32[256,256]{1,0:T(8,128)S(1)}, f32[256,256]{1,0:T(8,128)S(1)}, f32[256,256]{1,0:T(8,128)S(1)}) fusion(f32[4,256,256]{2,1,0:T(8,128)} %collective-permute-done.3, f32[4,256,256]{2,1,0:T(8,128)} %collective-permute-done.2, f32[4,256,256]{2,1,0:T(8,128)} %collective-permute-done.1, f32[4,256,256]{2,1,0:T(8,128)S(1)} %get-tuple-element.23), kind=kLoop, calls=%fused_computation.29 | loop fusion | flops 589824 | bytes 3932160 | tf_op jit(solution)/shard_map/add | solution.py:338
  115.6 0.1 collective-permute-start.6
  115.7 8.7 %collective-permute-start.5 = (f32[256,256]{1,0:T(8,128)S(1)}, f32[256,256]{1,0:T(8,128)S(1)}, u32[]{:S(2)}, u32[]{:S(2)}) collective-permute-start(f32[256,256]{1,0:T(8,128)S(1)} %get-tuple-element.35), channel_id=1, source_target_pairs={{0,8},{1,33},{2,10},{3,35},{4,12},{5,37},{6,14},{7,39},{8,0},{9,41... | collective-permute-start | bytes 786440 | tf_op jit(solution)/shard_map/ppermute | solution.py:339
  124.4 17.6 %collective-permute-done.10 = f32[4,256,256]{2,1,0:T(8,128)S(1)} collective-permute-done((f32[4,256,256]{2,1,0:T(8,128)S(1)}, f32[4,256,256]{2,1,0:T(8,128)S(1)}, u32[]{:S(2)}, u32[]{:S(2)}) %collective-permute-start.10) | collective-permute-done | bytes 1048608 | tf_op jit(solution)/shard_map/ppermute | solution.py:337
  142.0 5.5 %collective-permute-start.4 = (f32[256,256]{1,0:T(8,128)S(1)}, f32[256,256]{1,0:T(8,128)S(1)}, u32[]{:S(2)}, u32[]{:S(2)}) collective-permute-start(f32[256,256]{1,0:T(8,128)S(1)} %get-tuple-element.33), channel_id=1, source_target_pairs={{0,64},{1,17},{2,66},{3,19},{4,68},{5,21},{6,70},{7,23},{8,72},{9,... | collective-permute-start | bytes 786440 | tf_op jit(solution)/shard_map/ppermute | solution.py:339
  147.5 0.0 collective-permute-done.9
  147.5 0.0 collective-permute-done.8
  147.5 0.2 fusion.2
  147.7 0.1 collective-permute-start.13
  147.8 6.9 %collective-permute-start.12 = (f32[256,256]{1,0:T(8,128)S(1)}, f32[256,256]{1,0:T(8,128)S(1)}, u32[]{:S(2)}, u32[]{:S(2)}) collective-permute-start(f32[256,256]{1,0:T(8,128)S(1)} %get-tuple-element.38), channel_id=1, source_target_pairs={{0,8},{1,33},{2,10},{3,35},{4,12},{5,37},{6,14},{7,39},{8,0},{9,41... | collective-permute-start | bytes 786440 | tf_op jit(solution)/shard_map/ppermute | solution.py:339
  154.8 1.2 fusion.13
  156.0 1.0 collective-permute-done.13
  157.0 2.1 %collective-permute-done.12 = f32[256,256]{1,0:T(8,128)S(1)} collective-permute-done((f32[256,256]{1,0:T(8,128)S(1)}, f32[256,256]{1,0:T(8,128)S(1)}, u32[]{:S(2)}, u32[]{:S(2)}) %collective-permute-start.12) | collective-permute-done | bytes 262176 | tf_op jit(solution)/shard_map/ppermute | solution.py:339
  159.1 3.2 %collective-permute-done.11 = f32[256,256]{1,0:T(8,128)S(1)} collective-permute-done((f32[256,256]{1,0:T(8,128)S(1)}, f32[256,256]{1,0:T(8,128)S(1)}, u32[]{:S(2)}, u32[]{:S(2)}) %collective-permute-start.11) | collective-permute-done | bytes 262176 | tf_op jit(solution)/shard_map/ppermute | solution.py:339
  162.3 0.1 fusion.6
  162.5 0.9 pad_maximum_fusion
  (23 shorter events, 0.1 us)
Async XLA Ops:
  6.5 55.0 %all-gather.5.cloned.1.call-start = ((), (), s32[]{:S(2)}) async-start(), calls=%async_computation | async-start | bytes 4718592 | tf_op jit(solution)/shard_map/all_gather | solution.py:331
  6.5 1.6 copy-start.3
  8.1 1.2 copy-start.5
  11.4 0.8 copy-start.2
  12.1 30.3 %copy-start.6 = (s32[8,2]{0,1:T(2,128)S(1)}, s32[8,2]{0,1:T(2,128)}, u32[]{:S(2)}) copy-start(s32[8,2]{0,1:T(2,128)} %param.12) | copy-start | bytes 196
  12.2 30.4 %copy-start.7 = (s32[4,2]{0,1:T(2,128)S(1)}, s32[4,2]{0,1:T(2,128)}, u32[]{:S(2)}) copy-start(s32[4,2]{0,1:T(2,128)} %param.15) | copy-start | bytes 100
  12.2 30.4 %copy-start.8 = (s32[1,2]{1,0:T(1,128)S(1)}, s32[1,2]{1,0:T(1,128)}, u32[]{:S(2)}) copy-start(s32[1,2]{1,0:T(1,128)} %param.17) | copy-start | bytes 28
  12.2 30.4 %copy-start.9 = (s32[4]{0:T(128)S(1)}, s32[4]{0:T(128)}, u32[]{:S(2)}) copy-start(s32[4]{0:T(128)} %param.16) | copy-start | bytes 52
  12.2 30.5 %copy-start = (f32[2,4,96,512]{3,2,1,0:T(8,128)S(1)}, f32[2,4,96,512]{3,2,1,0:T(8,128)}, u32[]{:S(2)}) copy-start(f32[2,4,96,512]{3,2,1,0:T(8,128)} %u_ref.1) | copy-start | bytes 4718596
  12.2 30.5 %copy-start.1 = (f32[2,4,96,512]{3,2,1,0:T(8,128)S(1)}, f32[2,4,96,512]{3,2,1,0:T(8,128)}, u32[]{:S(2)}) copy-start(f32[2,4,96,512]{3,2,1,0:T(8,128)} %v_ref.1) | copy-start | bytes 4718596
  12.2 14.0 %collective-permute-start = (f32[512,256]{1,0:T(8,128)S(1)}, f32[512,256]{1,0:T(8,128)S(1)}, u32[]{:S(2)}, u32[]{:S(2)}) collective-permute-start(f32[512,256]{1,0:T(8,128)S(1)} %get-tuple-element.19), channel_id=1, source_target_pairs={{0,64},{64,0},{1,65},{65,1},{2,66},{66,2},{3,67},{67,3},{4,68},{68... | collective-permute-start | bytes 1572872 | tf_op jit(solution)/shard_map/ppermute | solution.py:330
  27.1 68.2 %all-gather.7.cloned.1.call-start = ((), (), s32[]{:S(2)}) async-start(), calls=%async_computation.1 | async-start | bytes 4718592 | tf_op jit(solution)/shard_map/all_gather | solution.py:331
  27.1 13.4 %collective-permute-start.7 = (f32[512,256]{1,0:T(8,128)}, f32[512,256]{1,0:T(8,128)S(1)}, u32[]{:S(2)}, u32[]{:S(2)}) collective-permute-start(f32[512,256]{1,0:T(8,128)} %copy-done.2), channel_id=1, source_target_pairs={{0,64},{64,0},{1,65},{65,1},{2,66},{66,2},{3,67},{67,3},{4,68},{68... | collective-permute-start | bytes 1572872 | tf_op jit(solution)/shard_map/ppermute | solution.py:330
  49.9 1.4 copy-start.4
  68.9 44.8 %collective-permute-start.3 = (f32[4,256,256]{2,1,0:T(8,128)}, f32[4,256,256]{2,1,0:T(8,128)}, u32[]{:S(2)}, u32[]{:S(2)}) collective-permute-start(f32[4,256,256]{2,1,0:T(8,128)} %get-tuple-element.26), channel_id=1, source_target_pairs={{0,48},{1,73},{2,50},{3,75},{4,52},{5,77},{6,54},{7,79},{8,56},{9,... | collective-permute-start | bytes 3145736 | tf_op jit(solution)/shard_map/ppermute | solution.py:337
  80.1 33.8 %collective-permute-start.2 = (f32[4,256,256]{2,1,0:T(8,128)S(1)}, f32[4,256,256]{2,1,0:T(8,128)}, u32[]{:S(2)}, u32[]{:S(2)}) collective-permute-start(f32[4,256,256]{2,1,0:T(8,128)S(1)} %get-tuple-element.25), channel_id=1, source_target_pairs={{0,32},{1,9},{2,34},{3,11},{4,36},{5,13},{6,38},{7,15},{8,40},{9,1... | collective-permute-start | bytes 3145736 | tf_op jit(solution)/shard_map/ppermute | solution.py:337
  80.9 32.9 %collective-permute-start.1 = (f32[4,256,256]{2,1,0:T(8,128)S(1)}, f32[4,256,256]{2,1,0:T(8,128)}, u32[]{:S(2)}, u32[]{:S(2)}) collective-permute-start(f32[4,256,256]{2,1,0:T(8,128)S(1)} %get-tuple-element.24), channel_id=1, source_target_pairs={{0,16},{1,65},{2,18},{3,67},{4,20},{5,69},{6,22},{7,71},{8,24},{9,... | collective-permute-start | bytes 3145736 | tf_op jit(solution)/shard_map/ppermute | solution.py:337
  101.9 40.2 %collective-permute-start.10 = (f32[4,256,256]{2,1,0:T(8,128)S(1)}, f32[4,256,256]{2,1,0:T(8,128)S(1)}, u32[]{:S(2)}, u32[]{:S(2)}) collective-permute-start(f32[4,256,256]{2,1,0:T(8,128)S(1)} %get-tuple-element.32), channel_id=1, source_target_pairs={{0,48},{1,73},{2,50},{3,75},{4,52},{5,77},{6,54},{7,79},{8,56},{9,... | collective-permute-start | bytes 3145736 | tf_op jit(solution)/shard_map/ppermute | solution.py:337
  112.9 34.6 %collective-permute-start.9 = (f32[4,256,256]{2,1,0:T(8,128)S(1)}, f32[4,256,256]{2,1,0:T(8,128)S(1)}, u32[]{:S(2)}, u32[]{:S(2)}) collective-permute-start(f32[4,256,256]{2,1,0:T(8,128)S(1)} %get-tuple-element.31), channel_id=1, source_target_pairs={{0,32},{1,9},{2,34},{3,11},{4,36},{5,13},{6,38},{7,15},{8,40},{9,1... | collective-permute-start | bytes 3145736 | tf_op jit(solution)/shard_map/ppermute | solution.py:337
  113.7 33.8 %collective-permute-start.8 = (f32[4,256,256]{2,1,0:T(8,128)S(1)}, f32[4,256,256]{2,1,0:T(8,128)S(1)}, u32[]{:S(2)}, u32[]{:S(2)}) collective-permute-start(f32[4,256,256]{2,1,0:T(8,128)S(1)} %get-tuple-element.30), channel_id=1, source_target_pairs={{0,16},{1,65},{2,18},{3,67},{4,20},{5,69},{6,22},{7,71},{8,24},{9,... | collective-permute-start | bytes 3145736 | tf_op jit(solution)/shard_map/ppermute | solution.py:337
  115.6 39.1 %collective-permute-start.6 = (f32[256,256]{1,0:T(8,128)S(1)}, f32[256,256]{1,0:T(8,128)S(1)}, u32[]{:S(2)}, u32[]{:S(2)}) collective-permute-start(f32[256,256]{1,0:T(8,128)S(1)} %get-tuple-element.34), channel_id=1, source_target_pairs={{0,72},{1,49},{2,74},{3,51},{4,76},{5,53},{6,78},{7,55},{8,64},{9,... | collective-permute-start | bytes 786440 | tf_op jit(solution)/shard_map/ppermute | solution.py:339
  115.7 39.0 %collective-permute-start.5 = (f32[256,256]{1,0:T(8,128)S(1)}, f32[256,256]{1,0:T(8,128)S(1)}, u32[]{:S(2)}, u32[]{:S(2)}) collective-permute-start(f32[256,256]{1,0:T(8,128)S(1)} %get-tuple-element.35), channel_id=1, source_target_pairs={{0,8},{1,33},{2,10},{3,35},{4,12},{5,37},{6,14},{7,39},{8,0},{9,41... | collective-permute-start | bytes 786440 | tf_op jit(solution)/shard_map/ppermute | solution.py:339
  142.0 12.7 %collective-permute-start.4 = (f32[256,256]{1,0:T(8,128)S(1)}, f32[256,256]{1,0:T(8,128)S(1)}, u32[]{:S(2)}, u32[]{:S(2)}) collective-permute-start(f32[256,256]{1,0:T(8,128)S(1)} %get-tuple-element.33), channel_id=1, source_target_pairs={{0,64},{1,17},{2,66},{3,19},{4,68},{5,21},{6,70},{7,23},{8,72},{9,... | collective-permute-start | bytes 786440 | tf_op jit(solution)/shard_map/ppermute | solution.py:339
  147.7 9.3 %collective-permute-start.13 = (f32[256,256]{1,0:T(8,128)S(1)}, f32[256,256]{1,0:T(8,128)S(1)}, u32[]{:S(2)}, u32[]{:S(2)}) collective-permute-start(f32[256,256]{1,0:T(8,128)S(1)} %get-tuple-element.37), channel_id=1, source_target_pairs={{0,72},{1,49},{2,74},{3,51},{4,76},{5,53},{6,78},{7,55},{8,64},{9,... | collective-permute-start | bytes 786440 | tf_op jit(solution)/shard_map/ppermute | solution.py:339
  147.8 11.3 %collective-permute-start.12 = (f32[256,256]{1,0:T(8,128)S(1)}, f32[256,256]{1,0:T(8,128)S(1)}, u32[]{:S(2)}, u32[]{:S(2)}) collective-permute-start(f32[256,256]{1,0:T(8,128)S(1)} %get-tuple-element.38), channel_id=1, source_target_pairs={{0,8},{1,33},{2,10},{3,35},{4,12},{5,37},{6,14},{7,39},{8,0},{9,41... | collective-permute-start | bytes 786440 | tf_op jit(solution)/shard_map/ppermute | solution.py:339
  154.7 7.6 %collective-permute-start.11 = (f32[256,256]{1,0:T(8,128)S(1)}, f32[256,256]{1,0:T(8,128)S(1)}, u32[]{:S(2)}, u32[]{:S(2)}) collective-permute-start(f32[256,256]{1,0:T(8,128)S(1)} %get-tuple-element.36), channel_id=1, source_target_pairs={{0,64},{1,17},{2,66},{3,19},{4,68},{5,21},{6,70},{7,23},{8,72},{9,... | collective-permute-start | bytes 786440 | tf_op jit(solution)/shard_map/ppermute | solution.py:339
Sparse Core Ops, SparseCore 0:
  27.2 34.2 all-gather.4
  63.2 32.0 all-gather.6

commit v2 on v1

v2 whole, which is shorter than its diff:
```python
import functools

import jax
import jax.numpy as jnp
from jax import lax
from jax.experimental import pallas as pl
from jax.experimental.pallas import tpu as pltpu
from jax.sharding import Mesh
from jax.sharding import PartitionSpec as P

AXES = ("dir", "y", "zhi", "x", "core")
ROW = ("y", "zhi")
COL = ("x", "core")
SIZES = (2, 4, 2, 4, 2)
CHUNKS = 2
CLUSTER = 512
HALF = 128
WIDE = 2 * HALF
PAD = 128
NEAR = 8
FAR = 4
VMEM_LIMIT = 60 << 20
SCOPED = 14 << 20

ANY = pl.BlockSpec(memory_space=pl.ANY)
SMEM = pl.BlockSpec(memory_space=pltpu.SMEM)
VMEM = pl.BlockSpec(memory_space=pltpu.VMEM)
TOKEN = jax.ShapeDtypeStruct((8, 128), jnp.float32)

N_NEAR, N_FAR, NEAR_A, NEAR_B, FAR_A, FAR_B, RANK, ORDER, CORE, X = 0, 1, 2, 10, 18, 22, 26, 30, 46, 47


def split(values):
    high = values.astype(jnp.bfloat16)
    low = (values - high.astype(jnp.float32)).astype(jnp.bfloat16)
    return high, low


def dot(left, right):
    return jnp.dot(left, right, preferred_element_type=jnp.float32)


def rings(first):
    def place(y, z, core):
        return ((z % 2 * 4 + y) * 2 + z // 2) * 2 + core

    round_y, round_z = (0, 1) if first else (1, 0)
    along_y = [[place(y, z, round_y) for y in range(4)] for z in range(4)]
    along_z = [[place(y, z, round_z) for z in range(4)] for y in range(4)]
    return along_y + along_z


def rhs_kernel(cot_ref, rad_ref, *out_refs):
    width = cot_ref.shape[1] // 2
    for chunk, out_ref in enumerate(out_refs):
        re = cot_ref[:, chunk * HALF : (chunk + 1) * HALF]
        im = cot_ref[:, width + chunk * HALF : width + (chunk + 1) * HALF]
        out_ref[...] = dot(rad_ref[0], jnp.concatenate([re, im], 1)) + dot(
            rad_ref[1], jnp.concatenate([-im, re], 1)
        )


def partial_rhs(cotangent, radiation):
    _, rows, dirs = radiation.shape
    tile = 128
    return pl.pallas_call(
        rhs_kernel,
        name="rhs",
        grid=(rows // tile,),
        in_specs=[
            pl.BlockSpec(cotangent.shape, lambda i: (0, 0)),
            pl.BlockSpec((2, tile, dirs), lambda i: (0, i, 0)),
        ],
        out_specs=[pl.BlockSpec((tile, WIDE), lambda i: (i, 0))] * CHUNKS,
        out_shape=[jax.ShapeDtypeStruct((rows, WIDE), jnp.float32)] * CHUNKS,
        compiler_params=pltpu.CompilerParams(vmem_limit_bytes=VMEM_LIMIT),
        cost_estimate=pl.CostEstimate(flops=1 << 30, bytes_accessed=4 << 20, transcendentals=0),
    )(cotangent, radiation)


def prepare_near_kernel(first, table, z_ref, out_ref, token, z_in, sem_in):
    slots, buffers = out_ref.shape[0], z_in.shape[0]
    token[...] = jnp.zeros_like(token)
    live = jnp.clip(table[N_NEAR] - first, 0, slots)

    def fetch(s):
        b = lax.rem(s, buffers)
        return pltpu.make_async_copy(z_ref.at[:, first + s], z_in.at[b], sem_in.at[b])

    for ahead in range(buffers - 1):

        @pl.when(ahead < live)
        def _():
            fetch(ahead).start()

    def near_step(s, _):
        @pl.when(s + buffers - 1 < live)
        def _():
            fetch(s + buffers - 1).start()

        fetch(s).wait()
        for part in range(2):
            high, low = split(z_in[lax.rem(s, buffers), part].T)
            out_ref[s, :, part * CLUSTER : (part + 1) * CLUSTER] = high
            out_ref[s, :, (part + 2) * CLUSTER : (part + 3) * CLUSTER] = low
        return 0

    lax.fori_loop(0, live, near_step, 0)


def prepare_near(table, near_z, first, slots):
    buffers = 3
    return pl.pallas_call(
        functools.partial(prepare_near_kernel, first),
        name=f"prepare_near_{first}",
        in_specs=[SMEM, ANY],
        out_specs=[VMEM, VMEM],
        out_shape=[pltpu.VMEM((slots, CLUSTER, 4 * CLUSTER), jnp.bfloat16), TOKEN],
        scratch_shapes=[
            pltpu.VMEM((buffers, 2, CLUSTER, CLUSTER), jnp.float32),
            pltpu.SemaphoreType.DMA((buffers,)),
        ],
        compiler_params=pltpu.CompilerParams(vmem_limit_bytes=SCOPED),
        cost_estimate=pl.CostEstimate(flops=1 << 28, bytes_accessed=slots << 21, transcendentals=0),
    )(table, near_z)


def prepare_far_kernel(table, u_ref, v_ref, u_out, v_out, token, u_in, v_in, sem_u, sem_v):
    token[...] = jnp.zeros_like(token)
    far, rank_most = table[N_FAR], u_in.shape[2]

    def fetch(s):
        return (
            pltpu.make_async_copy(u_ref.at[:, s], u_in.at[s], sem_u.at[s]),
            pltpu.make_async_copy(v_ref.at[:, s], v_in.at[s], sem_v.at[s]),
        )

    def start(s, _):
        for copy in fetch(s):
            copy.start()
        return 0

    lax.fori_loop(0, far, start, 0)

    def far_step(s, _):
        for copy in fetch(s):
            copy.wait()
        live = lax.broadcasted_iota(jnp.int32, (PAD, CLUSTER), 0) < table[RANK + s]
        fill = jnp.zeros((PAD - rank_most, CLUSTER), jnp.float32)
        for part in range(2):
            padded = jnp.concatenate([u_in[s, part], fill], 0)
            high, low = split(jnp.where(live, padded, 0.0))
            u_out[s, :, part * CLUSTER : (part + 1) * CLUSTER] = high
            u_out[s, :, (part + 2) * CLUSTER : (part + 3) * CLUSTER] = low
            padded = jnp.concatenate([v_in[s, part], fill], 0)
            high, low = split(padded.T)
            v_out[s, :, part * PAD : (part + 1) * PAD] = high
            v_out[s, :, (part + 2) * PAD : (part + 3) * PAD] = low
        return 0

    lax.fori_loop(0, far, far_step, 0)


def prepare_far(table, far_ut, far_vt):
    rank_most = far_ut.shape[2]
    return pl.pallas_call(
        prepare_far_kernel,
        name="prepare_far",
        in_specs=[SMEM, ANY, ANY],
        out_specs=[VMEM, VMEM, VMEM],
        out_shape=[
            pltpu.VMEM((FAR, PAD, 4 * CLUSTER), jnp.bfloat16),
            pltpu.VMEM((FAR, CLUSTER, 4 * PAD), jnp.bfloat16),
            TOKEN,
        ],
        scratch_shapes=[
            pltpu.VMEM((FAR, 2, rank_most, CLUSTER), jnp.float32),
            pltpu.VMEM((FAR, 2, rank_most, CLUSTER), jnp.float32),
            pltpu.SemaphoreType.DMA((FAR,)),
            pltpu.SemaphoreType.DMA((FAR,)),
        ],
        compiler_params=pltpu.CompilerParams(vmem_limit_bytes=SCOPED),
        cost_estimate=pl.CostEstimate(flops=1 << 28, bytes_accessed=4 << 20, transcendentals=0),
    )(table, far_ut, far_vt)


def parts_of(values):
    high, low = split(values)
    high = jnp.concatenate([high, jnp.concatenate([-high[:, HALF:], high[:, :HALF]], 1)], 0)
    low = jnp.concatenate([low, jnp.concatenate([-low[:, HALF:], low[:, :HALF]], 1)], 0)
    return high, low


def product(left, values):
    high, low = parts_of(values)
    return dot(left, jnp.concatenate([high, high], 0)) + dot(left[:, : left.shape[1] // 2], low)


def apply_kernel(table, *refs):
    held, (za_ref, zb_ref, u_ref, v_ref, out_ref, x_buf, fx_buf, sem_x, sem_fx) = refs[:8], refs[8:]
    near, far = table[N_NEAR], table[N_FAR]
    slots = za_ref.shape[0]

    def fetch(cluster, buf, sem):
        steps = lax.rem(table[X] + 4 - cluster // 2, 4)
        other = jnp.where(lax.rem(cluster, 2) == table[CORE], 0, 4)
        for place, ref in enumerate(held):

            @pl.when(steps + other == place)
            def _():
                pltpu.make_async_copy(ref, buf, sem).start()

    def fetched(buf, sem):
        pltpu.make_async_copy(held[0], buf, sem).wait()

    def add(cluster, term):
        for half in range(2):
            rows = CLUSTER // 2
            out_ref[table[ORDER + cluster * 2 + half]] += term[half * rows : (half + 1) * rows]

    fetch(table[NEAR_A], x_buf.at[0], sem_x.at[0])

    def far_start(s, _):
        fetch(table[FAR_A + s], fx_buf.at[s], sem_fx.at[s])
        return 0

    lax.fori_loop(0, far, far_start, 0)
    out_ref[...] = jnp.zeros_like(out_ref)

    def near_steps(z_ref, first, last):
        def near_step(s, _):
            b = lax.rem(s, 2)

            @pl.when(s + 1 < near)
            def _():
                fetch(table[NEAR_A + s + 1], x_buf.at[1 - b], sem_x.at[1 - b])

            fetched(x_buf.at[b], sem_x.at[b])
            add(table[NEAR_B + s], product(z_ref[s - first], x_buf[b]))
            return 0

        lax.fori_loop(first, last, near_step, 0)

    near_steps(za_ref, 0, jnp.minimum(near, slots))
    near_steps(zb_ref, slots, near)

    def far_step(s, _):
        fetched(fx_buf.at[s], sem_fx.at[s])
        add(table[FAR_B + s], product(v_ref[s], product(u_ref[s], fx_buf[s])))
        return 0

    lax.fori_loop(0, far, far_step, 0)


def apply_blocks(table, held, blocks, index):
    return pl.pallas_call(
        apply_kernel,
        name=f"apply_{index}",
        in_specs=[SMEM] + [ANY] * 8 + [VMEM] * 4,
        out_specs=VMEM,
        out_shape=pltpu.VMEM((16, CLUSTER // 2, WIDE), jnp.float32),
        scratch_shapes=[
            pltpu.VMEM((2, CLUSTER, WIDE), jnp.float32),
            pltpu.VMEM((FAR, CLUSTER, WIDE), jnp.float32),
            pltpu.SemaphoreType.DMA((2,)),
            pltpu.SemaphoreType.DMA((FAR,)),
        ],
        compiler_params=pltpu.CompilerParams(vmem_limit_bytes=SCOPED),
        cost_estimate=pl.CostEstimate(flops=8 << 30, bytes_accessed=8 << 20, transcendentals=0),
    )(table, *held, *blocks)


def scalars(near_pairs, far_pairs, far_ranks, block_counts):
    row_base = lax.axis_index(ROW) * 8
    col_base = lax.axis_index(COL) * 8
    core = lax.axis_index("core")
    index = lax.iota(jnp.int32, 16)
    y = index // 2 % 4
    z = index % 2 * 2 + index // 8
    order = jnp.where(core == 0, y * 4 + z, z * 4 + y)
    pieces = [
        block_counts[0],
        near_pairs[:, 0] - row_base,
        near_pairs[:, 1] - col_base,
        far_pairs[:, 0] - row_base,
        far_pairs[:, 1] - col_base,
        far_ranks,
        order,
        core[None],
        lax.axis_index("x")[None],
    ]
    return jnp.concatenate(pieces).astype(jnp.int32)


def exchange(values, axes, groups=None):
    return lax.all_to_all(values, axes, split_axis=0, concat_axis=0, tiled=True, axis_index_groups=groups)


def shards(cotangent, radiation, near_z, near_pairs, far_ut, far_vt, far_pairs, far_ranks, block_counts):
    table = scalars(near_pairs, far_pairs, far_ranks, block_counts)
    own_0, own_1 = partial_rhs(cotangent, radiation)
    swap = [(0, 1), (1, 0)]
    plane = ("dir", "y", "zhi", "core")

    def others(own):
        return [lax.ppermute(own, "x", [(i, (i + k) % 4) for i in range(4)]) for k in (1, 2, 3)]

    def both_cores(mine):
        return mine + [lax.ppermute(part, "core", swap) for part in mine]

    blocks_a, done_a = prepare_near(table, near_z, 0, NEAR // 2)
    own_0 = own_0 + (lax.ppermute(own_0, "dir", swap) + done_a[0, 0])
    own_0, own_1 = lax.optimization_barrier((own_0, own_1))
    around_0 = others(own_0)
    blocks_b, done_b = prepare_near(table, near_z, NEAR // 2, NEAR // 2)
    blocks_u, blocks_v, done_far = prepare_far(table, far_ut, far_vt)
    own_1 = own_1 + (lax.ppermute(own_1, "dir", swap) + (done_b[0, 0] + done_far[0, 0]))
    own_1, *around_0 = lax.optimization_barrier((own_1, *around_0))
    held_0 = both_cores([own_0, *around_0])
    around_1 = others(own_1)
    blocks = (blocks_a, blocks_b, blocks_u, blocks_v)

    sums = []
    for chunk, held in enumerate((held_0, None)):
        if held is None:
            held = both_cores([own_1, *around_1])
        terms = apply_blocks(table, held, blocks, chunk).reshape(4, 4, CLUSTER // 2, WIDE)
        if chunk == 0:
            terms, *around_1 = lax.optimization_barrier((terms, *around_1))
        sums.append(exchange(terms, plane, rings(True)).sum(axis=0))
    result = exchange(jnp.stack(sums, axis=1), plane, rings(False)).sum(axis=0)
    parts = [r[:, :HALF] for r in result] + [r[:, HALF:] for r in result]
    return jnp.concatenate(parts, axis=1)


def solution(mesh):
    finer = Mesh(mesh.devices.reshape(SIZES), AXES)
    blocks = P(None, AXES, None, None)
    in_specs = (
        P("dir", None),
        P(None, ("y", "zhi", "x", "core"), "dir"),
        blocks,
        P(AXES, None),
        blocks,
        blocks,
        P(AXES, None),
        P(AXES),
        P(AXES, None),
    )
    out_specs = P(("x", "core", "dir", "y", "zhi"), None)
    return jax.shard_map(shards, mesh=finer, in_specs=in_specs, out_specs=out_specs, check_vma=False)
```

time: 170 us -> 172 us (1.012)
  starting transfers between devices: 49.3 us -> 22.5 us
  blocking collectives: 0 us -> 24.5 us
  local copies, waits for them, and re-layouts: 5.11 us -> 28.3 us
  between operations: 13.6 us -> 1.55 us
  Pallas kernels: 23.1 us -> 17.4 us
  waiting for transfers between devices: 72 us -> 69.4 us
  other arithmetic: 7.02 us -> 8.82 us
    ppermute x14 -> x16, starting transfers between devices: 49.3 us -> 12.8 us  [the longest x6 7.45 us: others(): lax.ppermute(own, 'x', [(i, (i + k) % 4) for i in range(4)])]
    all_to_all x0 -> x2, waiting for transfers between devices: none -> 32.4 us  [exchange(): lax.all_to_all(values, axes, split_axis=0, concat_axis=0, tiled=True, axi...]
    all_gather x2 -> x0, waiting for transfers between devices: 24.5 us -> none  [shards(): gathered.append(lax.all_gather(rhs, COL, axis=0, tiled=False))]
    all_to_all x0 -> x1, blocking collectives: none -> 24.5 us  [exchange(): lax.all_to_all(values, axes, split_axis=0, concat_axis=0, tiled=True, axi...]
    unnamed x20 -> x40, local copies, waits for them, and re-layouts: 4.99 us -> 26.5 us
    ppermute x14 -> x16, waiting for transfers between devices: 47.4 us -> 37 us  [the longest x6 30.5 us: others(): lax.ppermute(own, 'x', [(i, (i + k) % 4) for i in range(4)])]
    all_to_all x0 -> x2, starting transfers between devices: none -> 9.73 us  [exchange(): lax.all_to_all(values, axes, split_axis=0, concat_axis=0, tiled=True, axi...]
    pallas_call x3 -> x5, Pallas kernels: 21.2 us -> 12.6 us  [the longest x2 8.65 us: apply_blocks(): pl.pallas_call(apply_kernel, name=f'apply_{index}', in_specs=[SMEM] + [AN...]
  transfers between devices with their start and end apart: 16 -> 18, of which waited for: 8 -> 12; matrix products, arithmetic and copies ran while one was open for 3% -> 3% of each run, Pallas kernels for 12% -> 7%
where the time goes in v2:
time: 172 us; the launch traced here: 173 us
  waiting for transfers between devices  69.4 us (40%)
  local copies, waits for them, and re-layouts  28.3 us (16%)
  blocking collectives  24.5 us (14%)
  starting transfers between devices  22.5 us (13%)
  Pallas kernels  17.4 us (10%)
  other arithmetic  8.82 us (5%)
    all_to_all x2, waiting for transfers between devices, exchange(): lax.all_to_all(values, axes, split_axis=0, concat_axis=0, tiled=True, axi...  32.4 us
    ppermute x6, waiting for transfers between devices, others(): lax.ppermute(own, 'x', [(i, (i + k) % 4) for i in range(4)])  30.5 us
    unnamed x40, local copies, waits for them, and re-layouts  26.5 us
    all_to_all x1, blocking collectives, exchange(): lax.all_to_all(values, axes, split_axis=0, concat_axis=0, tiled=True, axi...  24.5 us
    all_to_all x2, starting transfers between devices, exchange(): lax.all_to_all(values, axes, split_axis=0, concat_axis=0, tiled=True, axi...  9.73 us
    pallas_call x2, Pallas kernels, apply_blocks(): pl.pallas_call(apply_kernel, name=f'apply_{index}', in_specs=[SMEM] + [AN...  8.65 us
    ppermute x6, starting transfers between devices, others(): lax.ppermute(own, 'x', [(i, (i + k) % 4) for i in range(4)])  7.45 us
    reduce_sum x2, other arithmetic, shards(): sums.append(exchange(terms, plane, rings(True)).sum(axis=0))  5.21 us
  transfers between devices with their start and end apart: 18, of which 12 were waited for; matrix products, arithmetic and copies ran while one was open for 3% of the time, Pallas kernels for 7%

profile of v2, /device:TPU:0, one launch (start us, length us, event | category | flops | bytes accessed | tf_op | source)
XLA Modules:
  0.0 172.5 jit_solution(11842815726186079865)
XLA Ops:
  0.0 4.9 %rhs.1 = (f32[512,256]{1,0:T(8,128)}, f32[512,256]{1,0:T(8,128)}) custom-call(bf16[1024,512]{1,0:T(8,128)(2,1)} %cot_ref.1, bf16[2,512,1024]{2,1,0:T(8,128)(2,1)} %rad_ref.1), custom_call_target="tpu_custom_call" | custom-call | flops 1073741824 | bytes 4194304 | tf_op jit(solution)/shard_map/rhs/pallas_call | solution.py:66
  4.9 2.0 %collective-permute-start = (f32[512,256]{1,0:T(8,128)}, f32[512,256]{1,0:T(8,128)S(1)}, u32[]{:S(2)}, u32[]{:S(2)}) collective-permute-start(f32[512,256]{1,0:T(8,128)} %get-tuple-element.24), channel_id=1, source_target_pairs={{0,64},{64,0},{1,65},{65,1},{2,66},{66,2},{3,67},{67,3},{4,68},{68... | collective-permute-start | bytes 1572872 | tf_op jit(solution)/shard_map/ppermute | solution.py:312
  7.1 5.8 %copy-done = f32[2,8,512,512]{3,2,1,0:T(8,128)S(1)} copy-done((f32[2,8,512,512]{3,2,1,0:T(8,128)S(1)}, f32[2,8,512,512]{3,2,1,0:T(8,128)}, u32[]{:S(2)}) %copy-start) | copy-done | bytes 16777240
  12.8 2.2 %prepare_near_0.1 = (bf16[4,512,2048]{2,1,0:T(8,128)(2,1)S(1)}, f32[8,128]{1,0:T(8,128)S(1)}) custom-call(s32[48]{0:T(128)S(1)} %concatenate.6.table, f32[2,8,512,512]{3,2,1,0:T(8,128)S(1)} %copy-done), custom_call_target="tpu_custom_call" | custom-call | flops 268435456 | bytes 8388608 | tf_op jit(solution)/shard_map/prepare_near_0/pallas_call | solution.py:113
  15.1 0.6 slice.37
  15.7 3.3 %collective-permute-done = f32[512,256]{1,0:T(8,128)S(1)} collective-permute-done((f32[512,256]{1,0:T(8,128)}, f32[512,256]{1,0:T(8,128)S(1)}, u32[]{:S(2)}, u32[]{:S(2)}) %collective-permute-start) | collective-permute-done | bytes 524320 | tf_op jit(solution)/shard_map/ppermute | solution.py:312
  19.0 2.4 %add_add_fusion.1.refs_0_ = f32[512,256]{1,0:T(8,128)S(1)} fusion(f32[512,256]{1,0:T(8,128)} %get-tuple-element.24, f32[512,256]{1,0:T(8,128)S(1)} %collective-permute-done, f32[]{:T(128)} %bitcast.7), kind=kLoop, calls=%fused_computation.3 | loop fusion | flops 262144 | bytes 1572868 | tf_op jit(solution)/shard_map/add | solution.py:312
  21.4 1.6 collective-permute-start.1
  23.0 2.8 %collective-permute-start.4 = (f32[512,256]{1,0:T(8,128)S(1)}, f32[512,256]{1,0:T(8,128)S(1)}, u32[]{:S(2)}, u32[]{:S(2)}) collective-permute-start(f32[512,256]{1,0:T(8,128)S(1)} %add_add_fusion.1.refs_0_), channel_id=1, source_target_pairs={{0,6},{2,0},{4,2},{6,4},{1,7},{3,1},{5,3},{7,5},{8,14},{10,8},{12,... | collective-permute-start | bytes 1572872 | tf_op jit(solution)/shard_map/ppermute | solution.py:306
  25.9 0.7 collective-permute-start.3
  26.6 1.0 collective-permute-start.2
  27.6 1.1 prepare_far.1
  28.7 0.6 slice.39
  29.3 0.6 prepare_near_4.1
  29.9 3.3 %copy-done.8 = bf16[4,512,2048]{2,1,0:T(8,128)(2,1)} copy-done((bf16[4,512,2048]{2,1,0:T(8,128)(2,1)}, bf16[4,512,2048]{2,1,0:T(8,128)(2,1)S(1)}, u32[]{:S(2)}) %copy-start.8) | copy-done | bytes 8388632
  33.2 0.5 slice.38
  35.2 12.0 %collective-permute-done.4.refs_3_ = f32[512,256]{1,0:T(8,128)S(1)} collective-permute-done((f32[512,256]{1,0:T(8,128)S(1)}, f32[512,256]{1,0:T(8,128)S(1)}, u32[]{:S(2)}, u32[]{:S(2)}) %collective-permute-start.4) | collective-permute-done | bytes 524320 | tf_op jit(solution)/shard_map/ppermute | solution.py:306
  47.2 3.7 %collective-permute-done.2.refs_1_ = f32[512,256]{1,0:T(8,128)S(1)} collective-permute-done((f32[512,256]{1,0:T(8,128)S(1)}, f32[512,256]{1,0:T(8,128)S(1)}, u32[]{:S(2)}, u32[]{:S(2)}) %collective-permute-start.2) | collective-permute-done | bytes 524320 | tf_op jit(solution)/shard_map/ppermute | solution.py:306
  50.9 0.5 collective-permute-start.7
  51.4 0.6 collective-permute-start.11
  52.0 1.5 collective-permute-start.10
  53.5 0.8 collective-permute-start.9
  54.4 3.4 %copy-done.9 = bf16[4,512,2048]{2,1,0:T(8,128)(2,1)S(1)} copy-done((bf16[4,512,2048]{2,1,0:T(8,128)(2,1)S(1)}, bf16[4,512,2048]{2,1,0:T(8,128)(2,1)}, u32[]{:S(2)}) %copy-start.9) | copy-done | bytes 8388632
  57.8 4.2 %apply_0.1 = f32[16,256,256]{2,1,0:T(8,128)S(1)} custom-call(s32[48]{0:T(128)S(1)} %concatenate.6.table, f32[512,256]{1,0:T(8,128)S(1)} %add_add_fusion.1.refs_0_, f32[512,256]{1,0:T(8,128)S(1)} %collective-permute-done.2.refs_1_, f32[512,256]{1,0:T(8,128)S(1)} %collective-permute-done.3.refs_2_, f32[512,256]{1,0:T(8,128)S(1)} %collective-permute-done.4.refs_3_, ...), custom_call_target="tpu_custom_call" | custom-call | flops 8589934592 | bytes 8388608 | tf_op jit(solution)/shard_map/apply_0/pallas_call | solution.py:256
  62.0 2.0 %copy-done.2 = f32[16,256,256]{2,1,0:T(8,128)} copy-done((f32[16,256,256]{2,1,0:T(8,128)}, f32[16,256,256]{2,1,0:T(8,128)S(1)}, u32[]{:S(2)}) %copy-start.2) | copy-done | bytes 4194328
  64.0 2.1 %collective-permute-done.11.refs_3_ = f32[512,256]{1,0:T(8,128)S(1)} collective-permute-done((f32[512,256]{1,0:T(8,128)S(1)}, f32[512,256]{1,0:T(8,128)S(1)}, u32[]{:S(2)}, u32[]{:S(2)}) %collective-permute-start.11) | collective-permute-done | bytes 524320 | tf_op jit(solution)/shard_map/ppermute | solution.py:306
  66.1 2.2 %collective-permute-done.10.refs_2_ = f32[512,256]{1,0:T(8,128)S(1)} collective-permute-done((f32[512,256]{1,0:T(8,128)S(1)}, f32[512,256]{1,0:T(8,128)S(1)}, u32[]{:S(2)}, u32[]{:S(2)}) %collective-permute-start.10) | collective-permute-done | bytes 524320 | tf_op jit(solution)/shard_map/ppermute | solution.py:306
  68.3 10.5 %collective-permute-done.9.refs_1_ = f32[512,256]{1,0:T(8,128)S(1)} collective-permute-done((f32[512,256]{1,0:T(8,128)S(1)}, f32[512,256]{1,0:T(8,128)S(1)}, u32[]{:S(2)}, u32[]{:S(2)}) %collective-permute-start.9) | collective-permute-done | bytes 524320 | tf_op jit(solution)/shard_map/ppermute | solution.py:306
  78.8 4.8 %all-to-all-start = ((f32[4,4,256,256]{3,2,1,0:T(8,128)}), f32[4,4,256,256]{3,2,1,0:T(8,128)}, u32[]{:S(2)}, u32[]{:S(2)}) async-start(f32[4,4,256,256]{3,2,1,0:T(8,128)} %bitcast.21), calls=%async_computation | async-start | bytes 8388608 | tf_op jit(solution)/shard_map/all_to_all | solution.py:296
  83.8 0.5 collective-permute-start.13
  84.4 0.4 collective-permute-start.15
  84.8 0.9 collective-permute-done.12.refs_4_
  85.7 0.7 collective-permute-done.13.refs_5_
  86.4 0.7 collective-permute-done.14.refs_6_
  87.2 0.7 collective-permute-done.15.refs_7_
  87.9 3.4 %copy-done.7 = bf16[4,512,2048]{2,1,0:T(8,128)(2,1)S(1)} copy-done((bf16[4,512,2048]{2,1,0:T(8,128)(2,1)S(1)}, bf16[4,512,2048]{2,1,0:T(8,128)(2,1)}, u32[]{:S(2)}) %copy-start.7) | copy-done | bytes 8388632
  91.3 3.4 %copy-done.10 = bf16[4,512,2048]{2,1,0:T(8,128)(2,1)S(1)} copy-done((bf16[4,512,2048]{2,1,0:T(8,128)(2,1)S(1)}, bf16[4,512,2048]{2,1,0:T(8,128)(2,1)}, u32[]{:S(2)}) %copy-start.10) | copy-done | bytes 8388632
  94.7 1.6 copy-done.12
  96.3 1.6 copy-done.14
  97.9 4.4 %apply_1.1 = f32[16,256,256]{2,1,0:T(8,128)S(1)} custom-call(s32[48]{0:T(128)S(1)} %concatenate.6.table, f32[512,256]{1,0:T(8,128)S(1)} %add_add_fusion.refs_0_, f32[512,256]{1,0:T(8,128)S(1)} %collective-permute-done.9.refs_1_, f32[512,256]{1,0:T(8,128)S(1)} %collective-permute-done.10.refs_2_, f32[512,256]{1,0:T(8,128)S(1)} %collective-permute-done.11.refs_3_, ...), custom_call_target="tpu_custom_call" | custom-call | flops 8589934592 | bytes 8388608 | tf_op jit(solution)/shard_map/apply_1/pallas_call | solution.py:256
  102.3 2.0 %copy-done.3 = f32[16,256,256]{2,1,0:T(8,128)} copy-done((f32[16,256,256]{2,1,0:T(8,128)}, f32[16,256,256]{2,1,0:T(8,128)S(1)}, u32[]{:S(2)}) %copy-start.3) | copy-done | bytes 4194328
  104.3 7.2 %all-to-all-done = f32[4,4,256,256]{3,2,1,0:T(8,128)} async-done(((f32[4,4,256,256]{3,2,1,0:T(8,128)}), f32[4,4,256,256]{3,2,1,0:T(8,128)}, u32[]{:S(2)}, u32[]{:S(2)}) %all-to-all-start) | async-done | bytes 4194336 | tf_op jit(solution)/shard_map/all_to_all | solution.py:296
  111.5 4.9 %all-to-all-start.1 = ((f32[4,4,256,256]{3,2,1,0:T(8,128)}), f32[4,4,256,256]{3,2,1,0:T(8,128)}, u32[]{:S(2)}, u32[]{:S(2)}) async-start(f32[4,4,256,256]{3,2,1,0:T(8,128)} %bitcast.22), calls=%async_computation.1 | async-start | bytes 8388608 | tf_op jit(solution)/shard_map/all_to_all | solution.py:296
  116.4 2.6 %reduce_sum.27 = f32[4,256,256]{2,1,0:T(8,128)S(1)} reduce(f32[4,4,256,256]{3,2,1,0:T(8,128)} %all-to-all-done, f32[]{:T(128)} %constant.72.clone.1), dimensions={0}, to_apply=%region_0.1 | reduce | flops 786432 | bytes 5242884 | tf_op jit(solution)/shard_map/reduce_sum | solution.py:330
  119.0 25.2 %all-to-all-done.1 = f32[4,4,256,256]{3,2,1,0:T(8,128)} async-done(((f32[4,4,256,256]{3,2,1,0:T(8,128)}), f32[4,4,256,256]{3,2,1,0:T(8,128)}, u32[]{:S(2)}, u32[]{:S(2)}) %all-to-all-start.1) | async-done | bytes 4194336 | tf_op jit(solution)/shard_map/all_to_all | solution.py:296
  144.2 2.6 %reduce_sum.28 = f32[4,256,256]{2,1,0:T(8,128)S(1)} reduce(f32[4,4,256,256]{3,2,1,0:T(8,128)} %all-to-all-done.1, f32[]{:T(128)} %constant.72.clone.1), dimensions={0}, to_apply=%region_1.2 | reduce | flops 786432 | bytes 5242884 | tf_op jit(solution)/shard_map/reduce_sum | solution.py:330
  146.9 24.5 %all_to_all.15 = f32[4,2,256,256]{3,2,1,0:T(8,128)S(1)} all-to-all(f32[4,2,256,256]{3,2,1,0:T(8,128)S(1)} %pad_maximum_fusion), channel_id=1, replica_groups={{1,17,33,49},{65,81,97,113},{9,25,41,57},{73,89,105,121},{0,64,8,72},{1..., dimensions={0} | all-to-all | bytes 4194304 | tf_op jit(solution)/shard_map/all_to_all | solution.py:296
  171.7 0.8 pad_maximum_fusion.1
  (51 shorter events, 1.0 us)
Async XLA Ops:
  0.0 6.9 %copy-start.16 = (s32[8,2]{0,1:T(2,128)S(1)}, s32[8,2]{0,1:T(2,128)}, u32[]{:S(2)}) copy-start(s32[8,2]{0,1:T(2,128)} %param.12) | copy-start | bytes 196
  0.0 6.9 %copy-start.17 = (s32[4,2]{0,1:T(2,128)S(1)}, s32[4,2]{0,1:T(2,128)}, u32[]{:S(2)}) copy-start(s32[4,2]{0,1:T(2,128)} %param.15) | copy-start | bytes 100
  0.0 7.0 %copy-start.18 = (s32[1,2]{1,0:T(1,128)S(1)}, s32[1,2]{1,0:T(1,128)}, u32[]{:S(2)}) copy-start(s32[1,2]{1,0:T(1,128)} %param.17) | copy-start | bytes 28
  0.0 7.0 %copy-start.19 = (s32[4]{0:T(128)S(1)}, s32[4]{0:T(128)}, u32[]{:S(2)}) copy-start(s32[4]{0:T(128)} %param.16) | copy-start | bytes 52
  0.0 27.6 %copy-start.5 = (f32[2,4,96,512]{3,2,1,0:T(8,128)S(1)}, f32[2,4,96,512]{3,2,1,0:T(8,128)}, u32[]{:S(2)}) copy-start(f32[2,4,96,512]{3,2,1,0:T(8,128)} %v_ref.1) | copy-start | bytes 4718596
  4.9 14.2 %collective-permute-start = (f32[512,256]{1,0:T(8,128)}, f32[512,256]{1,0:T(8,128)S(1)}, u32[]{:S(2)}, u32[]{:S(2)}) collective-permute-start(f32[512,256]{1,0:T(8,128)} %get-tuple-element.24), channel_id=1, source_target_pairs={{0,64},{64,0},{1,65},{65,1},{2,66},{66,2},{3,67},{67,3},{4,68},{68... | collective-permute-start | bytes 1572872 | tf_op jit(solution)/shard_map/ppermute | solution.py:312
  7.1 5.8 %copy-start = (f32[2,8,512,512]{3,2,1,0:T(8,128)S(1)}, f32[2,8,512,512]{3,2,1,0:T(8,128)}, u32[]{:S(2)}) copy-start(f32[2,8,512,512]{3,2,1,0:T(8,128)} %z_ref.3) | copy-start | bytes 50331652
  12.8 16.4 %copy-start.1 = (f32[2,8,512,512]{3,2,1,0:T(8,128)S(1)}, f32[2,8,512,512]{3,2,1,0:T(8,128)}, u32[]{:S(2)}) copy-start(f32[2,8,512,512]{3,2,1,0:T(8,128)} %z_ref.3) | copy-start | bytes 50331652
  15.1 39.3 %copy-start.6 = (bf16[4,512,2048]{2,1,0:T(8,128)(2,1)}, bf16[4,512,2048]{2,1,0:T(8,128)(2,1)S(1)}, u32[]{:S(2)}) copy-start(bf16[4,512,2048]{2,1,0:T(8,128)(2,1)S(1)} %get-tuple-element.34.refs_8_) | copy-start | bytes 25165828
  15.1 12.5 %copy-start.4 = (f32[2,4,96,512]{3,2,1,0:T(8,128)S(1)}, f32[2,4,96,512]{3,2,1,0:T(8,128)}, u32[]{:S(2)}) copy-start(f32[2,4,96,512]{3,2,1,0:T(8,128)} %u_ref.1) | copy-start | bytes 4718596
  21.4 13.7 %collective-permute-start.1 = (f32[512,256]{1,0:T(8,128)}, f32[512,256]{1,0:T(8,128)S(1)}, u32[]{:S(2)}, u32[]{:S(2)}) collective-permute-start(f32[512,256]{1,0:T(8,128)} %get-tuple-element.28), channel_id=1, source_target_pairs={{0,64},{64,0},{1,65},{65,1},{2,66},{66,2},{3,67},{67,3},{4,68},{68... | collective-permute-start | bytes 1572872 | tf_op jit(solution)/shard_map/ppermute | solution.py:317
  23.0 24.2 %collective-permute-start.4 = (f32[512,256]{1,0:T(8,128)S(1)}, f32[512,256]{1,0:T(8,128)S(1)}, u32[]{:S(2)}, u32[]{:S(2)}) collective-permute-start(f32[512,256]{1,0:T(8,128)S(1)} %add_add_fusion.1.refs_0_), channel_id=1, source_target_pairs={{0,6},{2,0},{4,2},{6,4},{1,7},{3,1},{5,3},{7,5},{8,14},{10,8},{12,... | collective-permute-start | bytes 1572872 | tf_op jit(solution)/shard_map/ppermute | solution.py:306
  25.9 21.4 %collective-permute-start.3 = (f32[512,256]{1,0:T(8,128)S(1)}, f32[512,256]{1,0:T(8,128)S(1)}, u32[]{:S(2)}, u32[]{:S(2)}) collective-permute-start(f32[512,256]{1,0:T(8,128)S(1)} %add_add_fusion.1.refs_0_), channel_id=1, source_target_pairs={{0,4},{2,6},{4,0},{6,2},{1,5},{3,7},{5,1},{7,3},{8,12},{10,14},{12... | collective-permute-start | bytes 1572872 | tf_op jit(solution)/shard_map/ppermute | solution.py:306
  26.6 24.3 %collective-permute-start.2 = (f32[512,256]{1,0:T(8,128)S(1)}, f32[512,256]{1,0:T(8,128)S(1)}, u32[]{:S(2)}, u32[]{:S(2)}) collective-permute-start(f32[512,256]{1,0:T(8,128)S(1)} %add_add_fusion.1.refs_0_), channel_id=1, source_target_pairs={{0,2},{2,4},{4,6},{6,0},{1,3},{3,5},{5,7},{7,1},{8,10},{10,12},{12... | collective-permute-start | bytes 1572872 | tf_op jit(solution)/shard_map/ppermute | solution.py:306
  28.7 25.7 %copy-start.11 = (bf16[4,128,2048]{2,1,0:T(8,128)(2,1)}, bf16[4,128,2048]{2,1,0:T(8,128)(2,1)S(1)}, u32[]{:S(2)}) copy-start(bf16[4,128,2048]{2,1,0:T(8,128)(2,1)S(1)} %get-tuple-element.36.refs_10_) | copy-start | bytes 6291460
  28.7 25.7 %copy-start.13 = (bf16[4,512,512]{2,1,0:T(8,128)(2,1)}, bf16[4,512,512]{2,1,0:T(8,128)(2,1)S(1)}, u32[]{:S(2)}) copy-start(bf16[4,512,512]{2,1,0:T(8,128)(2,1)S(1)} %get-tuple-element.37.refs_11_) | copy-start | bytes 6291460
  29.3 5.8 %copy-start.15 = (f32[512,256]{1,0:T(8,128)S(1)}, f32[512,256]{1,0:T(8,128)}, u32[]{:S(2)}) copy-start(f32[512,256]{1,0:T(8,128)} %get-tuple-element.28) | copy-start | bytes 1572868
  29.9 3.3 %copy-start.8 = (bf16[4,512,2048]{2,1,0:T(8,128)(2,1)}, bf16[4,512,2048]{2,1,0:T(8,128)(2,1)S(1)}, u32[]{:S(2)}) copy-start(bf16[4,512,2048]{2,1,0:T(8,128)(2,1)S(1)} %get-tuple-element.35.refs_9_) | copy-start | bytes 25165828
  35.0 17.0 %collective-permute-start.5 = (f32[512,256]{1,0:T(8,128)S(1)}, f32[512,256]{1,0:T(8,128)S(1)}, u32[]{:S(2)}, u32[]{:S(2)}) collective-permute-start(f32[512,256]{1,0:T(8,128)S(1)} %add_add_fusion.1.refs_0_), channel_id=1, source_target_pairs={{0,1},{1,0},{2,3},{3,2},{4,5},{5,4},{6,7},{7,6},{8,9},{9,8},{10,11... | collective-permute-start | bytes 1572872 | tf_op jit(solution)/shard_map/ppermute | solution.py:309
  50.9 2.6 %collective-permute-start.6 = (f32[512,256]{1,0:T(8,128)S(1)}, f32[512,256]{1,0:T(8,128)S(1)}, u32[]{:S(2)}, u32[]{:S(2)}) collective-permute-start(f32[512,256]{1,0:T(8,128)S(1)} %collective-permute-done.2.refs_1_), channel_id=1, source_target_pairs={{0,1},{1,0},{2,3},{3,2},{4,5},{5,4},{6,7},{7,6},{8,9},{9,8},{10,11... | collective-permute-start | bytes 1572872 | tf_op jit(solution)/shard_map/ppermute | solution.py:309
  50.9 3.4 %collective-permute-start.7 = (f32[512,256]{1,0:T(8,128)S(1)}, f32[512,256]{1,0:T(8,128)S(1)}, u32[]{:S(2)}, u32[]{:S(2)}) collective-permute-start(f32[512,256]{1,0:T(8,128)S(1)} %collective-permute-done.3.refs_2_), channel_id=1, source_target_pairs={{0,1},{1,0},{2,3},{3,2},{4,5},{5,4},{6,7},{7,6},{8,9},{9,8},{10,11... | collective-permute-start | bytes 1572872 | tf_op jit(solution)/shard_map/ppermute | solution.py:309
  51.4 2.9 %collective-permute-start.8 = (f32[512,256]{1,0:T(8,128)S(1)}, f32[512,256]{1,0:T(8,128)S(1)}, u32[]{:S(2)}, u32[]{:S(2)}) collective-permute-start(f32[512,256]{1,0:T(8,128)S(1)} %collective-permute-done.4.refs_3_), channel_id=1, source_target_pairs={{0,1},{1,0},{2,3},{3,2},{4,5},{5,4},{6,7},{7,6},{8,9},{9,8},{10,11... | collective-permute-start | bytes 1572872 | tf_op jit(solution)/shard_map/ppermute | solution.py:309
  51.4 14.7 %collective-permute-start.11 = (f32[512,256]{1,0:T(8,128)S(1)}, f32[512,256]{1,0:T(8,128)S(1)}, u32[]{:S(2)}, u32[]{:S(2)}) collective-permute-start(f32[512,256]{1,0:T(8,128)S(1)} %add_add_fusion.refs_0_), channel_id=1, source_target_pairs={{0,6},{2,0},{4,2},{6,4},{1,7},{3,1},{5,3},{7,5},{8,14},{10,8},{12,... | collective-permute-start | bytes 1572872 | tf_op jit(solution)/shard_map/ppermute | solution.py:306
  52.0 16.3 %collective-permute-start.10 = (f32[512,256]{1,0:T(8,128)S(1)}, f32[512,256]{1,0:T(8,128)S(1)}, u32[]{:S(2)}, u32[]{:S(2)}) collective-permute-start(f32[512,256]{1,0:T(8,128)S(1)} %add_add_fusion.refs_0_), channel_id=1, source_target_pairs={{0,4},{2,6},{4,0},{6,2},{1,5},{3,7},{5,1},{7,3},{8,12},{10,14},{12... | collective-permute-start | bytes 1572872 | tf_op jit(solution)/shard_map/ppermute | solution.py:306
  53.5 25.3 %collective-permute-start.9 = (f32[512,256]{1,0:T(8,128)S(1)}, f32[512,256]{1,0:T(8,128)S(1)}, u32[]{:S(2)}, u32[]{:S(2)}) collective-permute-start(f32[512,256]{1,0:T(8,128)S(1)} %add_add_fusion.refs_0_), channel_id=1, source_target_pairs={{0,2},{2,4},{4,6},{6,0},{1,3},{3,5},{5,7},{7,1},{8,10},{10,12},{12... | collective-permute-start | bytes 1572872 | tf_op jit(solution)/shard_map/ppermute | solution.py:306
  54.4 3.4 %copy-start.9 = (bf16[4,512,2048]{2,1,0:T(8,128)(2,1)S(1)}, bf16[4,512,2048]{2,1,0:T(8,128)(2,1)}, u32[]{:S(2)}) copy-start(bf16[4,512,2048]{2,1,0:T(8,128)(2,1)} %copy-done.8) | copy-start | bytes 25165828
  62.0 2.0 %copy-start.2 = (f32[16,256,256]{2,1,0:T(8,128)}, f32[16,256,256]{2,1,0:T(8,128)S(1)}, u32[]{:S(2)}) copy-start(f32[16,256,256]{2,1,0:T(8,128)S(1)} %apply_0.1) | copy-start | bytes 12582916
  78.8 32.7 %all-to-all-start = ((f32[4,4,256,256]{3,2,1,0:T(8,128)}), f32[4,4,256,256]{3,2,1,0:T(8,128)}, u32[]{:S(2)}, u32[]{:S(2)}) async-start(f32[4,4,256,256]{3,2,1,0:T(8,128)} %bitcast.21), calls=%async_computation | async-start | bytes 8388608 | tf_op jit(solution)/shard_map/all_to_all | solution.py:296
  83.7 2.0 %collective-permute-start.12 = (f32[512,256]{1,0:T(8,128)S(1)}, f32[512,256]{1,0:T(8,128)S(1)}, u32[]{:S(2)}, u32[]{:S(2)}) collective-permute-start(f32[512,256]{1,0:T(8,128)S(1)} %add_add_fusion.refs_0_), channel_id=1, source_target_pairs={{0,1},{1,0},{2,3},{3,2},{4,5},{5,4},{6,7},{7,6},{8,9},{9,8},{10,11... | collective-permute-start | bytes 1572872 | tf_op jit(solution)/shard_map/ppermute | solution.py:309
  83.8 2.6 %collective-permute-start.13 = (f32[512,256]{1,0:T(8,128)S(1)}, f32[512,256]{1,0:T(8,128)S(1)}, u32[]{:S(2)}, u32[]{:S(2)}) collective-permute-start(f32[512,256]{1,0:T(8,128)S(1)} %collective-permute-done.9.refs_1_), channel_id=1, source_target_pairs={{0,1},{1,0},{2,3},{3,2},{4,5},{5,4},{6,7},{7,6},{8,9},{9,8},{10,11... | collective-permute-start | bytes 1572872 | tf_op jit(solution)/shard_map/ppermute | solution.py:309
  84.3 2.9 %collective-permute-start.14 = (f32[512,256]{1,0:T(8,128)S(1)}, f32[512,256]{1,0:T(8,128)S(1)}, u32[]{:S(2)}, u32[]{:S(2)}) collective-permute-start(f32[512,256]{1,0:T(8,128)S(1)} %collective-permute-done.10.refs_2_), channel_id=1, source_target_pairs={{0,1},{1,0},{2,3},{3,2},{4,5},{5,4},{6,7},{7,6},{8,9},{9,8},{10,11... | collective-permute-start | bytes 1572872 | tf_op jit(solution)/shard_map/ppermute | solution.py:309
  84.4 3.6 %collective-permute-start.15 = (f32[512,256]{1,0:T(8,128)S(1)}, f32[512,256]{1,0:T(8,128)S(1)}, u32[]{:S(2)}, u32[]{:S(2)}) collective-permute-start(f32[512,256]{1,0:T(8,128)S(1)} %collective-permute-done.11.refs_3_), channel_id=1, source_target_pairs={{0,1},{1,0},{2,3},{3,2},{4,5},{5,4},{6,7},{7,6},{8,9},{9,8},{10,11... | collective-permute-start | bytes 1572872 | tf_op jit(solution)/shard_map/ppermute | solution.py:309
  87.9 3.4 %copy-start.7 = (bf16[4,512,2048]{2,1,0:T(8,128)(2,1)S(1)}, bf16[4,512,2048]{2,1,0:T(8,128)(2,1)}, u32[]{:S(2)}) copy-start(bf16[4,512,2048]{2,1,0:T(8,128)(2,1)} %copy-done.6) | copy-start | bytes 25165828
  91.3 3.4 %copy-start.10 = (bf16[4,512,2048]{2,1,0:T(8,128)(2,1)S(1)}, bf16[4,512,2048]{2,1,0:T(8,128)(2,1)}, u32[]{:S(2)}) copy-start(bf16[4,512,2048]{2,1,0:T(8,128)(2,1)} %copy-done.8) | copy-start | bytes 25165828
  94.7 1.6 copy-start.12
  96.3 1.6 copy-start.14
  102.3 2.0 %copy-start.3 = (f32[16,256,256]{2,1,0:T(8,128)}, f32[16,256,256]{2,1,0:T(8,128)S(1)}, u32[]{:S(2)}) copy-start(f32[16,256,256]{2,1,0:T(8,128)S(1)} %apply_1.1) | copy-start | bytes 12582916
  111.5 32.7 %all-to-all-start.1 = ((f32[4,4,256,256]{3,2,1,0:T(8,128)}), f32[4,4,256,256]{3,2,1,0:T(8,128)}, u32[]{:S(2)}, u32[]{:S(2)}) async-start(f32[4,4,256,256]{3,2,1,0:T(8,128)} %bitcast.22), calls=%async_computation.1 | async-start | bytes 8388608 | tf_op jit(solution)/shard_map/all_to_all | solution.py:296

commit v3 on v2

--- a/solution.py
+++ b/solution.py
@@ -25,6 +25,7 @@
 ANY = pl.BlockSpec(memory_space=pl.ANY)
 SMEM = pl.BlockSpec(memory_space=pltpu.SMEM)
 VMEM = pl.BlockSpec(memory_space=pltpu.VMEM)
+HBM = pl.BlockSpec(memory_space=pltpu.HBM)
 TOKEN = jax.ShapeDtypeStruct((8, 128), jnp.float32)
 
 N_NEAR, N_FAR, NEAR_A, NEAR_B, FAR_A, FAR_B, RANK, ORDER, CORE, X = 0, 1, 2, 10, 18, 22, 26, 30, 46, 47
@@ -40,38 +41,59 @@
     return jnp.dot(left, right, preferred_element_type=jnp.float32)
 
 
-def rings(first):
-    def place(y, z, core):
-        return ((z % 2 * 4 + y) * 2 + z // 2) * 2 + core
-
-    round_y, round_z = (0, 1) if first else (1, 0)
-    along_y = [[place(y, z, round_y) for y in range(4)] for z in range(4)]
-    along_z = [[place(y, z, round_z) for z in range(4)] for y in range(4)]
-    return along_y + along_z
+def rotations():
+    tables = []
+    for first in (True, False):
+        for shift in (1, 2, 3):
+            pairs = []
+            for lo in range(2):
+                for y in range(4):
+                    for hi in range(2):
+                        for x in range(4):
+                            for core in range(2):
+                                z = hi * 2 + lo
+                                if (core == 0) == first:
+                                    to_y, to_z = (y + shift) % 4, z
+                                else:
+                                    to_y, to_z = y, (z + shift) % 4
+                                here = (((lo * 4 + y) * 2 + hi) * 4 + x) * 2 + core
+                                there = (((to_z % 2 * 4 + to_y) * 2 + to_z // 2) * 4 + x) * 2 + core
+                                pairs.append((here, there))
+            tables.append(pairs)
+    return tables[:3], tables[3:]
 
 
 def rhs_kernel(cot_ref, rad_ref, *out_refs):
     width = cot_ref.shape[1] // 2
+    first = pl.program_id(0) == 0
     for chunk, out_ref in enumerate(out_refs):
         re = cot_ref[:, chunk * HALF : (chunk + 1) * HALF]
         im = cot_ref[:, width + chunk * HALF : width + (chunk + 1) * HALF]
-        out_ref[...] = dot(rad_ref[0], jnp.concatenate([re, im], 1)) + dot(
+        term = dot(rad_ref[0], jnp.concatenate([re, im], 1)) + dot(
             rad_ref[1], jnp.concatenate([-im, re], 1)
         )
 
+        @pl.when(first)
+        def _():
+            out_ref[...] = term
+
+        @pl.when(jnp.logical_not(first))
+        def _():
+            out_ref[...] += term
+
 
 def partial_rhs(cotangent, radiation):
     _, rows, dirs = radiation.shape
-    tile = 128
+    tile = 256
     return pl.pallas_call(
         rhs_kernel,
         name="rhs",
-        grid=(rows // tile,),
+        grid=(dirs // tile,),
         in_specs=[
-            pl.BlockSpec(cotangent.shape, lambda i: (0, 0)),
-            pl.BlockSpec((2, tile, dirs), lambda i: (0, i, 0)),
-        ],
-        out_specs=[pl.BlockSpec((tile, WIDE), lambda i: (i, 0))] * CHUNKS,
+            pl.BlockSpec((tile, cotangent.shape[1]), lambda i: (i, 0)),
+            pl.BlockSpec((2, rows, tile), lambda i: (0, 0, i)),
+        ],
+        out_specs=[pl.BlockSpec((rows, WIDE), lambda i: (0, 0))] * CHUNKS,
         out_shape=[jax.ShapeDtypeStruct((rows, WIDE), jnp.float32)] * CHUNKS,
         compiler_params=pltpu.CompilerParams(vmem_limit_bytes=VMEM_LIMIT),
         cost_estimate=pl.CostEstimate(flops=1 << 30, bytes_accessed=4 << 20, transcendentals=0),
@@ -113,7 +135,7 @@
     return pl.pallas_call(
         functools.partial(prepare_near_kernel, first),
         name=f"prepare_near_{first}",
-        in_specs=[SMEM, ANY],
+        in_specs=[SMEM, HBM],
         out_specs=[VMEM, VMEM],
         out_shape=[pltpu.VMEM((slots, CLUSTER, 4 * CLUSTER), jnp.bfloat16), TOKEN],
         scratch_shapes=[
@@ -122,7 +144,7 @@
         ],
         compiler_params=pltpu.CompilerParams(vmem_limit_bytes=SCOPED),
         cost_estimate=pl.CostEstimate(flops=1 << 28, bytes_accessed=slots << 21, transcendentals=0),
-    )(table, near_z)
+    )(table, pltpu.with_memory_space_constraint(near_z, pltpu.HBM))
 
 
 def prepare_far_kernel(table, u_ref, v_ref, u_out, v_out, token, u_in, v_in, sem_u, sem_v):
@@ -166,7 +188,7 @@
     return pl.pallas_call(
         prepare_far_kernel,
         name="prepare_far",
-        in_specs=[SMEM, ANY, ANY],
+        in_specs=[SMEM, HBM, HBM],
         out_specs=[VMEM, VMEM, VMEM],
         out_shape=[
             pltpu.VMEM((FAR, PAD, 4 * CLUSTER), jnp.bfloat16),
@@ -181,7 +203,7 @@
         ],
         compiler_params=pltpu.CompilerParams(vmem_limit_bytes=SCOPED),
         cost_estimate=pl.CostEstimate(flops=1 << 28, bytes_accessed=4 << 20, transcendentals=0),
-    )(table, far_ut, far_vt)
+    )(table, *(pltpu.with_memory_space_constraint(f, pltpu.HBM) for f in (far_ut, far_vt)))
 
 
 def parts_of(values):
@@ -197,7 +219,7 @@
 
 
 def apply_kernel(table, *refs):
-    held, (za_ref, zb_ref, u_ref, v_ref, out_ref, x_buf, fx_buf, sem_x, sem_fx) = refs[:8], refs[8:]
+    held, (za_ref, zb_ref, u_ref, v_ref), outs, (token, x_buf, fx_buf, sem_x, sem_fx) = refs[:8], refs[8:12], refs[12:16], refs[16:]
     near, far = table[N_NEAR], table[N_FAR]
     slots = za_ref.shape[0]
 
@@ -216,7 +238,12 @@
     def add(cluster, term):
         for half in range(2):
             rows = CLUSTER // 2
-            out_ref[table[ORDER + cluster * 2 + half]] += term[half * rows : (half + 1) * rows]
+            place = table[ORDER + cluster * 2 + half]
+            for steps, out_ref in enumerate(outs):
+
+                @pl.when(place // 4 == steps)
+                def _():
+                    out_ref[lax.rem(place, 4)] += term[half * rows : (half + 1) * rows]
 
     fetch(table[NEAR_A], x_buf.at[0], sem_x.at[0])
 
@@ -225,7 +252,8 @@
         return 0
 
     lax.fori_loop(0, far, far_start, 0)
-    out_ref[...] = jnp.zeros_like(out_ref)
+    for out_ref in (*outs, token):
+        out_ref[...] = jnp.zeros_like(out_ref)
 
     def near_steps(z_ref, first, last):
         def near_step(s, _):
@@ -257,8 +285,8 @@
         apply_kernel,
         name=f"apply_{index}",
         in_specs=[SMEM] + [ANY] * 8 + [VMEM] * 4,
-        out_specs=VMEM,
-        out_shape=pltpu.VMEM((16, CLUSTER // 2, WIDE), jnp.float32),
+        out_specs=[VMEM] * 5,
+        out_shape=[jax.ShapeDtypeStruct((4, CLUSTER // 2, WIDE), jnp.float32)] * 4 + [TOKEN],
         scratch_shapes=[
             pltpu.VMEM((2, CLUSTER, WIDE), jnp.float32),
             pltpu.VMEM((FAR, CLUSTER, WIDE), jnp.float32),
@@ -266,7 +294,7 @@
             pltpu.SemaphoreType.DMA((FAR,)),
         ],
         compiler_params=pltpu.CompilerParams(vmem_limit_bytes=SCOPED),
-        cost_estimate=pl.CostEstimate(flops=8 << 30, bytes_accessed=8 << 20, transcendentals=0),
+        cost_estimate=pl.CostEstimate(flops=40 << 30, bytes_accessed=8 << 20, transcendentals=0),
     )(table, *held, *blocks)
 
 
@@ -275,9 +303,9 @@
     col_base = lax.axis_index(COL) * 8
     core = lax.axis_index("core")
     index = lax.iota(jnp.int32, 16)
-    y = index // 2 % 4
-    z = index % 2 * 2 + index // 8
-    order = jnp.where(core == 0, y * 4 + z, z * 4 + y)
+    steps_y = (index // 2 - lax.axis_index("y")) % 4
+    steps_z = (index % 2 * 2 + index // 8 - lax.axis_index("zhi") * 2 - lax.axis_index("dir")) % 4
+    order = jnp.where(core == 0, steps_y * 4 + steps_z, steps_z * 4 + steps_y)
     pieces = [
         block_counts[0],
         near_pairs[:, 0] - row_base,
@@ -292,15 +320,11 @@
     return jnp.concatenate(pieces).astype(jnp.int32)
 
 
-def exchange(values, axes, groups=None):
-    return lax.all_to_all(values, axes, split_axis=0, concat_axis=0, tiled=True, axis_index_groups=groups)
-
-
 def shards(cotangent, radiation, near_z, near_pairs, far_ut, far_vt, far_pairs, far_ranks, block_counts):
     table = scalars(near_pairs, far_pairs, far_ranks, block_counts)
     own_0, own_1 = partial_rhs(cotangent, radiation)
     swap = [(0, 1), (1, 0)]
-    plane = ("dir", "y", "zhi", "core")
+    first_turn, second_turn = rotations()
 
     def others(own):
         return [lax.ppermute(own, "x", [(i, (i + k) % 4) for i in range(4)]) for k in (1, 2, 3)]
@@ -320,16 +344,19 @@
     around_1 = others(own_1)
     blocks = (blocks_a, blocks_b, blocks_u, blocks_v)
 
-    sums = []
-    for chunk, held in enumerate((held_0, None)):
-        if held is None:
-            held = both_cores([own_1, *around_1])
-        terms = apply_blocks(table, held, blocks, chunk).reshape(4, 4, CLUSTER // 2, WIDE)
-        if chunk == 0:
-            terms, *around_1 = lax.optimization_barrier((terms, *around_1))
-        sums.append(exchange(terms, plane, rings(True)).sum(axis=0))
-    result = exchange(jnp.stack(sums, axis=1), plane, rings(False)).sum(axis=0)
-    parts = [r[:, :HALF] for r in result] + [r[:, HALF:] for r in result]
+
+    def to_owner(mine, away, zero):
+        came = [lax.ppermute(part, AXES, turn) for part, turn in zip(away, first_turn)]
+        mine, *away = [mine[k] + came[0][k] + came[1][k] + came[2][k] for k in range(4)]
+        came = [lax.ppermute(part, AXES, turn) for part, turn in zip(away, second_turn)]
+        return mine + (came[0] + zero) + came[1] + came[2]
+
+    mine, *away, done_0 = apply_blocks(table, held_0, blocks, 0)
+    *around_1, done_0 = lax.optimization_barrier((*around_1, done_0))
+    results = [to_owner(mine, away, done_0[0, 0])]
+    mine, *away, done_1 = apply_blocks(table, both_cores([own_1, *around_1]), blocks, 1)
+    results.append(to_owner(mine, away, done_1[0, 0]))
+    parts = [r[:, :HALF] for r in results] + [r[:, HALF:] for r in results]
     return jnp.concatenate(parts, axis=1)
 
 

time: 172 us -> 147 us (0.85)
  local copies, waits for them, and re-layouts: 28.3 us -> 2.83 us
  blocking collectives: 24.5 us -> 0 us
  starting transfers between devices: 22.5 us -> 40.8 us
  waiting for transfers between devices: 69.4 us -> 76.2 us
  other arithmetic: 8.82 us -> 3.6 us
  Pallas kernels: 17.4 us -> 21.4 us
    ppermute x0 -> x12, waiting for transfers between devices: none -> 35.6 us  [to_owner(): lax.ppermute(part, AXES, turn)]
    all_to_all x2 -> x0, waiting for transfers between devices: 32.4 us -> none  [exchange(): lax.all_to_all(values, axes, split_axis=0, concat_axis=0, tiled=True, axi...]
    unnamed x40 -> x12, local copies, waits for them, and re-layouts: 26.5 us -> 0.02 us
    ppermute x0 -> x12, starting transfers between devices: none -> 24.9 us  [to_owner(): lax.ppermute(part, AXES, turn)]
    all_to_all x1 -> x0, blocking collectives: 24.5 us -> none  [exchange(): lax.all_to_all(values, axes, split_axis=0, concat_axis=0, tiled=True, axi...]
    all_to_all x2 -> x0, starting transfers between devices: 9.73 us -> none  [exchange(): lax.all_to_all(values, axes, split_axis=0, concat_axis=0, tiled=True, axi...]
    reduce_sum x3 -> x0, other arithmetic: 5.37 us -> none  [the longest x2 5.21 us: shards(): sums.append(exchange(terms, plane, rings(True)).sum(axis=0))]
    ppermute x1, waiting for transfers between devices: 3.34 us -> 7.9 us  [shards(): own_0 = own_0 + (lax.ppermute(own_0, 'dir', swap) + done_a[0, 0])]
  transfers between devices with their start and end apart: 18 -> 28, of which waited for: 12 -> 15; matrix products, arithmetic and copies ran while one was open for 3% -> 3% of each run, Pallas kernels for 7% -> 10%
where the time goes in v3:
time: 147 us; the launch traced here: 146 us
  waiting for transfers between devices  76.2 us (52%)
  starting transfers between devices  40.8 us (28%)
  Pallas kernels  21.4 us (15%)
  other arithmetic  3.6 us (2%)
  local copies, waits for them, and re-layouts  2.83 us (2%)
  between operations  1.51 us (1%)
    ppermute x12, waiting for transfers between devices, to_owner(): lax.ppermute(part, AXES, turn)  35.6 us
    ppermute x6, waiting for transfers between devices, others(): lax.ppermute(own, 'x', [(i, (i + k) % 4) for i in range(4)])  32.1 us
    ppermute x12, starting transfers between devices, to_owner(): lax.ppermute(part, AXES, turn)  24.9 us
    ppermute x6, starting transfers between devices, others(): lax.ppermute(own, 'x', [(i, (i + k) % 4) for i in range(4)])  11 us
    pallas_call x2, Pallas kernels, apply_blocks(): pl.pallas_call(apply_kernel, name=f'apply_{index}', in_specs=[SMEM] + [AN...  9.25 us
    ppermute x1, waiting for transfers between devices, shards(): own_0 = own_0 + (lax.ppermute(own_0, 'dir', swap) + done_a[0, 0])  7.9 us
    pallas_call x1, Pallas kernels, partial_rhs(): pl.pallas_call(rhs_kernel, name='rhs', grid=(dirs // tile,), in_specs=[pl...  6.08 us
    pallas_call x2, Pallas kernels, prepare_near(): pl.pallas_call(functools.partial(prepare_near_kernel, first), name=f'prep...  4.1 us
  transfers between devices with their start and end apart: 28, of which 15 were waited for; matrix products, arithmetic and copies ran while one was open for 3% of the time, Pallas kernels for 10%

profile of v3, /device:TPU:0, one launch (start us, length us, event | category | flops | bytes accessed | tf_op | source)
XLA Modules:
  0.0 146.3 jit_solution(13220935428710623138)
XLA Ops:
  0.0 6.1 %rhs.1 = (f32[512,256]{1,0:T(8,128)}, f32[512,256]{1,0:T(8,128)}) custom-call(bf16[1024,512]{1,0:T(8,128)(2,1)} %cot_ref.1, bf16[2,512,1024]{2,1,0:T(8,128)(2,1)} %rad_ref.1), custom_call_target="tpu_custom_call" | custom-call | flops 1073741824 | bytes 4194304 | tf_op jit(solution)/shard_map/rhs/pallas_call | solution.py:88
  6.1 2.0 %collective-permute-start = (f32[512,256]{1,0:T(8,128)}, f32[512,256]{1,0:T(8,128)S(1)}, u32[]{:S(2)}, u32[]{:S(2)}) collective-permute-start(f32[512,256]{1,0:T(8,128)} %get-tuple-element.34), channel_id=1, source_target_pairs={{0,64},{64,0},{1,65},{65,1},{2,66},{66,2},{3,67},{67,3},{4,68},{68... | collective-permute-start | bytes 1572872 | tf_op jit(solution)/shard_map/ppermute | solution.py:336
  8.3 3.5 %prepare_near_0.1 = (bf16[4,512,2048]{2,1,0:T(8,128)(2,1)S(1)}, f32[8,128]{1,0:T(8,128)S(1)}) custom-call(s32[48]{0:T(128)S(1)} %concatenate.6.table, f32[2,8,512,512]{3,2,1,0:T(8,128)} %z_ref.3), custom_call_target="tpu_custom_call" | custom-call | flops 268435456 | bytes 8388608 | tf_op jit(solution)/shard_map/prepare_near_0/pallas_call | solution.py:135
  12.3 7.9 %collective-permute-done = f32[512,256]{1,0:T(8,128)S(1)} collective-permute-done((f32[512,256]{1,0:T(8,128)}, f32[512,256]{1,0:T(8,128)S(1)}, u32[]{:S(2)}, u32[]{:S(2)}) %collective-permute-start) | collective-permute-done | bytes 524320 | tf_op jit(solution)/shard_map/ppermute | solution.py:336
  20.2 0.6 add_add_fusion.1.refs_0_
  20.9 1.8 %collective-permute-start.1 = (f32[512,256]{1,0:T(8,128)S(1)}, f32[512,256]{1,0:T(8,128)S(1)}, u32[]{:S(2)}, u32[]{:S(2)}) collective-permute-start(f32[512,256]{1,0:T(8,128)S(1)} %copy-done), channel_id=1, source_target_pairs={{0,64},{64,0},{1,65},{65,1},{2,66},{66,2},{3,67},{67,3},{4,68},{68... | collective-permute-start | bytes 1572872 | tf_op jit(solution)/shard_map/ppermute | solution.py:341
  22.7 1.5 %collective-permute-start.2 = (f32[512,256]{1,0:T(8,128)S(1)}, f32[512,256]{1,0:T(8,128)S(1)}, u32[]{:S(2)}, u32[]{:S(2)}) collective-permute-start(f32[512,256]{1,0:T(8,128)S(1)} %add_add_fusion.1.refs_0_), channel_id=1, source_target_pairs={{0,2},{2,4},{4,6},{6,0},{1,3},{3,5},{5,7},{7,1},{8,10},{10,12},{12... | collective-permute-start | bytes 1572872 | tf_op jit(solution)/shard_map/ppermute | solution.py:330
  24.2 2.7 %collective-permute-start.3 = (f32[512,256]{1,0:T(8,128)S(1)}, f32[512,256]{1,0:T(8,128)S(1)}, u32[]{:S(2)}, u32[]{:S(2)}) collective-permute-start(f32[512,256]{1,0:T(8,128)S(1)} %add_add_fusion.1.refs_0_), channel_id=1, source_target_pairs={{0,4},{2,6},{4,0},{6,2},{1,5},{3,7},{5,1},{7,3},{8,12},{10,14},{12... | collective-permute-start | bytes 1572872 | tf_op jit(solution)/shard_map/ppermute | solution.py:330
  26.9 1.4 collective-permute-start.4
  28.4 2.0 %prepare_far.1 = (bf16[4,128,2048]{2,1,0:T(8,128)(2,1)S(1)}, bf16[4,512,512]{2,1,0:T(8,128)(2,1)S(1)}, f32[8,128]{1,0:T(8,128)S(1)}) custom-call(s32[48]{0:T(128)S(1)} %concatenate.6.table, f32[2,4,96,512]{3,2,1,0:T(8,128)} %u_ref.1, f32[2,4,96,512]{3,2,1,0:T(8,128)} %v_ref.1), custom_call_target="tpu_custom_call" | custom-call | flops 268435456 | bytes 4194304 | tf_op jit(solution)/shard_map/prepare_far/pallas_call | solution.py:188
  30.4 0.6 slice.141
  30.9 0.6 prepare_near_4.1
  31.5 0.5 slice.140
  33.4 0.6 collective-permute-done.1
  34.1 3.7 %collective-permute-done.2.refs_1_ = f32[512,256]{1,0:T(8,128)S(1)} collective-permute-done((f32[512,256]{1,0:T(8,128)S(1)}, f32[512,256]{1,0:T(8,128)S(1)}, u32[]{:S(2)}, u32[]{:S(2)}) %collective-permute-start.2) | collective-permute-done | bytes 524320 | tf_op jit(solution)/shard_map/ppermute | solution.py:330
  37.8 10.9 %collective-permute-done.3.refs_2_ = f32[512,256]{1,0:T(8,128)S(1)} collective-permute-done((f32[512,256]{1,0:T(8,128)S(1)}, f32[512,256]{1,0:T(8,128)S(1)}, u32[]{:S(2)}, u32[]{:S(2)}) %collective-permute-start.3) | collective-permute-done | bytes 524320 | tf_op jit(solution)/shard_map/ppermute | solution.py:330
  48.6 0.5 collective-permute-start.7
  49.2 1.3 collective-permute-start.13
  50.5 2.4 %collective-permute-start.14 = (f32[512,256]{1,0:T(8,128)S(1)}, f32[512,256]{1,0:T(8,128)S(1)}, u32[]{:S(2)}, u32[]{:S(2)}) collective-permute-start(f32[512,256]{1,0:T(8,128)S(1)} %add_add_fusion.refs_0_), channel_id=1, source_target_pairs={{0,4},{2,6},{4,0},{6,2},{1,5},{3,7},{5,1},{7,3},{8,12},{10,14},{12... | collective-permute-start | bytes 1572872 | tf_op jit(solution)/shard_map/ppermute | solution.py:330
  52.9 1.6 %collective-permute-start.15 = (f32[512,256]{1,0:T(8,128)S(1)}, f32[512,256]{1,0:T(8,128)S(1)}, u32[]{:S(2)}, u32[]{:S(2)}) collective-permute-start(f32[512,256]{1,0:T(8,128)S(1)} %add_add_fusion.refs_0_), channel_id=1, source_target_pairs={{0,6},{2,0},{4,2},{6,4},{1,7},{3,1},{5,3},{7,5},{8,14},{10,8},{12,... | collective-permute-start | bytes 1572872 | tf_op jit(solution)/shard_map/ppermute | solution.py:330
  54.5 4.5 %apply_0.1 = (f32[4,256,256]{2,1,0:T(8,128)S(1)}, f32[4,256,256]{2,1,0:T(8,128)S(1)}, f32[4,256,256]{2,1,0:T(8,128)S(1)}, f32[4,256,256]{2,1,0:T(8,128)S(1)}, f32[8,128]{1,0:T(8,128)S(1)}) custom-call(s32[48]{0:T(128)S(1)} %concatenate.6.table, f32[512,256]{1,0:T(8,128)S(1)} %add_add_fusion.1.refs_0_, f32[512,256]{1,0:T(8,128)S(1)} %collective-permute-done.2.refs_1_, ...), custom_call_target="tpu_custom_call" | custom-call | flops 42949672960 | bytes 8388608 | tf_op jit(solution)/shard_map/apply_0/pallas_call | solution.py:284
  59.0 5.7 %collective-permute-done.13.refs_1_ = f32[512,256]{1,0:T(8,128)S(1)} collective-permute-done((f32[512,256]{1,0:T(8,128)S(1)}, f32[512,256]{1,0:T(8,128)S(1)}, u32[]{:S(2)}, u32[]{:S(2)}) %collective-permute-start.13) | collective-permute-done | bytes 524320 | tf_op jit(solution)/shard_map/ppermute | solution.py:330
  64.7 11.7 %collective-permute-done.14.refs_2_ = f32[512,256]{1,0:T(8,128)S(1)} collective-permute-done((f32[512,256]{1,0:T(8,128)S(1)}, f32[512,256]{1,0:T(8,128)S(1)}, u32[]{:S(2)}, u32[]{:S(2)}) %collective-permute-start.14) | collective-permute-done | bytes 524320 | tf_op jit(solution)/shard_map/ppermute | solution.py:330
  76.6 0.5 collective-permute-start.20
  77.1 3.2 %collective-permute-start.10 = (f32[4,256,256]{2,1,0:T(8,128)S(1)}, f32[4,256,256]{2,1,0:T(8,128)S(1)}, u32[]{:S(2)}, u32[]{:S(2)}) collective-permute-start(f32[4,256,256]{2,1,0:T(8,128)S(1)} %get-tuple-element.50), channel_id=1, source_target_pairs={{0,32},{1,9},{2,34},{3,11},{4,36},{5,13},{6,38},{7,15},{8,40},{9,1... | collective-permute-start | bytes 3145736 | tf_op jit(solution)/shard_map/ppermute | solution.py:349
  80.3 1.1 collective-permute-start.11
  81.3 1.0 collective-permute-start.9
  82.3 4.7 %apply_1.1 = (f32[4,256,256]{2,1,0:T(8,128)S(1)}, f32[4,256,256]{2,1,0:T(8,128)S(1)}, f32[4,256,256]{2,1,0:T(8,128)S(1)}, f32[4,256,256]{2,1,0:T(8,128)S(1)}, f32[8,128]{1,0:T(8,128)S(1)}) custom-call(s32[48]{0:T(128)S(1)} %concatenate.6.table, f32[512,256]{1,0:T(8,128)S(1)} %add_add_fusion.refs_0_, f32[512,256]{1,0:T(8,128)S(1)} %collective-permute-done.13.refs_1_, ...), custom_call_target="tpu_custom_call" | custom-call | flops 42949672960 | bytes 8388608 | tf_op jit(solution)/shard_map/apply_1/pallas_call | solution.py:284
  87.0 0.7 collective-permute-start.22
  87.8 3.0 %collective-permute-start.23 = (f32[4,256,256]{2,1,0:T(8,128)S(1)}, f32[4,256,256]{2,1,0:T(8,128)S(1)}, u32[]{:S(2)}, u32[]{:S(2)}) collective-permute-start(f32[4,256,256]{2,1,0:T(8,128)S(1)} %get-tuple-element.60), channel_id=1, source_target_pairs={{0,32},{1,9},{2,34},{3,11},{4,36},{5,13},{6,38},{7,15},{8,40},{9,1... | collective-permute-start | bytes 3145736 | tf_op jit(solution)/shard_map/ppermute | solution.py:349
  90.8 2.7 %collective-permute-done.10 = f32[4,256,256]{2,1,0:T(8,128)S(1)} collective-permute-done((f32[4,256,256]{2,1,0:T(8,128)S(1)}, f32[4,256,256]{2,1,0:T(8,128)S(1)}, u32[]{:S(2)}, u32[]{:S(2)}) %collective-permute-start.10) | collective-permute-done | bytes 1048608 | tf_op jit(solution)/shard_map/ppermute | solution.py:349
  93.5 3.0 %collective-permute-start.24 = (f32[4,256,256]{2,1,0:T(8,128)S(1)}, f32[4,256,256]{2,1,0:T(8,128)S(1)}, u32[]{:S(2)}, u32[]{:S(2)}) collective-permute-start(f32[4,256,256]{2,1,0:T(8,128)S(1)} %get-tuple-element.61), channel_id=1, source_target_pairs={{0,48},{1,73},{2,50},{3,75},{4,52},{5,77},{6,54},{7,79},{8,56},{9,... | collective-permute-start | bytes 3145736 | tf_op jit(solution)/shard_map/ppermute | solution.py:349
  96.5 0.6 slice.150
  97.1 0.5 slice.168
  97.6 7.4 %collective-permute-done.11 = f32[4,256,256]{2,1,0:T(8,128)S(1)} collective-permute-done((f32[4,256,256]{2,1,0:T(8,128)S(1)}, f32[4,256,256]{2,1,0:T(8,128)S(1)}, u32[]{:S(2)}, u32[]{:S(2)}) %collective-permute-start.11) | collective-permute-done | bytes 1048608 | tf_op jit(solution)/shard_map/ppermute | solution.py:349
  105.3 0.5 collective-permute-start.12
  105.8 3.5 %collective-permute-start.16 = (f32[256,256]{1,0:T(8,128)S(1)}, f32[256,256]{1,0:T(8,128)S(1)}, u32[]{:S(2)}, u32[]{:S(2)}) collective-permute-start(f32[256,256]{1,0:T(8,128)S(1)} %get-tuple-element.65), channel_id=1, source_target_pairs={{0,8},{1,33},{2,10},{3,35},{4,12},{5,37},{6,14},{7,39},{8,0},{9,41... | collective-permute-start | bytes 786440 | tf_op jit(solution)/shard_map/ppermute | solution.py:351
  109.3 12.2 %collective-permute-done.22 = f32[4,256,256]{2,1,0:T(8,128)S(1)} collective-permute-done((f32[4,256,256]{2,1,0:T(8,128)S(1)}, f32[4,256,256]{2,1,0:T(8,128)S(1)}, u32[]{:S(2)}, u32[]{:S(2)}) %collective-permute-start.22) | collective-permute-done | bytes 1048608 | tf_op jit(solution)/shard_map/ppermute | solution.py:349
  121.5 2.5 %collective-permute-start.17 = (f32[256,256]{1,0:T(8,128)S(1)}, f32[256,256]{1,0:T(8,128)S(1)}, u32[]{:S(2)}, u32[]{:S(2)}) collective-permute-start(f32[256,256]{1,0:T(8,128)S(1)} %get-tuple-element.64), channel_id=1, source_target_pairs={{0,72},{1,49},{2,74},{3,51},{4,76},{5,53},{6,78},{7,55},{8,64},{9,... | collective-permute-start | bytes 786440 | tf_op jit(solution)/shard_map/ppermute | solution.py:351
  124.0 8.7 %collective-permute-done.23 = f32[4,256,256]{2,1,0:T(8,128)S(1)} collective-permute-done((f32[4,256,256]{2,1,0:T(8,128)S(1)}, f32[4,256,256]{2,1,0:T(8,128)S(1)}, u32[]{:S(2)}, u32[]{:S(2)}) %collective-permute-start.23) | collective-permute-done | bytes 1048608 | tf_op jit(solution)/shard_map/ppermute | solution.py:349
  133.4 0.5 collective-permute-start.25
  133.9 3.5 %collective-permute-start.26 = (f32[256,256]{1,0:T(8,128)S(1)}, f32[256,256]{1,0:T(8,128)S(1)}, u32[]{:S(2)}, u32[]{:S(2)}) collective-permute-start(f32[256,256]{1,0:T(8,128)S(1)} %get-tuple-element.68), channel_id=1, source_target_pairs={{0,8},{1,33},{2,10},{3,35},{4,12},{5,37},{6,14},{7,39},{8,0},{9,41... | collective-permute-start | bytes 786440 | tf_op jit(solution)/shard_map/ppermute | solution.py:351
  137.4 2.2 %collective-permute-start.27 = (f32[256,256]{1,0:T(8,128)S(1)}, f32[256,256]{1,0:T(8,128)S(1)}, u32[]{:S(2)}, u32[]{:S(2)}) collective-permute-start(f32[256,256]{1,0:T(8,128)S(1)} %get-tuple-element.67), channel_id=1, source_target_pairs={{0,72},{1,49},{2,74},{3,51},{4,76},{5,53},{6,78},{7,55},{8,64},{9,... | collective-permute-start | bytes 786440 | tf_op jit(solution)/shard_map/ppermute | solution.py:351
  139.7 0.8 fusion.13
  140.5 0.5 collective-permute-done.25
  141.0 3.5 %collective-permute-done.26 = f32[256,256]{1,0:T(8,128)S(1)} collective-permute-done((f32[256,256]{1,0:T(8,128)S(1)}, f32[256,256]{1,0:T(8,128)S(1)}, u32[]{:S(2)}, u32[]{:S(2)}) %collective-permute-start.26) | collective-permute-done | bytes 262176 | tf_op jit(solution)/shard_map/ppermute | solution.py:351
  144.7 0.8 fusion.6
  145.5 0.8 pad_maximum_fusion
  (44 shorter events, 2.0 us)
Async XLA Ops:
  0.0 8.1 %copy-start.2 = (s32[4,2]{0,1:T(2,128)S(1)}, s32[4,2]{0,1:T(2,128)}, u32[]{:S(2)}) copy-start(s32[4,2]{0,1:T(2,128)} %param.15) | copy-start | bytes 100
  0.0 8.2 %copy-start.3 = (s32[8,2]{0,1:T(2,128)S(1)}, s32[8,2]{0,1:T(2,128)}, u32[]{:S(2)}) copy-start(s32[8,2]{0,1:T(2,128)} %param.12) | copy-start | bytes 196
  0.0 8.2 %copy-start.4 = (s32[1,2]{1,0:T(1,128)S(1)}, s32[1,2]{1,0:T(1,128)}, u32[]{:S(2)}) copy-start(s32[1,2]{1,0:T(1,128)} %param.17) | copy-start | bytes 28
  0.0 8.2 %copy-start.5 = (s32[4]{0:T(128)S(1)}, s32[4]{0:T(128)}, u32[]{:S(2)}) copy-start(s32[4]{0:T(128)} %param.16) | copy-start | bytes 52
  6.1 14.1 %collective-permute-start = (f32[512,256]{1,0:T(8,128)}, f32[512,256]{1,0:T(8,128)S(1)}, u32[]{:S(2)}, u32[]{:S(2)}) collective-permute-start(f32[512,256]{1,0:T(8,128)} %get-tuple-element.34), channel_id=1, source_target_pairs={{0,64},{64,0},{1,65},{65,1},{2,66},{66,2},{3,67},{67,3},{4,68},{68... | collective-permute-start | bytes 1572872 | tf_op jit(solution)/shard_map/ppermute | solution.py:336
  8.3 11.9 %copy-start.1 = (f32[512,256]{1,0:T(8,128)S(1)}, f32[512,256]{1,0:T(8,128)}, u32[]{:S(2)}) copy-start(f32[512,256]{1,0:T(8,128)} %get-tuple-element.34) | copy-start | bytes 1572868
  8.3 12.6 %copy-start = (f32[512,256]{1,0:T(8,128)S(1)}, f32[512,256]{1,0:T(8,128)}, u32[]{:S(2)}) copy-start(f32[512,256]{1,0:T(8,128)} %get-tuple-element.38) | copy-start | bytes 1572868
  20.9 13.2 %collective-permute-start.1 = (f32[512,256]{1,0:T(8,128)S(1)}, f32[512,256]{1,0:T(8,128)S(1)}, u32[]{:S(2)}, u32[]{:S(2)}) collective-permute-start(f32[512,256]{1,0:T(8,128)S(1)} %copy-done), channel_id=1, source_target_pairs={{0,64},{64,0},{1,65},{65,1},{2,66},{66,2},{3,67},{67,3},{4,68},{68... | collective-permute-start | bytes 1572872 | tf_op jit(solution)/shard_map/ppermute | solution.py:341
  22.7 15.1 %collective-permute-start.2 = (f32[512,256]{1,0:T(8,128)S(1)}, f32[512,256]{1,0:T(8,128)S(1)}, u32[]{:S(2)}, u32[]{:S(2)}) collective-permute-start(f32[512,256]{1,0:T(8,128)S(1)} %add_add_fusion.1.refs_0_), channel_id=1, source_target_pairs={{0,2},{2,4},{4,6},{6,0},{1,3},{3,5},{5,7},{7,1},{8,10},{10,12},{12... | collective-permute-start | bytes 1572872 | tf_op jit(solution)/shard_map/ppermute | solution.py:330
  24.2 24.4 %collective-permute-start.3 = (f32[512,256]{1,0:T(8,128)S(1)}, f32[512,256]{1,0:T(8,128)S(1)}, u32[]{:S(2)}, u32[]{:S(2)}) collective-permute-start(f32[512,256]{1,0:T(8,128)S(1)} %add_add_fusion.1.refs_0_), channel_id=1, source_target_pairs={{0,4},{2,6},{4,0},{6,2},{1,5},{3,7},{5,1},{7,3},{8,12},{10,14},{12... | collective-permute-start | bytes 1572872 | tf_op jit(solution)/shard_map/ppermute | solution.py:330
  26.9 21.7 %collective-permute-start.4 = (f32[512,256]{1,0:T(8,128)S(1)}, f32[512,256]{1,0:T(8,128)S(1)}, u32[]{:S(2)}, u32[]{:S(2)}) collective-permute-start(f32[512,256]{1,0:T(8,128)S(1)} %add_add_fusion.1.refs_0_), channel_id=1, source_target_pairs={{0,6},{2,0},{4,2},{6,4},{1,7},{3,1},{5,3},{7,5},{8,14},{10,8},{12,... | collective-permute-start | bytes 1572872 | tf_op jit(solution)/shard_map/ppermute | solution.py:330
  33.4 17.1 %collective-permute-start.5 = (f32[512,256]{1,0:T(8,128)S(1)}, f32[512,256]{1,0:T(8,128)S(1)}, u32[]{:S(2)}, u32[]{:S(2)}) collective-permute-start(f32[512,256]{1,0:T(8,128)S(1)} %add_add_fusion.1.refs_0_), channel_id=1, source_target_pairs={{0,1},{1,0},{2,3},{3,2},{4,5},{5,4},{6,7},{7,6},{8,9},{9,8},{10,11... | collective-permute-start | bytes 1572872 | tf_op jit(solution)/shard_map/ppermute | solution.py:333
  48.6 4.3 %collective-permute-start.6 = (f32[512,256]{1,0:T(8,128)S(1)}, f32[512,256]{1,0:T(8,128)S(1)}, u32[]{:S(2)}, u32[]{:S(2)}) collective-permute-start(f32[512,256]{1,0:T(8,128)S(1)} %collective-permute-done.2.refs_1_), channel_id=1, source_target_pairs={{0,1},{1,0},{2,3},{3,2},{4,5},{5,4},{6,7},{7,6},{8,9},{9,8},{10,11... | collective-permute-start | bytes 1572872 | tf_op jit(solution)/shard_map/ppermute | solution.py:333
  48.6 5.8 %collective-permute-start.7 = (f32[512,256]{1,0:T(8,128)S(1)}, f32[512,256]{1,0:T(8,128)S(1)}, u32[]{:S(2)}, u32[]{:S(2)}) collective-permute-start(f32[512,256]{1,0:T(8,128)S(1)} %collective-permute-done.3.refs_2_), channel_id=1, source_target_pairs={{0,1},{1,0},{2,3},{3,2},{4,5},{5,4},{6,7},{7,6},{8,9},{9,8},{10,11... | collective-permute-start | bytes 1572872 | tf_op jit(solution)/shard_map/ppermute | solution.py:333
  49.2 5.3 %collective-permute-start.8 = (f32[512,256]{1,0:T(8,128)S(1)}, f32[512,256]{1,0:T(8,128)S(1)}, u32[]{:S(2)}, u32[]{:S(2)}) collective-permute-start(f32[512,256]{1,0:T(8,128)S(1)} %collective-permute-done.4.refs_3_), channel_id=1, source_target_pairs={{0,1},{1,0},{2,3},{3,2},{4,5},{5,4},{6,7},{7,6},{8,9},{9,8},{10,11... | collective-permute-start | bytes 1572872 | tf_op jit(solution)/shard_map/ppermute | solution.py:333
  49.2 15.5 %collective-permute-start.13 = (f32[512,256]{1,0:T(8,128)S(1)}, f32[512,256]{1,0:T(8,128)S(1)}, u32[]{:S(2)}, u32[]{:S(2)}) collective-permute-start(f32[512,256]{1,0:T(8,128)S(1)} %add_add_fusion.refs_0_), channel_id=1, source_target_pairs={{0,2},{2,4},{4,6},{6,0},{1,3},{3,5},{5,7},{7,1},{8,10},{10,12},{12... | collective-permute-start | bytes 1572872 | tf_op jit(solution)/shard_map/ppermute | solution.py:330
  50.5 25.9 %collective-permute-start.14 = (f32[512,256]{1,0:T(8,128)S(1)}, f32[512,256]{1,0:T(8,128)S(1)}, u32[]{:S(2)}, u32[]{:S(2)}) collective-permute-start(f32[512,256]{1,0:T(8,128)S(1)} %add_add_fusion.refs_0_), channel_id=1, source_target_pairs={{0,4},{2,6},{4,0},{6,2},{1,5},{3,7},{5,1},{7,3},{8,12},{10,14},{12... | collective-permute-start | bytes 1572872 | tf_op jit(solution)/shard_map/ppermute | solution.py:330
  52.9 23.7 %collective-permute-start.15 = (f32[512,256]{1,0:T(8,128)S(1)}, f32[512,256]{1,0:T(8,128)S(1)}, u32[]{:S(2)}, u32[]{:S(2)}) collective-permute-start(f32[512,256]{1,0:T(8,128)S(1)} %add_add_fusion.refs_0_), channel_id=1, source_target_pairs={{0,6},{2,0},{4,2},{6,4},{1,7},{3,1},{5,3},{7,5},{8,14},{10,8},{12,... | collective-permute-start | bytes 1572872 | tf_op jit(solution)/shard_map/ppermute | solution.py:330
  54.5 25.8 %collective-permute-start.18 = (f32[512,256]{1,0:T(8,128)S(1)}, f32[512,256]{1,0:T(8,128)S(1)}, u32[]{:S(2)}, u32[]{:S(2)}) collective-permute-start(f32[512,256]{1,0:T(8,128)S(1)} %add_add_fusion.refs_0_), channel_id=1, source_target_pairs={{0,1},{1,0},{2,3},{3,2},{4,5},{5,4},{6,7},{7,6},{8,9},{9,8},{10,11... | collective-permute-start | bytes 1572872 | tf_op jit(solution)/shard_map/ppermute | solution.py:333
  76.6 4.8 %collective-permute-start.19 = (f32[512,256]{1,0:T(8,128)S(1)}, f32[512,256]{1,0:T(8,128)S(1)}, u32[]{:S(2)}, u32[]{:S(2)}) collective-permute-start(f32[512,256]{1,0:T(8,128)S(1)} %collective-permute-done.13.refs_1_), channel_id=1, source_target_pairs={{0,1},{1,0},{2,3},{3,2},{4,5},{5,4},{6,7},{7,6},{8,9},{9,8},{10,11... | collective-permute-start | bytes 1572872 | tf_op jit(solution)/shard_map/ppermute | solution.py:333
  76.6 5.8 %collective-permute-start.20 = (f32[512,256]{1,0:T(8,128)S(1)}, f32[512,256]{1,0:T(8,128)S(1)}, u32[]{:S(2)}, u32[]{:S(2)}) collective-permute-start(f32[512,256]{1,0:T(8,128)S(1)} %collective-permute-done.14.refs_2_), channel_id=1, source_target_pairs={{0,1},{1,0},{2,3},{3,2},{4,5},{5,4},{6,7},{7,6},{8,9},{9,8},{10,11... | collective-permute-start | bytes 1572872 | tf_op jit(solution)/shard_map/ppermute | solution.py:333
  77.1 5.2 %collective-permute-start.21 = (f32[512,256]{1,0:T(8,128)S(1)}, f32[512,256]{1,0:T(8,128)S(1)}, u32[]{:S(2)}, u32[]{:S(2)}) collective-permute-start(f32[512,256]{1,0:T(8,128)S(1)} %collective-permute-done.15.refs_3_), channel_id=1, source_target_pairs={{0,1},{1,0},{2,3},{3,2},{4,5},{5,4},{6,7},{7,6},{8,9},{9,8},{10,11... | collective-permute-start | bytes 1572872 | tf_op jit(solution)/shard_map/ppermute | solution.py:333
  77.1 16.4 %collective-permute-start.10 = (f32[4,256,256]{2,1,0:T(8,128)S(1)}, f32[4,256,256]{2,1,0:T(8,128)S(1)}, u32[]{:S(2)}, u32[]{:S(2)}) collective-permute-start(f32[4,256,256]{2,1,0:T(8,128)S(1)} %get-tuple-element.50), channel_id=1, source_target_pairs={{0,32},{1,9},{2,34},{3,11},{4,36},{5,13},{6,38},{7,15},{8,40},{9,1... | collective-permute-start | bytes 3145736 | tf_op jit(solution)/shard_map/ppermute | solution.py:349
  80.3 24.7 %collective-permute-start.11 = (f32[4,256,256]{2,1,0:T(8,128)S(1)}, f32[4,256,256]{2,1,0:T(8,128)S(1)}, u32[]{:S(2)}, u32[]{:S(2)}) collective-permute-start(f32[4,256,256]{2,1,0:T(8,128)S(1)} %get-tuple-element.51), channel_id=1, source_target_pairs={{0,48},{1,73},{2,50},{3,75},{4,52},{5,77},{6,54},{7,79},{8,56},{9,... | collective-permute-start | bytes 3145736 | tf_op jit(solution)/shard_map/ppermute | solution.py:349
  81.3 23.7 %collective-permute-start.9 = (f32[4,256,256]{2,1,0:T(8,128)S(1)}, f32[4,256,256]{2,1,0:T(8,128)S(1)}, u32[]{:S(2)}, u32[]{:S(2)}) collective-permute-start(f32[4,256,256]{2,1,0:T(8,128)S(1)} %get-tuple-element.49), channel_id=1, source_target_pairs={{0,16},{1,65},{2,18},{3,67},{4,20},{5,69},{6,22},{7,71},{8,24},{9,... | collective-permute-start | bytes 3145736 | tf_op jit(solution)/shard_map/ppermute | solution.py:349
  87.0 34.4 %collective-permute-start.22 = (f32[4,256,256]{2,1,0:T(8,128)S(1)}, f32[4,256,256]{2,1,0:T(8,128)S(1)}, u32[]{:S(2)}, u32[]{:S(2)}) collective-permute-start(f32[4,256,256]{2,1,0:T(8,128)S(1)} %get-tuple-element.59), channel_id=1, source_target_pairs={{0,16},{1,65},{2,18},{3,67},{4,20},{5,69},{6,22},{7,71},{8,24},{9,... | collective-permute-start | bytes 3145736 | tf_op jit(solution)/shard_map/ppermute | solution.py:349
  87.8 45.0 %collective-permute-start.23 = (f32[4,256,256]{2,1,0:T(8,128)S(1)}, f32[4,256,256]{2,1,0:T(8,128)S(1)}, u32[]{:S(2)}, u32[]{:S(2)}) collective-permute-start(f32[4,256,256]{2,1,0:T(8,128)S(1)} %get-tuple-element.60), channel_id=1, source_target_pairs={{0,32},{1,9},{2,34},{3,11},{4,36},{5,13},{6,38},{7,15},{8,40},{9,1... | collective-permute-start | bytes 3145736 | tf_op jit(solution)/shard_map/ppermute | solution.py:349
  93.5 39.7 %collective-permute-start.24 = (f32[4,256,256]{2,1,0:T(8,128)S(1)}, f32[4,256,256]{2,1,0:T(8,128)S(1)}, u32[]{:S(2)}, u32[]{:S(2)}) collective-permute-start(f32[4,256,256]{2,1,0:T(8,128)S(1)} %get-tuple-element.61), channel_id=1, source_target_pairs={{0,48},{1,73},{2,50},{3,75},{4,52},{5,77},{6,54},{7,79},{8,56},{9,... | collective-permute-start | bytes 3145736 | tf_op jit(solution)/shard_map/ppermute | solution.py:349
  105.3 32.2 %collective-permute-start.12 = (f32[256,256]{1,0:T(8,128)S(1)}, f32[256,256]{1,0:T(8,128)S(1)}, u32[]{:S(2)}, u32[]{:S(2)}) collective-permute-start(f32[256,256]{1,0:T(8,128)S(1)} %get-tuple-element.63), channel_id=1, source_target_pairs={{0,64},{1,17},{2,66},{3,19},{4,68},{5,21},{6,70},{7,23},{8,72},{9,... | collective-permute-start | bytes 786440 | tf_op jit(solution)/shard_map/ppermute | solution.py:351
  105.8 33.9 %collective-permute-start.16 = (f32[256,256]{1,0:T(8,128)S(1)}, f32[256,256]{1,0:T(8,128)S(1)}, u32[]{:S(2)}, u32[]{:S(2)}) collective-permute-start(f32[256,256]{1,0:T(8,128)S(1)} %get-tuple-element.65), channel_id=1, source_target_pairs={{0,8},{1,33},{2,10},{3,35},{4,12},{5,37},{6,14},{7,39},{8,0},{9,41... | collective-permute-start | bytes 786440 | tf_op jit(solution)/shard_map/ppermute | solution.py:351
  121.5 18.2 %collective-permute-start.17 = (f32[256,256]{1,0:T(8,128)S(1)}, f32[256,256]{1,0:T(8,128)S(1)}, u32[]{:S(2)}, u32[]{:S(2)}) collective-permute-start(f32[256,256]{1,0:T(8,128)S(1)} %get-tuple-element.64), channel_id=1, source_target_pairs={{0,72},{1,49},{2,74},{3,51},{4,76},{5,53},{6,78},{7,55},{8,64},{9,... | collective-permute-start | bytes 786440 | tf_op jit(solution)/shard_map/ppermute | solution.py:351
  133.4 7.7 %collective-permute-start.25 = (f32[256,256]{1,0:T(8,128)S(1)}, f32[256,256]{1,0:T(8,128)S(1)}, u32[]{:S(2)}, u32[]{:S(2)}) collective-permute-start(f32[256,256]{1,0:T(8,128)S(1)} %get-tuple-element.66), channel_id=1, source_target_pairs={{0,64},{1,17},{2,66},{3,19},{4,68},{5,21},{6,70},{7,23},{8,72},{9,... | collective-permute-start | bytes 786440 | tf_op jit(solution)/shard_map/ppermute | solution.py:351
  133.9 10.7 %collective-permute-start.26 = (f32[256,256]{1,0:T(8,128)S(1)}, f32[256,256]{1,0:T(8,128)S(1)}, u32[]{:S(2)}, u32[]{:S(2)}) collective-permute-start(f32[256,256]{1,0:T(8,128)S(1)} %get-tuple-element.68), channel_id=1, source_target_pairs={{0,8},{1,33},{2,10},{3,35},{4,12},{5,37},{6,14},{7,39},{8,0},{9,41... | collective-permute-start | bytes 786440 | tf_op jit(solution)/shard_map/ppermute | solution.py:351
  137.4 7.3 %collective-permute-start.27 = (f32[256,256]{1,0:T(8,128)S(1)}, f32[256,256]{1,0:T(8,128)S(1)}, u32[]{:S(2)}, u32[]{:S(2)}) collective-permute-start(f32[256,256]{1,0:T(8,128)S(1)} %get-tuple-element.67), channel_id=1, source_target_pairs={{0,72},{1,49},{2,74},{3,51},{4,76},{5,53},{6,78},{7,55},{8,64},{9,... | collective-permute-start | bytes 786440 | tf_op jit(solution)/shard_map/ppermute | solution.py:351

commit v4 on v3

--- a/solution.py
+++ b/solution.py
@@ -63,41 +63,44 @@
     return tables[:3], tables[3:]
 
 
-def rhs_kernel(cot_ref, rad_ref, *out_refs):
-    width = cot_ref.shape[1] // 2
-    first = pl.program_id(0) == 0
-    for chunk, out_ref in enumerate(out_refs):
-        re = cot_ref[:, chunk * HALF : (chunk + 1) * HALF]
-        im = cot_ref[:, width + chunk * HALF : width + (chunk + 1) * HALF]
-        term = dot(rad_ref[0], jnp.concatenate([re, im], 1)) + dot(
-            rad_ref[1], jnp.concatenate([-im, re], 1)
-        )
-
-        @pl.when(first)
-        def _():
-            out_ref[...] = term
-
-        @pl.when(jnp.logical_not(first))
-        def _():
-            out_ref[...] += term
+def rhs_kernel(cot_ref, rad_ref, out_0, out_1, cot, rad, sem_c, sem_r):
+    width = cot.shape[1] // 2
+    rows = rad.shape[1] // sem_r.shape[0]
+    copies = [pltpu.make_async_copy(cot_ref, cot, sem_c.at[0])]
+    for i in range(sem_r.shape[0]):
+        tile = pl.ds(i * rows, rows)
+        copies.append(pltpu.make_async_copy(rad_ref.at[:, tile], rad.at[:, tile], sem_r.at[i]))
+    for copy in copies:
+        copy.start()
+    copies[0].wait()
+    for i, copy in enumerate(copies[1:]):
+        tile = slice(i * rows, (i + 1) * rows)
+        copy.wait()
+        for chunk, out_ref in enumerate((out_0, out_1)):
+            re = cot[:, chunk * HALF : (chunk + 1) * HALF]
+            im = cot[:, width + chunk * HALF : width + (chunk + 1) * HALF]
+            out_ref[tile] = dot(rad[0, tile], jnp.concatenate([re, im], 1)) + dot(
+                rad[1, tile], jnp.concatenate([-im, re], 1)
+            )
 
 
 def partial_rhs(cotangent, radiation):
-    _, rows, dirs = radiation.shape
-    tile = 256
+    rows = radiation.shape[1]
     return pl.pallas_call(
         rhs_kernel,
         name="rhs",
-        grid=(dirs // tile,),
-        in_specs=[
-            pl.BlockSpec((tile, cotangent.shape[1]), lambda i: (i, 0)),
-            pl.BlockSpec((2, rows, tile), lambda i: (0, 0, i)),
-        ],
-        out_specs=[pl.BlockSpec((rows, WIDE), lambda i: (0, 0))] * CHUNKS,
-        out_shape=[jax.ShapeDtypeStruct((rows, WIDE), jnp.float32)] * CHUNKS,
-        compiler_params=pltpu.CompilerParams(vmem_limit_bytes=VMEM_LIMIT),
+        in_specs=[HBM, HBM],
+        out_specs=[VMEM] * CHUNKS,
+        out_shape=[pltpu.VMEM((rows, WIDE), jnp.float32)] * CHUNKS,
+        scratch_shapes=[
+            pltpu.VMEM(cotangent.shape, cotangent.dtype),
+            pltpu.VMEM(radiation.shape, radiation.dtype),
+            pltpu.SemaphoreType.DMA((1,)),
+            pltpu.SemaphoreType.DMA((2,)),
+        ],
+        compiler_params=pltpu.CompilerParams(vmem_limit_bytes=SCOPED),
         cost_estimate=pl.CostEstimate(flops=1 << 30, bytes_accessed=4 << 20, transcendentals=0),
-    )(cotangent, radiation)
+    )(*(pltpu.with_memory_space_constraint(f, pltpu.HBM) for f in (cotangent, radiation)))
 
 
 def prepare_near_kernel(first, table, z_ref, out_ref, token, z_in, sem_in):
@@ -218,19 +221,20 @@
     return dot(left, jnp.concatenate([high, high], 0)) + dot(left[:, : left.shape[1] // 2], low)
 
 
-def apply_kernel(table, *refs):
-    held, (za_ref, zb_ref, u_ref, v_ref), outs, (token, x_buf, fx_buf, sem_x, sem_fx) = refs[:8], refs[8:12], refs[12:16], refs[16:]
+def apply_kernel(pieces, table, *refs):
+    held, refs = refs[: len(pieces)], refs[len(pieces) :]
+    (za_ref, zb_ref, u_ref, v_ref), outs, (token, x_buf, fx_buf, sem_x, sem_fx) = refs[:4], refs[4:8], refs[8:]
     near, far = table[N_NEAR], table[N_FAR]
     slots = za_ref.shape[0]
 
     def fetch(cluster, buf, sem):
         steps = lax.rem(table[X] + 4 - cluster // 2, 4)
-        other = jnp.where(lax.rem(cluster, 2) == table[CORE], 0, 4)
-        for place, ref in enumerate(held):
-
-            @pl.when(steps + other == place)
+        other = jnp.where(lax.rem(cluster, 2) == table[CORE], 0, 1)
+        for ref, (came, crossed, row) in zip(held, pieces):
+
+            @pl.when((steps == came) & (other == crossed))
             def _():
-                pltpu.make_async_copy(ref, buf, sem).start()
+                pltpu.make_async_copy(ref, buf.at[pl.ds(row, ref.shape[0])], sem).start()
 
     def fetched(buf, sem):
         pltpu.make_async_copy(held[0], buf, sem).wait()
@@ -280,11 +284,11 @@
     lax.fori_loop(0, far, far_step, 0)
 
 
-def apply_blocks(table, held, blocks, index):
+def apply_blocks(table, pieces, held, blocks, index):
     return pl.pallas_call(
-        apply_kernel,
+        functools.partial(apply_kernel, pieces),
         name=f"apply_{index}",
-        in_specs=[SMEM] + [ANY] * 8 + [VMEM] * 4,
+        in_specs=[SMEM] + [ANY] * len(held) + [VMEM] * 4,
         out_specs=[VMEM] * 5,
         out_shape=[jax.ShapeDtypeStruct((4, CLUSTER // 2, WIDE), jnp.float32)] * 4 + [TOKEN],
         scratch_shapes=[
@@ -326,22 +330,31 @@
     swap = [(0, 1), (1, 0)]
     first_turn, second_turn = rotations()
 
-    def others(own):
-        return [lax.ppermute(own, "x", [(i, (i + k) % 4) for i in range(4)]) for k in (1, 2, 3)]
+    def step(part, k):
+        return lax.ppermute(part, "x", [(i, (i + k) % 4) for i in range(4)])
 
     def both_cores(mine):
         return mine + [lax.ppermute(part, "core", swap) for part in mine]
+
+    def on_both(places):
+        return tuple((came, crossed, row) for crossed in range(2) for came, row in places)
 
     blocks_a, done_a = prepare_near(table, near_z, 0, NEAR // 2)
     own_0 = own_0 + (lax.ppermute(own_0, "dir", swap) + done_a[0, 0])
     own_0, own_1 = lax.optimization_barrier((own_0, own_1))
-    around_0 = others(own_0)
+    left_0, right_0 = step(own_0, 1), step(own_0, 3)
     blocks_b, done_b = prepare_near(table, near_z, NEAR // 2, NEAR // 2)
     blocks_u, blocks_v, done_far = prepare_far(table, far_ut, far_vt)
     own_1 = own_1 + (lax.ppermute(own_1, "dir", swap) + (done_b[0, 0] + done_far[0, 0]))
-    own_1, *around_0 = lax.optimization_barrier((own_1, *around_0))
-    held_0 = both_cores([own_0, *around_0])
-    around_1 = others(own_1)
+    own_1, left_0, right_0 = lax.optimization_barrier((own_1, left_0, right_0))
+    middle = CLUSTER // 2
+    upper_0, lower_0 = step(left_0[:middle], 1), step(right_0[middle:], 3)
+    left_1, right_1 = step(own_1, 1), step(own_1, 3)
+    own_1, upper_0, lower_0 = lax.optimization_barrier((own_1, upper_0, lower_0))
+    around_1 = [left_1, step(own_1, 2), right_1]
+    held_0 = both_cores([own_0, left_0, right_0, upper_0, lower_0])
+    places_0 = on_both([(0, 0), (1, 0), (3, 0), (2, 0), (2, middle)])
+    places_1 = on_both([(0, 0), (1, 0), (2, 0), (3, 0)])
     blocks = (blocks_a, blocks_b, blocks_u, blocks_v)
 
 
@@ -351,10 +364,10 @@
         came = [lax.ppermute(part, AXES, turn) for part, turn in zip(away, second_turn)]
         return mine + (came[0] + zero) + came[1] + came[2]
 
-    mine, *away, done_0 = apply_blocks(table, held_0, blocks, 0)
+    mine, *away, done_0 = apply_blocks(table, places_0, held_0, blocks, 0)
     *around_1, done_0 = lax.optimization_barrier((*around_1, done_0))
     results = [to_owner(mine, away, done_0[0, 0])]
-    mine, *away, done_1 = apply_blocks(table, both_cores([own_1, *around_1]), blocks, 1)
+    mine, *away, done_1 = apply_blocks(table, places_1, both_cores([own_1, *around_1]), blocks, 1)
     results.append(to_owner(mine, away, done_1[0, 0]))
     parts = [r[:, :HALF] for r in results] + [r[:, HALF:] for r in results]
     return jnp.concatenate(parts, axis=1)

time: 147 us -> 143 us (0.973)
  waiting for transfers between devices: 76.2 us -> 56.1 us
  Pallas kernels: 21.4 us -> 38.9 us
  starting transfers between devices: 40.8 us -> 38.7 us
    ppermute x6 -> x7, waiting for transfers between devices: 32.1 us -> 18.1 us  [step(): return lax.ppermute(part, 'x', [(i, (i + k) % 4) for i in range(4)])]
    pallas_call x3, Pallas kernels: 15.3 us -> 26.3 us  [the longest x2 23.3 us: apply_blocks(): pl.pallas_call(functools.partial(apply_kernel, pieces), name=f'apply_{ind...]
    pallas_call x2, Pallas kernels: 4.1 us -> 10.5 us  [prepare_near(): pl.pallas_call(functools.partial(prepare_near_kernel, first), name=f'prep...]
    ppermute x12, waiting for transfers between devices: 35.6 us -> 32.1 us  [to_owner(): lax.ppermute(part, AXES, turn)]
    ppermute x12, starting transfers between devices: 24.9 us -> 22 us  [to_owner(): lax.ppermute(part, AXES, turn)]
    ppermute x1, waiting for transfers between devices: 7.9 us -> 5.95 us  [shards(): own_0 = own_0 + (lax.ppermute(own_0, 'dir', swap) + done_a[0, 0])]
    ppermute x6 -> x7, starting transfers between devices: 11 us -> 11.6 us  [step(): return lax.ppermute(part, 'x', [(i, (i + k) % 4) for i in range(4)])]
  transfers between devices with their start and end apart: 28 -> 30, of which waited for: 15 -> 12; matrix products, arithmetic and copies ran while one was open for 3% -> 3% of each run, Pallas kernels for 10% -> 25%
where the time goes in v4:
time: 143 us; the launch traced here: 142 us
  waiting for transfers between devices  56.1 us (39%)
  Pallas kernels  38.9 us (27%)
  starting transfers between devices  38.7 us (27%)
  other arithmetic  3.68 us (3%)
  local copies, waits for them, and re-layouts  2.86 us (2%)
  between operations  1.55 us (1%)
    ppermute x12, waiting for transfers between devices, to_owner(): lax.ppermute(part, AXES, turn)  32.1 us
    pallas_call x2, Pallas kernels, apply_blocks(): pl.pallas_call(functools.partial(apply_kernel, pieces), name=f'apply_{ind...  23.3 us
    ppermute x12, starting transfers between devices, to_owner(): lax.ppermute(part, AXES, turn)  22 us
    ppermute x7, waiting for transfers between devices, step(): return lax.ppermute(part, 'x', [(i, (i + k) % 4) for i in range(4)])  18.1 us
    ppermute x7, starting transfers between devices, step(): return lax.ppermute(part, 'x', [(i, (i + k) % 4) for i in range(4)])  11.6 us
    pallas_call x2, Pallas kernels, prepare_near(): pl.pallas_call(functools.partial(prepare_near_kernel, first), name=f'prep...  10.5 us
    ppermute x1, waiting for transfers between devices, shards(): own_0 = own_0 + (lax.ppermute(own_0, 'dir', swap) + done_a[0, 0])  5.95 us
    pallas_call x1, Pallas kernels, partial_rhs(): pl.pallas_call(rhs_kernel, name='rhs', in_specs=[HBM, HBM], out_specs=[VM...  3.04 us
  transfers between devices with their start and end apart: 30, of which 12 were waited for; matrix products, arithmetic and copies ran while one was open for 3% of the time, Pallas kernels for 25%

profile of v4, /device:TPU:0, one launch (start us, length us, event | category | flops | bytes accessed | tf_op | source)
XLA Modules:
  0.0 141.8 jit_solution(10218275402721830744)
XLA Ops:
  0.0 3.0 %rhs.1 = (f32[512,256]{1,0:T(8,128)S(1)}, f32[512,256]{1,0:T(8,128)S(1)}) custom-call(bf16[1024,512]{1,0:T(8,128)(2,1)} %cot_ref.1, bf16[2,512,1024]{2,1,0:T(8,128)(2,1)} %rad_ref.1), custom_call_target="tpu_custom_call" | custom-call | flops 1073741824 | bytes 4194304 | tf_op jit(solution)/shard_map/rhs/pallas_call | solution.py:89
  3.1 2.1 %collective-permute-start = (f32[512,256]{1,0:T(8,128)S(1)}, f32[512,256]{1,0:T(8,128)S(1)}, u32[]{:S(2)}, u32[]{:S(2)}) collective-permute-start(f32[512,256]{1,0:T(8,128)S(1)} %get-tuple-element.36), channel_id=1, source_target_pairs={{0,64},{64,0},{1,65},{65,1},{2,66},{66,2},{3,67},{67,3},{4,68},{68... | collective-permute-start | bytes 1572872 | tf_op jit(solution)/shard_map/ppermute | solution.py:343
  5.3 5.3 %prepare_near_0.1 = (bf16[4,512,2048]{2,1,0:T(8,128)(2,1)S(1)}, f32[8,128]{1,0:T(8,128)S(1)}) custom-call(s32[48]{0:T(128)S(1)} %concatenate.6.table, f32[2,8,512,512]{3,2,1,0:T(8,128)} %z_ref.3), custom_call_target="tpu_custom_call" | custom-call | flops 268435456 | bytes 8388608 | tf_op jit(solution)/shard_map/prepare_near_0/pallas_call | solution.py:138
  10.6 0.5 slice.145
  11.1 5.9 %collective-permute-done = f32[512,256]{1,0:T(8,128)S(1)} collective-permute-done((f32[512,256]{1,0:T(8,128)S(1)}, f32[512,256]{1,0:T(8,128)S(1)}, u32[]{:S(2)}, u32[]{:S(2)}) %collective-permute-start) | collective-permute-done | bytes 524320 | tf_op jit(solution)/shard_map/ppermute | solution.py:343
  17.1 0.7 add_add_fusion.1.refs_0_
  17.8 1.8 %collective-permute-start.1 = (f32[512,256]{1,0:T(8,128)S(1)}, f32[512,256]{1,0:T(8,128)S(1)}, u32[]{:S(2)}, u32[]{:S(2)}) collective-permute-start(f32[512,256]{1,0:T(8,128)S(1)} %get-tuple-element.40), channel_id=1, source_target_pairs={{0,64},{64,0},{1,65},{65,1},{2,66},{66,2},{3,67},{67,3},{4,68},{68... | collective-permute-start | bytes 1572872 | tf_op jit(solution)/shard_map/ppermute | solution.py:348
  19.6 1.5 %collective-permute-start.2 = (f32[512,256]{1,0:T(8,128)S(1)}, f32[512,256]{1,0:T(8,128)S(1)}, u32[]{:S(2)}, u32[]{:S(2)}) collective-permute-start(f32[512,256]{1,0:T(8,128)S(1)} %add_add_fusion.1.refs_0_), channel_id=1, source_target_pairs={{0,2},{2,4},{4,6},{6,0},{1,3},{3,5},{5,7},{7,1},{8,10},{10,12},{12... | collective-permute-start | bytes 1572872 | tf_op jit(solution)/shard_map/ppermute | solution.py:334
  21.1 1.7 %collective-permute-start.3 = (f32[512,256]{1,0:T(8,128)S(1)}, f32[512,256]{1,0:T(8,128)S(1)}, u32[]{:S(2)}, u32[]{:S(2)}) collective-permute-start(f32[512,256]{1,0:T(8,128)S(1)} %add_add_fusion.1.refs_0_), channel_id=1, source_target_pairs={{0,6},{2,0},{4,2},{6,4},{1,7},{3,1},{5,3},{7,5},{8,14},{10,8},{12,... | collective-permute-start | bytes 1572872 | tf_op jit(solution)/shard_map/ppermute | solution.py:334
  22.8 2.0 %prepare_far.1 = (bf16[4,128,2048]{2,1,0:T(8,128)(2,1)S(1)}, bf16[4,512,512]{2,1,0:T(8,128)(2,1)S(1)}, f32[8,128]{1,0:T(8,128)S(1)}) custom-call(s32[48]{0:T(128)S(1)} %concatenate.6.table, f32[2,4,96,512]{3,2,1,0:T(8,128)} %u_ref.1, f32[2,4,96,512]{3,2,1,0:T(8,128)} %v_ref.1), custom_call_target="tpu_custom_call" | custom-call | flops 268435456 | bytes 4194304 | tf_op jit(solution)/shard_map/prepare_far/pallas_call | solution.py:191
  24.8 0.6 slice.147
  25.4 5.3 %prepare_near_4.1 = (bf16[4,512,2048]{2,1,0:T(8,128)(2,1)S(1)}, f32[8,128]{1,0:T(8,128)S(1)}) custom-call(s32[48]{0:T(128)S(1)} %concatenate.6.table, f32[2,8,512,512]{3,2,1,0:T(8,128)} %z_ref.3), custom_call_target="tpu_custom_call" | custom-call | flops 268435456 | bytes 8388608 | tf_op jit(solution)/shard_map/prepare_near_4/pallas_call | solution.py:138
  30.7 0.5 slice.146
  32.7 0.6 collective-permute-done.2.refs_1_
  33.4 1.6 %collective-permute-start.4 = (f32[256,256]{1,0:T(8,128)S(1)}, f32[256,256]{1,0:T(8,128)S(1)}, u32[]{:S(2)}, u32[]{:S(2)}) collective-permute-start(f32[256,256]{1,0:T(8,128)S(1)} %slice.148), channel_id=1, source_target_pairs={{0,2},{2,4},{4,6},{6,0},{1,3},{3,5},{5,7},{7,1},{8,10},{10,12},{12... | collective-permute-start | bytes 786440 | tf_op jit(solution)/shard_map/ppermute | solution.py:334
  35.0 1.8 %collective-permute-start.5 = (f32[256,256]{1,0:T(8,128)S(1)}, f32[256,256]{1,0:T(8,128)S(1)}, u32[]{:S(2)}, u32[]{:S(2)}) collective-permute-start(f32[256,256]{1,0:T(8,128)S(1)} %slice.149), channel_id=1, source_target_pairs={{0,6},{2,0},{4,2},{6,4},{1,7},{3,1},{5,3},{7,5},{8,14},{10,8},{12,... | collective-permute-start | bytes 786440 | tf_op jit(solution)/shard_map/ppermute | solution.py:334
  36.8 6.5 %collective-permute-done.4.refs_3_ = f32[256,256]{1,0:T(8,128)S(1)} collective-permute-done((f32[256,256]{1,0:T(8,128)S(1)}, f32[256,256]{1,0:T(8,128)S(1)}, u32[]{:S(2)}, u32[]{:S(2)}) %collective-permute-start.4) | collective-permute-done | bytes 262176 | tf_op jit(solution)/shard_map/ppermute | solution.py:334
  43.5 0.5 collective-permute-start.9
  44.0 1.2 collective-permute-start.15
  45.2 2.0 %collective-permute-start.17 = (f32[512,256]{1,0:T(8,128)S(1)}, f32[512,256]{1,0:T(8,128)S(1)}, u32[]{:S(2)}, u32[]{:S(2)}) collective-permute-start(f32[512,256]{1,0:T(8,128)S(1)} %add_add_fusion.refs_0_), channel_id=1, source_target_pairs={{0,6},{2,0},{4,2},{6,4},{1,7},{3,1},{5,3},{7,5},{8,14},{10,8},{12,... | collective-permute-start | bytes 1572872 | tf_op jit(solution)/shard_map/ppermute | solution.py:334
  47.2 1.7 %collective-permute-start.16 = (f32[512,256]{1,0:T(8,128)S(1)}, f32[512,256]{1,0:T(8,128)S(1)}, u32[]{:S(2)}, u32[]{:S(2)}) collective-permute-start(f32[512,256]{1,0:T(8,128)S(1)} %add_add_fusion.refs_0_), channel_id=1, source_target_pairs={{0,4},{2,6},{4,0},{6,2},{1,5},{3,7},{5,1},{7,3},{8,12},{10,14},{12... | collective-permute-start | bytes 1572872 | tf_op jit(solution)/shard_map/ppermute | solution.py:334
  48.9 11.6 %apply_0.1 = (f32[4,256,256]{2,1,0:T(8,128)S(1)}, f32[4,256,256]{2,1,0:T(8,128)S(1)}, f32[4,256,256]{2,1,0:T(8,128)S(1)}, f32[4,256,256]{2,1,0:T(8,128)S(1)}, f32[8,128]{1,0:T(8,128)S(1)}) custom-call(s32[48]{0:T(128)S(1)} %concatenate.6.table, f32[512,256]{1,0:T(8,128)S(1)} %add_add_fusion.1.refs_0_, f32[512,256]{1,0:T(8,128)S(1)} %collective-permute-done.2.refs_1_, ...), custom_call_target="tpu_custom_call" | custom-call | flops 42949672960 | bytes 8388608 | tf_op jit(solution)/shard_map/apply_0/pallas_call | solution.py:288
  60.6 9.0 %collective-permute-done.17.refs_3_ = f32[512,256]{1,0:T(8,128)S(1)} collective-permute-done((f32[512,256]{1,0:T(8,128)S(1)}, f32[512,256]{1,0:T(8,128)S(1)}, u32[]{:S(2)}, u32[]{:S(2)}) %collective-permute-start.17) | collective-permute-done | bytes 524320 | tf_op jit(solution)/shard_map/ppermute | solution.py:334
  69.6 1.8 %collective-permute-done.16.refs_2_ = f32[512,256]{1,0:T(8,128)S(1)} collective-permute-done((f32[512,256]{1,0:T(8,128)S(1)}, f32[512,256]{1,0:T(8,128)S(1)}, u32[]{:S(2)}, u32[]{:S(2)}) %collective-permute-start.16) | collective-permute-done | bytes 524320 | tf_op jit(solution)/shard_map/ppermute | solution.py:334
  71.4 0.5 collective-permute-start.22
  72.0 1.6 %collective-permute-start.11 = (f32[4,256,256]{2,1,0:T(8,128)S(1)}, f32[4,256,256]{2,1,0:T(8,128)S(1)}, u32[]{:S(2)}, u32[]{:S(2)}) collective-permute-start(f32[4,256,256]{2,1,0:T(8,128)S(1)} %get-tuple-element.53), channel_id=1, source_target_pairs={{0,16},{1,65},{2,18},{3,67},{4,20},{5,69},{6,22},{7,71},{8,24},{9,... | collective-permute-start | bytes 3145736 | tf_op jit(solution)/shard_map/ppermute | solution.py:362
  73.5 2.9 %collective-permute-start.12 = (f32[4,256,256]{2,1,0:T(8,128)S(1)}, f32[4,256,256]{2,1,0:T(8,128)S(1)}, u32[]{:S(2)}, u32[]{:S(2)}) collective-permute-start(f32[4,256,256]{2,1,0:T(8,128)S(1)} %get-tuple-element.54), channel_id=1, source_target_pairs={{0,32},{1,9},{2,34},{3,11},{4,36},{5,13},{6,38},{7,15},{8,40},{9,1... | collective-permute-start | bytes 3145736 | tf_op jit(solution)/shard_map/ppermute | solution.py:362
  76.4 1.3 collective-permute-start.13
  77.8 11.7 %apply_1.1 = (f32[4,256,256]{2,1,0:T(8,128)S(1)}, f32[4,256,256]{2,1,0:T(8,128)S(1)}, f32[4,256,256]{2,1,0:T(8,128)S(1)}, f32[4,256,256]{2,1,0:T(8,128)S(1)}, f32[8,128]{1,0:T(8,128)S(1)}) custom-call(s32[48]{0:T(128)S(1)} %concatenate.6.table, f32[512,256]{1,0:T(8,128)S(1)} %add_add_fusion.refs_0_, f32[512,256]{1,0:T(8,128)S(1)} %collective-permute-done.15.refs_1_, ...), custom_call_target="tpu_custom_call" | custom-call | flops 42949672960 | bytes 8388608 | tf_op jit(solution)/shard_map/apply_1/pallas_call | solution.py:288
  89.5 1.5 %collective-permute-start.25 = (f32[4,256,256]{2,1,0:T(8,128)S(1)}, f32[4,256,256]{2,1,0:T(8,128)S(1)}, u32[]{:S(2)}, u32[]{:S(2)}) collective-permute-start(f32[4,256,256]{2,1,0:T(8,128)S(1)} %get-tuple-element.64), channel_id=1, source_target_pairs={{0,32},{1,9},{2,34},{3,11},{4,36},{5,13},{6,38},{7,15},{8,40},{9,1... | collective-permute-start | bytes 3145736 | tf_op jit(solution)/shard_map/ppermute | solution.py:362
  91.1 1.7 %collective-permute-start.26 = (f32[4,256,256]{2,1,0:T(8,128)S(1)}, f32[4,256,256]{2,1,0:T(8,128)S(1)}, u32[]{:S(2)}, u32[]{:S(2)}) collective-permute-start(f32[4,256,256]{2,1,0:T(8,128)S(1)} %get-tuple-element.65), channel_id=1, source_target_pairs={{0,48},{1,73},{2,50},{3,75},{4,52},{5,77},{6,54},{7,79},{8,56},{9,... | collective-permute-start | bytes 3145736 | tf_op jit(solution)/shard_map/ppermute | solution.py:362
  92.8 0.6 slice.158
  93.4 0.5 slice.176
  93.9 6.7 %collective-permute-done.12 = f32[4,256,256]{2,1,0:T(8,128)S(1)} collective-permute-done((f32[4,256,256]{2,1,0:T(8,128)S(1)}, f32[4,256,256]{2,1,0:T(8,128)S(1)}, u32[]{:S(2)}, u32[]{:S(2)}) %collective-permute-start.12) | collective-permute-done | bytes 1048608 | tf_op jit(solution)/shard_map/ppermute | solution.py:362
  100.6 0.2 fusion.9
  100.8 0.6 collective-permute-start.14
  101.3 3.5 %collective-permute-start.18 = (f32[256,256]{1,0:T(8,128)S(1)}, f32[256,256]{1,0:T(8,128)S(1)}, u32[]{:S(2)}, u32[]{:S(2)}) collective-permute-start(f32[256,256]{1,0:T(8,128)S(1)} %get-tuple-element.69), channel_id=1, source_target_pairs={{0,8},{1,33},{2,10},{3,35},{4,12},{5,37},{6,14},{7,39},{8,0},{9,41... | collective-permute-start | bytes 786440 | tf_op jit(solution)/shard_map/ppermute | solution.py:364
  104.8 12.5 %collective-permute-done.24 = f32[4,256,256]{2,1,0:T(8,128)S(1)} collective-permute-done((f32[4,256,256]{2,1,0:T(8,128)S(1)}, f32[4,256,256]{2,1,0:T(8,128)S(1)}, u32[]{:S(2)}, u32[]{:S(2)}) %collective-permute-start.24) | collective-permute-done | bytes 1048608 | tf_op jit(solution)/shard_map/ppermute | solution.py:362
  117.3 2.5 %collective-permute-start.19 = (f32[256,256]{1,0:T(8,128)S(1)}, f32[256,256]{1,0:T(8,128)S(1)}, u32[]{:S(2)}, u32[]{:S(2)}) collective-permute-start(f32[256,256]{1,0:T(8,128)S(1)} %get-tuple-element.68), channel_id=1, source_target_pairs={{0,72},{1,49},{2,74},{3,51},{4,76},{5,53},{6,78},{7,55},{8,64},{9,... | collective-permute-start | bytes 786440 | tf_op jit(solution)/shard_map/ppermute | solution.py:364
  119.8 8.8 %collective-permute-done.25 = f32[4,256,256]{2,1,0:T(8,128)S(1)} collective-permute-done((f32[4,256,256]{2,1,0:T(8,128)S(1)}, f32[4,256,256]{2,1,0:T(8,128)S(1)}, u32[]{:S(2)}, u32[]{:S(2)}) %collective-permute-start.25) | collective-permute-done | bytes 1048608 | tf_op jit(solution)/shard_map/ppermute | solution.py:362
  128.8 0.6 collective-permute-start.27
  129.4 3.5 %collective-permute-start.28 = (f32[256,256]{1,0:T(8,128)S(1)}, f32[256,256]{1,0:T(8,128)S(1)}, u32[]{:S(2)}, u32[]{:S(2)}) collective-permute-start(f32[256,256]{1,0:T(8,128)S(1)} %get-tuple-element.72), channel_id=1, source_target_pairs={{0,8},{1,33},{2,10},{3,35},{4,12},{5,37},{6,14},{7,39},{8,0},{9,41... | collective-permute-start | bytes 786440 | tf_op jit(solution)/shard_map/ppermute | solution.py:364
  132.9 2.2 %collective-permute-start.29 = (f32[256,256]{1,0:T(8,128)S(1)}, f32[256,256]{1,0:T(8,128)S(1)}, u32[]{:S(2)}, u32[]{:S(2)}) collective-permute-start(f32[256,256]{1,0:T(8,128)S(1)} %get-tuple-element.71), channel_id=1, source_target_pairs={{0,72},{1,49},{2,74},{3,51},{4,76},{5,53},{6,78},{7,55},{8,64},{9,... | collective-permute-start | bytes 786440 | tf_op jit(solution)/shard_map/ppermute | solution.py:364
  135.1 0.8 fusion.13
  135.9 0.5 collective-permute-done.27
  136.5 3.6 %collective-permute-done.28 = f32[256,256]{1,0:T(8,128)S(1)} collective-permute-done((f32[256,256]{1,0:T(8,128)S(1)}, f32[256,256]{1,0:T(8,128)S(1)}, u32[]{:S(2)}, u32[]{:S(2)}) %collective-permute-start.28) | collective-permute-done | bytes 262176 | tf_op jit(solution)/shard_map/ppermute | solution.py:364
  140.1 0.8 fusion.6
  140.9 0.8 pad_maximum_fusion
  (46 shorter events, 1.0 us)
Async XLA Ops:
  0.0 5.2 %copy-start = (s32[4,2]{0,1:T(2,128)S(1)}, s32[4,2]{0,1:T(2,128)}, u32[]{:S(2)}) copy-start(s32[4,2]{0,1:T(2,128)} %param.15) | copy-start | bytes 100
  0.0 5.2 %copy-start.1 = (s32[8,2]{0,1:T(2,128)S(1)}, s32[8,2]{0,1:T(2,128)}, u32[]{:S(2)}) copy-start(s32[8,2]{0,1:T(2,128)} %param.12) | copy-start | bytes 196
  0.0 5.2 %copy-start.2 = (s32[1,2]{1,0:T(1,128)S(1)}, s32[1,2]{1,0:T(1,128)}, u32[]{:S(2)}) copy-start(s32[1,2]{1,0:T(1,128)} %param.17) | copy-start | bytes 28
  0.0 5.2 %copy-start.3 = (s32[4]{0:T(128)S(1)}, s32[4]{0:T(128)}, u32[]{:S(2)}) copy-start(s32[4]{0:T(128)} %param.16) | copy-start | bytes 52
  3.1 14.0 %collective-permute-start = (f32[512,256]{1,0:T(8,128)S(1)}, f32[512,256]{1,0:T(8,128)S(1)}, u32[]{:S(2)}, u32[]{:S(2)}) collective-permute-start(f32[512,256]{1,0:T(8,128)S(1)} %get-tuple-element.36), channel_id=1, source_target_pairs={{0,64},{64,0},{1,65},{65,1},{2,66},{66,2},{3,67},{67,3},{4,68},{68... | collective-permute-start | bytes 1572872 | tf_op jit(solution)/shard_map/ppermute | solution.py:343
  17.8 14.8 %collective-permute-start.1 = (f32[512,256]{1,0:T(8,128)S(1)}, f32[512,256]{1,0:T(8,128)S(1)}, u32[]{:S(2)}, u32[]{:S(2)}) collective-permute-start(f32[512,256]{1,0:T(8,128)S(1)} %get-tuple-element.40), channel_id=1, source_target_pairs={{0,64},{64,0},{1,65},{65,1},{2,66},{66,2},{3,67},{67,3},{4,68},{68... | collective-permute-start | bytes 1572872 | tf_op jit(solution)/shard_map/ppermute | solution.py:348
  19.6 13.7 %collective-permute-start.2 = (f32[512,256]{1,0:T(8,128)S(1)}, f32[512,256]{1,0:T(8,128)S(1)}, u32[]{:S(2)}, u32[]{:S(2)}) collective-permute-start(f32[512,256]{1,0:T(8,128)S(1)} %add_add_fusion.1.refs_0_), channel_id=1, source_target_pairs={{0,2},{2,4},{4,6},{6,0},{1,3},{3,5},{5,7},{7,1},{8,10},{10,12},{12... | collective-permute-start | bytes 1572872 | tf_op jit(solution)/shard_map/ppermute | solution.py:334
  21.1 12.2 %collective-permute-start.3 = (f32[512,256]{1,0:T(8,128)S(1)}, f32[512,256]{1,0:T(8,128)S(1)}, u32[]{:S(2)}, u32[]{:S(2)}) collective-permute-start(f32[512,256]{1,0:T(8,128)S(1)} %add_add_fusion.1.refs_0_), channel_id=1, source_target_pairs={{0,6},{2,0},{4,2},{6,4},{1,7},{3,1},{5,3},{7,5},{8,14},{10,8},{12,... | collective-permute-start | bytes 1572872 | tf_op jit(solution)/shard_map/ppermute | solution.py:334
  32.5 11.5 %collective-permute-start.6 = (f32[512,256]{1,0:T(8,128)S(1)}, f32[512,256]{1,0:T(8,128)S(1)}, u32[]{:S(2)}, u32[]{:S(2)}) collective-permute-start(f32[512,256]{1,0:T(8,128)S(1)} %add_add_fusion.1.refs_0_), channel_id=1, source_target_pairs={{0,1},{1,0},{2,3},{3,2},{4,5},{5,4},{6,7},{7,6},{8,9},{9,8},{10,11... | collective-permute-start | bytes 1572872 | tf_op jit(solution)/shard_map/ppermute | solution.py:337
  33.3 11.8 %collective-permute-start.7 = (f32[512,256]{1,0:T(8,128)S(1)}, f32[512,256]{1,0:T(8,128)S(1)}, u32[]{:S(2)}, u32[]{:S(2)}) collective-permute-start(f32[512,256]{1,0:T(8,128)S(1)} %collective-permute-done.2.refs_1_), channel_id=1, source_target_pairs={{0,1},{1,0},{2,3},{3,2},{4,5},{5,4},{6,7},{7,6},{8,9},{9,8},{10,11... | collective-permute-start | bytes 1572872 | tf_op jit(solution)/shard_map/ppermute | solution.py:337
  33.4 9.9 %collective-permute-start.4 = (f32[256,256]{1,0:T(8,128)S(1)}, f32[256,256]{1,0:T(8,128)S(1)}, u32[]{:S(2)}, u32[]{:S(2)}) collective-permute-start(f32[256,256]{1,0:T(8,128)S(1)} %slice.148), channel_id=1, source_target_pairs={{0,2},{2,4},{4,6},{6,0},{1,3},{3,5},{5,7},{7,1},{8,10},{10,12},{12... | collective-permute-start | bytes 786440 | tf_op jit(solution)/shard_map/ppermute | solution.py:334
  35.0 8.4 %collective-permute-start.5 = (f32[256,256]{1,0:T(8,128)S(1)}, f32[256,256]{1,0:T(8,128)S(1)}, u32[]{:S(2)}, u32[]{:S(2)}) collective-permute-start(f32[256,256]{1,0:T(8,128)S(1)} %slice.149), channel_id=1, source_target_pairs={{0,6},{2,0},{4,2},{6,4},{1,7},{3,1},{5,3},{7,5},{8,14},{10,8},{12,... | collective-permute-start | bytes 786440 | tf_op jit(solution)/shard_map/ppermute | solution.py:334
  36.8 10.4 %collective-permute-start.8 = (f32[512,256]{1,0:T(8,128)S(1)}, f32[512,256]{1,0:T(8,128)S(1)}, u32[]{:S(2)}, u32[]{:S(2)}) collective-permute-start(f32[512,256]{1,0:T(8,128)S(1)} %collective-permute-done.3.refs_2_), channel_id=1, source_target_pairs={{0,1},{1,0},{2,3},{3,2},{4,5},{5,4},{6,7},{7,6},{8,9},{9,8},{10,11... | collective-permute-start | bytes 1572872 | tf_op jit(solution)/shard_map/ppermute | solution.py:337
  43.5 5.5 %collective-permute-start.10 = (f32[256,256]{1,0:T(8,128)S(1)}, f32[256,256]{1,0:T(8,128)S(1)}, u32[]{:S(2)}, u32[]{:S(2)}) collective-permute-start(f32[256,256]{1,0:T(8,128)S(1)} %collective-permute-done.5.refs_4_), channel_id=1, source_target_pairs={{0,1},{1,0},{2,3},{3,2},{4,5},{5,4},{6,7},{7,6},{8,9},{9,8},{10,11... | collective-permute-start | bytes 786440 | tf_op jit(solution)/shard_map/ppermute | solution.py:337
  43.5 5.5 %collective-permute-start.9 = (f32[256,256]{1,0:T(8,128)S(1)}, f32[256,256]{1,0:T(8,128)S(1)}, u32[]{:S(2)}, u32[]{:S(2)}) collective-permute-start(f32[256,256]{1,0:T(8,128)S(1)} %collective-permute-done.4.refs_3_), channel_id=1, source_target_pairs={{0,1},{1,0},{2,3},{3,2},{4,5},{5,4},{6,7},{7,6},{8,9},{9,8},{10,11... | collective-permute-start | bytes 786440 | tf_op jit(solution)/shard_map/ppermute | solution.py:337
  44.0 16.6 %collective-permute-start.15 = (f32[512,256]{1,0:T(8,128)S(1)}, f32[512,256]{1,0:T(8,128)S(1)}, u32[]{:S(2)}, u32[]{:S(2)}) collective-permute-start(f32[512,256]{1,0:T(8,128)S(1)} %add_add_fusion.refs_0_), channel_id=1, source_target_pairs={{0,2},{2,4},{4,6},{6,0},{1,3},{3,5},{5,7},{7,1},{8,10},{10,12},{12... | collective-permute-start | bytes 1572872 | tf_op jit(solution)/shard_map/ppermute | solution.py:334
  45.2 24.5 %collective-permute-start.17 = (f32[512,256]{1,0:T(8,128)S(1)}, f32[512,256]{1,0:T(8,128)S(1)}, u32[]{:S(2)}, u32[]{:S(2)}) collective-permute-start(f32[512,256]{1,0:T(8,128)S(1)} %add_add_fusion.refs_0_), channel_id=1, source_target_pairs={{0,6},{2,0},{4,2},{6,4},{1,7},{3,1},{5,3},{7,5},{8,14},{10,8},{12,... | collective-permute-start | bytes 1572872 | tf_op jit(solution)/shard_map/ppermute | solution.py:334
  47.2 24.2 %collective-permute-start.16 = (f32[512,256]{1,0:T(8,128)S(1)}, f32[512,256]{1,0:T(8,128)S(1)}, u32[]{:S(2)}, u32[]{:S(2)}) collective-permute-start(f32[512,256]{1,0:T(8,128)S(1)} %add_add_fusion.refs_0_), channel_id=1, source_target_pairs={{0,4},{2,6},{4,0},{6,2},{1,5},{3,7},{5,1},{7,3},{8,12},{10,14},{12... | collective-permute-start | bytes 1572872 | tf_op jit(solution)/shard_map/ppermute | solution.py:334
  48.9 24.6 %collective-permute-start.20 = (f32[512,256]{1,0:T(8,128)S(1)}, f32[512,256]{1,0:T(8,128)S(1)}, u32[]{:S(2)}, u32[]{:S(2)}) collective-permute-start(f32[512,256]{1,0:T(8,128)S(1)} %add_add_fusion.refs_0_), channel_id=1, source_target_pairs={{0,1},{1,0},{2,3},{3,2},{4,5},{5,4},{6,7},{7,6},{8,9},{9,8},{10,11... | collective-permute-start | bytes 1572872 | tf_op jit(solution)/shard_map/ppermute | solution.py:337
  71.4 5.0 %collective-permute-start.21 = (f32[512,256]{1,0:T(8,128)S(1)}, f32[512,256]{1,0:T(8,128)S(1)}, u32[]{:S(2)}, u32[]{:S(2)}) collective-permute-start(f32[512,256]{1,0:T(8,128)S(1)} %collective-permute-done.15.refs_1_), channel_id=1, source_target_pairs={{0,1},{1,0},{2,3},{3,2},{4,5},{5,4},{6,7},{7,6},{8,9},{9,8},{10,11... | collective-permute-start | bytes 1572872 | tf_op jit(solution)/shard_map/ppermute | solution.py:337
  71.4 6.4 %collective-permute-start.22 = (f32[512,256]{1,0:T(8,128)S(1)}, f32[512,256]{1,0:T(8,128)S(1)}, u32[]{:S(2)}, u32[]{:S(2)}) collective-permute-start(f32[512,256]{1,0:T(8,128)S(1)} %collective-permute-done.16.refs_2_), channel_id=1, source_target_pairs={{0,1},{1,0},{2,3},{3,2},{4,5},{5,4},{6,7},{7,6},{8,9},{9,8},{10,11... | collective-permute-start | bytes 1572872 | tf_op jit(solution)/shard_map/ppermute | solution.py:337
  72.0 5.8 %collective-permute-start.23 = (f32[512,256]{1,0:T(8,128)S(1)}, f32[512,256]{1,0:T(8,128)S(1)}, u32[]{:S(2)}, u32[]{:S(2)}) collective-permute-start(f32[512,256]{1,0:T(8,128)S(1)} %collective-permute-done.17.refs_3_), channel_id=1, source_target_pairs={{0,1},{1,0},{2,3},{3,2},{4,5},{5,4},{6,7},{7,6},{8,9},{9,8},{10,11... | collective-permute-start | bytes 1572872 | tf_op jit(solution)/shard_map/ppermute | solution.py:337
  72.0 19.1 %collective-permute-start.11 = (f32[4,256,256]{2,1,0:T(8,128)S(1)}, f32[4,256,256]{2,1,0:T(8,128)S(1)}, u32[]{:S(2)}, u32[]{:S(2)}) collective-permute-start(f32[4,256,256]{2,1,0:T(8,128)S(1)} %get-tuple-element.53), channel_id=1, source_target_pairs={{0,16},{1,65},{2,18},{3,67},{4,20},{5,69},{6,22},{7,71},{8,24},{9,... | collective-permute-start | bytes 3145736 | tf_op jit(solution)/shard_map/ppermute | solution.py:362
  73.5 27.0 %collective-permute-start.12 = (f32[4,256,256]{2,1,0:T(8,128)S(1)}, f32[4,256,256]{2,1,0:T(8,128)S(1)}, u32[]{:S(2)}, u32[]{:S(2)}) collective-permute-start(f32[4,256,256]{2,1,0:T(8,128)S(1)} %get-tuple-element.54), channel_id=1, source_target_pairs={{0,32},{1,9},{2,34},{3,11},{4,36},{5,13},{6,38},{7,15},{8,40},{9,1... | collective-permute-start | bytes 3145736 | tf_op jit(solution)/shard_map/ppermute | solution.py:362
  76.4 24.1 %collective-permute-start.13 = (f32[4,256,256]{2,1,0:T(8,128)S(1)}, f32[4,256,256]{2,1,0:T(8,128)S(1)}, u32[]{:S(2)}, u32[]{:S(2)}) collective-permute-start(f32[4,256,256]{2,1,0:T(8,128)S(1)} %get-tuple-element.55), channel_id=1, source_target_pairs={{0,48},{1,73},{2,50},{3,75},{4,52},{5,77},{6,54},{7,79},{8,56},{9,... | collective-permute-start | bytes 3145736 | tf_op jit(solution)/shard_map/ppermute | solution.py:362
  89.5 27.8 %collective-permute-start.24 = (f32[4,256,256]{2,1,0:T(8,128)S(1)}, f32[4,256,256]{2,1,0:T(8,128)S(1)}, u32[]{:S(2)}, u32[]{:S(2)}) collective-permute-start(f32[4,256,256]{2,1,0:T(8,128)S(1)} %get-tuple-element.63), channel_id=1, source_target_pairs={{0,16},{1,65},{2,18},{3,67},{4,20},{5,69},{6,22},{7,71},{8,24},{9,... | collective-permute-start | bytes 3145736 | tf_op jit(solution)/shard_map/ppermute | solution.py:362
  89.5 39.0 %collective-permute-start.25 = (f32[4,256,256]{2,1,0:T(8,128)S(1)}, f32[4,256,256]{2,1,0:T(8,128)S(1)}, u32[]{:S(2)}, u32[]{:S(2)}) collective-permute-start(f32[4,256,256]{2,1,0:T(8,128)S(1)} %get-tuple-element.64), channel_id=1, source_target_pairs={{0,32},{1,9},{2,34},{3,11},{4,36},{5,13},{6,38},{7,15},{8,40},{9,1... | collective-permute-start | bytes 3145736 | tf_op jit(solution)/shard_map/ppermute | solution.py:362
  91.1 37.5 %collective-permute-start.26 = (f32[4,256,256]{2,1,0:T(8,128)S(1)}, f32[4,256,256]{2,1,0:T(8,128)S(1)}, u32[]{:S(2)}, u32[]{:S(2)}) collective-permute-start(f32[4,256,256]{2,1,0:T(8,128)S(1)} %get-tuple-element.65), channel_id=1, source_target_pairs={{0,48},{1,73},{2,50},{3,75},{4,52},{5,77},{6,54},{7,79},{8,56},{9,... | collective-permute-start | bytes 3145736 | tf_op jit(solution)/shard_map/ppermute | solution.py:362
  100.8 32.1 %collective-permute-start.14 = (f32[256,256]{1,0:T(8,128)S(1)}, f32[256,256]{1,0:T(8,128)S(1)}, u32[]{:S(2)}, u32[]{:S(2)}) collective-permute-start(f32[256,256]{1,0:T(8,128)S(1)} %get-tuple-element.67), channel_id=1, source_target_pairs={{0,64},{1,17},{2,66},{3,19},{4,68},{5,21},{6,70},{7,23},{8,72},{9,... | collective-permute-start | bytes 786440 | tf_op jit(solution)/shard_map/ppermute | solution.py:364
  101.3 33.7 %collective-permute-start.18 = (f32[256,256]{1,0:T(8,128)S(1)}, f32[256,256]{1,0:T(8,128)S(1)}, u32[]{:S(2)}, u32[]{:S(2)}) collective-permute-start(f32[256,256]{1,0:T(8,128)S(1)} %get-tuple-element.69), channel_id=1, source_target_pairs={{0,8},{1,33},{2,10},{3,35},{4,12},{5,37},{6,14},{7,39},{8,0},{9,41... | collective-permute-start | bytes 786440 | tf_op jit(solution)/shard_map/ppermute | solution.py:364
  117.3 17.8 %collective-permute-start.19 = (f32[256,256]{1,0:T(8,128)S(1)}, f32[256,256]{1,0:T(8,128)S(1)}, u32[]{:S(2)}, u32[]{:S(2)}) collective-permute-start(f32[256,256]{1,0:T(8,128)S(1)} %get-tuple-element.68), channel_id=1, source_target_pairs={{0,72},{1,49},{2,74},{3,51},{4,76},{5,53},{6,78},{7,55},{8,64},{9,... | collective-permute-start | bytes 786440 | tf_op jit(solution)/shard_map/ppermute | solution.py:364
  128.8 7.7 %collective-permute-start.27 = (f32[256,256]{1,0:T(8,128)S(1)}, f32[256,256]{1,0:T(8,128)S(1)}, u32[]{:S(2)}, u32[]{:S(2)}) collective-permute-start(f32[256,256]{1,0:T(8,128)S(1)} %get-tuple-element.70), channel_id=1, source_target_pairs={{0,64},{1,17},{2,66},{3,19},{4,68},{5,21},{6,70},{7,23},{8,72},{9,... | collective-permute-start | bytes 786440 | tf_op jit(solution)/shard_map/ppermute | solution.py:364
  129.4 10.7 %collective-permute-start.28 = (f32[256,256]{1,0:T(8,128)S(1)}, f32[256,256]{1,0:T(8,128)S(1)}, u32[]{:S(2)}, u32[]{:S(2)}) collective-permute-start(f32[256,256]{1,0:T(8,128)S(1)} %get-tuple-element.72), channel_id=1, source_target_pairs={{0,8},{1,33},{2,10},{3,35},{4,12},{5,37},{6,14},{7,39},{8,0},{9,41... | collective-permute-start | bytes 786440 | tf_op jit(solution)/shard_map/ppermute | solution.py:364
  132.9 7.3 %collective-permute-start.29 = (f32[256,256]{1,0:T(8,128)S(1)}, f32[256,256]{1,0:T(8,128)S(1)}, u32[]{:S(2)}, u32[]{:S(2)}) collective-permute-start(f32[256,256]{1,0:T(8,128)S(1)} %get-tuple-element.71), channel_id=1, source_target_pairs={{0,72},{1,49},{2,74},{3,51},{4,76},{5,53},{6,78},{7,55},{8,64},{9,... | collective-permute-start | bytes 786440 | tf_op jit(solution)/shard_map/ppermute | solution.py:364

commit v5 on v4

--- a/solution.py
+++ b/solution.py
@@ -221,23 +221,51 @@
     return dot(left, jnp.concatenate([high, high], 0)) + dot(left[:, : left.shape[1] // 2], low)
 
 
-def apply_kernel(pieces, table, *refs):
-    held, refs = refs[: len(pieces)], refs[len(pieces) :]
-    (za_ref, zb_ref, u_ref, v_ref), outs, (token, x_buf, fx_buf, sem_x, sem_fx) = refs[:4], refs[4:8], refs[8:]
+def pack_kernel(*refs):
+    parts, out_ref, sem = refs[:-2], refs[-2], refs[-1]
+    copies, first = [], 0
+    for i, part in enumerate(parts):
+        rows = part.shape[0]
+        copies.append(pltpu.make_async_copy(part, out_ref.at[pl.ds(first, rows)], sem.at[i]))
+        first += rows
+    for copy in copies:
+        copy.start()
+    for copy in copies:
+        copy.wait()
+
+
+def pack(parts, index):
+    rows = sum(part.shape[0] for part in parts)
+    return pl.pallas_call(
+        pack_kernel,
+        name=f"pack_{index}",
+        in_specs=[ANY] * len(parts),
+        out_specs=ANY,
+        out_shape=jax.ShapeDtypeStruct((rows, parts[0].shape[1]), jnp.float32),
+        scratch_shapes=[pltpu.SemaphoreType.DMA((len(parts),))],
+        compiler_params=pltpu.CompilerParams(vmem_limit_bytes=SCOPED),
+        cost_estimate=pl.CostEstimate(flops=0, bytes_accessed=4 << 20, transcendentals=0),
+    )(*parts)
+
+
+def apply_kernel(table, *refs):
+    held, (za_ref, zb_ref, u_ref, v_ref) = refs[:2], refs[2:6]
+    outs, (token, x_buf, fx_buf, sem_x, sem_fx) = refs[6:10], refs[10:]
     near, far = table[N_NEAR], table[N_FAR]
     slots = za_ref.shape[0]
 
     def fetch(cluster, buf, sem):
         steps = lax.rem(table[X] + 4 - cluster // 2, 4)
-        other = jnp.where(lax.rem(cluster, 2) == table[CORE], 0, 1)
-        for ref, (came, crossed, row) in zip(held, pieces):
-
-            @pl.when((steps == came) & (other == crossed))
+        rows = pl.ds(pl.multiple_of(steps * CLUSTER, CLUSTER), CLUSTER)
+        own_core = lax.rem(cluster, 2) == table[CORE]
+        for ref, here in zip(held, (own_core, jnp.logical_not(own_core))):
+
+            @pl.when(here)
             def _():
-                pltpu.make_async_copy(ref, buf.at[pl.ds(row, ref.shape[0])], sem).start()
+                pltpu.make_async_copy(ref.at[rows], buf, sem).start()
 
     def fetched(buf, sem):
-        pltpu.make_async_copy(held[0], buf, sem).wait()
+        pltpu.make_async_copy(held[0].at[pl.ds(0, CLUSTER)], buf, sem).wait()
 
     def add(cluster, term):
         for half in range(2):
@@ -284,11 +312,11 @@
     lax.fori_loop(0, far, far_step, 0)
 
 
-def apply_blocks(table, pieces, held, blocks, index):
+def apply_blocks(table, held, blocks, index):
     return pl.pallas_call(
-        functools.partial(apply_kernel, pieces),
+        apply_kernel,
         name=f"apply_{index}",
-        in_specs=[SMEM] + [ANY] * len(held) + [VMEM] * 4,
+        in_specs=[SMEM] + [ANY] * 2 + [VMEM] * 4,
         out_specs=[VMEM] * 5,
         out_shape=[jax.ShapeDtypeStruct((4, CLUSTER // 2, WIDE), jnp.float32)] * 4 + [TOKEN],
         scratch_shapes=[
@@ -333,11 +361,9 @@
     def step(part, k):
         return lax.ppermute(part, "x", [(i, (i + k) % 4) for i in range(4)])
 
-    def both_cores(mine):
-        return mine + [lax.ppermute(part, "core", swap) for part in mine]
-
-    def on_both(places):
-        return tuple((came, crossed, row) for crossed in range(2) for came, row in places)
+    def both_cores(parts, index):
+        mine = pack(parts, index)
+        return mine, lax.ppermute(mine, "core", swap)
 
     blocks_a, done_a = prepare_near(table, near_z, 0, NEAR // 2)
     own_0 = own_0 + (lax.ppermute(own_0, "dir", swap) + done_a[0, 0])
@@ -351,10 +377,8 @@
     upper_0, lower_0 = step(left_0[:middle], 1), step(right_0[middle:], 3)
     left_1, right_1 = step(own_1, 1), step(own_1, 3)
     own_1, upper_0, lower_0 = lax.optimization_barrier((own_1, upper_0, lower_0))
-    around_1 = [left_1, step(own_1, 2), right_1]
-    held_0 = both_cores([own_0, left_0, right_0, upper_0, lower_0])
-    places_0 = on_both([(0, 0), (1, 0), (3, 0), (2, 0), (2, middle)])
-    places_1 = on_both([(0, 0), (1, 0), (2, 0), (3, 0)])
+    across_1 = step(own_1, 2)
+    held_0 = both_cores([own_0, left_0, upper_0, lower_0, right_0], 0)
     blocks = (blocks_a, blocks_b, blocks_u, blocks_v)
 
 
@@ -364,10 +388,10 @@
         came = [lax.ppermute(part, AXES, turn) for part, turn in zip(away, second_turn)]
         return mine + (came[0] + zero) + came[1] + came[2]
 
-    mine, *away, done_0 = apply_blocks(table, places_0, held_0, blocks, 0)
-    *around_1, done_0 = lax.optimization_barrier((*around_1, done_0))
+    mine, *away, done_0 = apply_blocks(table, held_0, blocks, 0)
+    *parts_1, done_0 = lax.optimization_barrier((own_1, left_1, across_1, right_1, done_0))
     results = [to_owner(mine, away, done_0[0, 0])]
-    mine, *away, done_1 = apply_blocks(table, places_1, both_cores([own_1, *around_1]), blocks, 1)
+    mine, *away, done_1 = apply_blocks(table, both_cores(parts_1, 1), blocks, 1)
     results.append(to_owner(mine, away, done_1[0, 0]))
     parts = [r[:, :HALF] for r in results] + [r[:, HALF:] for r in results]
     return jnp.concatenate(parts, axis=1)

time: 143 us -> 141 us (0.986)
  Pallas kernels: 38.9 us -> 18.5 us
  waiting for transfers between devices: 56.1 us -> 73.2 us
  starting transfers between devices: 38.7 us -> 40.3 us
    pallas_call x2 -> x4, Pallas kernels: 23.3 us -> 9.4 us  [the longest x2 9.02 us: apply_blocks(): pl.pallas_call(apply_kernel, name=f'apply_{index}', in_specs=[SMEM] + [AN...]
    ppermute x7, waiting for transfers between devices: 18.1 us -> 25.4 us  [step(): return lax.ppermute(part, 'x', [(i, (i + k) % 4) for i in range(4)])]
    pallas_call x2, Pallas kernels: 10.5 us -> 4.1 us  [prepare_near(): pl.pallas_call(functools.partial(prepare_near_kernel, first), name=f'prep...]
    ppermute x12, waiting for transfers between devices: 32.1 us -> 36.8 us  [to_owner(): lax.ppermute(part, AXES, turn)]
    ppermute x1, waiting for transfers between devices: 0.01 us -> 3.29 us  [shards(): lax.ppermute(own_1, 'dir', swap) + (done_b[0, 0] + done_far[0, 0])]
    ppermute x12, starting transfers between devices: 22 us -> 24.6 us  [to_owner(): lax.ppermute(part, AXES, turn)]
    ppermute x1, waiting for transfers between devices: 5.95 us -> 7.68 us  [shards(): own_0 = own_0 + (lax.ppermute(own_0, 'dir', swap) + done_a[0, 0])]
  transfers between devices with their start and end apart: 30 -> 23, of which waited for: 12 -> 14; matrix products, arithmetic and copies ran while one was open for 3% -> 3% of each run, Pallas kernels for 25% -> 11%
where the time goes in v5:
time: 141 us; the launch traced here: 140 us
  waiting for transfers between devices  73.2 us (52%)
  starting transfers between devices  40.3 us (29%)
  Pallas kernels  18.5 us (13%)
  other arithmetic  3.63 us (3%)
  local copies, waits for them, and re-layouts  2.73 us (2%)
  between operations  1.43 us (1%)
    ppermute x12, waiting for transfers between devices, to_owner(): lax.ppermute(part, AXES, turn)  36.8 us
    ppermute x7, waiting for transfers between devices, step(): return lax.ppermute(part, 'x', [(i, (i + k) % 4) for i in range(4)])  25.4 us
    ppermute x12, starting transfers between devices, to_owner(): lax.ppermute(part, AXES, turn)  24.6 us
    ppermute x7, starting transfers between devices, step(): return lax.ppermute(part, 'x', [(i, (i + k) % 4) for i in range(4)])  11.6 us
    pallas_call x2, Pallas kernels, apply_blocks(): pl.pallas_call(apply_kernel, name=f'apply_{index}', in_specs=[SMEM] + [AN...  9.02 us
    ppermute x1, waiting for transfers between devices, shards(): own_0 = own_0 + (lax.ppermute(own_0, 'dir', swap) + done_a[0, 0])  7.68 us
    pallas_call x2, Pallas kernels, prepare_near(): pl.pallas_call(functools.partial(prepare_near_kernel, first), name=f'prep...  4.1 us
    ppermute x1, waiting for transfers between devices, shards(): lax.ppermute(own_1, 'dir', swap) + (done_b[0, 0] + done_far[0, 0])  3.29 us
  transfers between devices with their start and end apart: 23, of which 14 were waited for; matrix products, arithmetic and copies ran while one was open for 3% of the time, Pallas kernels for 11%

profile of v5, /device:TPU:0, one launch (start us, length us, event | category | flops | bytes accessed | tf_op | source)
XLA Modules:
  0.0 139.8 jit_solution(5422614487525504390)
XLA Ops:
  0.0 3.0 %rhs.1 = (f32[512,256]{1,0:T(8,128)S(1)}, f32[512,256]{1,0:T(8,128)S(1)}) custom-call(bf16[1024,512]{1,0:T(8,128)(2,1)} %cot_ref.1, bf16[2,512,1024]{2,1,0:T(8,128)(2,1)} %rad_ref.1), custom_call_target="tpu_custom_call" | custom-call | flops 1073741824 | bytes 4194304 | tf_op jit(solution)/shard_map/rhs/pallas_call | solution.py:89
  3.1 2.1 %collective-permute-start = (f32[512,256]{1,0:T(8,128)S(1)}, f32[512,256]{1,0:T(8,128)S(1)}, u32[]{:S(2)}, u32[]{:S(2)}) collective-permute-start(f32[512,256]{1,0:T(8,128)S(1)} %get-tuple-element.37), channel_id=1, source_target_pairs={{0,64},{64,0},{1,65},{65,1},{2,66},{66,2},{3,67},{67,3},{4,68},{68... | collective-permute-start | bytes 1572872 | tf_op jit(solution)/shard_map/ppermute | solution.py:369
  5.3 3.5 %prepare_near_0.1 = (bf16[4,512,2048]{2,1,0:T(8,128)(2,1)S(1)}, f32[8,128]{1,0:T(8,128)S(1)}) custom-call(s32[48]{0:T(128)S(1)} %concatenate.6.table, f32[2,8,512,512]{3,2,1,0:T(8,128)} %z_ref.3), custom_call_target="tpu_custom_call" | custom-call | flops 268435456 | bytes 8388608 | tf_op jit(solution)/shard_map/prepare_near_0/pallas_call | solution.py:138
  8.9 0.5 slice.145
  9.4 7.7 %collective-permute-done = f32[512,256]{1,0:T(8,128)S(1)} collective-permute-done((f32[512,256]{1,0:T(8,128)S(1)}, f32[512,256]{1,0:T(8,128)S(1)}, u32[]{:S(2)}, u32[]{:S(2)}) %collective-permute-start) | collective-permute-done | bytes 524320 | tf_op jit(solution)/shard_map/ppermute | solution.py:369
  17.1 0.7 add_add_fusion.1.refs_0_
  17.8 1.8 %collective-permute-start.1 = (f32[512,256]{1,0:T(8,128)S(1)}, f32[512,256]{1,0:T(8,128)S(1)}, u32[]{:S(2)}, u32[]{:S(2)}) collective-permute-start(f32[512,256]{1,0:T(8,128)S(1)} %get-tuple-element.41), channel_id=1, source_target_pairs={{0,64},{64,0},{1,65},{65,1},{2,66},{66,2},{3,67},{67,3},{4,68},{68... | collective-permute-start | bytes 1572872 | tf_op jit(solution)/shard_map/ppermute | solution.py:374
  19.6 1.5 %collective-permute-start.2 = (f32[512,256]{1,0:T(8,128)S(1)}, f32[512,256]{1,0:T(8,128)S(1)}, u32[]{:S(2)}, u32[]{:S(2)}) collective-permute-start(f32[512,256]{1,0:T(8,128)S(1)} %add_add_fusion.1.refs_0_), channel_id=1, source_target_pairs={{0,2},{2,4},{4,6},{6,0},{1,3},{3,5},{5,7},{7,1},{8,10},{10,12},{12... | collective-permute-start | bytes 1572872 | tf_op jit(solution)/shard_map/ppermute | solution.py:362
  21.1 1.7 %collective-permute-start.3 = (f32[512,256]{1,0:T(8,128)S(1)}, f32[512,256]{1,0:T(8,128)S(1)}, u32[]{:S(2)}, u32[]{:S(2)}) collective-permute-start(f32[512,256]{1,0:T(8,128)S(1)} %add_add_fusion.1.refs_0_), channel_id=1, source_target_pairs={{0,6},{2,0},{4,2},{6,4},{1,7},{3,1},{5,3},{7,5},{8,14},{10,8},{12,... | collective-permute-start | bytes 1572872 | tf_op jit(solution)/shard_map/ppermute | solution.py:362
  22.8 2.0 %prepare_far.1 = (bf16[4,128,2048]{2,1,0:T(8,128)(2,1)S(1)}, bf16[4,512,512]{2,1,0:T(8,128)(2,1)S(1)}, f32[8,128]{1,0:T(8,128)S(1)}) custom-call(s32[48]{0:T(128)S(1)} %concatenate.6.table, f32[2,4,96,512]{3,2,1,0:T(8,128)} %u_ref.1, f32[2,4,96,512]{3,2,1,0:T(8,128)} %v_ref.1), custom_call_target="tpu_custom_call" | custom-call | flops 268435456 | bytes 4194304 | tf_op jit(solution)/shard_map/prepare_far/pallas_call | solution.py:191
  24.8 0.5 slice.147
  25.3 0.6 prepare_near_4.1
  25.9 0.5 slice.146
  27.7 3.3 %collective-permute-done.1 = f32[512,256]{1,0:T(8,128)S(1)} collective-permute-done((f32[512,256]{1,0:T(8,128)S(1)}, f32[512,256]{1,0:T(8,128)S(1)}, u32[]{:S(2)}, u32[]{:S(2)}) %collective-permute-start.1) | collective-permute-done | bytes 524320 | tf_op jit(solution)/shard_map/ppermute | solution.py:374
  31.0 2.3 %collective-permute-done.2.refs_1_ = f32[512,256]{1,0:T(8,128)S(1)} collective-permute-done((f32[512,256]{1,0:T(8,128)S(1)}, f32[512,256]{1,0:T(8,128)S(1)}, u32[]{:S(2)}, u32[]{:S(2)}) %collective-permute-start.2) | collective-permute-done | bytes 524320 | tf_op jit(solution)/shard_map/ppermute | solution.py:362
  33.3 1.6 %collective-permute-start.4 = (f32[256,256]{1,0:T(8,128)S(1)}, f32[256,256]{1,0:T(8,128)S(1)}, u32[]{:S(2)}, u32[]{:S(2)}) collective-permute-start(f32[256,256]{1,0:T(8,128)S(1)} %slice.148), channel_id=1, source_target_pairs={{0,2},{2,4},{4,6},{6,0},{1,3},{3,5},{5,7},{7,1},{8,10},{10,12},{12... | collective-permute-start | bytes 786440 | tf_op jit(solution)/shard_map/ppermute | solution.py:362
  34.9 1.8 %collective-permute-start.5 = (f32[256,256]{1,0:T(8,128)S(1)}, f32[256,256]{1,0:T(8,128)S(1)}, u32[]{:S(2)}, u32[]{:S(2)}) collective-permute-start(f32[256,256]{1,0:T(8,128)S(1)} %slice.149), channel_id=1, source_target_pairs={{0,6},{2,0},{4,2},{6,4},{1,7},{3,1},{5,3},{7,5},{8,14},{10,8},{12,... | collective-permute-start | bytes 786440 | tf_op jit(solution)/shard_map/ppermute | solution.py:362
  36.7 4.3 %collective-permute-done.4.refs_2_ = f32[256,256]{1,0:T(8,128)S(1)} collective-permute-done((f32[256,256]{1,0:T(8,128)S(1)}, f32[256,256]{1,0:T(8,128)S(1)}, u32[]{:S(2)}, u32[]{:S(2)}) %collective-permute-start.4) | collective-permute-done | bytes 262176 | tf_op jit(solution)/shard_map/ppermute | solution.py:362
  41.7 1.3 collective-permute-start.11
  42.9 2.0 %collective-permute-start.13 = (f32[512,256]{1,0:T(8,128)S(1)}, f32[512,256]{1,0:T(8,128)S(1)}, u32[]{:S(2)}, u32[]{:S(2)}) collective-permute-start(f32[512,256]{1,0:T(8,128)S(1)} %add_add_fusion.refs_0_), channel_id=1, source_target_pairs={{0,6},{2,0},{4,2},{6,4},{1,7},{3,1},{5,3},{7,5},{8,14},{10,8},{12,... | collective-permute-start | bytes 1572872 | tf_op jit(solution)/shard_map/ppermute | solution.py:362
  45.0 1.7 %collective-permute-start.12 = (f32[512,256]{1,0:T(8,128)S(1)}, f32[512,256]{1,0:T(8,128)S(1)}, u32[]{:S(2)}, u32[]{:S(2)}) collective-permute-start(f32[512,256]{1,0:T(8,128)S(1)} %add_add_fusion.refs_0_), channel_id=1, source_target_pairs={{0,4},{2,6},{4,0},{6,2},{1,5},{3,7},{5,1},{7,3},{8,12},{10,14},{12... | collective-permute-start | bytes 1572872 | tf_op jit(solution)/shard_map/ppermute | solution.py:362
  46.7 4.4 %apply_0.1 = (f32[4,256,256]{2,1,0:T(8,128)S(1)}, f32[4,256,256]{2,1,0:T(8,128)S(1)}, f32[4,256,256]{2,1,0:T(8,128)S(1)}, f32[4,256,256]{2,1,0:T(8,128)S(1)}, f32[8,128]{1,0:T(8,128)S(1)}) custom-call(s32[48]{0:T(128)S(1)} %concatenate.6.table, f32[2048,256]{1,0:T(8,128)S(1)} %pack_0.1.refs_0_, f32[2048,256]{1,0:T(8,128)S(1)} %collective-permute-done.6.refs_1_, ...), custom_call_target="tpu_custom_call" | custom-call | flops 42949672960 | bytes 8388608 | tf_op jit(solution)/shard_map/apply_0/pallas_call | solution.py:316
  51.1 6.1 %collective-permute-done.11.refs_1_ = f32[512,256]{1,0:T(8,128)S(1)} collective-permute-done((f32[512,256]{1,0:T(8,128)S(1)}, f32[512,256]{1,0:T(8,128)S(1)}, u32[]{:S(2)}, u32[]{:S(2)}) %collective-permute-start.11) | collective-permute-done | bytes 524320 | tf_op jit(solution)/shard_map/ppermute | solution.py:362
  57.2 10.5 %collective-permute-done.13.refs_3_ = f32[512,256]{1,0:T(8,128)S(1)} collective-permute-done((f32[512,256]{1,0:T(8,128)S(1)}, f32[512,256]{1,0:T(8,128)S(1)}, u32[]{:S(2)}, u32[]{:S(2)}) %collective-permute-start.13) | collective-permute-done | bytes 524320 | tf_op jit(solution)/shard_map/ppermute | solution.py:362
  67.7 1.9 %collective-permute-done.12.refs_2_ = f32[512,256]{1,0:T(8,128)S(1)} collective-permute-done((f32[512,256]{1,0:T(8,128)S(1)}, f32[512,256]{1,0:T(8,128)S(1)}, u32[]{:S(2)}, u32[]{:S(2)}) %collective-permute-start.12) | collective-permute-done | bytes 524320 | tf_op jit(solution)/shard_map/ppermute | solution.py:362
  69.9 1.6 %collective-permute-start.7 = (f32[4,256,256]{2,1,0:T(8,128)S(1)}, f32[4,256,256]{2,1,0:T(8,128)S(1)}, u32[]{:S(2)}, u32[]{:S(2)}) collective-permute-start(f32[4,256,256]{2,1,0:T(8,128)S(1)} %get-tuple-element.54), channel_id=1, source_target_pairs={{0,16},{1,65},{2,18},{3,67},{4,20},{5,69},{6,22},{7,71},{8,24},{9,... | collective-permute-start | bytes 3145736 | tf_op jit(solution)/shard_map/ppermute | solution.py:386
  71.6 2.9 %collective-permute-start.8 = (f32[4,256,256]{2,1,0:T(8,128)S(1)}, f32[4,256,256]{2,1,0:T(8,128)S(1)}, u32[]{:S(2)}, u32[]{:S(2)}) collective-permute-start(f32[4,256,256]{2,1,0:T(8,128)S(1)} %get-tuple-element.55), channel_id=1, source_target_pairs={{0,32},{1,9},{2,34},{3,11},{4,36},{5,13},{6,38},{7,15},{8,40},{9,1... | collective-permute-start | bytes 3145736 | tf_op jit(solution)/shard_map/ppermute | solution.py:386
  74.5 1.3 collective-permute-start.9
  75.8 4.6 %apply_1.1 = (f32[4,256,256]{2,1,0:T(8,128)S(1)}, f32[4,256,256]{2,1,0:T(8,128)S(1)}, f32[4,256,256]{2,1,0:T(8,128)S(1)}, f32[4,256,256]{2,1,0:T(8,128)S(1)}, f32[8,128]{1,0:T(8,128)S(1)}) custom-call(s32[48]{0:T(128)S(1)} %concatenate.6.table, f32[2048,256]{1,0:T(8,128)S(1)} %pack_1.1.refs_0_, f32[2048,256]{1,0:T(8,128)S(1)} %collective-permute-done.16.refs_1_, ...), custom_call_target="tpu_custom_call" | custom-call | flops 42949672960 | bytes 8388608 | tf_op jit(solution)/shard_map/apply_1/pallas_call | solution.py:316
  80.4 0.7 collective-permute-start.17
  81.2 2.0 %collective-permute-start.18 = (f32[4,256,256]{2,1,0:T(8,128)S(1)}, f32[4,256,256]{2,1,0:T(8,128)S(1)}, u32[]{:S(2)}, u32[]{:S(2)}) collective-permute-start(f32[4,256,256]{2,1,0:T(8,128)S(1)} %get-tuple-element.66), channel_id=1, source_target_pairs={{0,32},{1,9},{2,34},{3,11},{4,36},{5,13},{6,38},{7,15},{8,40},{9,1... | collective-permute-start | bytes 3145736 | tf_op jit(solution)/shard_map/ppermute | solution.py:386
  83.2 2.8 %collective-permute-done.7 = f32[4,256,256]{2,1,0:T(8,128)S(1)} collective-permute-done((f32[4,256,256]{2,1,0:T(8,128)S(1)}, f32[4,256,256]{2,1,0:T(8,128)S(1)}, u32[]{:S(2)}, u32[]{:S(2)}) %collective-permute-start.7) | collective-permute-done | bytes 1048608 | tf_op jit(solution)/shard_map/ppermute | solution.py:386
  86.0 1.8 %collective-permute-start.19 = (f32[4,256,256]{2,1,0:T(8,128)S(1)}, f32[4,256,256]{2,1,0:T(8,128)S(1)}, u32[]{:S(2)}, u32[]{:S(2)}) collective-permute-start(f32[4,256,256]{2,1,0:T(8,128)S(1)} %get-tuple-element.67), channel_id=1, source_target_pairs={{0,48},{1,73},{2,50},{3,75},{4,52},{5,77},{6,54},{7,79},{8,56},{9,... | collective-permute-start | bytes 3145736 | tf_op jit(solution)/shard_map/ppermute | solution.py:386
  87.8 0.5 slice.158
  88.3 10.3 %collective-permute-done.8 = f32[4,256,256]{2,1,0:T(8,128)S(1)} collective-permute-done((f32[4,256,256]{2,1,0:T(8,128)S(1)}, f32[4,256,256]{2,1,0:T(8,128)S(1)}, u32[]{:S(2)}, u32[]{:S(2)}) %collective-permute-start.8) | collective-permute-done | bytes 1048608 | tf_op jit(solution)/shard_map/ppermute | solution.py:386
  98.8 0.6 collective-permute-start.10
  99.3 3.5 %collective-permute-start.14 = (f32[256,256]{1,0:T(8,128)S(1)}, f32[256,256]{1,0:T(8,128)S(1)}, u32[]{:S(2)}, u32[]{:S(2)}) collective-permute-start(f32[256,256]{1,0:T(8,128)S(1)} %get-tuple-element.71), channel_id=1, source_target_pairs={{0,8},{1,33},{2,10},{3,35},{4,12},{5,37},{6,14},{7,39},{8,0},{9,41... | collective-permute-start | bytes 786440 | tf_op jit(solution)/shard_map/ppermute | solution.py:388
  102.8 11.2 %collective-permute-done.17 = f32[4,256,256]{2,1,0:T(8,128)S(1)} collective-permute-done((f32[4,256,256]{2,1,0:T(8,128)S(1)}, f32[4,256,256]{2,1,0:T(8,128)S(1)}, u32[]{:S(2)}, u32[]{:S(2)}) %collective-permute-start.17) | collective-permute-done | bytes 1048608 | tf_op jit(solution)/shard_map/ppermute | solution.py:386
  114.1 3.8 %collective-permute-start.15 = (f32[256,256]{1,0:T(8,128)S(1)}, f32[256,256]{1,0:T(8,128)S(1)}, u32[]{:S(2)}, u32[]{:S(2)}) collective-permute-start(f32[256,256]{1,0:T(8,128)S(1)} %get-tuple-element.70), channel_id=1, source_target_pairs={{0,72},{1,49},{2,74},{3,51},{4,76},{5,53},{6,78},{7,55},{8,64},{9,... | collective-permute-start | bytes 786440 | tf_op jit(solution)/shard_map/ppermute | solution.py:388
  117.9 8.8 %collective-permute-done.18 = f32[4,256,256]{2,1,0:T(8,128)S(1)} collective-permute-done((f32[4,256,256]{2,1,0:T(8,128)S(1)}, f32[4,256,256]{2,1,0:T(8,128)S(1)}, u32[]{:S(2)}, u32[]{:S(2)}) %collective-permute-start.18) | collective-permute-done | bytes 1048608 | tf_op jit(solution)/shard_map/ppermute | solution.py:386
  126.8 0.6 collective-permute-start.20
  127.4 3.5 %collective-permute-start.21 = (f32[256,256]{1,0:T(8,128)S(1)}, f32[256,256]{1,0:T(8,128)S(1)}, u32[]{:S(2)}, u32[]{:S(2)}) collective-permute-start(f32[256,256]{1,0:T(8,128)S(1)} %get-tuple-element.74), channel_id=1, source_target_pairs={{0,8},{1,33},{2,10},{3,35},{4,12},{5,37},{6,14},{7,39},{8,0},{9,41... | collective-permute-start | bytes 786440 | tf_op jit(solution)/shard_map/ppermute | solution.py:388
  130.9 2.2 %collective-permute-start.22 = (f32[256,256]{1,0:T(8,128)S(1)}, f32[256,256]{1,0:T(8,128)S(1)}, u32[]{:S(2)}, u32[]{:S(2)}) collective-permute-start(f32[256,256]{1,0:T(8,128)S(1)} %get-tuple-element.73), channel_id=1, source_target_pairs={{0,72},{1,49},{2,74},{3,51},{4,76},{5,53},{6,78},{7,55},{8,64},{9,... | collective-permute-start | bytes 786440 | tf_op jit(solution)/shard_map/ppermute | solution.py:388
  133.1 0.8 fusion.13
  133.9 0.5 slice.176
  134.5 3.6 %collective-permute-done.21 = f32[256,256]{1,0:T(8,128)S(1)} collective-permute-done((f32[256,256]{1,0:T(8,128)S(1)}, f32[256,256]{1,0:T(8,128)S(1)}, u32[]{:S(2)}, u32[]{:S(2)}) %collective-permute-start.21) | collective-permute-done | bytes 262176 | tf_op jit(solution)/shard_map/ppermute | solution.py:388
  138.1 0.8 fusion.6
  139.0 0.8 pad_maximum_fusion
  (34 shorter events, 1.8 us)
Async XLA Ops:
  0.0 5.2 %copy-start = (s32[4,2]{0,1:T(2,128)S(1)}, s32[4,2]{0,1:T(2,128)}, u32[]{:S(2)}) copy-start(s32[4,2]{0,1:T(2,128)} %param.15) | copy-start | bytes 100
  0.0 5.2 %copy-start.1 = (s32[8,2]{0,1:T(2,128)S(1)}, s32[8,2]{0,1:T(2,128)}, u32[]{:S(2)}) copy-start(s32[8,2]{0,1:T(2,128)} %param.12) | copy-start | bytes 196
  0.0 5.2 %copy-start.2 = (s32[1,2]{1,0:T(1,128)S(1)}, s32[1,2]{1,0:T(1,128)}, u32[]{:S(2)}) copy-start(s32[1,2]{1,0:T(1,128)} %param.17) | copy-start | bytes 28
  0.0 5.2 %copy-start.3 = (s32[4]{0:T(128)S(1)}, s32[4]{0:T(128)}, u32[]{:S(2)}) copy-start(s32[4]{0:T(128)} %param.16) | copy-start | bytes 52
  3.1 14.0 %collective-permute-start = (f32[512,256]{1,0:T(8,128)S(1)}, f32[512,256]{1,0:T(8,128)S(1)}, u32[]{:S(2)}, u32[]{:S(2)}) collective-permute-start(f32[512,256]{1,0:T(8,128)S(1)} %get-tuple-element.37), channel_id=1, source_target_pairs={{0,64},{64,0},{1,65},{65,1},{2,66},{66,2},{3,67},{67,3},{4,68},{68... | collective-permute-start | bytes 1572872 | tf_op jit(solution)/shard_map/ppermute | solution.py:369
  17.8 13.2 %collective-permute-start.1 = (f32[512,256]{1,0:T(8,128)S(1)}, f32[512,256]{1,0:T(8,128)S(1)}, u32[]{:S(2)}, u32[]{:S(2)}) collective-permute-start(f32[512,256]{1,0:T(8,128)S(1)} %get-tuple-element.41), channel_id=1, source_target_pairs={{0,64},{64,0},{1,65},{65,1},{2,66},{66,2},{3,67},{67,3},{4,68},{68... | collective-permute-start | bytes 1572872 | tf_op jit(solution)/shard_map/ppermute | solution.py:374
  19.6 13.7 %collective-permute-start.2 = (f32[512,256]{1,0:T(8,128)S(1)}, f32[512,256]{1,0:T(8,128)S(1)}, u32[]{:S(2)}, u32[]{:S(2)}) collective-permute-start(f32[512,256]{1,0:T(8,128)S(1)} %add_add_fusion.1.refs_0_), channel_id=1, source_target_pairs={{0,2},{2,4},{4,6},{6,0},{1,3},{3,5},{5,7},{7,1},{8,10},{10,12},{12... | collective-permute-start | bytes 1572872 | tf_op jit(solution)/shard_map/ppermute | solution.py:362
  21.1 12.2 %collective-permute-start.3 = (f32[512,256]{1,0:T(8,128)S(1)}, f32[512,256]{1,0:T(8,128)S(1)}, u32[]{:S(2)}, u32[]{:S(2)}) collective-permute-start(f32[512,256]{1,0:T(8,128)S(1)} %add_add_fusion.1.refs_0_), channel_id=1, source_target_pairs={{0,6},{2,0},{4,2},{6,4},{1,7},{3,1},{5,3},{7,5},{8,14},{10,8},{12,... | collective-permute-start | bytes 1572872 | tf_op jit(solution)/shard_map/ppermute | solution.py:362
  33.3 7.7 %collective-permute-start.4 = (f32[256,256]{1,0:T(8,128)S(1)}, f32[256,256]{1,0:T(8,128)S(1)}, u32[]{:S(2)}, u32[]{:S(2)}) collective-permute-start(f32[256,256]{1,0:T(8,128)S(1)} %slice.148), channel_id=1, source_target_pairs={{0,2},{2,4},{4,6},{6,0},{1,3},{3,5},{5,7},{7,1},{8,10},{10,12},{12... | collective-permute-start | bytes 786440 | tf_op jit(solution)/shard_map/ppermute | solution.py:362
  34.9 6.4 %collective-permute-start.5 = (f32[256,256]{1,0:T(8,128)S(1)}, f32[256,256]{1,0:T(8,128)S(1)}, u32[]{:S(2)}, u32[]{:S(2)}) collective-permute-start(f32[256,256]{1,0:T(8,128)S(1)} %slice.149), channel_id=1, source_target_pairs={{0,6},{2,0},{4,2},{6,4},{1,7},{3,1},{5,3},{7,5},{8,14},{10,8},{12,... | collective-permute-start | bytes 786440 | tf_op jit(solution)/shard_map/ppermute | solution.py:362
  41.6 5.1 %collective-permute-start.6 = (f32[2048,256]{1,0:T(8,128)S(1)}, f32[2048,256]{1,0:T(8,128)S(1)}, u32[]{:S(2)}, u32[]{:S(2)}) collective-permute-start(f32[2048,256]{1,0:T(8,128)S(1)} %pack_0.1.refs_0_), channel_id=1, source_target_pairs={{0,1},{1,0},{2,3},{3,2},{4,5},{5,4},{6,7},{7,6},{8,9},{9,8},{10,11... | collective-permute-start | bytes 6291464 | tf_op jit(solution)/shard_map/ppermute | solution.py:366
  41.7 15.6 %collective-permute-start.11 = (f32[512,256]{1,0:T(8,128)S(1)}, f32[512,256]{1,0:T(8,128)S(1)}, u32[]{:S(2)}, u32[]{:S(2)}) collective-permute-start(f32[512,256]{1,0:T(8,128)S(1)} %add_add_fusion.refs_0_), channel_id=1, source_target_pairs={{0,2},{2,4},{4,6},{6,0},{1,3},{3,5},{5,7},{7,1},{8,10},{10,12},{12... | collective-permute-start | bytes 1572872 | tf_op jit(solution)/shard_map/ppermute | solution.py:362
  42.9 24.8 %collective-permute-start.13 = (f32[512,256]{1,0:T(8,128)S(1)}, f32[512,256]{1,0:T(8,128)S(1)}, u32[]{:S(2)}, u32[]{:S(2)}) collective-permute-start(f32[512,256]{1,0:T(8,128)S(1)} %add_add_fusion.refs_0_), channel_id=1, source_target_pairs={{0,6},{2,0},{4,2},{6,4},{1,7},{3,1},{5,3},{7,5},{8,14},{10,8},{12,... | collective-permute-start | bytes 1572872 | tf_op jit(solution)/shard_map/ppermute | solution.py:362
  45.0 24.7 %collective-permute-start.12 = (f32[512,256]{1,0:T(8,128)S(1)}, f32[512,256]{1,0:T(8,128)S(1)}, u32[]{:S(2)}, u32[]{:S(2)}) collective-permute-start(f32[512,256]{1,0:T(8,128)S(1)} %add_add_fusion.refs_0_), channel_id=1, source_target_pairs={{0,4},{2,6},{4,0},{6,2},{1,5},{3,7},{5,1},{7,3},{8,12},{10,14},{12... | collective-permute-start | bytes 1572872 | tf_op jit(solution)/shard_map/ppermute | solution.py:362
  69.8 6.0 %collective-permute-start.16 = (f32[2048,256]{1,0:T(8,128)S(1)}, f32[2048,256]{1,0:T(8,128)S(1)}, u32[]{:S(2)}, u32[]{:S(2)}) collective-permute-start(f32[2048,256]{1,0:T(8,128)S(1)} %pack_1.1.refs_0_), channel_id=1, source_target_pairs={{0,1},{1,0},{2,3},{3,2},{4,5},{5,4},{6,7},{7,6},{8,9},{9,8},{10,11... | collective-permute-start | bytes 6291464 | tf_op jit(solution)/shard_map/ppermute | solution.py:366
  69.9 16.1 %collective-permute-start.7 = (f32[4,256,256]{2,1,0:T(8,128)S(1)}, f32[4,256,256]{2,1,0:T(8,128)S(1)}, u32[]{:S(2)}, u32[]{:S(2)}) collective-permute-start(f32[4,256,256]{2,1,0:T(8,128)S(1)} %get-tuple-element.54), channel_id=1, source_target_pairs={{0,16},{1,65},{2,18},{3,67},{4,20},{5,69},{6,22},{7,71},{8,24},{9,... | collective-permute-start | bytes 3145736 | tf_op jit(solution)/shard_map/ppermute | solution.py:386
  71.6 27.0 %collective-permute-start.8 = (f32[4,256,256]{2,1,0:T(8,128)S(1)}, f32[4,256,256]{2,1,0:T(8,128)S(1)}, u32[]{:S(2)}, u32[]{:S(2)}) collective-permute-start(f32[4,256,256]{2,1,0:T(8,128)S(1)} %get-tuple-element.55), channel_id=1, source_target_pairs={{0,32},{1,9},{2,34},{3,11},{4,36},{5,13},{6,38},{7,15},{8,40},{9,1... | collective-permute-start | bytes 3145736 | tf_op jit(solution)/shard_map/ppermute | solution.py:386
  74.5 24.1 %collective-permute-start.9 = (f32[4,256,256]{2,1,0:T(8,128)S(1)}, f32[4,256,256]{2,1,0:T(8,128)S(1)}, u32[]{:S(2)}, u32[]{:S(2)}) collective-permute-start(f32[4,256,256]{2,1,0:T(8,128)S(1)} %get-tuple-element.56), channel_id=1, source_target_pairs={{0,48},{1,73},{2,50},{3,75},{4,52},{5,77},{6,54},{7,79},{8,56},{9,... | collective-permute-start | bytes 3145736 | tf_op jit(solution)/shard_map/ppermute | solution.py:386
  80.4 33.7 %collective-permute-start.17 = (f32[4,256,256]{2,1,0:T(8,128)S(1)}, f32[4,256,256]{2,1,0:T(8,128)S(1)}, u32[]{:S(2)}, u32[]{:S(2)}) collective-permute-start(f32[4,256,256]{2,1,0:T(8,128)S(1)} %get-tuple-element.65), channel_id=1, source_target_pairs={{0,16},{1,65},{2,18},{3,67},{4,20},{5,69},{6,22},{7,71},{8,24},{9,... | collective-permute-start | bytes 3145736 | tf_op jit(solution)/shard_map/ppermute | solution.py:386
  81.2 45.4 %collective-permute-start.18 = (f32[4,256,256]{2,1,0:T(8,128)S(1)}, f32[4,256,256]{2,1,0:T(8,128)S(1)}, u32[]{:S(2)}, u32[]{:S(2)}) collective-permute-start(f32[4,256,256]{2,1,0:T(8,128)S(1)} %get-tuple-element.66), channel_id=1, source_target_pairs={{0,32},{1,9},{2,34},{3,11},{4,36},{5,13},{6,38},{7,15},{8,40},{9,1... | collective-permute-start | bytes 3145736 | tf_op jit(solution)/shard_map/ppermute | solution.py:386
  86.0 40.6 %collective-permute-start.19 = (f32[4,256,256]{2,1,0:T(8,128)S(1)}, f32[4,256,256]{2,1,0:T(8,128)S(1)}, u32[]{:S(2)}, u32[]{:S(2)}) collective-permute-start(f32[4,256,256]{2,1,0:T(8,128)S(1)} %get-tuple-element.67), channel_id=1, source_target_pairs={{0,48},{1,73},{2,50},{3,75},{4,52},{5,77},{6,54},{7,79},{8,56},{9,... | collective-permute-start | bytes 3145736 | tf_op jit(solution)/shard_map/ppermute | solution.py:386
  98.8 32.1 %collective-permute-start.10 = (f32[256,256]{1,0:T(8,128)S(1)}, f32[256,256]{1,0:T(8,128)S(1)}, u32[]{:S(2)}, u32[]{:S(2)}) collective-permute-start(f32[256,256]{1,0:T(8,128)S(1)} %get-tuple-element.69), channel_id=1, source_target_pairs={{0,64},{1,17},{2,66},{3,19},{4,68},{5,21},{6,70},{7,23},{8,72},{9,... | collective-permute-start | bytes 786440 | tf_op jit(solution)/shard_map/ppermute | solution.py:388
  99.3 33.8 %collective-permute-start.14 = (f32[256,256]{1,0:T(8,128)S(1)}, f32[256,256]{1,0:T(8,128)S(1)}, u32[]{:S(2)}, u32[]{:S(2)}) collective-permute-start(f32[256,256]{1,0:T(8,128)S(1)} %get-tuple-element.71), channel_id=1, source_target_pairs={{0,8},{1,33},{2,10},{3,35},{4,12},{5,37},{6,14},{7,39},{8,0},{9,41... | collective-permute-start | bytes 786440 | tf_op jit(solution)/shard_map/ppermute | solution.py:388
  114.1 19.0 %collective-permute-start.15 = (f32[256,256]{1,0:T(8,128)S(1)}, f32[256,256]{1,0:T(8,128)S(1)}, u32[]{:S(2)}, u32[]{:S(2)}) collective-permute-start(f32[256,256]{1,0:T(8,128)S(1)} %get-tuple-element.70), channel_id=1, source_target_pairs={{0,72},{1,49},{2,74},{3,51},{4,76},{5,53},{6,78},{7,55},{8,64},{9,... | collective-permute-start | bytes 786440 | tf_op jit(solution)/shard_map/ppermute | solution.py:388
  126.8 7.7 %collective-permute-start.20 = (f32[256,256]{1,0:T(8,128)S(1)}, f32[256,256]{1,0:T(8,128)S(1)}, u32[]{:S(2)}, u32[]{:S(2)}) collective-permute-start(f32[256,256]{1,0:T(8,128)S(1)} %get-tuple-element.72), channel_id=1, source_target_pairs={{0,64},{1,17},{2,66},{3,19},{4,68},{5,21},{6,70},{7,23},{8,72},{9,... | collective-permute-start | bytes 786440 | tf_op jit(solution)/shard_map/ppermute | solution.py:388
  127.4 10.7 %collective-permute-start.21 = (f32[256,256]{1,0:T(8,128)S(1)}, f32[256,256]{1,0:T(8,128)S(1)}, u32[]{:S(2)}, u32[]{:S(2)}) collective-permute-start(f32[256,256]{1,0:T(8,128)S(1)} %get-tuple-element.74), channel_id=1, source_target_pairs={{0,8},{1,33},{2,10},{3,35},{4,12},{5,37},{6,14},{7,39},{8,0},{9,41... | collective-permute-start | bytes 786440 | tf_op jit(solution)/shard_map/ppermute | solution.py:388
  130.9 7.3 %collective-permute-start.22 = (f32[256,256]{1,0:T(8,128)S(1)}, f32[256,256]{1,0:T(8,128)S(1)}, u32[]{:S(2)}, u32[]{:S(2)}) collective-permute-start(f32[256,256]{1,0:T(8,128)S(1)} %get-tuple-element.73), channel_id=1, source_target_pairs={{0,72},{1,49},{2,74},{3,51},{4,76},{5,53},{6,78},{7,55},{8,64},{9,... | collective-permute-start | bytes 786440 | tf_op jit(solution)/shard_map/ppermute | solution.py:388

commit v6 on v5

--- a/solution.py
+++ b/solution.py
@@ -13,6 +13,7 @@
 COL = ("x", "core")
 SIZES = (2, 4, 2, 4, 2)
 CHUNKS = 2
+COST = (40 << 30, 40 << 30)
 CLUSTER = 512
 HALF = 128
 WIDE = 2 * HALF
@@ -326,7 +327,7 @@
             pltpu.SemaphoreType.DMA((FAR,)),
         ],
         compiler_params=pltpu.CompilerParams(vmem_limit_bytes=SCOPED),
-        cost_estimate=pl.CostEstimate(flops=40 << 30, bytes_accessed=8 << 20, transcendentals=0),
+        cost_estimate=pl.CostEstimate(flops=COST[index], bytes_accessed=1, transcendentals=0),
     )(table, *held, *blocks)
 
 
@@ -358,41 +359,52 @@
     swap = [(0, 1), (1, 0)]
     first_turn, second_turn = rotations()
 
-    def step(part, k):
-        return lax.ppermute(part, "x", [(i, (i + k) % 4) for i in range(4)])
+    def across_dir(part, name):
+        with jax.named_scope(name):
+            return lax.ppermute(part, "dir", swap)
+
+    def step(part, k, name):
+        with jax.named_scope(name):
+            return lax.ppermute(part, "x", [(i, (i + k) % 4) for i in range(4)])
 
     def both_cores(parts, index):
         mine = pack(parts, index)
-        return mine, lax.ppermute(mine, "core", swap)
-
+        with jax.named_scope(f"P_S{index}"):
+            return mine, lax.ppermute(mine, "core", swap)
+
+    middle = CLUSTER // 2
     blocks_a, done_a = prepare_near(table, near_z, 0, NEAR // 2)
-    own_0 = own_0 + (lax.ppermute(own_0, "dir", swap) + done_a[0, 0])
-    own_0, own_1 = lax.optimization_barrier((own_0, own_1))
-    left_0, right_0 = step(own_0, 1), step(own_0, 3)
+    upper, lower = own_0[:middle], own_0[middle:]
+    upper = upper + (across_dir(upper, "P_ZU") + done_a[0, 0])
     blocks_b, done_b = prepare_near(table, near_z, NEAR // 2, NEAR // 2)
     blocks_u, blocks_v, done_far = prepare_far(table, far_ut, far_vt)
-    own_1 = own_1 + (lax.ppermute(own_1, "dir", swap) + (done_b[0, 0] + done_far[0, 0]))
-    own_1, left_0, right_0 = lax.optimization_barrier((own_1, left_0, right_0))
-    middle = CLUSTER // 2
-    upper_0, lower_0 = step(left_0[:middle], 1), step(right_0[middle:], 3)
-    left_1, right_1 = step(own_1, 1), step(own_1, 3)
+    upper, lower = lax.optimization_barrier((upper, lower))
+    left_u, right_u = step(upper, 1, "P_LU"), step(upper, 3, "P_RU")
+    lower = lower + (across_dir(lower, "P_ZL") + done_b[0, 0])
+    own_1, lower, left_u, right_u = lax.optimization_barrier((own_1, lower, left_u, right_u))
+    left_l, right_l = step(lower, 1, "P_LL"), step(lower, 3, "P_RL")
+    own_1 = own_1 + (across_dir(own_1, "P_Z1") + done_far[0, 0])
+    upper_0, lower_0 = step(left_u, 1, "P_A0"), step(right_l, 3, "P_B0")
     own_1, upper_0, lower_0 = lax.optimization_barrier((own_1, upper_0, lower_0))
-    across_1 = step(own_1, 2)
-    held_0 = both_cores([own_0, left_0, upper_0, lower_0, right_0], 0)
+    left_1, right_1 = step(own_1, 1, "P_L1"), step(own_1, 3, "P_R1")
+    across_1 = step(own_1, 2, "P_K1")
+    held_0 = both_cores([upper, lower, left_u, left_l, upper_0, lower_0, right_u, right_l], 0)
     blocks = (blocks_a, blocks_b, blocks_u, blocks_v)
 
 
-    def to_owner(mine, away, zero):
-        came = [lax.ppermute(part, AXES, turn) for part, turn in zip(away, first_turn)]
+    def to_owner(mine, away, zero, index):
+        with jax.named_scope(f"P_F{index}"):
+            came = [lax.ppermute(part, AXES, turn) for part, turn in zip(away, first_turn)]
         mine, *away = [mine[k] + came[0][k] + came[1][k] + came[2][k] for k in range(4)]
-        came = [lax.ppermute(part, AXES, turn) for part, turn in zip(away, second_turn)]
+        with jax.named_scope(f"P_G{index}"):
+            came = [lax.ppermute(part, AXES, turn) for part, turn in zip(away, second_turn)]
         return mine + (came[0] + zero) + came[1] + came[2]
 
     mine, *away, done_0 = apply_blocks(table, held_0, blocks, 0)
     *parts_1, done_0 = lax.optimization_barrier((own_1, left_1, across_1, right_1, done_0))
-    results = [to_owner(mine, away, done_0[0, 0])]
+    results = [to_owner(mine, away, done_0[0, 0], 0)]
     mine, *away, done_1 = apply_blocks(table, both_cores(parts_1, 1), blocks, 1)
-    results.append(to_owner(mine, away, done_1[0, 0]))
+    results.append(to_owner(mine, away, done_1[0, 0], 1))
     parts = [r[:, :HALF] for r in results] + [r[:, HALF:] for r in results]
     return jnp.concatenate(parts, axis=1)
 

time: 141 us -> 141 us (level)
  Pallas kernels: 18.5 us -> 38.7 us
  waiting for transfers between devices: 73.2 us -> 54.1 us
    pallas_call x2, Pallas kernels: 9.02 us -> 22.8 us  [apply_blocks(): pl.pallas_call(apply_kernel, name=f'apply_{index}', in_specs=[SMEM] + [AN...]
    ppermute x2 -> x3, waiting for transfers between devices: 11 us -> 0.83 us  [across_dir(): return lax.ppermute(part, 'dir', swap)]
    pallas_call x2, Pallas kernels: 4.1 us -> 10.5 us  [prepare_near(): pl.pallas_call(functools.partial(prepare_near_kernel, first), name=f'prep...]
    ppermute x7 -> x9, waiting for transfers between devices: 25.4 us -> 20.4 us  [step(): return lax.ppermute(part, 'x', [(i, (i + k) % 4) for i in range(4)])]
    ppermute x12, waiting for transfers between devices: 36.8 us -> 32 us  [to_owner(): lax.ppermute(part, AXES, turn)]
    ppermute x7 -> x9, starting transfers between devices: 11.6 us -> 11.4 us  [step(): return lax.ppermute(part, 'x', [(i, (i + k) % 4) for i in range(4)])]
    ppermute x2 -> x3, starting transfers between devices: 3.9 us -> 3.99 us  [across_dir(): return lax.ppermute(part, 'dir', swap)]
  transfers between devices with their start and end apart: 23 -> 26, of which waited for: 14 -> 14; matrix products, arithmetic and copies ran while one was open for 3% -> 4% of each run, Pallas kernels for 11% -> 25%
where the time goes in v6:
time: 141 us; the launch traced here: 140 us
  waiting for transfers between devices  54.1 us (38%)
  starting transfers between devices  39 us (28%)
  Pallas kernels  38.7 us (27%)
  other arithmetic  4.9 us (3%)
  local copies, waits for them, and re-layouts  2.72 us (2%)
    ppermute x12, waiting for transfers between devices, to_owner(): lax.ppermute(part, AXES, turn)  32 us
    ppermute x12, starting transfers between devices, to_owner(): lax.ppermute(part, AXES, turn)  23.5 us
    pallas_call x2, Pallas kernels, apply_blocks(): pl.pallas_call(apply_kernel, name=f'apply_{index}', in_specs=[SMEM] + [AN...  22.8 us
    ppermute x9, waiting for transfers between devices, step(): return lax.ppermute(part, 'x', [(i, (i + k) % 4) for i in range(4)])  20.4 us
    ppermute x9, starting transfers between devices, step(): return lax.ppermute(part, 'x', [(i, (i + k) % 4) for i in range(4)])  11.4 us
    pallas_call x2, Pallas kernels, prepare_near(): pl.pallas_call(functools.partial(prepare_near_kernel, first), name=f'prep...  10.5 us
    ppermute x3, starting transfers between devices, across_dir(): return lax.ppermute(part, 'dir', swap)  3.99 us
    pallas_call x1, Pallas kernels, partial_rhs(): pl.pallas_call(rhs_kernel, name='rhs', in_specs=[HBM, HBM], out_specs=[VM...  3.04 us
  transfers between devices with their start and end apart: 26, of which 14 were waited for; matrix products, arithmetic and copies ran while one was open for 4% of the time, Pallas kernels for 25%

profile of v6, /device:TPU:0, one launch (start us, length us, event | category | flops | bytes accessed | tf_op | source)
XLA Modules:
  0.0 139.8 jit_solution(1660254196383393674)
XLA Ops:
  0.0 3.0 %rhs.1 = (f32[512,256]{1,0:T(8,128)S(1)}, f32[512,256]{1,0:T(8,128)S(1)}) custom-call(bf16[1024,512]{1,0:T(8,128)(2,1)} %cot_ref.1, bf16[2,512,1024]{2,1,0:T(8,128)(2,1)} %rad_ref.1), custom_call_target="tpu_custom_call" | custom-call | flops 1073741824 | bytes 4194304 | tf_op jit(solution)/shard_map/rhs/pallas_call | solution.py:90
  3.1 2.1 %collective-permute-start = (f32[256,256]{1,0:T(8,128)S(1)}, f32[256,256]{1,0:T(8,128)S(1)}, u32[]{:S(2)}, u32[]{:S(2)}) collective-permute-start(f32[256,256]{1,0:T(8,128)S(1)} %slice.145), channel_id=1, source_target_pairs={{0,64},{64,0},{1,65},{65,1},{2,66},{66,2},{3,67},{67,3},{4,68},{68... | collective-permute-start | bytes 786440 | tf_op jit(solution)/shard_map/P_ZU/ppermute | solution.py:364
  5.3 5.3 %prepare_near_0.1 = (bf16[4,512,2048]{2,1,0:T(8,128)(2,1)S(1)}, f32[8,128]{1,0:T(8,128)S(1)}) custom-call(s32[48]{0:T(128)S(1)} %concatenate.6.table, f32[2,8,512,512]{3,2,1,0:T(8,128)} %z_ref.3), custom_call_target="tpu_custom_call" | custom-call | flops 268435456 | bytes 8388608 | tf_op jit(solution)/shard_map/prepare_near_0/pallas_call | solution.py:139
  10.6 0.5 slice.146
  11.1 0.4 collective-permute-done
  11.5 0.7 fusion.21
  12.2 1.8 %collective-permute-start.1 = (f32[256,256]{1,0:T(8,128)S(1)}, f32[256,256]{1,0:T(8,128)S(1)}, u32[]{:S(2)}, u32[]{:S(2)}) collective-permute-start(f32[256,256]{1,0:T(8,128)S(1)} %get-tuple-element.42), channel_id=1, source_target_pairs={{0,64},{64,0},{1,65},{65,1},{2,66},{66,2},{3,67},{67,3},{4,68},{68... | collective-permute-start | bytes 786440 | tf_op jit(solution)/shard_map/P_ZL/ppermute | solution.py:364
  14.0 1.5 %collective-permute-start.2 = (f32[256,256]{1,0:T(8,128)S(1)}, f32[256,256]{1,0:T(8,128)S(1)}, u32[]{:S(2)}, u32[]{:S(2)}) collective-permute-start(f32[256,256]{1,0:T(8,128)S(1)} %get-tuple-element.40.refs_0_), channel_id=1, source_target_pairs={{0,2},{2,4},{4,6},{6,0},{1,3},{3,5},{5,7},{7,1},{8,10},{10,12},{12... | collective-permute-start | bytes 786440 | tf_op jit(solution)/shard_map/P_LU/ppermute | solution.py:368
  15.5 1.7 %collective-permute-start.3 = (f32[256,256]{1,0:T(8,128)S(1)}, f32[256,256]{1,0:T(8,128)S(1)}, u32[]{:S(2)}, u32[]{:S(2)}) collective-permute-start(f32[256,256]{1,0:T(8,128)S(1)} %get-tuple-element.40.refs_0_), channel_id=1, source_target_pairs={{0,6},{2,0},{4,2},{6,4},{1,7},{3,1},{5,3},{7,5},{8,14},{10,8},{12,... | collective-permute-start | bytes 786440 | tf_op jit(solution)/shard_map/P_RU/ppermute | solution.py:368
  17.2 5.3 %prepare_near_4.1 = (bf16[4,512,2048]{2,1,0:T(8,128)(2,1)S(1)}, f32[8,128]{1,0:T(8,128)S(1)}) custom-call(s32[48]{0:T(128)S(1)} %concatenate.6.table, f32[2,8,512,512]{3,2,1,0:T(8,128)} %z_ref.3), custom_call_target="tpu_custom_call" | custom-call | flops 268435456 | bytes 8388608 | tf_op jit(solution)/shard_map/prepare_near_4/pallas_call | solution.py:139
  22.5 0.5 slice.148
  23.0 0.7 add_add_fusion.1.refs_1_
  23.8 1.8 %collective-permute-start.7 = (f32[256,256]{1,0:T(8,128)S(1)}, f32[256,256]{1,0:T(8,128)S(1)}, u32[]{:S(2)}, u32[]{:S(2)}) collective-permute-start(f32[256,256]{1,0:T(8,128)S(1)} %add_add_fusion.1.refs_1_), channel_id=1, source_target_pairs={{0,6},{2,0},{4,2},{6,4},{1,7},{3,1},{5,3},{7,5},{8,14},{10,8},{12,... | collective-permute-start | bytes 786440 | tf_op jit(solution)/shard_map/P_RL/ppermute | solution.py:368
  25.6 2.0 %prepare_far.1 = (bf16[4,128,2048]{2,1,0:T(8,128)(2,1)S(1)}, bf16[4,512,512]{2,1,0:T(8,128)(2,1)S(1)}, f32[8,128]{1,0:T(8,128)S(1)}) custom-call(s32[48]{0:T(128)S(1)} %concatenate.6.table, f32[2,4,96,512]{3,2,1,0:T(8,128)} %u_ref.1, f32[2,4,96,512]{3,2,1,0:T(8,128)} %v_ref.1), custom_call_target="tpu_custom_call" | custom-call | flops 268435456 | bytes 4194304 | tf_op jit(solution)/shard_map/prepare_far/pallas_call | solution.py:192
  27.6 0.5 slice.149
  28.2 1.0 collective-permute-start.4
  29.2 2.0 %collective-permute-done.7.refs_7_ = f32[256,256]{1,0:T(8,128)S(1)} collective-permute-done((f32[256,256]{1,0:T(8,128)S(1)}, f32[256,256]{1,0:T(8,128)S(1)}, u32[]{:S(2)}, u32[]{:S(2)}) %collective-permute-start.7) | collective-permute-done | bytes 262176 | tf_op jit(solution)/shard_map/P_RL/ppermute | solution.py:368
  31.3 2.0 %collective-permute-start.8 = (f32[256,256]{1,0:T(8,128)S(1)}, f32[256,256]{1,0:T(8,128)S(1)}, u32[]{:S(2)}, u32[]{:S(2)}) collective-permute-start(f32[256,256]{1,0:T(8,128)S(1)} %collective-permute-done.7.refs_7_), channel_id=1, source_target_pairs={{0,6},{2,0},{4,2},{6,4},{1,7},{3,1},{5,3},{7,5},{8,14},{10,8},{12,... | collective-permute-start | bytes 786440 | tf_op jit(solution)/shard_map/P_B0/ppermute | solution.py:368
  33.2 0.5 collective-permute-done.5
  33.7 0.7 add_add_fusion.refs_0_
  34.4 6.4 %collective-permute-done.6.refs_4_ = f32[256,256]{1,0:T(8,128)S(1)} collective-permute-done((f32[256,256]{1,0:T(8,128)S(1)}, f32[256,256]{1,0:T(8,128)S(1)}, u32[]{:S(2)}, u32[]{:S(2)}) %collective-permute-start.6) | collective-permute-done | bytes 262176 | tf_op jit(solution)/shard_map/P_A0/ppermute | solution.py:368
  41.2 1.4 %collective-permute-start.15 = (f32[512,256]{1,0:T(8,128)S(1)}, f32[512,256]{1,0:T(8,128)S(1)}, u32[]{:S(2)}, u32[]{:S(2)}) collective-permute-start(f32[512,256]{1,0:T(8,128)S(1)} %add_add_fusion.refs_0_), channel_id=1, source_target_pairs={{0,4},{2,6},{4,0},{6,2},{1,5},{3,7},{5,1},{7,3},{8,12},{10,14},{12... | collective-permute-start | bytes 1572872 | tf_op jit(solution)/shard_map/P_K1/ppermute | solution.py:368
  42.7 1.8 %collective-permute-start.16 = (f32[512,256]{1,0:T(8,128)S(1)}, f32[512,256]{1,0:T(8,128)S(1)}, u32[]{:S(2)}, u32[]{:S(2)}) collective-permute-start(f32[512,256]{1,0:T(8,128)S(1)} %add_add_fusion.refs_0_), channel_id=1, source_target_pairs={{0,6},{2,0},{4,2},{6,4},{1,7},{3,1},{5,3},{7,5},{8,14},{10,8},{12,... | collective-permute-start | bytes 1572872 | tf_op jit(solution)/shard_map/P_R1/ppermute | solution.py:368
  44.5 0.8 collective-permute-done.9.refs_1_
  45.3 11.3 %apply_0.1 = (f32[4,256,256]{2,1,0:T(8,128)S(1)}, f32[4,256,256]{2,1,0:T(8,128)S(1)}, f32[4,256,256]{2,1,0:T(8,128)S(1)}, f32[4,256,256]{2,1,0:T(8,128)S(1)}, f32[8,128]{1,0:T(8,128)S(1)}) custom-call(s32[48]{0:T(128)S(1)} %concatenate.6.table, f32[2048,256]{1,0:T(8,128)S(1)} %pack_0.1.refs_0_, f32[2048,256]{1,0:T(8,128)S(1)} %collective-permute-done.9.refs_1_, ...), custom_call_target="tpu_custom_call" | custom-call | flops 42949672960 | bytes 1 | tf_op jit(solution)/shard_map/apply_0/pallas_call | solution.py:317
  56.6 11.3 %collective-permute-done.14.refs_1_ = f32[512,256]{1,0:T(8,128)S(1)} collective-permute-done((f32[512,256]{1,0:T(8,128)S(1)}, f32[512,256]{1,0:T(8,128)S(1)}, u32[]{:S(2)}, u32[]{:S(2)}) %collective-permute-start.14) | collective-permute-done | bytes 524320 | tf_op jit(solution)/shard_map/P_L1/ppermute | solution.py:368
  67.9 0.6 collective-permute-done.16.refs_3_
  68.8 1.9 %collective-permute-start.10 = (f32[4,256,256]{2,1,0:T(8,128)S(1)}, f32[4,256,256]{2,1,0:T(8,128)S(1)}, u32[]{:S(2)}, u32[]{:S(2)}) collective-permute-start(f32[4,256,256]{2,1,0:T(8,128)S(1)} %get-tuple-element.56), channel_id=1, source_target_pairs={{0,16},{1,65},{2,18},{3,67},{4,20},{5,69},{6,22},{7,71},{8,24},{9,... | collective-permute-start | bytes 3145736 | tf_op jit(solution)/shard_map/P_F0/ppermute | solution.py:397
  70.7 2.1 %collective-permute-start.11 = (f32[4,256,256]{2,1,0:T(8,128)S(1)}, f32[4,256,256]{2,1,0:T(8,128)S(1)}, u32[]{:S(2)}, u32[]{:S(2)}) collective-permute-start(f32[4,256,256]{2,1,0:T(8,128)S(1)} %get-tuple-element.57), channel_id=1, source_target_pairs={{0,32},{1,9},{2,34},{3,11},{4,36},{5,13},{6,38},{7,15},{8,40},{9,1... | collective-permute-start | bytes 3145736 | tf_op jit(solution)/shard_map/P_F0/ppermute | solution.py:397
  72.8 1.3 collective-permute-start.12
  74.2 11.5 %apply_1.1 = (f32[4,256,256]{2,1,0:T(8,128)S(1)}, f32[4,256,256]{2,1,0:T(8,128)S(1)}, f32[4,256,256]{2,1,0:T(8,128)S(1)}, f32[4,256,256]{2,1,0:T(8,128)S(1)}, f32[8,128]{1,0:T(8,128)S(1)}) custom-call(s32[48]{0:T(128)S(1)} %concatenate.6.table, f32[2048,256]{1,0:T(8,128)S(1)} %pack_1.1.refs_0_, f32[2048,256]{1,0:T(8,128)S(1)} %collective-permute-done.19.refs_1_, ...), custom_call_target="tpu_custom_call" | custom-call | flops 42949672960 | bytes 1 | tf_op jit(solution)/shard_map/apply_1/pallas_call | solution.py:317
  85.8 3.1 %collective-permute-start.22 = (f32[4,256,256]{2,1,0:T(8,128)S(1)}, f32[4,256,256]{2,1,0:T(8,128)S(1)}, u32[]{:S(2)}, u32[]{:S(2)}) collective-permute-start(f32[4,256,256]{2,1,0:T(8,128)S(1)} %get-tuple-element.69), channel_id=1, source_target_pairs={{0,48},{1,73},{2,50},{3,75},{4,52},{5,77},{6,54},{7,79},{8,56},{9,... | collective-permute-start | bytes 3145736 | tf_op jit(solution)/shard_map/P_F1/ppermute | solution.py:397
  89.0 0.5 slice.158
  89.5 7.4 %collective-permute-done.11 = f32[4,256,256]{2,1,0:T(8,128)S(1)} collective-permute-done((f32[4,256,256]{2,1,0:T(8,128)S(1)}, f32[4,256,256]{2,1,0:T(8,128)S(1)}, u32[]{:S(2)}, u32[]{:S(2)}) %collective-permute-start.11) | collective-permute-done | bytes 1048608 | tf_op jit(solution)/shard_map/P_F0/ppermute | solution.py:397
  97.3 2.5 %collective-permute-start.13 = (f32[256,256]{1,0:T(8,128)S(1)}, f32[256,256]{1,0:T(8,128)S(1)}, u32[]{:S(2)}, u32[]{:S(2)}) collective-permute-start(f32[256,256]{1,0:T(8,128)S(1)} %get-tuple-element.71), channel_id=1, source_target_pairs={{0,64},{1,17},{2,66},{3,19},{4,68},{5,21},{6,70},{7,23},{8,72},{9,... | collective-permute-start | bytes 786440 | tf_op jit(solution)/shard_map/P_G0/ppermute | solution.py:400
  99.8 2.6 %collective-permute-start.17 = (f32[256,256]{1,0:T(8,128)S(1)}, f32[256,256]{1,0:T(8,128)S(1)}, u32[]{:S(2)}, u32[]{:S(2)}) collective-permute-start(f32[256,256]{1,0:T(8,128)S(1)} %get-tuple-element.73), channel_id=1, source_target_pairs={{0,8},{1,33},{2,10},{3,35},{4,12},{5,37},{6,14},{7,39},{8,0},{9,41... | collective-permute-start | bytes 786440 | tf_op jit(solution)/shard_map/P_G0/ppermute | solution.py:400
  102.4 11.2 %collective-permute-done.20 = f32[4,256,256]{2,1,0:T(8,128)S(1)} collective-permute-done((f32[4,256,256]{2,1,0:T(8,128)S(1)}, f32[4,256,256]{2,1,0:T(8,128)S(1)}, u32[]{:S(2)}, u32[]{:S(2)}) %collective-permute-start.20) | collective-permute-done | bytes 1048608 | tf_op jit(solution)/shard_map/P_F1/ppermute | solution.py:397
  113.7 3.5 %collective-permute-start.18 = (f32[256,256]{1,0:T(8,128)S(1)}, f32[256,256]{1,0:T(8,128)S(1)}, u32[]{:S(2)}, u32[]{:S(2)}) collective-permute-start(f32[256,256]{1,0:T(8,128)S(1)} %get-tuple-element.72), channel_id=1, source_target_pairs={{0,72},{1,49},{2,74},{3,51},{4,76},{5,53},{6,78},{7,55},{8,64},{9,... | collective-permute-start | bytes 786440 | tf_op jit(solution)/shard_map/P_G0/ppermute | solution.py:400
  117.1 7.8 %collective-permute-done.21 = f32[4,256,256]{2,1,0:T(8,128)S(1)} collective-permute-done((f32[4,256,256]{2,1,0:T(8,128)S(1)}, f32[4,256,256]{2,1,0:T(8,128)S(1)}, u32[]{:S(2)}, u32[]{:S(2)}) %collective-permute-start.21) | collective-permute-done | bytes 1048608 | tf_op jit(solution)/shard_map/P_F1/ppermute | solution.py:397
  125.4 1.6 %collective-permute-start.23 = (f32[256,256]{1,0:T(8,128)S(1)}, f32[256,256]{1,0:T(8,128)S(1)}, u32[]{:S(2)}, u32[]{:S(2)}) collective-permute-start(f32[256,256]{1,0:T(8,128)S(1)} %get-tuple-element.74), channel_id=1, source_target_pairs={{0,64},{1,17},{2,66},{3,19},{4,68},{5,21},{6,70},{7,23},{8,72},{9,... | collective-permute-start | bytes 786440 | tf_op jit(solution)/shard_map/P_G1/ppermute | solution.py:400
  127.0 4.0 %collective-permute-start.24 = (f32[256,256]{1,0:T(8,128)S(1)}, f32[256,256]{1,0:T(8,128)S(1)}, u32[]{:S(2)}, u32[]{:S(2)}) collective-permute-start(f32[256,256]{1,0:T(8,128)S(1)} %get-tuple-element.76), channel_id=1, source_target_pairs={{0,8},{1,33},{2,10},{3,35},{4,12},{5,37},{6,14},{7,39},{8,0},{9,41... | collective-permute-start | bytes 786440 | tf_op jit(solution)/shard_map/P_G1/ppermute | solution.py:400
  131.0 0.7 collective-permute-start.25
  131.7 0.8 fusion.13
  132.5 0.5 slice.176
  133.0 0.9 collective-permute-done.23
  133.9 4.3 %collective-permute-done.24 = f32[256,256]{1,0:T(8,128)S(1)} collective-permute-done((f32[256,256]{1,0:T(8,128)S(1)}, f32[256,256]{1,0:T(8,128)S(1)}, u32[]{:S(2)}, u32[]{:S(2)}) %collective-permute-start.24) | collective-permute-done | bytes 262176 | tf_op jit(solution)/shard_map/P_G1/ppermute | solution.py:400
  138.1 0.8 fusion.6
  138.9 0.8 pad_maximum_fusion
  (40 shorter events, 2.0 us)
Async XLA Ops:
  0.0 5.2 %copy-start = (s32[4,2]{0,1:T(2,128)S(1)}, s32[4,2]{0,1:T(2,128)}, u32[]{:S(2)}) copy-start(s32[4,2]{0,1:T(2,128)} %param.15) | copy-start | bytes 100
  0.0 5.2 %copy-start.1 = (s32[8,2]{0,1:T(2,128)S(1)}, s32[8,2]{0,1:T(2,128)}, u32[]{:S(2)}) copy-start(s32[8,2]{0,1:T(2,128)} %param.12) | copy-start | bytes 196
  0.0 5.2 %copy-start.2 = (s32[1,2]{1,0:T(1,128)S(1)}, s32[1,2]{1,0:T(1,128)}, u32[]{:S(2)}) copy-start(s32[1,2]{1,0:T(1,128)} %param.17) | copy-start | bytes 28
  0.0 5.2 %copy-start.3 = (s32[4]{0:T(128)S(1)}, s32[4]{0:T(128)}, u32[]{:S(2)}) copy-start(s32[4]{0:T(128)} %param.16) | copy-start | bytes 52
  3.1 8.4 %collective-permute-start = (f32[256,256]{1,0:T(8,128)S(1)}, f32[256,256]{1,0:T(8,128)S(1)}, u32[]{:S(2)}, u32[]{:S(2)}) collective-permute-start(f32[256,256]{1,0:T(8,128)S(1)} %slice.145), channel_id=1, source_target_pairs={{0,64},{64,0},{1,65},{65,1},{2,66},{66,2},{3,67},{67,3},{4,68},{68... | collective-permute-start | bytes 786440 | tf_op jit(solution)/shard_map/P_ZU/ppermute | solution.py:364
  12.2 10.8 %collective-permute-start.1 = (f32[256,256]{1,0:T(8,128)S(1)}, f32[256,256]{1,0:T(8,128)S(1)}, u32[]{:S(2)}, u32[]{:S(2)}) collective-permute-start(f32[256,256]{1,0:T(8,128)S(1)} %get-tuple-element.42), channel_id=1, source_target_pairs={{0,64},{64,0},{1,65},{65,1},{2,66},{66,2},{3,67},{67,3},{4,68},{68... | collective-permute-start | bytes 786440 | tf_op jit(solution)/shard_map/P_ZL/ppermute | solution.py:364
  14.0 9.7 %collective-permute-start.2 = (f32[256,256]{1,0:T(8,128)S(1)}, f32[256,256]{1,0:T(8,128)S(1)}, u32[]{:S(2)}, u32[]{:S(2)}) collective-permute-start(f32[256,256]{1,0:T(8,128)S(1)} %get-tuple-element.40.refs_0_), channel_id=1, source_target_pairs={{0,2},{2,4},{4,6},{6,0},{1,3},{3,5},{5,7},{7,1},{8,10},{10,12},{12... | collective-permute-start | bytes 786440 | tf_op jit(solution)/shard_map/P_LU/ppermute | solution.py:368
  15.5 8.2 %collective-permute-start.3 = (f32[256,256]{1,0:T(8,128)S(1)}, f32[256,256]{1,0:T(8,128)S(1)}, u32[]{:S(2)}, u32[]{:S(2)}) collective-permute-start(f32[256,256]{1,0:T(8,128)S(1)} %get-tuple-element.40.refs_0_), channel_id=1, source_target_pairs={{0,6},{2,0},{4,2},{6,4},{1,7},{3,1},{5,3},{7,5},{8,14},{10,8},{12,... | collective-permute-start | bytes 786440 | tf_op jit(solution)/shard_map/P_RU/ppermute | solution.py:368
  23.7 10.0 %collective-permute-start.5 = (f32[512,256]{1,0:T(8,128)S(1)}, f32[512,256]{1,0:T(8,128)S(1)}, u32[]{:S(2)}, u32[]{:S(2)}) collective-permute-start(f32[512,256]{1,0:T(8,128)S(1)} %get-tuple-element.46), channel_id=1, source_target_pairs={{0,64},{64,0},{1,65},{65,1},{2,66},{66,2},{3,67},{67,3},{4,68},{68... | collective-permute-start | bytes 1572872 | tf_op jit(solution)/shard_map/P_Z1/ppermute | solution.py:364
  23.8 7.4 %collective-permute-start.7 = (f32[256,256]{1,0:T(8,128)S(1)}, f32[256,256]{1,0:T(8,128)S(1)}, u32[]{:S(2)}, u32[]{:S(2)}) collective-permute-start(f32[256,256]{1,0:T(8,128)S(1)} %add_add_fusion.1.refs_1_), channel_id=1, source_target_pairs={{0,6},{2,0},{4,2},{6,4},{1,7},{3,1},{5,3},{7,5},{8,14},{10,8},{12,... | collective-permute-start | bytes 786440 | tf_op jit(solution)/shard_map/P_RL/ppermute | solution.py:368
  28.2 12.7 %collective-permute-start.4 = (f32[256,256]{1,0:T(8,128)S(1)}, f32[256,256]{1,0:T(8,128)S(1)}, u32[]{:S(2)}, u32[]{:S(2)}) collective-permute-start(f32[256,256]{1,0:T(8,128)S(1)} %add_add_fusion.1.refs_1_), channel_id=1, source_target_pairs={{0,2},{2,4},{4,6},{6,0},{1,3},{3,5},{5,7},{7,1},{8,10},{10,12},{12... | collective-permute-start | bytes 786440 | tf_op jit(solution)/shard_map/P_LL/ppermute | solution.py:368
  29.2 11.6 %collective-permute-start.6 = (f32[256,256]{1,0:T(8,128)S(1)}, f32[256,256]{1,0:T(8,128)S(1)}, u32[]{:S(2)}, u32[]{:S(2)}) collective-permute-start(f32[256,256]{1,0:T(8,128)S(1)} %collective-permute-done.2.refs_2_), channel_id=1, source_target_pairs={{0,2},{2,4},{4,6},{6,0},{1,3},{3,5},{5,7},{7,1},{8,10},{10,12},{12... | collective-permute-start | bytes 786440 | tf_op jit(solution)/shard_map/P_A0/ppermute | solution.py:368
  31.3 9.6 %collective-permute-start.8 = (f32[256,256]{1,0:T(8,128)S(1)}, f32[256,256]{1,0:T(8,128)S(1)}, u32[]{:S(2)}, u32[]{:S(2)}) collective-permute-start(f32[256,256]{1,0:T(8,128)S(1)} %collective-permute-done.7.refs_7_), channel_id=1, source_target_pairs={{0,6},{2,0},{4,2},{6,4},{1,7},{3,1},{5,3},{7,5},{8,14},{10,8},{12,... | collective-permute-start | bytes 786440 | tf_op jit(solution)/shard_map/P_B0/ppermute | solution.py:368
  41.1 4.2 %collective-permute-start.9 = (f32[2048,256]{1,0:T(8,128)S(1)}, f32[2048,256]{1,0:T(8,128)S(1)}, u32[]{:S(2)}, u32[]{:S(2)}) collective-permute-start(f32[2048,256]{1,0:T(8,128)S(1)} %pack_0.1.refs_0_), channel_id=1, source_target_pairs={{0,1},{1,0},{2,3},{3,2},{4,5},{5,4},{6,7},{7,6},{8,9},{9,8},{10,11... | collective-permute-start | bytes 6291464 | tf_op jit(solution)/shard_map/P_S0/ppermute | solution.py:373
  41.2 26.8 %collective-permute-start.14 = (f32[512,256]{1,0:T(8,128)S(1)}, f32[512,256]{1,0:T(8,128)S(1)}, u32[]{:S(2)}, u32[]{:S(2)}) collective-permute-start(f32[512,256]{1,0:T(8,128)S(1)} %add_add_fusion.refs_0_), channel_id=1, source_target_pairs={{0,2},{2,4},{4,6},{6,0},{1,3},{3,5},{5,7},{7,1},{8,10},{10,12},{12... | collective-permute-start | bytes 1572872 | tf_op jit(solution)/shard_map/P_L1/ppermute | solution.py:368
  41.2 26.7 %collective-permute-start.15 = (f32[512,256]{1,0:T(8,128)S(1)}, f32[512,256]{1,0:T(8,128)S(1)}, u32[]{:S(2)}, u32[]{:S(2)}) collective-permute-start(f32[512,256]{1,0:T(8,128)S(1)} %add_add_fusion.refs_0_), channel_id=1, source_target_pairs={{0,4},{2,6},{4,0},{6,2},{1,5},{3,7},{5,1},{7,3},{8,12},{10,14},{12... | collective-permute-start | bytes 1572872 | tf_op jit(solution)/shard_map/P_K1/ppermute | solution.py:368
  42.7 25.9 %collective-permute-start.16 = (f32[512,256]{1,0:T(8,128)S(1)}, f32[512,256]{1,0:T(8,128)S(1)}, u32[]{:S(2)}, u32[]{:S(2)}) collective-permute-start(f32[512,256]{1,0:T(8,128)S(1)} %add_add_fusion.refs_0_), channel_id=1, source_target_pairs={{0,6},{2,0},{4,2},{6,4},{1,7},{3,1},{5,3},{7,5},{8,14},{10,8},{12,... | collective-permute-start | bytes 1572872 | tf_op jit(solution)/shard_map/P_R1/ppermute | solution.py:368
  68.8 5.4 %collective-permute-start.19 = (f32[2048,256]{1,0:T(8,128)S(1)}, f32[2048,256]{1,0:T(8,128)S(1)}, u32[]{:S(2)}, u32[]{:S(2)}) collective-permute-start(f32[2048,256]{1,0:T(8,128)S(1)} %pack_1.1.refs_0_), channel_id=1, source_target_pairs={{0,1},{1,0},{2,3},{3,2},{4,5},{5,4},{6,7},{7,6},{8,9},{9,8},{10,11... | collective-permute-start | bytes 6291464 | tf_op jit(solution)/shard_map/P_S1/ppermute | solution.py:373
  68.8 17.0 %collective-permute-start.10 = (f32[4,256,256]{2,1,0:T(8,128)S(1)}, f32[4,256,256]{2,1,0:T(8,128)S(1)}, u32[]{:S(2)}, u32[]{:S(2)}) collective-permute-start(f32[4,256,256]{2,1,0:T(8,128)S(1)} %get-tuple-element.56), channel_id=1, source_target_pairs={{0,16},{1,65},{2,18},{3,67},{4,20},{5,69},{6,22},{7,71},{8,24},{9,... | collective-permute-start | bytes 3145736 | tf_op jit(solution)/shard_map/P_F0/ppermute | solution.py:397
  70.7 26.2 %collective-permute-start.11 = (f32[4,256,256]{2,1,0:T(8,128)S(1)}, f32[4,256,256]{2,1,0:T(8,128)S(1)}, u32[]{:S(2)}, u32[]{:S(2)}) collective-permute-start(f32[4,256,256]{2,1,0:T(8,128)S(1)} %get-tuple-element.57), channel_id=1, source_target_pairs={{0,32},{1,9},{2,34},{3,11},{4,36},{5,13},{6,38},{7,15},{8,40},{9,1... | collective-permute-start | bytes 3145736 | tf_op jit(solution)/shard_map/P_F0/ppermute | solution.py:397
  72.8 24.3 %collective-permute-start.12 = (f32[4,256,256]{2,1,0:T(8,128)S(1)}, f32[4,256,256]{2,1,0:T(8,128)S(1)}, u32[]{:S(2)}, u32[]{:S(2)}) collective-permute-start(f32[4,256,256]{2,1,0:T(8,128)S(1)} %get-tuple-element.58), channel_id=1, source_target_pairs={{0,48},{1,73},{2,50},{3,75},{4,52},{5,77},{6,54},{7,79},{8,56},{9,... | collective-permute-start | bytes 3145736 | tf_op jit(solution)/shard_map/P_F0/ppermute | solution.py:397
  85.7 28.0 %collective-permute-start.20 = (f32[4,256,256]{2,1,0:T(8,128)S(1)}, f32[4,256,256]{2,1,0:T(8,128)S(1)}, u32[]{:S(2)}, u32[]{:S(2)}) collective-permute-start(f32[4,256,256]{2,1,0:T(8,128)S(1)} %get-tuple-element.67), channel_id=1, source_target_pairs={{0,16},{1,65},{2,18},{3,67},{4,20},{5,69},{6,22},{7,71},{8,24},{9,... | collective-permute-start | bytes 3145736 | tf_op jit(solution)/shard_map/P_F1/ppermute | solution.py:397
  85.7 39.2 %collective-permute-start.21 = (f32[4,256,256]{2,1,0:T(8,128)S(1)}, f32[4,256,256]{2,1,0:T(8,128)S(1)}, u32[]{:S(2)}, u32[]{:S(2)}) collective-permute-start(f32[4,256,256]{2,1,0:T(8,128)S(1)} %get-tuple-element.68), channel_id=1, source_target_pairs={{0,32},{1,9},{2,34},{3,11},{4,36},{5,13},{6,38},{7,15},{8,40},{9,1... | collective-permute-start | bytes 3145736 | tf_op jit(solution)/shard_map/P_F1/ppermute | solution.py:397
  85.8 39.4 %collective-permute-start.22 = (f32[4,256,256]{2,1,0:T(8,128)S(1)}, f32[4,256,256]{2,1,0:T(8,128)S(1)}, u32[]{:S(2)}, u32[]{:S(2)}) collective-permute-start(f32[4,256,256]{2,1,0:T(8,128)S(1)} %get-tuple-element.69), channel_id=1, source_target_pairs={{0,48},{1,73},{2,50},{3,75},{4,52},{5,77},{6,54},{7,79},{8,56},{9,... | collective-permute-start | bytes 3145736 | tf_op jit(solution)/shard_map/P_F1/ppermute | solution.py:397
  97.3 33.7 %collective-permute-start.13 = (f32[256,256]{1,0:T(8,128)S(1)}, f32[256,256]{1,0:T(8,128)S(1)}, u32[]{:S(2)}, u32[]{:S(2)}) collective-permute-start(f32[256,256]{1,0:T(8,128)S(1)} %get-tuple-element.71), channel_id=1, source_target_pairs={{0,64},{1,17},{2,66},{3,19},{4,68},{5,21},{6,70},{7,23},{8,72},{9,... | collective-permute-start | bytes 786440 | tf_op jit(solution)/shard_map/P_G0/ppermute | solution.py:400
  99.8 31.9 %collective-permute-start.17 = (f32[256,256]{1,0:T(8,128)S(1)}, f32[256,256]{1,0:T(8,128)S(1)}, u32[]{:S(2)}, u32[]{:S(2)}) collective-permute-start(f32[256,256]{1,0:T(8,128)S(1)} %get-tuple-element.73), channel_id=1, source_target_pairs={{0,8},{1,33},{2,10},{3,35},{4,12},{5,37},{6,14},{7,39},{8,0},{9,41... | collective-permute-start | bytes 786440 | tf_op jit(solution)/shard_map/P_G0/ppermute | solution.py:400
  113.7 18.0 %collective-permute-start.18 = (f32[256,256]{1,0:T(8,128)S(1)}, f32[256,256]{1,0:T(8,128)S(1)}, u32[]{:S(2)}, u32[]{:S(2)}) collective-permute-start(f32[256,256]{1,0:T(8,128)S(1)} %get-tuple-element.72), channel_id=1, source_target_pairs={{0,72},{1,49},{2,74},{3,51},{4,76},{5,53},{6,78},{7,55},{8,64},{9,... | collective-permute-start | bytes 786440 | tf_op jit(solution)/shard_map/P_G0/ppermute | solution.py:400
  125.4 8.5 %collective-permute-start.23 = (f32[256,256]{1,0:T(8,128)S(1)}, f32[256,256]{1,0:T(8,128)S(1)}, u32[]{:S(2)}, u32[]{:S(2)}) collective-permute-start(f32[256,256]{1,0:T(8,128)S(1)} %get-tuple-element.74), channel_id=1, source_target_pairs={{0,64},{1,17},{2,66},{3,19},{4,68},{5,21},{6,70},{7,23},{8,72},{9,... | collective-permute-start | bytes 786440 | tf_op jit(solution)/shard_map/P_G1/ppermute | solution.py:400
  127.0 11.1 %collective-permute-start.24 = (f32[256,256]{1,0:T(8,128)S(1)}, f32[256,256]{1,0:T(8,128)S(1)}, u32[]{:S(2)}, u32[]{:S(2)}) collective-permute-start(f32[256,256]{1,0:T(8,128)S(1)} %get-tuple-element.76), channel_id=1, source_target_pairs={{0,8},{1,33},{2,10},{3,35},{4,12},{5,37},{6,14},{7,39},{8,0},{9,41... | collective-permute-start | bytes 786440 | tf_op jit(solution)/shard_map/P_G1/ppermute | solution.py:400
  131.0 7.2 %collective-permute-start.25 = (f32[256,256]{1,0:T(8,128)S(1)}, f32[256,256]{1,0:T(8,128)S(1)}, u32[]{:S(2)}, u32[]{:S(2)}) collective-permute-start(f32[256,256]{1,0:T(8,128)S(1)} %get-tuple-element.75), channel_id=1, source_target_pairs={{0,72},{1,49},{2,74},{3,51},{4,76},{5,53},{6,78},{7,55},{8,64},{9,... | collective-permute-start | bytes 786440 | tf_op jit(solution)/shard_map/P_G1/ppermute | solution.py:400

commit v7 on v6

--- a/solution.py
+++ b/solution.py
@@ -21,7 +21,7 @@
 NEAR = 8
 FAR = 4
 VMEM_LIMIT = 60 << 20
-SCOPED = 14 << 20
+SCOPED = 10 << 20
 
 ANY = pl.BlockSpec(memory_space=pl.ANY)
 SMEM = pl.BlockSpec(memory_space=pltpu.SMEM)
@@ -251,7 +251,8 @@
 
 def apply_kernel(table, *refs):
     held, (za_ref, zb_ref, u_ref, v_ref) = refs[:2], refs[2:6]
-    outs, (token, x_buf, fx_buf, sem_x, sem_fx) = refs[6:10], refs[10:]
+    outs, (token, x_buf, fx_buf, sem_x, sem_fx) = refs[6:11], refs[11:]
+    turns = ((0, outs[0], 0, 4), (1, outs[1], 0, 4), (2, outs[2], 0, 2), (2, outs[3], 2, 4), (3, outs[4], 0, 4))
     near, far = table[N_NEAR], table[N_FAR]
     slots = za_ref.shape[0]
 
@@ -272,11 +273,12 @@
         for half in range(2):
             rows = CLUSTER // 2
             place = table[ORDER + cluster * 2 + half]
-            for steps, out_ref in enumerate(outs):
-
-                @pl.when(place // 4 == steps)
+            second = lax.rem(place, 4)
+            for steps, out_ref, low, high in turns:
+
+                @pl.when((place // 4 == steps) & (second >= low) & (second < high))
                 def _():
-                    out_ref[lax.rem(place, 4)] += term[half * rows : (half + 1) * rows]
+                    out_ref[second - low] += term[half * rows : (half + 1) * rows]
 
     fetch(table[NEAR_A], x_buf.at[0], sem_x.at[0])
 
@@ -318,8 +320,8 @@
         apply_kernel,
         name=f"apply_{index}",
         in_specs=[SMEM] + [ANY] * 2 + [VMEM] * 4,
-        out_specs=[VMEM] * 5,
-        out_shape=[jax.ShapeDtypeStruct((4, CLUSTER // 2, WIDE), jnp.float32)] * 4 + [TOKEN],
+        out_specs=[VMEM] * 6,
+        out_shape=[jax.ShapeDtypeStruct((n, CLUSTER // 2, WIDE), jnp.float32) for n in (4, 4, 2, 2, 4)] + [TOKEN],
         scratch_shapes=[
             pltpu.VMEM((2, CLUSTER, WIDE), jnp.float32),
             pltpu.VMEM((FAR, CLUSTER, WIDE), jnp.float32),
@@ -329,6 +331,29 @@
         compiler_params=pltpu.CompilerParams(vmem_limit_bytes=SCOPED),
         cost_estimate=pl.CostEstimate(flops=COST[index], bytes_accessed=1, transcendentals=0),
     )(table, *held, *blocks)
+
+
+def finish_kernel(*refs):
+    parts, tokens, out_ref = refs[:8], refs[8:10], refs[10]
+    for chunk in range(CHUNKS):
+        own, *came = parts[chunk * 4 : chunk * 4 + 4]
+        total = own[...] + came[0][...] + came[1][...] + came[2][...] + tokens[chunk][0, 0]
+        for part in range(2):
+            first = part * CHUNKS * HALF + chunk * HALF
+            out_ref[:, first : first + HALF] = total[:, part * HALF : (part + 1) * HALF]
+
+
+def finish(parts, tokens):
+    rows = parts[0].shape[0]
+    return pl.pallas_call(
+        finish_kernel,
+        name="finish",
+        in_specs=[VMEM] * 10,
+        out_specs=VMEM,
+        out_shape=jax.ShapeDtypeStruct((rows, CHUNKS * WIDE), jnp.float32),
+        compiler_params=pltpu.CompilerParams(vmem_limit_bytes=SCOPED),
+        cost_estimate=pl.CostEstimate(flops=1 << 20, bytes_accessed=3 << 20, transcendentals=0),
+    )(*parts, *tokens)
 
 
 def scalars(near_pairs, far_pairs, far_ranks, block_counts):
@@ -392,21 +417,32 @@
     blocks = (blocks_a, blocks_b, blocks_u, blocks_v)
 
 
-    def to_owner(mine, away, zero, index):
-        with jax.named_scope(f"P_F{index}"):
-            came = [lax.ppermute(part, AXES, turn) for part, turn in zip(away, first_turn)]
-        mine, *away = [mine[k] + came[0][k] + came[1][k] + came[2][k] for k in range(4)]
-        with jax.named_scope(f"P_G{index}"):
-            came = [lax.ppermute(part, AXES, turn) for part, turn in zip(away, second_turn)]
-        return mine + (came[0] + zero) + came[1] + came[2]
-
-    mine, *away, done_0 = apply_blocks(table, held_0, blocks, 0)
-    *parts_1, done_0 = lax.optimization_barrier((own_1, left_1, across_1, right_1, done_0))
-    results = [to_owner(mine, away, done_0[0, 0], 0)]
-    mine, *away, done_1 = apply_blocks(table, both_cores(parts_1, 1), blocks, 1)
-    results.append(to_owner(mine, away, done_1[0, 0], 1))
-    parts = [r[:, :HALF] for r in results] + [r[:, HALF:] for r in results]
-    return jnp.concatenate(parts, axis=1)
+    def go(part, turn, name):
+        with jax.named_scope(name):
+            return lax.ppermute(part, AXES, turn)
+
+    def first_step(upper, lower, index):
+        return go(upper, first_turn[0], f"P_H{index}"), go(lower, first_turn[2], f"P_H{index}")
+
+    def second_step(ahead, behind, came, index):
+        ahead, behind = ahead.at[:2].add(came[0]), behind.at[2:].add(came[1])
+        return go(ahead, first_turn[0], f"P_F{index}"), go(behind, first_turn[2], f"P_F{index}")
+
+    def other_ring(mine, came, index):
+        mine, *away = [mine[k] + came[0][k] + came[1][k] for k in range(4)]
+        return mine, [go(part, turn, f"P_G{index}") for part, turn in zip(away, second_turn)]
+
+    mine, ahead, upper_0, lower_0, behind, done_0 = apply_blocks(table, held_0, blocks, 0)
+    came_0 = first_step(upper_0, lower_0, 0)
+    *parts_1, came_u, came_l, done_0 = lax.optimization_barrier((own_1, left_1, across_1, right_1, *came_0, done_0))
+    came_0 = came_u, came_l
+    came_0 = second_step(ahead, behind, came_0, 0)
+    mine_1, ahead, upper_1, lower_1, behind, done_1 = apply_blocks(table, both_cores(parts_1, 1), blocks, 1)
+    upper_1, lower_1, *came_0 = lax.optimization_barrier((upper_1, lower_1, *came_0))
+    first = other_ring(mine, came_0, 0)
+    came_1 = second_step(ahead, behind, first_step(upper_1, lower_1, 1), 1)
+    last = other_ring(mine_1, came_1, 1)
+    return finish([first[0], *first[1], last[0], *last[1]], [done_0, done_1])
 
 
 def solution(mesh):

time: 141 us -> 138 us (0.979)
  Pallas kernels: 38.7 us -> 19.5 us
  waiting for transfers between devices: 54.1 us -> 72.9 us
  other arithmetic: 4.9 us -> 3.03 us
  starting transfers between devices: 39 us -> 40.8 us
    pallas_call x2, Pallas kernels: 22.8 us -> 8.94 us  [apply_blocks(): pl.pallas_call(apply_kernel, name=f'apply_{index}', in_specs=[SMEM] + [AN...]
    ppermute x12 -> x14, waiting for transfers between devices: 32 us -> 39.2 us  [go(): return lax.ppermute(part, AXES, turn)]
    pallas_call x2, Pallas kernels: 10.5 us -> 4.1 us  [prepare_near(): pl.pallas_call(functools.partial(prepare_near_kernel, first), name=f'prep...]
    ppermute x3, waiting for transfers between devices: 0.83 us -> 6.22 us  [across_dir(): return lax.ppermute(part, 'dir', swap)]
    ppermute x9, waiting for transfers between devices: 20.4 us -> 25.7 us  [step(): return lax.ppermute(part, 'x', [(i, (i + k) % 4) for i in range(4)])]
    ppermute x12 -> x14, starting transfers between devices: 23.5 us -> 27.1 us  [go(): return lax.ppermute(part, AXES, turn)]
    ppermute x9, starting transfers between devices: 11.4 us -> 9.1 us  [step(): return lax.ppermute(part, 'x', [(i, (i + k) % 4) for i in range(4)])]
    add x4 -> x2, other arithmetic: 1.95 us -> 0.41 us  [other_ring(): mine, *away = [mine[k] + came[0][k] + came[1][k] for k in range(4)]]
  transfers between devices with their start and end apart: 26 -> 28, of which waited for: 14 -> 19; matrix products, arithmetic and copies ran while one was open for 4% -> 3% of each run, Pallas kernels for 25% -> 11%
where the time goes in v7:
time: 138 us
  waiting for transfers between devices  72.9 us (53%)
  starting transfers between devices  40.8 us (30%)
  Pallas kernels  19.5 us (14%)
  other arithmetic  3.03 us (2%)
  local copies, waits for them, and re-layouts  1.66 us (1%)
    ppermute x14, waiting for transfers between devices, go(): return lax.ppermute(part, AXES, turn)  39.2 us
    ppermute x14, starting transfers between devices, go(): return lax.ppermute(part, AXES, turn)  27.1 us
    ppermute x9, waiting for transfers between devices, step(): return lax.ppermute(part, 'x', [(i, (i + k) % 4) for i in range(4)])  25.7 us
    ppermute x9, starting transfers between devices, step(): return lax.ppermute(part, 'x', [(i, (i + k) % 4) for i in range(4)])  9.1 us
    pallas_call x2, Pallas kernels, apply_blocks(): pl.pallas_call(apply_kernel, name=f'apply_{index}', in_specs=[SMEM] + [AN...  8.94 us
    ppermute x3, waiting for transfers between devices, across_dir(): return lax.ppermute(part, 'dir', swap)  6.22 us
    ppermute x3, starting transfers between devices, across_dir(): return lax.ppermute(part, 'dir', swap)  4.39 us
    pallas_call x2, Pallas kernels, prepare_near(): pl.pallas_call(functools.partial(prepare_near_kernel, first), name=f'prep...  4.1 us
  transfers between devices with their start and end apart: 28, of which 19 were waited for; matrix products, arithmetic and copies ran while one was open for 3% of the time, Pallas kernels for 11%

profile of v7, /device:TPU:0, one launch (start us, length us, event | category | flops | bytes accessed | tf_op | source)
XLA Modules:
  0.0 138.0 jit_solution(15193970677033513305)
XLA Ops:
  0.0 3.0 %rhs.5 = (f32[512,256]{1,0:T(8,128)S(1)}, f32[512,256]{1,0:T(8,128)S(1)}) custom-call(bf16[1024,512]{1,0:T(8,128)(2,1)} %cot_ref.1, bf16[2,512,1024]{2,1,0:T(8,128)(2,1)} %rad_ref.1), custom_call_target="tpu_custom_call" | custom-call | flops 1073741824 | bytes 4194304 | tf_op jit(solution)/shard_map/rhs/pallas_call | solution.py:90
  3.1 2.1 %collective-permute-start = (f32[256,256]{1,0:T(8,128)S(1)}, f32[256,256]{1,0:T(8,128)S(1)}, u32[]{:S(2)}, u32[]{:S(2)}) collective-permute-start(f32[256,256]{1,0:T(8,128)S(1)} %slice.199), channel_id=1, source_target_pairs={{0,64},{64,0},{1,65},{65,1},{2,66},{66,2},{3,67},{67,3},{4,68},{68... | collective-permute-start | bytes 786440 | tf_op jit(solution)/shard_map/P_ZU/ppermute | solution.py:389
  5.3 3.5 %prepare_near_0.1 = (bf16[4,512,2048]{2,1,0:T(8,128)(2,1)S(1)}, f32[8,128]{1,0:T(8,128)S(1)}) custom-call(s32[48]{0:T(128)S(1)} %concatenate.11.table, f32[2,8,512,512]{3,2,1,0:T(8,128)} %z_ref.3), custom_call_target="tpu_custom_call" | custom-call | flops 268435456 | bytes 8388608 | tf_op jit(solution)/shard_map/prepare_near_0/pallas_call | solution.py:139
  8.9 0.5 slice.200
  9.4 2.1 %collective-permute-done = f32[256,256]{1,0:T(8,128)S(1)} collective-permute-done((f32[256,256]{1,0:T(8,128)S(1)}, f32[256,256]{1,0:T(8,128)S(1)}, u32[]{:S(2)}, u32[]{:S(2)}) %collective-permute-start) | collective-permute-done | bytes 262176 | tf_op jit(solution)/shard_map/P_ZU/ppermute | solution.py:389
  11.5 0.7 fusion.11
  12.2 1.8 %collective-permute-start.1 = (f32[256,256]{1,0:T(8,128)S(1)}, f32[256,256]{1,0:T(8,128)S(1)}, u32[]{:S(2)}, u32[]{:S(2)}) collective-permute-start(f32[256,256]{1,0:T(8,128)S(1)} %get-tuple-element.98), channel_id=1, source_target_pairs={{0,64},{64,0},{1,65},{65,1},{2,66},{66,2},{3,67},{67,3},{4,68},{68... | collective-permute-start | bytes 786440 | tf_op jit(solution)/shard_map/P_ZL/ppermute | solution.py:389
  14.0 2.8 %collective-permute-start.3 = (f32[256,256]{1,0:T(8,128)S(1)}, f32[256,256]{1,0:T(8,128)S(1)}, u32[]{:S(2)}, u32[]{:S(2)}) collective-permute-start(f32[256,256]{1,0:T(8,128)S(1)} %get-tuple-element.96.refs_0_), channel_id=1, source_target_pairs={{0,6},{2,0},{4,2},{6,4},{1,7},{3,1},{5,3},{7,5},{8,14},{10,8},{12,... | collective-permute-start | bytes 786440 | tf_op jit(solution)/shard_map/P_RU/ppermute | solution.py:393
  16.8 0.6 prepare_near_4.1
  17.3 0.5 slice.202
  17.9 1.9 %collective-permute-done.1 = f32[256,256]{1,0:T(8,128)S(1)} collective-permute-done((f32[256,256]{1,0:T(8,128)S(1)}, f32[256,256]{1,0:T(8,128)S(1)}, u32[]{:S(2)}, u32[]{:S(2)}) %collective-permute-start.1) | collective-permute-done | bytes 262176 | tf_op jit(solution)/shard_map/P_ZL/ppermute | solution.py:389
  19.7 0.7 add_add_fusion.1.refs_1_
  20.4 0.8 collective-permute-done.3.refs_6_
  21.2 3.4 %collective-permute-done.2.refs_2_ = f32[256,256]{1,0:T(8,128)S(1)} collective-permute-done((f32[256,256]{1,0:T(8,128)S(1)}, f32[256,256]{1,0:T(8,128)S(1)}, u32[]{:S(2)}, u32[]{:S(2)}) %collective-permute-start.2) | collective-permute-done | bytes 262176 | tf_op jit(solution)/shard_map/P_LU/ppermute | solution.py:393
  25.3 2.0 %prepare_far.1 = (bf16[4,128,2048]{2,1,0:T(8,128)(2,1)S(1)}, bf16[4,512,512]{2,1,0:T(8,128)(2,1)S(1)}, f32[8,128]{1,0:T(8,128)S(1)}) custom-call(s32[48]{0:T(128)S(1)} %concatenate.11.table, f32[2,4,96,512]{3,2,1,0:T(8,128)} %u_ref.1, f32[2,4,96,512]{3,2,1,0:T(8,128)} %v_ref.1), custom_call_target="tpu_custom_call" | custom-call | flops 268435456 | bytes 4194304 | tf_op jit(solution)/shard_map/prepare_far/pallas_call | solution.py:192
  27.3 0.5 slice.203
  27.9 2.5 %collective-permute-start.4 = (f32[256,256]{1,0:T(8,128)S(1)}, f32[256,256]{1,0:T(8,128)S(1)}, u32[]{:S(2)}, u32[]{:S(2)}) collective-permute-start(f32[256,256]{1,0:T(8,128)S(1)} %add_add_fusion.1.refs_1_), channel_id=1, source_target_pairs={{0,2},{2,4},{4,6},{6,0},{1,3},{3,5},{5,7},{7,1},{8,10},{10,12},{12... | collective-permute-start | bytes 786440 | tf_op jit(solution)/shard_map/P_LL/ppermute | solution.py:393
  30.4 2.1 %collective-permute-done.7.refs_7_ = f32[256,256]{1,0:T(8,128)S(1)} collective-permute-done((f32[256,256]{1,0:T(8,128)S(1)}, f32[256,256]{1,0:T(8,128)S(1)}, u32[]{:S(2)}, u32[]{:S(2)}) %collective-permute-start.7) | collective-permute-done | bytes 262176 | tf_op jit(solution)/shard_map/P_RL/ppermute | solution.py:393
  32.5 1.1 collective-permute-start.8
  33.6 2.3 %collective-permute-done.5 = f32[512,256]{1,0:T(8,128)S(1)} collective-permute-done((f32[512,256]{1,0:T(8,128)S(1)}, f32[512,256]{1,0:T(8,128)S(1)}, u32[]{:S(2)}, u32[]{:S(2)}) %collective-permute-start.5) | collective-permute-done | bytes 524320 | tf_op jit(solution)/shard_map/P_Z1/ppermute | solution.py:389
  35.9 0.7 add_add_fusion.refs_0_
  36.6 3.7 %collective-permute-done.6.refs_4_ = f32[256,256]{1,0:T(8,128)S(1)} collective-permute-done((f32[256,256]{1,0:T(8,128)S(1)}, f32[256,256]{1,0:T(8,128)S(1)}, u32[]{:S(2)}, u32[]{:S(2)}) %collective-permute-start.6) | collective-permute-done | bytes 262176 | tf_op jit(solution)/shard_map/P_A0/ppermute | solution.py:393
  40.6 1.0 collective-permute-start.12
  41.6 1.4 %collective-permute-start.11 = (f32[512,256]{1,0:T(8,128)S(1)}, f32[512,256]{1,0:T(8,128)S(1)}, u32[]{:S(2)}, u32[]{:S(2)}) collective-permute-start(f32[512,256]{1,0:T(8,128)S(1)} %add_add_fusion.refs_0_), channel_id=1, source_target_pairs={{0,4},{2,6},{4,0},{6,2},{1,5},{3,7},{5,1},{7,3},{8,12},{10,14},{12... | collective-permute-start | bytes 1572872 | tf_op jit(solution)/shard_map/P_K1/ppermute | solution.py:393
  43.0 1.8 %collective-permute-done.9.refs_1_ = f32[2048,256]{1,0:T(8,128)S(1)} collective-permute-done((f32[2048,256]{1,0:T(8,128)S(1)}, f32[2048,256]{1,0:T(8,128)S(1)}, u32[]{:S(2)}, u32[]{:S(2)}) %collective-permute-start.9) | collective-permute-done | bytes 2097184 | tf_op jit(solution)/shard_map/P_S0/ppermute | solution.py:398
  44.8 4.5 %apply_0.1 = (f32[4,256,256]{2,1,0:T(8,128)S(1)}, f32[4,256,256]{2,1,0:T(8,128)S(1)}, f32[2,256,256]{2,1,0:T(8,128)S(1)}, f32[2,256,256]{2,1,0:T(8,128)S(1)}, f3...) custom-call(s32[48]{0:T(128)S(1)} %concatenate.11.table, f32[2048,256]{1,0:T(8,128)S(1)} %pack_0.1.refs_0_, ...), custom_call_target="tpu_custom_call" | custom-call | flops 42949672960 | bytes 1 | tf_op jit(solution)/shard_map/apply_0/pallas_call | solution.py:319
  49.3 1.7 %collective-permute-start.13 = (f32[2,256,256]{2,1,0:T(8,128)S(1)}, f32[2,256,256]{2,1,0:T(8,128)S(1)}, u32[]{:S(2)}, u32[]{:S(2)}) collective-permute-start(f32[2,256,256]{2,1,0:T(8,128)S(1)} %get-tuple-element.113), channel_id=1, source_target_pairs={{0,16},{1,65},{2,18},{3,67},{4,20},{5,69},{6,22},{7,71},{8,24},{9,... | collective-permute-start | bytes 1572872 | tf_op jit(solution)/shard_map/P_H0/ppermute | solution.py:422
  50.9 1.7 %collective-permute-start.14 = (f32[2,256,256]{2,1,0:T(8,128)S(1)}, f32[2,256,256]{2,1,0:T(8,128)S(1)}, u32[]{:S(2)}, u32[]{:S(2)}) collective-permute-start(f32[2,256,256]{2,1,0:T(8,128)S(1)} %get-tuple-element.114), channel_id=1, source_target_pairs={{0,48},{1,73},{2,50},{3,75},{4,52},{5,77},{6,54},{7,79},{8,56},{9,... | collective-permute-start | bytes 1572872 | tf_op jit(solution)/shard_map/P_H0/ppermute | solution.py:422
  52.6 2.9 %collective-permute-done.12.refs_3_ = f32[512,256]{1,0:T(8,128)S(1)} collective-permute-done((f32[512,256]{1,0:T(8,128)S(1)}, f32[512,256]{1,0:T(8,128)S(1)}, u32[]{:S(2)}, u32[]{:S(2)}) %collective-permute-start.12) | collective-permute-done | bytes 524320 | tf_op jit(solution)/shard_map/P_R1/ppermute | solution.py:393
  55.4 2.5 %collective-permute-done.11.refs_2_ = f32[512,256]{1,0:T(8,128)S(1)} collective-permute-done((f32[512,256]{1,0:T(8,128)S(1)}, f32[512,256]{1,0:T(8,128)S(1)}, u32[]{:S(2)}, u32[]{:S(2)}) %collective-permute-start.11) | collective-permute-done | bytes 524320 | tf_op jit(solution)/shard_map/P_K1/ppermute | solution.py:393
  57.9 10.4 %collective-permute-done.10.refs_1_ = f32[512,256]{1,0:T(8,128)S(1)} collective-permute-done((f32[512,256]{1,0:T(8,128)S(1)}, f32[512,256]{1,0:T(8,128)S(1)}, u32[]{:S(2)}, u32[]{:S(2)}) %collective-permute-start.10) | collective-permute-done | bytes 524320 | tf_op jit(solution)/shard_map/P_L1/ppermute | solution.py:393
  68.8 3.7 %collective-permute-start.16 = (f32[4,256,256]{2,1,0:T(8,128)S(1)}, f32[4,256,256]{2,1,0:T(8,128)S(1)}, u32[]{:S(2)}, u32[]{:S(2)}) collective-permute-start(f32[4,256,256]{2,1,0:T(8,128)S(1)} %add_dynamic-update-slice_fusion.3), channel_id=1, source_target_pairs={{0,16},{1,65},{2,18},{3,67},{4,20},{5,69},{6,22},{7,71},{8,24},{9,... | collective-permute-start | bytes 3145736 | tf_op jit(solution)/shard_map/P_F0/ppermute | solution.py:422
  72.6 2.0 %collective-permute-start.17 = (f32[4,256,256]{2,1,0:T(8,128)S(1)}, f32[4,256,256]{2,1,0:T(8,128)S(1)}, u32[]{:S(2)}, u32[]{:S(2)}) collective-permute-start(f32[4,256,256]{2,1,0:T(8,128)S(1)} %add_dynamic-update-slice_fusion.2), channel_id=1, source_target_pairs={{0,48},{1,73},{2,50},{3,75},{4,52},{5,77},{6,54},{7,79},{8,56},{9,... | collective-permute-start | bytes 3145736 | tf_op jit(solution)/shard_map/P_F0/ppermute | solution.py:422
  74.6 4.5 %apply_1.1 = (f32[4,256,256]{2,1,0:T(8,128)S(1)}, f32[4,256,256]{2,1,0:T(8,128)S(1)}, f32[2,256,256]{2,1,0:T(8,128)S(1)}, f32[2,256,256]{2,1,0:T(8,128)S(1)}, f3...) custom-call(s32[48]{0:T(128)S(1)} %concatenate.11.table, f32[2048,256]{1,0:T(8,128)S(1)} %pack_1.1.refs_0_, ...), custom_call_target="tpu_custom_call" | custom-call | flops 42949672960 | bytes 1 | tf_op jit(solution)/shard_map/apply_1/pallas_call | solution.py:319
  79.1 8.1 %collective-permute-done.16 = f32[4,256,256]{2,1,0:T(8,128)S(1)} collective-permute-done((f32[4,256,256]{2,1,0:T(8,128)S(1)}, f32[4,256,256]{2,1,0:T(8,128)S(1)}, u32[]{:S(2)}, u32[]{:S(2)}) %collective-permute-start.16) | collective-permute-done | bytes 1048608 | tf_op jit(solution)/shard_map/P_F0/ppermute | solution.py:422
  87.5 3.1 %collective-permute-start.23 = (f32[2,256,256]{2,1,0:T(8,128)S(1)}, f32[2,256,256]{2,1,0:T(8,128)S(1)}, u32[]{:S(2)}, u32[]{:S(2)}) collective-permute-start(f32[2,256,256]{2,1,0:T(8,128)S(1)} %get-tuple-element.132), channel_id=1, source_target_pairs={{0,48},{1,73},{2,50},{3,75},{4,52},{5,77},{6,54},{7,79},{8,56},{9,... | collective-permute-start | bytes 1572872 | tf_op jit(solution)/shard_map/P_H1/ppermute | solution.py:422
  90.6 6.7 %collective-permute-done.23 = f32[2,256,256]{2,1,0:T(8,128)S(1)} collective-permute-done((f32[2,256,256]{2,1,0:T(8,128)S(1)}, f32[2,256,256]{2,1,0:T(8,128)S(1)}, u32[]{:S(2)}, u32[]{:S(2)}) %collective-permute-start.23) | collective-permute-done | bytes 524320 | tf_op jit(solution)/shard_map/P_H1/ppermute | solution.py:422
  97.5 3.8 %collective-permute-start.24 = (f32[4,256,256]{2,1,0:T(8,128)S(1)}, f32[4,256,256]{2,1,0:T(8,128)S(1)}, u32[]{:S(2)}, u32[]{:S(2)}) collective-permute-start(f32[4,256,256]{2,1,0:T(8,128)S(1)} %add_dynamic-update-slice_fusion), channel_id=1, source_target_pairs={{0,48},{1,73},{2,50},{3,75},{4,52},{5,77},{6,54},{7,79},{8,56},{9,... | collective-permute-start | bytes 3145736 | tf_op jit(solution)/shard_map/P_F1/ppermute | solution.py:422
  101.7 3.1 %collective-permute-start.20 = (f32[256,256]{1,0:T(8,128)S(1)}, f32[256,256]{1,0:T(8,128)S(1)}, u32[]{:S(2)}, u32[]{:S(2)}) collective-permute-start(f32[256,256]{1,0:T(8,128)S(1)} %get-tuple-element.139), channel_id=1, source_target_pairs={{0,72},{1,49},{2,74},{3,51},{4,76},{5,53},{6,78},{7,55},{8,64},{9,... | collective-permute-start | bytes 786440 | tf_op jit(solution)/shard_map/P_G0/ppermute | solution.py:422
  104.8 3.1 %collective-permute-start.19 = (f32[256,256]{1,0:T(8,128)S(1)}, f32[256,256]{1,0:T(8,128)S(1)}, u32[]{:S(2)}, u32[]{:S(2)}) collective-permute-start(f32[256,256]{1,0:T(8,128)S(1)} %get-tuple-element.140), channel_id=1, source_target_pairs={{0,8},{1,33},{2,10},{3,35},{4,12},{5,37},{6,14},{7,39},{8,0},{9,41... | collective-permute-start | bytes 786440 | tf_op jit(solution)/shard_map/P_G0/ppermute | solution.py:422
  107.9 11.3 %collective-permute-done.24 = f32[4,256,256]{2,1,0:T(8,128)S(1)} collective-permute-done((f32[4,256,256]{2,1,0:T(8,128)S(1)}, f32[4,256,256]{2,1,0:T(8,128)S(1)}, u32[]{:S(2)}, u32[]{:S(2)}) %collective-permute-start.24) | collective-permute-done | bytes 1048608 | tf_op jit(solution)/shard_map/P_F1/ppermute | solution.py:422
  119.2 3.9 %collective-permute-done.22 = f32[4,256,256]{2,1,0:T(8,128)S(1)} collective-permute-done((f32[4,256,256]{2,1,0:T(8,128)S(1)}, f32[4,256,256]{2,1,0:T(8,128)S(1)}, u32[]{:S(2)}, u32[]{:S(2)}) %collective-permute-start.22) | collective-permute-done | bytes 1048608 | tf_op jit(solution)/shard_map/P_F1/ppermute | solution.py:422
  123.3 3.1 %collective-permute-start.27 = (f32[256,256]{1,0:T(8,128)S(1)}, f32[256,256]{1,0:T(8,128)S(1)}, u32[]{:S(2)}, u32[]{:S(2)}) collective-permute-start(f32[256,256]{1,0:T(8,128)S(1)} %get-tuple-element.135), channel_id=1, source_target_pairs={{0,72},{1,49},{2,74},{3,51},{4,76},{5,53},{6,78},{7,55},{8,64},{9,... | collective-permute-start | bytes 786440 | tf_op jit(solution)/shard_map/P_G1/ppermute | solution.py:422
  126.4 1.7 %collective-permute-start.26 = (f32[256,256]{1,0:T(8,128)S(1)}, f32[256,256]{1,0:T(8,128)S(1)}, u32[]{:S(2)}, u32[]{:S(2)}) collective-permute-start(f32[256,256]{1,0:T(8,128)S(1)} %get-tuple-element.136), channel_id=1, source_target_pairs={{0,8},{1,33},{2,10},{3,35},{4,12},{5,37},{6,14},{7,39},{8,0},{9,41... | collective-permute-start | bytes 786440 | tf_op jit(solution)/shard_map/P_G1/ppermute | solution.py:422
  128.1 5.0 %collective-permute-done.27.refs_7_ = f32[256,256]{1,0:T(8,128)S(1)} collective-permute-done((f32[256,256]{1,0:T(8,128)S(1)}, f32[256,256]{1,0:T(8,128)S(1)}, u32[]{:S(2)}, u32[]{:S(2)}) %collective-permute-start.27) | collective-permute-done | bytes 262176 | tf_op jit(solution)/shard_map/P_G1/ppermute | solution.py:422
  133.1 1.2 collective-permute-done.26.refs_6_
  134.3 2.7 %collective-permute-done.25.refs_5_ = f32[256,256]{1,0:T(8,128)S(1)} collective-permute-done((f32[256,256]{1,0:T(8,128)S(1)}, f32[256,256]{1,0:T(8,128)S(1)}, u32[]{:S(2)}, u32[]{:S(2)}) %collective-permute-start.25) | collective-permute-done | bytes 262176 | tf_op jit(solution)/shard_map/P_G1/ppermute | solution.py:422
  137.1 1.0 finish.1
  (42 shorter events, 2.9 us)
Async XLA Ops:
  0.0 5.2 %copy-start = (s32[8,2]{0,1:T(2,128)S(1)}, s32[8,2]{0,1:T(2,128)}, u32[]{:S(2)}) copy-start(s32[8,2]{0,1:T(2,128)} %param.20) | copy-start | bytes 196
  0.0 5.2 %copy-start.1 = (s32[4,2]{0,1:T(2,128)S(1)}, s32[4,2]{0,1:T(2,128)}, u32[]{:S(2)}) copy-start(s32[4,2]{0,1:T(2,128)} %param.23) | copy-start | bytes 100
  0.0 5.2 %copy-start.2 = (s32[1,2]{1,0:T(1,128)S(1)}, s32[1,2]{1,0:T(1,128)}, u32[]{:S(2)}) copy-start(s32[1,2]{1,0:T(1,128)} %param.25) | copy-start | bytes 28
  0.0 5.2 %copy-start.3 = (s32[4]{0:T(128)S(1)}, s32[4]{0:T(128)}, u32[]{:S(2)}) copy-start(s32[4]{0:T(128)} %param.24) | copy-start | bytes 52
  3.1 8.4 %collective-permute-start = (f32[256,256]{1,0:T(8,128)S(1)}, f32[256,256]{1,0:T(8,128)S(1)}, u32[]{:S(2)}, u32[]{:S(2)}) collective-permute-start(f32[256,256]{1,0:T(8,128)S(1)} %slice.199), channel_id=1, source_target_pairs={{0,64},{64,0},{1,65},{65,1},{2,66},{66,2},{3,67},{67,3},{4,68},{68... | collective-permute-start | bytes 786440 | tf_op jit(solution)/shard_map/P_ZU/ppermute | solution.py:389
  12.2 7.6 %collective-permute-start.1 = (f32[256,256]{1,0:T(8,128)S(1)}, f32[256,256]{1,0:T(8,128)S(1)}, u32[]{:S(2)}, u32[]{:S(2)}) collective-permute-start(f32[256,256]{1,0:T(8,128)S(1)} %get-tuple-element.98), channel_id=1, source_target_pairs={{0,64},{64,0},{1,65},{65,1},{2,66},{66,2},{3,67},{67,3},{4,68},{68... | collective-permute-start | bytes 786440 | tf_op jit(solution)/shard_map/P_ZL/ppermute | solution.py:389
  14.0 7.2 %collective-permute-start.3 = (f32[256,256]{1,0:T(8,128)S(1)}, f32[256,256]{1,0:T(8,128)S(1)}, u32[]{:S(2)}, u32[]{:S(2)}) collective-permute-start(f32[256,256]{1,0:T(8,128)S(1)} %get-tuple-element.96.refs_0_), channel_id=1, source_target_pairs={{0,6},{2,0},{4,2},{6,4},{1,7},{3,1},{5,3},{7,5},{8,14},{10,8},{12,... | collective-permute-start | bytes 786440 | tf_op jit(solution)/shard_map/P_RU/ppermute | solution.py:393
  16.8 7.8 %collective-permute-start.2 = (f32[256,256]{1,0:T(8,128)S(1)}, f32[256,256]{1,0:T(8,128)S(1)}, u32[]{:S(2)}, u32[]{:S(2)}) collective-permute-start(f32[256,256]{1,0:T(8,128)S(1)} %get-tuple-element.96.refs_0_), channel_id=1, source_target_pairs={{0,2},{2,4},{4,6},{6,0},{1,3},{3,5},{5,7},{7,1},{8,10},{10,12},{12... | collective-permute-start | bytes 786440 | tf_op jit(solution)/shard_map/P_LU/ppermute | solution.py:393
  24.6 11.3 %collective-permute-start.5 = (f32[512,256]{1,0:T(8,128)S(1)}, f32[512,256]{1,0:T(8,128)S(1)}, u32[]{:S(2)}, u32[]{:S(2)}) collective-permute-start(f32[512,256]{1,0:T(8,128)S(1)} %get-tuple-element.102), channel_id=1, source_target_pairs={{0,64},{64,0},{1,65},{65,1},{2,66},{66,2},{3,67},{67,3},{4,68},{68... | collective-permute-start | bytes 1572872 | tf_op jit(solution)/shard_map/P_Z1/ppermute | solution.py:389
  25.1 7.5 %collective-permute-start.7 = (f32[256,256]{1,0:T(8,128)S(1)}, f32[256,256]{1,0:T(8,128)S(1)}, u32[]{:S(2)}, u32[]{:S(2)}) collective-permute-start(f32[256,256]{1,0:T(8,128)S(1)} %add_add_fusion.1.refs_1_), channel_id=1, source_target_pairs={{0,6},{2,0},{4,2},{6,4},{1,7},{3,1},{5,3},{7,5},{8,14},{10,8},{12,... | collective-permute-start | bytes 786440 | tf_op jit(solution)/shard_map/P_RL/ppermute | solution.py:393
  27.9 12.4 %collective-permute-start.4 = (f32[256,256]{1,0:T(8,128)S(1)}, f32[256,256]{1,0:T(8,128)S(1)}, u32[]{:S(2)}, u32[]{:S(2)}) collective-permute-start(f32[256,256]{1,0:T(8,128)S(1)} %add_add_fusion.1.refs_1_), channel_id=1, source_target_pairs={{0,2},{2,4},{4,6},{6,0},{1,3},{3,5},{5,7},{7,1},{8,10},{10,12},{12... | collective-permute-start | bytes 786440 | tf_op jit(solution)/shard_map/P_LL/ppermute | solution.py:393
  30.4 9.9 %collective-permute-start.6 = (f32[256,256]{1,0:T(8,128)S(1)}, f32[256,256]{1,0:T(8,128)S(1)}, u32[]{:S(2)}, u32[]{:S(2)}) collective-permute-start(f32[256,256]{1,0:T(8,128)S(1)} %collective-permute-done.2.refs_2_), channel_id=1, source_target_pairs={{0,2},{2,4},{4,6},{6,0},{1,3},{3,5},{5,7},{7,1},{8,10},{10,12},{12... | collective-permute-start | bytes 786440 | tf_op jit(solution)/shard_map/P_A0/ppermute | solution.py:393
  32.5 7.8 %collective-permute-start.8 = (f32[256,256]{1,0:T(8,128)S(1)}, f32[256,256]{1,0:T(8,128)S(1)}, u32[]{:S(2)}, u32[]{:S(2)}) collective-permute-start(f32[256,256]{1,0:T(8,128)S(1)} %collective-permute-done.7.refs_7_), channel_id=1, source_target_pairs={{0,6},{2,0},{4,2},{6,4},{1,7},{3,1},{5,3},{7,5},{8,14},{10,8},{12,... | collective-permute-start | bytes 786440 | tf_op jit(solution)/shard_map/P_B0/ppermute | solution.py:393
  40.5 4.2 %collective-permute-start.9 = (f32[2048,256]{1,0:T(8,128)S(1)}, f32[2048,256]{1,0:T(8,128)S(1)}, u32[]{:S(2)}, u32[]{:S(2)}) collective-permute-start(f32[2048,256]{1,0:T(8,128)S(1)} %pack_0.1.refs_0_), channel_id=1, source_target_pairs={{0,1},{1,0},{2,3},{3,2},{4,5},{5,4},{6,7},{7,6},{8,9},{9,8},{10,11... | collective-permute-start | bytes 6291464 | tf_op jit(solution)/shard_map/P_S0/ppermute | solution.py:398
  40.6 14.8 %collective-permute-start.12 = (f32[512,256]{1,0:T(8,128)S(1)}, f32[512,256]{1,0:T(8,128)S(1)}, u32[]{:S(2)}, u32[]{:S(2)}) collective-permute-start(f32[512,256]{1,0:T(8,128)S(1)} %add_add_fusion.refs_0_), channel_id=1, source_target_pairs={{0,6},{2,0},{4,2},{6,4},{1,7},{3,1},{5,3},{7,5},{8,14},{10,8},{12,... | collective-permute-start | bytes 1572872 | tf_op jit(solution)/shard_map/P_R1/ppermute | solution.py:393
  41.6 16.3 %collective-permute-start.11 = (f32[512,256]{1,0:T(8,128)S(1)}, f32[512,256]{1,0:T(8,128)S(1)}, u32[]{:S(2)}, u32[]{:S(2)}) collective-permute-start(f32[512,256]{1,0:T(8,128)S(1)} %add_add_fusion.refs_0_), channel_id=1, source_target_pairs={{0,4},{2,6},{4,0},{6,2},{1,5},{3,7},{5,1},{7,3},{8,12},{10,14},{12... | collective-permute-start | bytes 1572872 | tf_op jit(solution)/shard_map/P_K1/ppermute | solution.py:393
  43.0 25.3 %collective-permute-start.10 = (f32[512,256]{1,0:T(8,128)S(1)}, f32[512,256]{1,0:T(8,128)S(1)}, u32[]{:S(2)}, u32[]{:S(2)}) collective-permute-start(f32[512,256]{1,0:T(8,128)S(1)} %add_add_fusion.refs_0_), channel_id=1, source_target_pairs={{0,2},{2,4},{4,6},{6,0},{1,3},{3,5},{5,7},{7,1},{8,10},{10,12},{12... | collective-permute-start | bytes 1572872 | tf_op jit(solution)/shard_map/P_L1/ppermute | solution.py:393
  49.3 19.1 %collective-permute-start.13 = (f32[2,256,256]{2,1,0:T(8,128)S(1)}, f32[2,256,256]{2,1,0:T(8,128)S(1)}, u32[]{:S(2)}, u32[]{:S(2)}) collective-permute-start(f32[2,256,256]{2,1,0:T(8,128)S(1)} %get-tuple-element.113), channel_id=1, source_target_pairs={{0,16},{1,65},{2,18},{3,67},{4,20},{5,69},{6,22},{7,71},{8,24},{9,... | collective-permute-start | bytes 1572872 | tf_op jit(solution)/shard_map/P_H0/ppermute | solution.py:422
  50.9 17.4 %collective-permute-start.14 = (f32[2,256,256]{2,1,0:T(8,128)S(1)}, f32[2,256,256]{2,1,0:T(8,128)S(1)}, u32[]{:S(2)}, u32[]{:S(2)}) collective-permute-start(f32[2,256,256]{2,1,0:T(8,128)S(1)} %get-tuple-element.114), channel_id=1, source_target_pairs={{0,48},{1,73},{2,50},{3,75},{4,52},{5,77},{6,54},{7,79},{8,56},{9,... | collective-permute-start | bytes 1572872 | tf_op jit(solution)/shard_map/P_H0/ppermute | solution.py:422
  68.5 6.1 %collective-permute-start.15 = (f32[2048,256]{1,0:T(8,128)S(1)}, f32[2048,256]{1,0:T(8,128)S(1)}, u32[]{:S(2)}, u32[]{:S(2)}) collective-permute-start(f32[2048,256]{1,0:T(8,128)S(1)} %pack_1.1.refs_0_), channel_id=1, source_target_pairs={{0,1},{1,0},{2,3},{3,2},{4,5},{5,4},{6,7},{7,6},{8,9},{9,8},{10,11... | collective-permute-start | bytes 6291464 | tf_op jit(solution)/shard_map/P_S1/ppermute | solution.py:398
  68.8 18.4 %collective-permute-start.16 = (f32[4,256,256]{2,1,0:T(8,128)S(1)}, f32[4,256,256]{2,1,0:T(8,128)S(1)}, u32[]{:S(2)}, u32[]{:S(2)}) collective-permute-start(f32[4,256,256]{2,1,0:T(8,128)S(1)} %add_dynamic-update-slice_fusion.3), channel_id=1, source_target_pairs={{0,16},{1,65},{2,18},{3,67},{4,20},{5,69},{6,22},{7,71},{8,24},{9,... | collective-permute-start | bytes 3145736 | tf_op jit(solution)/shard_map/P_F0/ppermute | solution.py:422
  72.6 14.9 %collective-permute-start.17 = (f32[4,256,256]{2,1,0:T(8,128)S(1)}, f32[4,256,256]{2,1,0:T(8,128)S(1)}, u32[]{:S(2)}, u32[]{:S(2)}) collective-permute-start(f32[4,256,256]{2,1,0:T(8,128)S(1)} %add_dynamic-update-slice_fusion.2), channel_id=1, source_target_pairs={{0,48},{1,73},{2,50},{3,75},{4,52},{5,77},{6,54},{7,79},{8,56},{9,... | collective-permute-start | bytes 3145736 | tf_op jit(solution)/shard_map/P_F0/ppermute | solution.py:422
  87.5 9.8 %collective-permute-start.23 = (f32[2,256,256]{2,1,0:T(8,128)S(1)}, f32[2,256,256]{2,1,0:T(8,128)S(1)}, u32[]{:S(2)}, u32[]{:S(2)}) collective-permute-start(f32[2,256,256]{2,1,0:T(8,128)S(1)} %get-tuple-element.132), channel_id=1, source_target_pairs={{0,48},{1,73},{2,50},{3,75},{4,52},{5,77},{6,54},{7,79},{8,56},{9,... | collective-permute-start | bytes 1572872 | tf_op jit(solution)/shard_map/P_H1/ppermute | solution.py:422
  90.6 10.6 %collective-permute-start.21 = (f32[2,256,256]{2,1,0:T(8,128)S(1)}, f32[2,256,256]{2,1,0:T(8,128)S(1)}, u32[]{:S(2)}, u32[]{:S(2)}) collective-permute-start(f32[2,256,256]{2,1,0:T(8,128)S(1)} %get-tuple-element.130), channel_id=1, source_target_pairs={{0,16},{1,65},{2,18},{3,67},{4,20},{5,69},{6,22},{7,71},{8,24},{9,... | collective-permute-start | bytes 1572872 | tf_op jit(solution)/shard_map/P_H1/ppermute | solution.py:422
  97.5 21.7 %collective-permute-start.24 = (f32[4,256,256]{2,1,0:T(8,128)S(1)}, f32[4,256,256]{2,1,0:T(8,128)S(1)}, u32[]{:S(2)}, u32[]{:S(2)}) collective-permute-start(f32[4,256,256]{2,1,0:T(8,128)S(1)} %add_dynamic-update-slice_fusion), channel_id=1, source_target_pairs={{0,48},{1,73},{2,50},{3,75},{4,52},{5,77},{6,54},{7,79},{8,56},{9,... | collective-permute-start | bytes 3145736 | tf_op jit(solution)/shard_map/P_F1/ppermute | solution.py:422
  101.4 21.7 %collective-permute-start.22 = (f32[4,256,256]{2,1,0:T(8,128)S(1)}, f32[4,256,256]{2,1,0:T(8,128)S(1)}, u32[]{:S(2)}, u32[]{:S(2)}) collective-permute-start(f32[4,256,256]{2,1,0:T(8,128)S(1)} %add_dynamic-update-slice_fusion.1), channel_id=1, source_target_pairs={{0,16},{1,65},{2,18},{3,67},{4,20},{5,69},{6,22},{7,71},{8,24},{9,... | collective-permute-start | bytes 3145736 | tf_op jit(solution)/shard_map/P_F1/ppermute | solution.py:422
  101.7 26.5 %collective-permute-start.20 = (f32[256,256]{1,0:T(8,128)S(1)}, f32[256,256]{1,0:T(8,128)S(1)}, u32[]{:S(2)}, u32[]{:S(2)}) collective-permute-start(f32[256,256]{1,0:T(8,128)S(1)} %get-tuple-element.139), channel_id=1, source_target_pairs={{0,72},{1,49},{2,74},{3,51},{4,76},{5,53},{6,78},{7,55},{8,64},{9,... | collective-permute-start | bytes 786440 | tf_op jit(solution)/shard_map/P_G0/ppermute | solution.py:422
  104.8 23.4 %collective-permute-start.19 = (f32[256,256]{1,0:T(8,128)S(1)}, f32[256,256]{1,0:T(8,128)S(1)}, u32[]{:S(2)}, u32[]{:S(2)}) collective-permute-start(f32[256,256]{1,0:T(8,128)S(1)} %get-tuple-element.140), channel_id=1, source_target_pairs={{0,8},{1,33},{2,10},{3,35},{4,12},{5,37},{6,14},{7,39},{8,0},{9,41... | collective-permute-start | bytes 786440 | tf_op jit(solution)/shard_map/P_G0/ppermute | solution.py:422
  107.9 20.3 %collective-permute-start.18 = (f32[256,256]{1,0:T(8,128)S(1)}, f32[256,256]{1,0:T(8,128)S(1)}, u32[]{:S(2)}, u32[]{:S(2)}) collective-permute-start(f32[256,256]{1,0:T(8,128)S(1)} %get-tuple-element.141), channel_id=1, source_target_pairs={{0,64},{1,17},{2,66},{3,19},{4,68},{5,21},{6,70},{7,23},{8,72},{9,... | collective-permute-start | bytes 786440 | tf_op jit(solution)/shard_map/P_G0/ppermute | solution.py:422
  123.3 9.8 %collective-permute-start.27 = (f32[256,256]{1,0:T(8,128)S(1)}, f32[256,256]{1,0:T(8,128)S(1)}, u32[]{:S(2)}, u32[]{:S(2)}) collective-permute-start(f32[256,256]{1,0:T(8,128)S(1)} %get-tuple-element.135), channel_id=1, source_target_pairs={{0,72},{1,49},{2,74},{3,51},{4,76},{5,53},{6,78},{7,55},{8,64},{9,... | collective-permute-start | bytes 786440 | tf_op jit(solution)/shard_map/P_G1/ppermute | solution.py:422
  126.4 8.0 %collective-permute-start.26 = (f32[256,256]{1,0:T(8,128)S(1)}, f32[256,256]{1,0:T(8,128)S(1)}, u32[]{:S(2)}, u32[]{:S(2)}) collective-permute-start(f32[256,256]{1,0:T(8,128)S(1)} %get-tuple-element.136), channel_id=1, source_target_pairs={{0,8},{1,33},{2,10},{3,35},{4,12},{5,37},{6,14},{7,39},{8,0},{9,41... | collective-permute-start | bytes 786440 | tf_op jit(solution)/shard_map/P_G1/ppermute | solution.py:422
  128.1 8.9 %collective-permute-start.25 = (f32[256,256]{1,0:T(8,128)S(1)}, f32[256,256]{1,0:T(8,128)S(1)}, u32[]{:S(2)}, u32[]{:S(2)}) collective-permute-start(f32[256,256]{1,0:T(8,128)S(1)} %get-tuple-element.137), channel_id=1, source_target_pairs={{0,64},{1,17},{2,66},{3,19},{4,68},{5,21},{6,70},{7,23},{8,72},{9,... | collective-permute-start | bytes 786440 | tf_op jit(solution)/shard_map/P_G1/ppermute | solution.py:422

commit v8 on v7

--- a/solution.py
+++ b/solution.py
@@ -280,7 +280,25 @@
                 def _():
                     out_ref[second - low] += term[half * rows : (half + 1) * rows]
 
-    fetch(table[NEAR_A], x_buf.at[0], sem_x.at[0])
+    def fetch_near(s):
+        @pl.when(s < near)
+        def _():
+            b = lax.rem(s, 4)
+            fetch(table[NEAR_A + jnp.minimum(s, NEAR - 1)], x_buf.at[b], sem_x.at[b])
+
+    def near_term(z_ref, first, s):
+        b = lax.rem(s, 4)
+        return product(z_ref[s - first], x_buf[b])
+
+    def near_ready(s):
+        b = lax.rem(s, 4)
+        fetched(x_buf.at[b], sem_x.at[b])
+
+    def far_term(s):
+        return product(v_ref[s], product(u_ref[s], fx_buf[s]))
+
+    fetch_near(0)
+    fetch_near(1)
 
     def far_start(s, _):
         fetch(table[FAR_A + s], fx_buf.at[s], sem_fx.at[s])
@@ -290,29 +308,53 @@
     for out_ref in (*outs, token):
         out_ref[...] = jnp.zeros_like(out_ref)
 
-    def near_steps(z_ref, first, last):
-        def near_step(s, _):
-            b = lax.rem(s, 2)
-
-            @pl.when(s + 1 < near)
-            def _():
-                fetch(table[NEAR_A + s + 1], x_buf.at[1 - b], sem_x.at[1 - b])
-
-            fetched(x_buf.at[b], sem_x.at[b])
-            add(table[NEAR_B + s], product(z_ref[s - first], x_buf[b]))
+    def both_step(s, _):
+        fetch_near(s + 2)
+        near_ready(s)
+        fetched(fx_buf.at[s], sem_fx.at[s])
+        near_part, far_part = near_term(za_ref, 0, s), far_term(s)
+        add(table[NEAR_B + s], near_part)
+        add(table[FAR_B + s], far_part)
+        return 0
+
+    def near_step(z_ref, first):
+        def step(s, _):
+            fetch_near(s + 2)
+            near_ready(s)
+            add(table[NEAR_B + s], near_term(z_ref, first, s))
             return 0
 
-        lax.fori_loop(first, last, near_step, 0)
-
-    near_steps(za_ref, 0, jnp.minimum(near, slots))
-    near_steps(zb_ref, slots, near)
+        return step
+
+    def near_steps(z_ref, first, start, stop):
+        pairs = lax.div(stop - start, 2)
+
+        def two_steps(i, _):
+            s = start + 2 * i
+            fetch_near(s + 2)
+            fetch_near(s + 3)
+            near_ready(s)
+            near_ready(s + 1)
+            terms = near_term(z_ref, first, s), near_term(z_ref, first, s + 1)
+            add(table[NEAR_B + s], terms[0])
+            add(table[NEAR_B + s + 1], terms[1])
+            return 0
+
+        lax.fori_loop(0, pairs, two_steps, 0)
+        lax.fori_loop(start + 2 * pairs, stop, near_step(z_ref, first), 0)
+
+    together = jnp.minimum(near, far)
+    lax.fori_loop(0, together, both_step, 0)
+    first_stop = jnp.minimum(near, slots)
+    near_steps(za_ref, 0, together, first_stop)
+    near_steps(zb_ref, slots, first_stop, near)
 
     def far_step(s, _):
         fetched(fx_buf.at[s], sem_fx.at[s])
-        add(table[FAR_B + s], product(v_ref[s], product(u_ref[s], fx_buf[s])))
+        add(table[FAR_B + s], far_term(s))
         return 0
 
-    lax.fori_loop(0, far, far_step, 0)
+    lax.fori_loop(together, far, far_step, 0)
 
 
 def apply_blocks(table, held, blocks, index):
@@ -323,9 +365,9 @@
         out_specs=[VMEM] * 6,
         out_shape=[jax.ShapeDtypeStruct((n, CLUSTER // 2, WIDE), jnp.float32) for n in (4, 4, 2, 2, 4)] + [TOKEN],
         scratch_shapes=[
-            pltpu.VMEM((2, CLUSTER, WIDE), jnp.float32),
+            pltpu.VMEM((4, CLUSTER, WIDE), jnp.float32),
             pltpu.VMEM((FAR, CLUSTER, WIDE), jnp.float32),
-            pltpu.SemaphoreType.DMA((2,)),
+            pltpu.SemaphoreType.DMA((4,)),
             pltpu.SemaphoreType.DMA((FAR,)),
         ],
         compiler_params=pltpu.CompilerParams(vmem_limit_bytes=SCOPED),

time: 138 us -> 137 us (level)
  Pallas kernels: 19.5 us -> 38.6 us
  waiting for transfers between devices: 72.9 us -> 57.8 us
  starting transfers between devices: 40.8 us -> 35.9 us
    pallas_call x2, Pallas kernels: 8.94 us -> 21.6 us  [apply_blocks(): pl.pallas_call(apply_kernel, name=f'apply_{index}', in_specs=[SMEM] + [AN...]
    ppermute x9, waiting for transfers between devices: 25.7 us -> 19.1 us  [step(): return lax.ppermute(part, 'x', [(i, (i + k) % 4) for i in range(4)])]
    pallas_call x2, Pallas kernels: 4.1 us -> 10.5 us  [prepare_near(): pl.pallas_call(functools.partial(prepare_near_kernel, first), name=f'prep...]
    ppermute x14, waiting for transfers between devices: 39.2 us -> 34.3 us  [go(): return lax.ppermute(part, AXES, turn)]
    ppermute x14, starting transfers between devices: 27.1 us -> 22.3 us  [go(): return lax.ppermute(part, AXES, turn)]
    ppermute x3, waiting for transfers between devices: 6.22 us -> 1.91 us  [across_dir(): return lax.ppermute(part, 'dir', swap)]
  transfers between devices with their start and end apart: 28 -> 28, of which waited for: 19 -> 16; matrix products, arithmetic and copies ran while one was open for 3% -> 3% of each run, Pallas kernels for 11% -> 25%
where the time goes in v8:
time: 137 us
  waiting for transfers between devices  57.8 us (42%)
  Pallas kernels  38.6 us (28%)
  starting transfers between devices  35.9 us (26%)
  other arithmetic  3.03 us (2%)
  local copies, waits for them, and re-layouts  1.66 us (1%)
    ppermute x14, waiting for transfers between devices, go(): return lax.ppermute(part, AXES, turn)  34.3 us
    ppermute x14, starting transfers between devices, go(): return lax.ppermute(part, AXES, turn)  22.3 us
    pallas_call x2, Pallas kernels, apply_blocks(): pl.pallas_call(apply_kernel, name=f'apply_{index}', in_specs=[SMEM] + [AN...  21.6 us
    ppermute x9, waiting for transfers between devices, step(): return lax.ppermute(part, 'x', [(i, (i + k) % 4) for i in range(4)])  19.1 us
    pallas_call x2, Pallas kernels, prepare_near(): pl.pallas_call(functools.partial(prepare_near_kernel, first), name=f'prep...  10.5 us
    ppermute x9, starting transfers between devices, step(): return lax.ppermute(part, 'x', [(i, (i + k) % 4) for i in range(4)])  8.99 us
    ppermute x3, starting transfers between devices, across_dir(): return lax.ppermute(part, 'dir', swap)  4.42 us
    pallas_call x1, Pallas kernels, partial_rhs(): pl.pallas_call(rhs_kernel, name='rhs', in_specs=[HBM, HBM], out_specs=[VM...  3.04 us
  transfers between devices with their start and end apart: 28, of which 16 were waited for; matrix products, arithmetic and copies ran while one was open for 3% of the time, Pallas kernels for 25%

profile of v8, /device:TPU:0, one launch (start us, length us, event | category | flops | bytes accessed | tf_op | source)
XLA Modules:
  0.0 137.3 jit_solution(1418795968594360174)
XLA Ops:
  0.0 3.0 %rhs.5 = (f32[512,256]{1,0:T(8,128)S(1)}, f32[512,256]{1,0:T(8,128)S(1)}) custom-call(bf16[1024,512]{1,0:T(8,128)(2,1)} %cot_ref.1, bf16[2,512,1024]{2,1,0:T(8,128)(2,1)} %rad_ref.1), custom_call_target="tpu_custom_call" | custom-call | flops 1073741824 | bytes 4194304 | tf_op jit(solution)/shard_map/rhs/pallas_call | solution.py:90
  3.1 2.1 %collective-permute-start = (f32[256,256]{1,0:T(8,128)S(1)}, f32[256,256]{1,0:T(8,128)S(1)}, u32[]{:S(2)}, u32[]{:S(2)}) collective-permute-start(f32[256,256]{1,0:T(8,128)S(1)} %slice.199), channel_id=1, source_target_pairs={{0,64},{64,0},{1,65},{65,1},{2,66},{66,2},{3,67},{67,3},{4,68},{68... | collective-permute-start | bytes 786440 | tf_op jit(solution)/shard_map/P_ZU/ppermute | solution.py:431
  5.3 5.3 %prepare_near_0.1 = (bf16[4,512,2048]{2,1,0:T(8,128)(2,1)S(1)}, f32[8,128]{1,0:T(8,128)S(1)}) custom-call(s32[48]{0:T(128)S(1)} %concatenate.11.table, f32[2,8,512,512]{3,2,1,0:T(8,128)} %z_ref.3), custom_call_target="tpu_custom_call" | custom-call | flops 268435456 | bytes 8388608 | tf_op jit(solution)/shard_map/prepare_near_0/pallas_call | solution.py:139
  10.6 0.5 slice.200
  11.1 0.4 collective-permute-done
  11.5 0.7 fusion.11
  12.2 1.8 %collective-permute-start.1 = (f32[256,256]{1,0:T(8,128)S(1)}, f32[256,256]{1,0:T(8,128)S(1)}, u32[]{:S(2)}, u32[]{:S(2)}) collective-permute-start(f32[256,256]{1,0:T(8,128)S(1)} %get-tuple-element.98), channel_id=1, source_target_pairs={{0,64},{64,0},{1,65},{65,1},{2,66},{66,2},{3,67},{67,3},{4,68},{68... | collective-permute-start | bytes 786440 | tf_op jit(solution)/shard_map/P_ZL/ppermute | solution.py:431
  14.0 2.8 %collective-permute-start.3 = (f32[256,256]{1,0:T(8,128)S(1)}, f32[256,256]{1,0:T(8,128)S(1)}, u32[]{:S(2)}, u32[]{:S(2)}) collective-permute-start(f32[256,256]{1,0:T(8,128)S(1)} %get-tuple-element.96.refs_0_), channel_id=1, source_target_pairs={{0,6},{2,0},{4,2},{6,4},{1,7},{3,1},{5,3},{7,5},{8,14},{10,8},{12,... | collective-permute-start | bytes 786440 | tf_op jit(solution)/shard_map/P_RU/ppermute | solution.py:435
  16.8 5.3 %prepare_near_4.1 = (bf16[4,512,2048]{2,1,0:T(8,128)(2,1)S(1)}, f32[8,128]{1,0:T(8,128)S(1)}) custom-call(s32[48]{0:T(128)S(1)} %concatenate.11.table, f32[2,8,512,512]{3,2,1,0:T(8,128)} %z_ref.3), custom_call_target="tpu_custom_call" | custom-call | flops 268435456 | bytes 8388608 | tf_op jit(solution)/shard_map/prepare_near_4/pallas_call | solution.py:139
  22.0 0.5 slice.202
  22.5 0.7 add_add_fusion.1.refs_1_
  23.2 1.3 collective-permute-done.2.refs_2_
  24.6 0.5 collective-permute-start.5
  25.1 1.5 %collective-permute-start.7 = (f32[256,256]{1,0:T(8,128)S(1)}, f32[256,256]{1,0:T(8,128)S(1)}, u32[]{:S(2)}, u32[]{:S(2)}) collective-permute-start(f32[256,256]{1,0:T(8,128)S(1)} %add_add_fusion.1.refs_1_), channel_id=1, source_target_pairs={{0,6},{2,0},{4,2},{6,4},{1,7},{3,1},{5,3},{7,5},{8,14},{10,8},{12,... | collective-permute-start | bytes 786440 | tf_op jit(solution)/shard_map/P_RL/ppermute | solution.py:435
  26.6 2.0 %prepare_far.1 = (bf16[4,128,2048]{2,1,0:T(8,128)(2,1)S(1)}, bf16[4,512,512]{2,1,0:T(8,128)(2,1)S(1)}, f32[8,128]{1,0:T(8,128)S(1)}) custom-call(s32[48]{0:T(128)S(1)} %concatenate.11.table, f32[2,4,96,512]{3,2,1,0:T(8,128)} %u_ref.1, f32[2,4,96,512]{3,2,1,0:T(8,128)} %v_ref.1), custom_call_target="tpu_custom_call" | custom-call | flops 268435456 | bytes 4194304 | tf_op jit(solution)/shard_map/prepare_far/pallas_call | solution.py:192
  28.6 0.5 slice.203
  29.2 0.5 collective-permute-start.4
  29.7 2.6 %collective-permute-done.7.refs_7_ = f32[256,256]{1,0:T(8,128)S(1)} collective-permute-done((f32[256,256]{1,0:T(8,128)S(1)}, f32[256,256]{1,0:T(8,128)S(1)}, u32[]{:S(2)}, u32[]{:S(2)}) %collective-permute-start.7) | collective-permute-done | bytes 262176 | tf_op jit(solution)/shard_map/P_RL/ppermute | solution.py:435
  32.3 2.1 %collective-permute-start.8 = (f32[256,256]{1,0:T(8,128)S(1)}, f32[256,256]{1,0:T(8,128)S(1)}, u32[]{:S(2)}, u32[]{:S(2)}) collective-permute-start(f32[256,256]{1,0:T(8,128)S(1)} %collective-permute-done.7.refs_7_), channel_id=1, source_target_pairs={{0,6},{2,0},{4,2},{6,4},{1,7},{3,1},{5,3},{7,5},{8,14},{10,8},{12,... | collective-permute-start | bytes 786440 | tf_op jit(solution)/shard_map/P_B0/ppermute | solution.py:435
  34.3 1.5 %collective-permute-done.5 = f32[512,256]{1,0:T(8,128)S(1)} collective-permute-done((f32[512,256]{1,0:T(8,128)S(1)}, f32[512,256]{1,0:T(8,128)S(1)}, u32[]{:S(2)}, u32[]{:S(2)}) %collective-permute-start.5) | collective-permute-done | bytes 524320 | tf_op jit(solution)/shard_map/P_Z1/ppermute | solution.py:431
  35.9 0.7 add_add_fusion.refs_0_
  36.6 6.4 %collective-permute-done.6.refs_4_ = f32[256,256]{1,0:T(8,128)S(1)} collective-permute-done((f32[256,256]{1,0:T(8,128)S(1)}, f32[256,256]{1,0:T(8,128)S(1)}, u32[]{:S(2)}, u32[]{:S(2)}) %collective-permute-start.6) | collective-permute-done | bytes 262176 | tf_op jit(solution)/shard_map/P_A0/ppermute | solution.py:435
  43.4 1.1 collective-permute-start.11
  44.5 0.9 collective-permute-start.10
  45.4 2.0 %collective-permute-done.9.refs_1_ = f32[2048,256]{1,0:T(8,128)S(1)} collective-permute-done((f32[2048,256]{1,0:T(8,128)S(1)}, f32[2048,256]{1,0:T(8,128)S(1)}, u32[]{:S(2)}, u32[]{:S(2)}) %collective-permute-start.9) | collective-permute-done | bytes 2097184 | tf_op jit(solution)/shard_map/P_S0/ppermute | solution.py:440
  47.5 10.8 %apply_0.1 = (f32[4,256,256]{2,1,0:T(8,128)S(1)}, f32[4,256,256]{2,1,0:T(8,128)S(1)}, f32[2,256,256]{2,1,0:T(8,128)S(1)}, f32[2,256,256]{2,1,0:T(8,128)S(1)}, f3...) custom-call(s32[48]{0:T(128)S(1)} %concatenate.11.table, f32[2048,256]{1,0:T(8,128)S(1)} %pack_0.1.refs_0_, ...), custom_call_target="tpu_custom_call" | custom-call | flops 42949672960 | bytes 1 | tf_op jit(solution)/shard_map/apply_0/pallas_call | solution.py:361
  58.4 3.2 %collective-permute-start.14 = (f32[2,256,256]{2,1,0:T(8,128)S(1)}, f32[2,256,256]{2,1,0:T(8,128)S(1)}, u32[]{:S(2)}, u32[]{:S(2)}) collective-permute-start(f32[2,256,256]{2,1,0:T(8,128)S(1)} %get-tuple-element.114), channel_id=1, source_target_pairs={{0,48},{1,73},{2,50},{3,75},{4,52},{5,77},{6,54},{7,79},{8,56},{9,... | collective-permute-start | bytes 1572872 | tf_op jit(solution)/shard_map/P_H0/ppermute | solution.py:464
  61.6 8.8 %collective-permute-done.10.refs_1_ = f32[512,256]{1,0:T(8,128)S(1)} collective-permute-done((f32[512,256]{1,0:T(8,128)S(1)}, f32[512,256]{1,0:T(8,128)S(1)}, u32[]{:S(2)}, u32[]{:S(2)}) %collective-permute-start.10) | collective-permute-done | bytes 524320 | tf_op jit(solution)/shard_map/P_L1/ppermute | solution.py:435
  70.9 1.4 %collective-permute-start.16 = (f32[4,256,256]{2,1,0:T(8,128)S(1)}, f32[4,256,256]{2,1,0:T(8,128)S(1)}, u32[]{:S(2)}, u32[]{:S(2)}) collective-permute-start(f32[4,256,256]{2,1,0:T(8,128)S(1)} %add_dynamic-update-slice_fusion.3), channel_id=1, source_target_pairs={{0,16},{1,65},{2,18},{3,67},{4,20},{5,69},{6,22},{7,71},{8,24},{9,... | collective-permute-start | bytes 3145736 | tf_op jit(solution)/shard_map/P_F0/ppermute | solution.py:464
  72.5 1.9 %collective-permute-start.17 = (f32[4,256,256]{2,1,0:T(8,128)S(1)}, f32[4,256,256]{2,1,0:T(8,128)S(1)}, u32[]{:S(2)}, u32[]{:S(2)}) collective-permute-start(f32[4,256,256]{2,1,0:T(8,128)S(1)} %add_dynamic-update-slice_fusion.2), channel_id=1, source_target_pairs={{0,48},{1,73},{2,50},{3,75},{4,52},{5,77},{6,54},{7,79},{8,56},{9,... | collective-permute-start | bytes 3145736 | tf_op jit(solution)/shard_map/P_F0/ppermute | solution.py:464
  74.4 0.4 collective-permute-done.15.refs_1_
  74.8 10.8 %apply_1.1 = (f32[4,256,256]{2,1,0:T(8,128)S(1)}, f32[4,256,256]{2,1,0:T(8,128)S(1)}, f32[2,256,256]{2,1,0:T(8,128)S(1)}, f32[2,256,256]{2,1,0:T(8,128)S(1)}, f3...) custom-call(s32[48]{0:T(128)S(1)} %concatenate.11.table, f32[2048,256]{1,0:T(8,128)S(1)} %pack_1.1.refs_0_, ...), custom_call_target="tpu_custom_call" | custom-call | flops 42949672960 | bytes 1 | tf_op jit(solution)/shard_map/apply_1/pallas_call | solution.py:361
  85.7 1.3 collective-permute-done.16
  87.0 0.3 collective-permute-done.17
  87.3 3.1 %collective-permute-start.23 = (f32[2,256,256]{2,1,0:T(8,128)S(1)}, f32[2,256,256]{2,1,0:T(8,128)S(1)}, u32[]{:S(2)}, u32[]{:S(2)}) collective-permute-start(f32[2,256,256]{2,1,0:T(8,128)S(1)} %get-tuple-element.132), channel_id=1, source_target_pairs={{0,48},{1,73},{2,50},{3,75},{4,52},{5,77},{6,54},{7,79},{8,56},{9,... | collective-permute-start | bytes 1572872 | tf_op jit(solution)/shard_map/P_H1/ppermute | solution.py:464
  90.4 6.7 %collective-permute-done.23 = f32[2,256,256]{2,1,0:T(8,128)S(1)} collective-permute-done((f32[2,256,256]{2,1,0:T(8,128)S(1)}, f32[2,256,256]{2,1,0:T(8,128)S(1)}, u32[]{:S(2)}, u32[]{:S(2)}) %collective-permute-start.23) | collective-permute-done | bytes 524320 | tf_op jit(solution)/shard_map/P_H1/ppermute | solution.py:464
  97.2 3.8 %collective-permute-start.24 = (f32[4,256,256]{2,1,0:T(8,128)S(1)}, f32[4,256,256]{2,1,0:T(8,128)S(1)}, u32[]{:S(2)}, u32[]{:S(2)}) collective-permute-start(f32[4,256,256]{2,1,0:T(8,128)S(1)} %add_dynamic-update-slice_fusion), channel_id=1, source_target_pairs={{0,48},{1,73},{2,50},{3,75},{4,52},{5,77},{6,54},{7,79},{8,56},{9,... | collective-permute-start | bytes 3145736 | tf_op jit(solution)/shard_map/P_F1/ppermute | solution.py:464
  101.4 2.8 %collective-permute-start.20 = (f32[256,256]{1,0:T(8,128)S(1)}, f32[256,256]{1,0:T(8,128)S(1)}, u32[]{:S(2)}, u32[]{:S(2)}) collective-permute-start(f32[256,256]{1,0:T(8,128)S(1)} %get-tuple-element.139), channel_id=1, source_target_pairs={{0,72},{1,49},{2,74},{3,51},{4,76},{5,53},{6,78},{7,55},{8,64},{9,... | collective-permute-start | bytes 786440 | tf_op jit(solution)/shard_map/P_G0/ppermute | solution.py:464
  104.3 0.8 collective-permute-start.19
  105.1 1.2 collective-permute-start.18
  106.3 12.7 %collective-permute-done.24 = f32[4,256,256]{2,1,0:T(8,128)S(1)} collective-permute-done((f32[4,256,256]{2,1,0:T(8,128)S(1)}, f32[4,256,256]{2,1,0:T(8,128)S(1)}, u32[]{:S(2)}, u32[]{:S(2)}) %collective-permute-start.24) | collective-permute-done | bytes 1048608 | tf_op jit(solution)/shard_map/P_F1/ppermute | solution.py:464
  118.9 3.9 %collective-permute-done.22 = f32[4,256,256]{2,1,0:T(8,128)S(1)} collective-permute-done((f32[4,256,256]{2,1,0:T(8,128)S(1)}, f32[4,256,256]{2,1,0:T(8,128)S(1)}, u32[]{:S(2)}, u32[]{:S(2)}) %collective-permute-start.22) | collective-permute-done | bytes 1048608 | tf_op jit(solution)/shard_map/P_F1/ppermute | solution.py:464
  123.0 2.8 %collective-permute-start.27 = (f32[256,256]{1,0:T(8,128)S(1)}, f32[256,256]{1,0:T(8,128)S(1)}, u32[]{:S(2)}, u32[]{:S(2)}) collective-permute-start(f32[256,256]{1,0:T(8,128)S(1)} %get-tuple-element.135), channel_id=1, source_target_pairs={{0,72},{1,49},{2,74},{3,51},{4,76},{5,53},{6,78},{7,55},{8,64},{9,... | collective-permute-start | bytes 786440 | tf_op jit(solution)/shard_map/P_G1/ppermute | solution.py:464
  125.9 0.9 collective-permute-start.25
  126.8 5.8 %collective-permute-done.27.refs_7_ = f32[256,256]{1,0:T(8,128)S(1)} collective-permute-done((f32[256,256]{1,0:T(8,128)S(1)}, f32[256,256]{1,0:T(8,128)S(1)}, u32[]{:S(2)}, u32[]{:S(2)}) %collective-permute-start.27) | collective-permute-done | bytes 262176 | tf_op jit(solution)/shard_map/P_G1/ppermute | solution.py:464
  132.6 1.3 collective-permute-done.26.refs_6_
  133.9 2.4 %collective-permute-done.25.refs_5_ = f32[256,256]{1,0:T(8,128)S(1)} collective-permute-done((f32[256,256]{1,0:T(8,128)S(1)}, f32[256,256]{1,0:T(8,128)S(1)}, u32[]{:S(2)}, u32[]{:S(2)}) %collective-permute-start.25) | collective-permute-done | bytes 262176 | tf_op jit(solution)/shard_map/P_G1/ppermute | solution.py:464
  136.3 1.0 finish.1
  (42 shorter events, 2.0 us)
Async XLA Ops:
  0.0 5.2 %copy-start = (s32[8,2]{0,1:T(2,128)S(1)}, s32[8,2]{0,1:T(2,128)}, u32[]{:S(2)}) copy-start(s32[8,2]{0,1:T(2,128)} %param.20) | copy-start | bytes 196
  0.0 5.2 %copy-start.1 = (s32[4,2]{0,1:T(2,128)S(1)}, s32[4,2]{0,1:T(2,128)}, u32[]{:S(2)}) copy-start(s32[4,2]{0,1:T(2,128)} %param.23) | copy-start | bytes 100
  0.0 5.2 %copy-start.2 = (s32[1,2]{1,0:T(1,128)S(1)}, s32[1,2]{1,0:T(1,128)}, u32[]{:S(2)}) copy-start(s32[1,2]{1,0:T(1,128)} %param.25) | copy-start | bytes 28
  0.0 5.2 %copy-start.3 = (s32[4]{0:T(128)S(1)}, s32[4]{0:T(128)}, u32[]{:S(2)}) copy-start(s32[4]{0:T(128)} %param.24) | copy-start | bytes 52
  3.1 8.4 %collective-permute-start = (f32[256,256]{1,0:T(8,128)S(1)}, f32[256,256]{1,0:T(8,128)S(1)}, u32[]{:S(2)}, u32[]{:S(2)}) collective-permute-start(f32[256,256]{1,0:T(8,128)S(1)} %slice.199), channel_id=1, source_target_pairs={{0,64},{64,0},{1,65},{65,1},{2,66},{66,2},{3,67},{67,3},{4,68},{68... | collective-permute-start | bytes 786440 | tf_op jit(solution)/shard_map/P_ZU/ppermute | solution.py:431
  12.2 10.4 %collective-permute-start.1 = (f32[256,256]{1,0:T(8,128)S(1)}, f32[256,256]{1,0:T(8,128)S(1)}, u32[]{:S(2)}, u32[]{:S(2)}) collective-permute-start(f32[256,256]{1,0:T(8,128)S(1)} %get-tuple-element.98), channel_id=1, source_target_pairs={{0,64},{64,0},{1,65},{65,1},{2,66},{66,2},{3,67},{67,3},{4,68},{68... | collective-permute-start | bytes 786440 | tf_op jit(solution)/shard_map/P_ZL/ppermute | solution.py:431
  14.0 9.2 %collective-permute-start.3 = (f32[256,256]{1,0:T(8,128)S(1)}, f32[256,256]{1,0:T(8,128)S(1)}, u32[]{:S(2)}, u32[]{:S(2)}) collective-permute-start(f32[256,256]{1,0:T(8,128)S(1)} %get-tuple-element.96.refs_0_), channel_id=1, source_target_pairs={{0,6},{2,0},{4,2},{6,4},{1,7},{3,1},{5,3},{7,5},{8,14},{10,8},{12,... | collective-permute-start | bytes 786440 | tf_op jit(solution)/shard_map/P_RU/ppermute | solution.py:435
  16.8 7.8 %collective-permute-start.2 = (f32[256,256]{1,0:T(8,128)S(1)}, f32[256,256]{1,0:T(8,128)S(1)}, u32[]{:S(2)}, u32[]{:S(2)}) collective-permute-start(f32[256,256]{1,0:T(8,128)S(1)} %get-tuple-element.96.refs_0_), channel_id=1, source_target_pairs={{0,2},{2,4},{4,6},{6,0},{1,3},{3,5},{5,7},{7,1},{8,10},{10,12},{12... | collective-permute-start | bytes 786440 | tf_op jit(solution)/shard_map/P_LU/ppermute | solution.py:435
  24.6 11.3 %collective-permute-start.5 = (f32[512,256]{1,0:T(8,128)S(1)}, f32[512,256]{1,0:T(8,128)S(1)}, u32[]{:S(2)}, u32[]{:S(2)}) collective-permute-start(f32[512,256]{1,0:T(8,128)S(1)} %get-tuple-element.102), channel_id=1, source_target_pairs={{0,64},{64,0},{1,65},{65,1},{2,66},{66,2},{3,67},{67,3},{4,68},{68... | collective-permute-start | bytes 1572872 | tf_op jit(solution)/shard_map/P_Z1/ppermute | solution.py:431
  25.1 7.2 %collective-permute-start.7 = (f32[256,256]{1,0:T(8,128)S(1)}, f32[256,256]{1,0:T(8,128)S(1)}, u32[]{:S(2)}, u32[]{:S(2)}) collective-permute-start(f32[256,256]{1,0:T(8,128)S(1)} %add_add_fusion.1.refs_1_), channel_id=1, source_target_pairs={{0,6},{2,0},{4,2},{6,4},{1,7},{3,1},{5,3},{7,5},{8,14},{10,8},{12,... | collective-permute-start | bytes 786440 | tf_op jit(solution)/shard_map/P_RL/ppermute | solution.py:435
  29.2 13.8 %collective-permute-start.4 = (f32[256,256]{1,0:T(8,128)S(1)}, f32[256,256]{1,0:T(8,128)S(1)}, u32[]{:S(2)}, u32[]{:S(2)}) collective-permute-start(f32[256,256]{1,0:T(8,128)S(1)} %add_add_fusion.1.refs_1_), channel_id=1, source_target_pairs={{0,2},{2,4},{4,6},{6,0},{1,3},{3,5},{5,7},{7,1},{8,10},{10,12},{12... | collective-permute-start | bytes 786440 | tf_op jit(solution)/shard_map/P_LL/ppermute | solution.py:435
  29.6 13.3 %collective-permute-start.6 = (f32[256,256]{1,0:T(8,128)S(1)}, f32[256,256]{1,0:T(8,128)S(1)}, u32[]{:S(2)}, u32[]{:S(2)}) collective-permute-start(f32[256,256]{1,0:T(8,128)S(1)} %collective-permute-done.2.refs_2_), channel_id=1, source_target_pairs={{0,2},{2,4},{4,6},{6,0},{1,3},{3,5},{5,7},{7,1},{8,10},{10,12},{12... | collective-permute-start | bytes 786440 | tf_op jit(solution)/shard_map/P_A0/ppermute | solution.py:435
  32.3 10.7 %collective-permute-start.8 = (f32[256,256]{1,0:T(8,128)S(1)}, f32[256,256]{1,0:T(8,128)S(1)}, u32[]{:S(2)}, u32[]{:S(2)}) collective-permute-start(f32[256,256]{1,0:T(8,128)S(1)} %collective-permute-done.7.refs_7_), channel_id=1, source_target_pairs={{0,6},{2,0},{4,2},{6,4},{1,7},{3,1},{5,3},{7,5},{8,14},{10,8},{12,... | collective-permute-start | bytes 786440 | tf_op jit(solution)/shard_map/P_B0/ppermute | solution.py:435
  43.2 4.2 %collective-permute-start.9 = (f32[2048,256]{1,0:T(8,128)S(1)}, f32[2048,256]{1,0:T(8,128)S(1)}, u32[]{:S(2)}, u32[]{:S(2)}) collective-permute-start(f32[2048,256]{1,0:T(8,128)S(1)} %pack_0.1.refs_0_), channel_id=1, source_target_pairs={{0,1},{1,0},{2,3},{3,2},{4,5},{5,4},{6,7},{7,6},{8,9},{9,8},{10,11... | collective-permute-start | bytes 6291464 | tf_op jit(solution)/shard_map/P_S0/ppermute | solution.py:440
  43.3 18.3 %collective-permute-start.12 = (f32[512,256]{1,0:T(8,128)S(1)}, f32[512,256]{1,0:T(8,128)S(1)}, u32[]{:S(2)}, u32[]{:S(2)}) collective-permute-start(f32[512,256]{1,0:T(8,128)S(1)} %add_add_fusion.refs_0_), channel_id=1, source_target_pairs={{0,6},{2,0},{4,2},{6,4},{1,7},{3,1},{5,3},{7,5},{8,14},{10,8},{12,... | collective-permute-start | bytes 1572872 | tf_op jit(solution)/shard_map/P_R1/ppermute | solution.py:435
  43.4 18.2 %collective-permute-start.11 = (f32[512,256]{1,0:T(8,128)S(1)}, f32[512,256]{1,0:T(8,128)S(1)}, u32[]{:S(2)}, u32[]{:S(2)}) collective-permute-start(f32[512,256]{1,0:T(8,128)S(1)} %add_add_fusion.refs_0_), channel_id=1, source_target_pairs={{0,4},{2,6},{4,0},{6,2},{1,5},{3,7},{5,1},{7,3},{8,12},{10,14},{12... | collective-permute-start | bytes 1572872 | tf_op jit(solution)/shard_map/P_K1/ppermute | solution.py:435
  44.5 25.9 %collective-permute-start.10 = (f32[512,256]{1,0:T(8,128)S(1)}, f32[512,256]{1,0:T(8,128)S(1)}, u32[]{:S(2)}, u32[]{:S(2)}) collective-permute-start(f32[512,256]{1,0:T(8,128)S(1)} %add_add_fusion.refs_0_), channel_id=1, source_target_pairs={{0,2},{2,4},{4,6},{6,0},{1,3},{3,5},{5,7},{7,1},{8,10},{10,12},{12... | collective-permute-start | bytes 1572872 | tf_op jit(solution)/shard_map/P_L1/ppermute | solution.py:435
  58.3 12.1 %collective-permute-start.13 = (f32[2,256,256]{2,1,0:T(8,128)S(1)}, f32[2,256,256]{2,1,0:T(8,128)S(1)}, u32[]{:S(2)}, u32[]{:S(2)}) collective-permute-start(f32[2,256,256]{2,1,0:T(8,128)S(1)} %get-tuple-element.113), channel_id=1, source_target_pairs={{0,16},{1,65},{2,18},{3,67},{4,20},{5,69},{6,22},{7,71},{8,24},{9,... | collective-permute-start | bytes 1572872 | tf_op jit(solution)/shard_map/P_H0/ppermute | solution.py:464
  58.4 12.0 %collective-permute-start.14 = (f32[2,256,256]{2,1,0:T(8,128)S(1)}, f32[2,256,256]{2,1,0:T(8,128)S(1)}, u32[]{:S(2)}, u32[]{:S(2)}) collective-permute-start(f32[2,256,256]{2,1,0:T(8,128)S(1)} %get-tuple-element.114), channel_id=1, source_target_pairs={{0,48},{1,73},{2,50},{3,75},{4,52},{5,77},{6,54},{7,79},{8,56},{9,... | collective-permute-start | bytes 1572872 | tf_op jit(solution)/shard_map/P_H0/ppermute | solution.py:464
  70.6 4.2 %collective-permute-start.15 = (f32[2048,256]{1,0:T(8,128)S(1)}, f32[2048,256]{1,0:T(8,128)S(1)}, u32[]{:S(2)}, u32[]{:S(2)}) collective-permute-start(f32[2048,256]{1,0:T(8,128)S(1)} %pack_1.1.refs_0_), channel_id=1, source_target_pairs={{0,1},{1,0},{2,3},{3,2},{4,5},{5,4},{6,7},{7,6},{8,9},{9,8},{10,11... | collective-permute-start | bytes 6291464 | tf_op jit(solution)/shard_map/P_S1/ppermute | solution.py:440
  70.9 16.1 %collective-permute-start.16 = (f32[4,256,256]{2,1,0:T(8,128)S(1)}, f32[4,256,256]{2,1,0:T(8,128)S(1)}, u32[]{:S(2)}, u32[]{:S(2)}) collective-permute-start(f32[4,256,256]{2,1,0:T(8,128)S(1)} %add_dynamic-update-slice_fusion.3), channel_id=1, source_target_pairs={{0,16},{1,65},{2,18},{3,67},{4,20},{5,69},{6,22},{7,71},{8,24},{9,... | collective-permute-start | bytes 3145736 | tf_op jit(solution)/shard_map/P_F0/ppermute | solution.py:464
  72.5 14.9 %collective-permute-start.17 = (f32[4,256,256]{2,1,0:T(8,128)S(1)}, f32[4,256,256]{2,1,0:T(8,128)S(1)}, u32[]{:S(2)}, u32[]{:S(2)}) collective-permute-start(f32[4,256,256]{2,1,0:T(8,128)S(1)} %add_dynamic-update-slice_fusion.2), channel_id=1, source_target_pairs={{0,48},{1,73},{2,50},{3,75},{4,52},{5,77},{6,54},{7,79},{8,56},{9,... | collective-permute-start | bytes 3145736 | tf_op jit(solution)/shard_map/P_F0/ppermute | solution.py:464
  87.3 9.8 %collective-permute-start.23 = (f32[2,256,256]{2,1,0:T(8,128)S(1)}, f32[2,256,256]{2,1,0:T(8,128)S(1)}, u32[]{:S(2)}, u32[]{:S(2)}) collective-permute-start(f32[2,256,256]{2,1,0:T(8,128)S(1)} %get-tuple-element.132), channel_id=1, source_target_pairs={{0,48},{1,73},{2,50},{3,75},{4,52},{5,77},{6,54},{7,79},{8,56},{9,... | collective-permute-start | bytes 1572872 | tf_op jit(solution)/shard_map/P_H1/ppermute | solution.py:464
  90.4 10.6 %collective-permute-start.21 = (f32[2,256,256]{2,1,0:T(8,128)S(1)}, f32[2,256,256]{2,1,0:T(8,128)S(1)}, u32[]{:S(2)}, u32[]{:S(2)}) collective-permute-start(f32[2,256,256]{2,1,0:T(8,128)S(1)} %get-tuple-element.130), channel_id=1, source_target_pairs={{0,16},{1,65},{2,18},{3,67},{4,20},{5,69},{6,22},{7,71},{8,24},{9,... | collective-permute-start | bytes 1572872 | tf_op jit(solution)/shard_map/P_H1/ppermute | solution.py:464
  97.2 21.7 %collective-permute-start.24 = (f32[4,256,256]{2,1,0:T(8,128)S(1)}, f32[4,256,256]{2,1,0:T(8,128)S(1)}, u32[]{:S(2)}, u32[]{:S(2)}) collective-permute-start(f32[4,256,256]{2,1,0:T(8,128)S(1)} %add_dynamic-update-slice_fusion), channel_id=1, source_target_pairs={{0,48},{1,73},{2,50},{3,75},{4,52},{5,77},{6,54},{7,79},{8,56},{9,... | collective-permute-start | bytes 3145736 | tf_op jit(solution)/shard_map/P_F1/ppermute | solution.py:464
  101.1 21.7 %collective-permute-start.22 = (f32[4,256,256]{2,1,0:T(8,128)S(1)}, f32[4,256,256]{2,1,0:T(8,128)S(1)}, u32[]{:S(2)}, u32[]{:S(2)}) collective-permute-start(f32[4,256,256]{2,1,0:T(8,128)S(1)} %add_dynamic-update-slice_fusion.1), channel_id=1, source_target_pairs={{0,16},{1,65},{2,18},{3,67},{4,20},{5,69},{6,22},{7,71},{8,24},{9,... | collective-permute-start | bytes 3145736 | tf_op jit(solution)/shard_map/P_F1/ppermute | solution.py:464
  101.4 24.5 %collective-permute-start.20 = (f32[256,256]{1,0:T(8,128)S(1)}, f32[256,256]{1,0:T(8,128)S(1)}, u32[]{:S(2)}, u32[]{:S(2)}) collective-permute-start(f32[256,256]{1,0:T(8,128)S(1)} %get-tuple-element.139), channel_id=1, source_target_pairs={{0,72},{1,49},{2,74},{3,51},{4,76},{5,53},{6,78},{7,55},{8,64},{9,... | collective-permute-start | bytes 786440 | tf_op jit(solution)/shard_map/P_G0/ppermute | solution.py:464
  104.3 22.6 %collective-permute-start.19 = (f32[256,256]{1,0:T(8,128)S(1)}, f32[256,256]{1,0:T(8,128)S(1)}, u32[]{:S(2)}, u32[]{:S(2)}) collective-permute-start(f32[256,256]{1,0:T(8,128)S(1)} %get-tuple-element.140), channel_id=1, source_target_pairs={{0,8},{1,33},{2,10},{3,35},{4,12},{5,37},{6,14},{7,39},{8,0},{9,41... | collective-permute-start | bytes 786440 | tf_op jit(solution)/shard_map/P_G0/ppermute | solution.py:464
  105.1 21.7 %collective-permute-start.18 = (f32[256,256]{1,0:T(8,128)S(1)}, f32[256,256]{1,0:T(8,128)S(1)}, u32[]{:S(2)}, u32[]{:S(2)}) collective-permute-start(f32[256,256]{1,0:T(8,128)S(1)} %get-tuple-element.141), channel_id=1, source_target_pairs={{0,64},{1,17},{2,66},{3,19},{4,68},{5,21},{6,70},{7,23},{8,72},{9,... | collective-permute-start | bytes 786440 | tf_op jit(solution)/shard_map/P_G0/ppermute | solution.py:464
  123.0 9.6 %collective-permute-start.27 = (f32[256,256]{1,0:T(8,128)S(1)}, f32[256,256]{1,0:T(8,128)S(1)}, u32[]{:S(2)}, u32[]{:S(2)}) collective-permute-start(f32[256,256]{1,0:T(8,128)S(1)} %get-tuple-element.135), channel_id=1, source_target_pairs={{0,72},{1,49},{2,74},{3,51},{4,76},{5,53},{6,78},{7,55},{8,64},{9,... | collective-permute-start | bytes 786440 | tf_op jit(solution)/shard_map/P_G1/ppermute | solution.py:464
  125.9 8.0 %collective-permute-start.26 = (f32[256,256]{1,0:T(8,128)S(1)}, f32[256,256]{1,0:T(8,128)S(1)}, u32[]{:S(2)}, u32[]{:S(2)}) collective-permute-start(f32[256,256]{1,0:T(8,128)S(1)} %get-tuple-element.136), channel_id=1, source_target_pairs={{0,8},{1,33},{2,10},{3,35},{4,12},{5,37},{6,14},{7,39},{8,0},{9,41... | collective-permute-start | bytes 786440 | tf_op jit(solution)/shard_map/P_G1/ppermute | solution.py:464
  125.9 10.4 %collective-permute-start.25 = (f32[256,256]{1,0:T(8,128)S(1)}, f32[256,256]{1,0:T(8,128)S(1)}, u32[]{:S(2)}, u32[]{:S(2)}) collective-permute-start(f32[256,256]{1,0:T(8,128)S(1)} %get-tuple-element.137), channel_id=1, source_target_pairs={{0,64},{1,17},{2,66},{3,19},{4,68},{5,21},{6,70},{7,23},{8,72},{9,... | collective-permute-start | bytes 786440 | tf_op jit(solution)/shard_map/P_G1/ppermute | solution.py:464

commit v9 on v8

--- a/solution.py
+++ b/solution.py
@@ -444,14 +444,16 @@
     upper, lower = own_0[:middle], own_0[middle:]
     upper = upper + (across_dir(upper, "P_ZU") + done_a[0, 0])
     blocks_b, done_b = prepare_near(table, near_z, NEAR // 2, NEAR // 2)
-    blocks_u, blocks_v, done_far = prepare_far(table, far_ut, far_vt)
     upper, lower = lax.optimization_barrier((upper, lower))
     left_u, right_u = step(upper, 1, "P_LU"), step(upper, 3, "P_RU")
     lower = lower + (across_dir(lower, "P_ZL") + done_b[0, 0])
     own_1, lower, left_u, right_u = lax.optimization_barrier((own_1, lower, left_u, right_u))
     left_l, right_l = step(lower, 1, "P_LL"), step(lower, 3, "P_RL")
-    own_1 = own_1 + (across_dir(own_1, "P_Z1") + done_far[0, 0])
+    came_1 = across_dir(own_1, "P_Z1")
+    right_l, table_far = lax.optimization_barrier((right_l, table))
+    blocks_u, blocks_v, done_far = prepare_far(table_far, far_ut, far_vt)
     upper_0, lower_0 = step(left_u, 1, "P_A0"), step(right_l, 3, "P_B0")
+    own_1 = own_1 + (came_1 + done_far[0, 0])
     own_1, upper_0, lower_0 = lax.optimization_barrier((own_1, upper_0, lower_0))
     left_1, right_1 = step(own_1, 1, "P_L1"), step(own_1, 3, "P_R1")
     across_1 = step(own_1, 2, "P_K1")

time: 137 us -> 137 us (level)
  Pallas kernels: 38.6 us -> 19 us
  waiting for transfers between devices: 57.8 us -> 73.4 us
  starting transfers between devices: 35.9 us -> 39.4 us
    pallas_call x2, Pallas kernels: 21.6 us -> 8.45 us  [apply_blocks(): pl.pallas_call(apply_kernel, name=f'apply_{index}', in_specs=[SMEM] + [AN...]
    ppermute x9, waiting for transfers between devices: 19.1 us -> 28 us  [step(): return lax.ppermute(part, 'x', [(i, (i + k) % 4) for i in range(4)])]
    pallas_call x2, Pallas kernels: 10.5 us -> 4.1 us  [prepare_near(): pl.pallas_call(functools.partial(prepare_near_kernel, first), name=f'prep...]
    ppermute x14, waiting for transfers between devices: 34.3 us -> 40.5 us  [go(): return lax.ppermute(part, AXES, turn)]
    ppermute x9, starting transfers between devices: 8.99 us -> 11.1 us  [step(): return lax.ppermute(part, 'x', [(i, (i + k) % 4) for i in range(4)])]
    ppermute x3, waiting for transfers between devices: 1.91 us -> 3.97 us  [across_dir(): return lax.ppermute(part, 'dir', swap)]
    ppermute x14, starting transfers between devices: 22.3 us -> 23.7 us  [go(): return lax.ppermute(part, AXES, turn)]
    ppermute x2, waiting for transfers between devices: 2.47 us -> 1.01 us  [both_cores(): return (mine, lax.ppermute(mine, 'core', swap))]
  transfers between devices with their start and end apart: 28 -> 28, of which waited for: 16 -> 17; matrix products, arithmetic and copies ran while one was open for 3% -> 3% of each run, Pallas kernels for 25% -> 11%
where the time goes in v9:
time: 137 us
  waiting for transfers between devices  73.4 us (54%)
  starting transfers between devices  39.4 us (29%)
  Pallas kernels  19 us (14%)
  other arithmetic  3.03 us (2%)
  local copies, waits for them, and re-layouts  1.66 us (1%)
    ppermute x14, waiting for transfers between devices, go(): return lax.ppermute(part, AXES, turn)  40.5 us
    ppermute x9, waiting for transfers between devices, step(): return lax.ppermute(part, 'x', [(i, (i + k) % 4) for i in range(4)])  28 us
    ppermute x14, starting transfers between devices, go(): return lax.ppermute(part, AXES, turn)  23.7 us
    ppermute x9, starting transfers between devices, step(): return lax.ppermute(part, 'x', [(i, (i + k) % 4) for i in range(4)])  11.1 us
    pallas_call x2, Pallas kernels, apply_blocks(): pl.pallas_call(apply_kernel, name=f'apply_{index}', in_specs=[SMEM] + [AN...  8.45 us
    ppermute x3, starting transfers between devices, across_dir(): return lax.ppermute(part, 'dir', swap)  4.42 us
    pallas_call x2, Pallas kernels, prepare_near(): pl.pallas_call(functools.partial(prepare_near_kernel, first), name=f'prep...  4.1 us
    ppermute x3, waiting for transfers between devices, across_dir(): return lax.ppermute(part, 'dir', swap)  3.97 us
  transfers between devices with their start and end apart: 28, of which 17 were waited for; matrix products, arithmetic and copies ran while one was open for 3% of the time, Pallas kernels for 11%

profile of v9, /device:TPU:0, one launch (start us, length us, event | category | flops | bytes accessed | tf_op | source)
XLA Modules:
  0.0 136.7 jit_solution(16608367134838463808)
XLA Ops:
  0.0 3.0 %rhs.5 = (f32[512,256]{1,0:T(8,128)S(1)}, f32[512,256]{1,0:T(8,128)S(1)}) custom-call(bf16[1024,512]{1,0:T(8,128)(2,1)} %cot_ref.1, bf16[2,512,1024]{2,1,0:T(8,128)(2,1)} %rad_ref.1), custom_call_target="tpu_custom_call" | custom-call | flops 1073741824 | bytes 4194304 | tf_op jit(solution)/shard_map/rhs/pallas_call | solution.py:90
  3.1 2.1 %collective-permute-start = (f32[256,256]{1,0:T(8,128)S(1)}, f32[256,256]{1,0:T(8,128)S(1)}, u32[]{:S(2)}, u32[]{:S(2)}) collective-permute-start(f32[256,256]{1,0:T(8,128)S(1)} %slice.199), channel_id=1, source_target_pairs={{0,64},{64,0},{1,65},{65,1},{2,66},{66,2},{3,67},{67,3},{4,68},{68... | collective-permute-start | bytes 786440 | tf_op jit(solution)/shard_map/P_ZU/ppermute | solution.py:431
  5.3 3.5 %prepare_near_0.1 = (bf16[4,512,2048]{2,1,0:T(8,128)(2,1)S(1)}, f32[8,128]{1,0:T(8,128)S(1)}) custom-call(s32[48]{0:T(128)S(1)} %concatenate.11.table, f32[2,8,512,512]{3,2,1,0:T(8,128)} %z_ref.3), custom_call_target="tpu_custom_call" | custom-call | flops 268435456 | bytes 8388608 | tf_op jit(solution)/shard_map/prepare_near_0/pallas_call | solution.py:139
  8.9 0.5 slice.200
  9.4 2.1 %collective-permute-done = f32[256,256]{1,0:T(8,128)S(1)} collective-permute-done((f32[256,256]{1,0:T(8,128)S(1)}, f32[256,256]{1,0:T(8,128)S(1)}, u32[]{:S(2)}, u32[]{:S(2)}) %collective-permute-start) | collective-permute-done | bytes 262176 | tf_op jit(solution)/shard_map/P_ZU/ppermute | solution.py:431
  11.5 0.7 fusion.11
  12.2 1.8 %collective-permute-start.1 = (f32[256,256]{1,0:T(8,128)S(1)}, f32[256,256]{1,0:T(8,128)S(1)}, u32[]{:S(2)}, u32[]{:S(2)}) collective-permute-start(f32[256,256]{1,0:T(8,128)S(1)} %get-tuple-element.100), channel_id=1, source_target_pairs={{0,64},{64,0},{1,65},{65,1},{2,66},{66,2},{3,67},{67,3},{4,68},{68... | collective-permute-start | bytes 786440 | tf_op jit(solution)/shard_map/P_ZL/ppermute | solution.py:431
  14.0 2.8 %collective-permute-start.3 = (f32[256,256]{1,0:T(8,128)S(1)}, f32[256,256]{1,0:T(8,128)S(1)}, u32[]{:S(2)}, u32[]{:S(2)}) collective-permute-start(f32[256,256]{1,0:T(8,128)S(1)} %get-tuple-element.98.refs_0_), channel_id=1, source_target_pairs={{0,6},{2,0},{4,2},{6,4},{1,7},{3,1},{5,3},{7,5},{8,14},{10,8},{12,... | collective-permute-start | bytes 786440 | tf_op jit(solution)/shard_map/P_RU/ppermute | solution.py:435
  16.8 0.6 prepare_near_4.1
  17.3 0.5 slice.202
  17.9 1.9 %collective-permute-done.1 = f32[256,256]{1,0:T(8,128)S(1)} collective-permute-done((f32[256,256]{1,0:T(8,128)S(1)}, f32[256,256]{1,0:T(8,128)S(1)}, u32[]{:S(2)}, u32[]{:S(2)}) %collective-permute-start.1) | collective-permute-done | bytes 262176 | tf_op jit(solution)/shard_map/P_ZL/ppermute | solution.py:431
  19.7 0.7 add_add_fusion.1.refs_1_
  20.4 0.8 collective-permute-done.3.refs_6_
  21.2 3.4 %collective-permute-done.2.refs_2_ = f32[256,256]{1,0:T(8,128)S(1)} collective-permute-done((f32[256,256]{1,0:T(8,128)S(1)}, f32[256,256]{1,0:T(8,128)S(1)}, u32[]{:S(2)}, u32[]{:S(2)}) %collective-permute-start.2) | collective-permute-done | bytes 262176 | tf_op jit(solution)/shard_map/P_LU/ppermute | solution.py:435
  24.6 0.5 collective-permute-start.5
  25.4 1.7 %collective-permute-start.4 = (f32[256,256]{1,0:T(8,128)S(1)}, f32[256,256]{1,0:T(8,128)S(1)}, u32[]{:S(2)}, u32[]{:S(2)}) collective-permute-start(f32[256,256]{1,0:T(8,128)S(1)} %add_add_fusion.1.refs_1_), channel_id=1, source_target_pairs={{0,2},{2,4},{4,6},{6,0},{1,3},{3,5},{5,7},{7,1},{8,10},{10,12},{12... | collective-permute-start | bytes 786440 | tf_op jit(solution)/shard_map/P_LL/ppermute | solution.py:435
  27.2 4.3 %collective-permute-done.6.refs_7_ = f32[256,256]{1,0:T(8,128)S(1)} collective-permute-done((f32[256,256]{1,0:T(8,128)S(1)}, f32[256,256]{1,0:T(8,128)S(1)}, u32[]{:S(2)}, u32[]{:S(2)}) %collective-permute-start.6) | collective-permute-done | bytes 262176 | tf_op jit(solution)/shard_map/P_RL/ppermute | solution.py:435
  31.5 2.7 %collective-permute-start.8 = (f32[256,256]{1,0:T(8,128)S(1)}, f32[256,256]{1,0:T(8,128)S(1)}, u32[]{:S(2)}, u32[]{:S(2)}) collective-permute-start(f32[256,256]{1,0:T(8,128)S(1)} %collective-permute-done.6.refs_7_), channel_id=1, source_target_pairs={{0,6},{2,0},{4,2},{6,4},{1,7},{3,1},{5,3},{7,5},{8,14},{10,8},{12,... | collective-permute-start | bytes 786440 | tf_op jit(solution)/shard_map/P_B0/ppermute | solution.py:435
  34.2 2.0 %prepare_far.1 = (bf16[4,128,2048]{2,1,0:T(8,128)(2,1)S(1)}, bf16[4,512,512]{2,1,0:T(8,128)(2,1)S(1)}, f32[8,128]{1,0:T(8,128)S(1)}) custom-call(s32[48]{0:T(128)S(1)} %concatenate.11.table, f32[2,4,96,512]{3,2,1,0:T(8,128)} %u_ref.1, f32[2,4,96,512]{3,2,1,0:T(8,128)} %v_ref.1), custom_call_target="tpu_custom_call" | custom-call | flops 268435456 | bytes 4194304 | tf_op jit(solution)/shard_map/prepare_far/pallas_call | solution.py:192
  36.2 0.5 slice.203
  36.7 0.7 add_add_fusion.refs_0_
  37.4 2.1 %collective-permute-done.7.refs_4_ = f32[256,256]{1,0:T(8,128)S(1)} collective-permute-done((f32[256,256]{1,0:T(8,128)S(1)}, f32[256,256]{1,0:T(8,128)S(1)}, u32[]{:S(2)}, u32[]{:S(2)}) %collective-permute-start.7) | collective-permute-done | bytes 262176 | tf_op jit(solution)/shard_map/P_A0/ppermute | solution.py:435
  39.9 2.6 %collective-permute-start.12 = (f32[512,256]{1,0:T(8,128)S(1)}, f32[512,256]{1,0:T(8,128)S(1)}, u32[]{:S(2)}, u32[]{:S(2)}) collective-permute-start(f32[512,256]{1,0:T(8,128)S(1)} %add_add_fusion.refs_0_), channel_id=1, source_target_pairs={{0,6},{2,0},{4,2},{6,4},{1,7},{3,1},{5,3},{7,5},{8,14},{10,8},{12,... | collective-permute-start | bytes 1572872 | tf_op jit(solution)/shard_map/P_R1/ppermute | solution.py:435
  42.5 0.9 collective-permute-start.10
  43.4 0.6 collective-permute-done.9.refs_1_
  44.0 4.2 %apply_0.1 = (f32[4,256,256]{2,1,0:T(8,128)S(1)}, f32[4,256,256]{2,1,0:T(8,128)S(1)}, f32[2,256,256]{2,1,0:T(8,128)S(1)}, f32[2,256,256]{2,1,0:T(8,128)S(1)}, f3...) custom-call(s32[48]{0:T(128)S(1)} %concatenate.11.table, f32[2048,256]{1,0:T(8,128)S(1)} %pack_0.1.refs_0_, ...), custom_call_target="tpu_custom_call" | custom-call | flops 42949672960 | bytes 1 | tf_op jit(solution)/shard_map/apply_0/pallas_call | solution.py:361
  48.2 1.0 collective-permute-start.13
  49.2 2.3 %collective-permute-start.14 = (f32[2,256,256]{2,1,0:T(8,128)S(1)}, f32[2,256,256]{2,1,0:T(8,128)S(1)}, u32[]{:S(2)}, u32[]{:S(2)}) collective-permute-start(f32[2,256,256]{2,1,0:T(8,128)S(1)} %get-tuple-element.118), channel_id=1, source_target_pairs={{0,48},{1,73},{2,50},{3,75},{4,52},{5,77},{6,54},{7,79},{8,56},{9,... | collective-permute-start | bytes 1572872 | tf_op jit(solution)/shard_map/P_H0/ppermute | solution.py:466
  51.5 14.0 %collective-permute-done.12.refs_3_ = f32[512,256]{1,0:T(8,128)S(1)} collective-permute-done((f32[512,256]{1,0:T(8,128)S(1)}, f32[512,256]{1,0:T(8,128)S(1)}, u32[]{:S(2)}, u32[]{:S(2)}) %collective-permute-start.12) | collective-permute-done | bytes 524320 | tf_op jit(solution)/shard_map/P_R1/ppermute | solution.py:435
  65.5 3.4 %collective-permute-done.10.refs_1_ = f32[512,256]{1,0:T(8,128)S(1)} collective-permute-done((f32[512,256]{1,0:T(8,128)S(1)}, f32[512,256]{1,0:T(8,128)S(1)}, u32[]{:S(2)}, u32[]{:S(2)}) %collective-permute-start.10) | collective-permute-done | bytes 524320 | tf_op jit(solution)/shard_map/P_L1/ppermute | solution.py:435
  69.3 0.4 collective-permute-start.16
  69.8 3.1 %collective-permute-start.17 = (f32[4,256,256]{2,1,0:T(8,128)S(1)}, f32[4,256,256]{2,1,0:T(8,128)S(1)}, u32[]{:S(2)}, u32[]{:S(2)}) collective-permute-start(f32[4,256,256]{2,1,0:T(8,128)S(1)} %add_dynamic-update-slice_fusion.2), channel_id=1, source_target_pairs={{0,48},{1,73},{2,50},{3,75},{4,52},{5,77},{6,54},{7,79},{8,56},{9,... | collective-permute-start | bytes 3145736 | tf_op jit(solution)/shard_map/P_F0/ppermute | solution.py:466
  72.9 0.4 collective-permute-done.15.refs_1_
  73.3 4.2 %apply_1.1 = (f32[4,256,256]{2,1,0:T(8,128)S(1)}, f32[4,256,256]{2,1,0:T(8,128)S(1)}, f32[2,256,256]{2,1,0:T(8,128)S(1)}, f32[2,256,256]{2,1,0:T(8,128)S(1)}, f3...) custom-call(s32[48]{0:T(128)S(1)} %concatenate.11.table, f32[2048,256]{1,0:T(8,128)S(1)} %pack_1.1.refs_0_, ...), custom_call_target="tpu_custom_call" | custom-call | flops 42949672960 | bytes 1 | tf_op jit(solution)/shard_map/apply_1/pallas_call | solution.py:361
  77.6 7.9 %collective-permute-done.16 = f32[4,256,256]{2,1,0:T(8,128)S(1)} collective-permute-done((f32[4,256,256]{2,1,0:T(8,128)S(1)}, f32[4,256,256]{2,1,0:T(8,128)S(1)}, u32[]{:S(2)}, u32[]{:S(2)}) %collective-permute-start.16) | collective-permute-done | bytes 1048608 | tf_op jit(solution)/shard_map/P_F0/ppermute | solution.py:466
  85.5 3.4 %collective-permute-start.23 = (f32[2,256,256]{2,1,0:T(8,128)S(1)}, f32[2,256,256]{2,1,0:T(8,128)S(1)}, u32[]{:S(2)}, u32[]{:S(2)}) collective-permute-start(f32[2,256,256]{2,1,0:T(8,128)S(1)} %get-tuple-element.136), channel_id=1, source_target_pairs={{0,48},{1,73},{2,50},{3,75},{4,52},{5,77},{6,54},{7,79},{8,56},{9,... | collective-permute-start | bytes 1572872 | tf_op jit(solution)/shard_map/P_H1/ppermute | solution.py:466
  88.9 6.7 %collective-permute-done.23 = f32[2,256,256]{2,1,0:T(8,128)S(1)} collective-permute-done((f32[2,256,256]{2,1,0:T(8,128)S(1)}, f32[2,256,256]{2,1,0:T(8,128)S(1)}, u32[]{:S(2)}, u32[]{:S(2)}) %collective-permute-start.23) | collective-permute-done | bytes 524320 | tf_op jit(solution)/shard_map/P_H1/ppermute | solution.py:466
  95.8 3.8 %collective-permute-start.24 = (f32[4,256,256]{2,1,0:T(8,128)S(1)}, f32[4,256,256]{2,1,0:T(8,128)S(1)}, u32[]{:S(2)}, u32[]{:S(2)}) collective-permute-start(f32[4,256,256]{2,1,0:T(8,128)S(1)} %add_dynamic-update-slice_fusion), channel_id=1, source_target_pairs={{0,48},{1,73},{2,50},{3,75},{4,52},{5,77},{6,54},{7,79},{8,56},{9,... | collective-permute-start | bytes 3145736 | tf_op jit(solution)/shard_map/P_F1/ppermute | solution.py:466
  99.9 3.8 %collective-permute-start.20 = (f32[256,256]{1,0:T(8,128)S(1)}, f32[256,256]{1,0:T(8,128)S(1)}, u32[]{:S(2)}, u32[]{:S(2)}) collective-permute-start(f32[256,256]{1,0:T(8,128)S(1)} %get-tuple-element.143), channel_id=1, source_target_pairs={{0,72},{1,49},{2,74},{3,51},{4,76},{5,53},{6,78},{7,55},{8,64},{9,... | collective-permute-start | bytes 786440 | tf_op jit(solution)/shard_map/P_G0/ppermute | solution.py:466
  103.8 1.1 collective-permute-start.18
  104.9 12.6 %collective-permute-done.24 = f32[4,256,256]{2,1,0:T(8,128)S(1)} collective-permute-done((f32[4,256,256]{2,1,0:T(8,128)S(1)}, f32[4,256,256]{2,1,0:T(8,128)S(1)}, u32[]{:S(2)}, u32[]{:S(2)}) %collective-permute-start.24) | collective-permute-done | bytes 1048608 | tf_op jit(solution)/shard_map/P_F1/ppermute | solution.py:466
  117.5 3.9 %collective-permute-done.22 = f32[4,256,256]{2,1,0:T(8,128)S(1)} collective-permute-done((f32[4,256,256]{2,1,0:T(8,128)S(1)}, f32[4,256,256]{2,1,0:T(8,128)S(1)}, u32[]{:S(2)}, u32[]{:S(2)}) %collective-permute-start.22) | collective-permute-done | bytes 1048608 | tf_op jit(solution)/shard_map/P_F1/ppermute | solution.py:466
  121.6 3.8 %collective-permute-start.27 = (f32[256,256]{1,0:T(8,128)S(1)}, f32[256,256]{1,0:T(8,128)S(1)}, u32[]{:S(2)}, u32[]{:S(2)}) collective-permute-start(f32[256,256]{1,0:T(8,128)S(1)} %get-tuple-element.139), channel_id=1, source_target_pairs={{0,72},{1,49},{2,74},{3,51},{4,76},{5,53},{6,78},{7,55},{8,64},{9,... | collective-permute-start | bytes 786440 | tf_op jit(solution)/shard_map/P_G1/ppermute | solution.py:466
  125.4 0.9 collective-permute-start.25
  126.3 5.7 %collective-permute-done.27.refs_7_ = f32[256,256]{1,0:T(8,128)S(1)} collective-permute-done((f32[256,256]{1,0:T(8,128)S(1)}, f32[256,256]{1,0:T(8,128)S(1)}, u32[]{:S(2)}, u32[]{:S(2)}) %collective-permute-start.27) | collective-permute-done | bytes 262176 | tf_op jit(solution)/shard_map/P_G1/ppermute | solution.py:466
  132.0 1.3 collective-permute-done.26.refs_6_
  133.3 2.4 %collective-permute-done.25.refs_5_ = f32[256,256]{1,0:T(8,128)S(1)} collective-permute-done((f32[256,256]{1,0:T(8,128)S(1)}, f32[256,256]{1,0:T(8,128)S(1)}, u32[]{:S(2)}, u32[]{:S(2)}) %collective-permute-start.25) | collective-permute-done | bytes 262176 | tf_op jit(solution)/shard_map/P_G1/ppermute | solution.py:466
  135.7 1.0 finish.1
  (42 shorter events, 2.2 us)
Async XLA Ops:
  0.0 5.2 %copy-start = (s32[8,2]{0,1:T(2,128)S(1)}, s32[8,2]{0,1:T(2,128)}, u32[]{:S(2)}) copy-start(s32[8,2]{0,1:T(2,128)} %param.20) | copy-start | bytes 196
  0.0 5.2 %copy-start.1 = (s32[4,2]{0,1:T(2,128)S(1)}, s32[4,2]{0,1:T(2,128)}, u32[]{:S(2)}) copy-start(s32[4,2]{0,1:T(2,128)} %param.23) | copy-start | bytes 100
  0.0 5.2 %copy-start.2 = (s32[1,2]{1,0:T(1,128)S(1)}, s32[1,2]{1,0:T(1,128)}, u32[]{:S(2)}) copy-start(s32[1,2]{1,0:T(1,128)} %param.25) | copy-start | bytes 28
  0.0 5.2 %copy-start.3 = (s32[4]{0:T(128)S(1)}, s32[4]{0:T(128)}, u32[]{:S(2)}) copy-start(s32[4]{0:T(128)} %param.24) | copy-start | bytes 52
  3.1 8.4 %collective-permute-start = (f32[256,256]{1,0:T(8,128)S(1)}, f32[256,256]{1,0:T(8,128)S(1)}, u32[]{:S(2)}, u32[]{:S(2)}) collective-permute-start(f32[256,256]{1,0:T(8,128)S(1)} %slice.199), channel_id=1, source_target_pairs={{0,64},{64,0},{1,65},{65,1},{2,66},{66,2},{3,67},{67,3},{4,68},{68... | collective-permute-start | bytes 786440 | tf_op jit(solution)/shard_map/P_ZU/ppermute | solution.py:431
  12.2 7.6 %collective-permute-start.1 = (f32[256,256]{1,0:T(8,128)S(1)}, f32[256,256]{1,0:T(8,128)S(1)}, u32[]{:S(2)}, u32[]{:S(2)}) collective-permute-start(f32[256,256]{1,0:T(8,128)S(1)} %get-tuple-element.100), channel_id=1, source_target_pairs={{0,64},{64,0},{1,65},{65,1},{2,66},{66,2},{3,67},{67,3},{4,68},{68... | collective-permute-start | bytes 786440 | tf_op jit(solution)/shard_map/P_ZL/ppermute | solution.py:431
  14.0 7.2 %collective-permute-start.3 = (f32[256,256]{1,0:T(8,128)S(1)}, f32[256,256]{1,0:T(8,128)S(1)}, u32[]{:S(2)}, u32[]{:S(2)}) collective-permute-start(f32[256,256]{1,0:T(8,128)S(1)} %get-tuple-element.98.refs_0_), channel_id=1, source_target_pairs={{0,6},{2,0},{4,2},{6,4},{1,7},{3,1},{5,3},{7,5},{8,14},{10,8},{12,... | collective-permute-start | bytes 786440 | tf_op jit(solution)/shard_map/P_RU/ppermute | solution.py:435
  16.8 7.8 %collective-permute-start.2 = (f32[256,256]{1,0:T(8,128)S(1)}, f32[256,256]{1,0:T(8,128)S(1)}, u32[]{:S(2)}, u32[]{:S(2)}) collective-permute-start(f32[256,256]{1,0:T(8,128)S(1)} %get-tuple-element.98.refs_0_), channel_id=1, source_target_pairs={{0,2},{2,4},{4,6},{6,0},{1,3},{3,5},{5,7},{7,1},{8,10},{10,12},{12... | collective-permute-start | bytes 786440 | tf_op jit(solution)/shard_map/P_LU/ppermute | solution.py:435
  24.6 12.1 %collective-permute-start.5 = (f32[512,256]{1,0:T(8,128)S(1)}, f32[512,256]{1,0:T(8,128)S(1)}, u32[]{:S(2)}, u32[]{:S(2)}) collective-permute-start(f32[512,256]{1,0:T(8,128)S(1)} %get-tuple-element.104), channel_id=1, source_target_pairs={{0,64},{64,0},{1,65},{65,1},{2,66},{66,2},{3,67},{67,3},{4,68},{68... | collective-permute-start | bytes 1572872 | tf_op jit(solution)/shard_map/P_Z1/ppermute | solution.py:431
  25.1 6.4 %collective-permute-start.6 = (f32[256,256]{1,0:T(8,128)S(1)}, f32[256,256]{1,0:T(8,128)S(1)}, u32[]{:S(2)}, u32[]{:S(2)}) collective-permute-start(f32[256,256]{1,0:T(8,128)S(1)} %add_add_fusion.1.refs_1_), channel_id=1, source_target_pairs={{0,6},{2,0},{4,2},{6,4},{1,7},{3,1},{5,3},{7,5},{8,14},{10,8},{12,... | collective-permute-start | bytes 786440 | tf_op jit(solution)/shard_map/P_RL/ppermute | solution.py:435
  25.4 14.1 %collective-permute-start.4 = (f32[256,256]{1,0:T(8,128)S(1)}, f32[256,256]{1,0:T(8,128)S(1)}, u32[]{:S(2)}, u32[]{:S(2)}) collective-permute-start(f32[256,256]{1,0:T(8,128)S(1)} %add_add_fusion.1.refs_1_), channel_id=1, source_target_pairs={{0,2},{2,4},{4,6},{6,0},{1,3},{3,5},{5,7},{7,1},{8,10},{10,12},{12... | collective-permute-start | bytes 786440 | tf_op jit(solution)/shard_map/P_LL/ppermute | solution.py:435
  27.1 12.4 %collective-permute-start.7 = (f32[256,256]{1,0:T(8,128)S(1)}, f32[256,256]{1,0:T(8,128)S(1)}, u32[]{:S(2)}, u32[]{:S(2)}) collective-permute-start(f32[256,256]{1,0:T(8,128)S(1)} %collective-permute-done.2.refs_2_), channel_id=1, source_target_pairs={{0,2},{2,4},{4,6},{6,0},{1,3},{3,5},{5,7},{7,1},{8,10},{10,12},{12... | collective-permute-start | bytes 786440 | tf_op jit(solution)/shard_map/P_A0/ppermute | solution.py:435
  31.5 8.1 %collective-permute-start.8 = (f32[256,256]{1,0:T(8,128)S(1)}, f32[256,256]{1,0:T(8,128)S(1)}, u32[]{:S(2)}, u32[]{:S(2)}) collective-permute-start(f32[256,256]{1,0:T(8,128)S(1)} %collective-permute-done.6.refs_7_), channel_id=1, source_target_pairs={{0,6},{2,0},{4,2},{6,4},{1,7},{3,1},{5,3},{7,5},{8,14},{10,8},{12,... | collective-permute-start | bytes 786440 | tf_op jit(solution)/shard_map/P_B0/ppermute | solution.py:435
  39.8 4.2 %collective-permute-start.9 = (f32[2048,256]{1,0:T(8,128)S(1)}, f32[2048,256]{1,0:T(8,128)S(1)}, u32[]{:S(2)}, u32[]{:S(2)}) collective-permute-start(f32[2048,256]{1,0:T(8,128)S(1)} %pack_0.1.refs_0_), channel_id=1, source_target_pairs={{0,1},{1,0},{2,3},{3,2},{4,5},{5,4},{6,7},{7,6},{8,9},{9,8},{10,11... | collective-permute-start | bytes 6291464 | tf_op jit(solution)/shard_map/P_S0/ppermute | solution.py:440
  39.9 25.7 %collective-permute-start.12 = (f32[512,256]{1,0:T(8,128)S(1)}, f32[512,256]{1,0:T(8,128)S(1)}, u32[]{:S(2)}, u32[]{:S(2)}) collective-permute-start(f32[512,256]{1,0:T(8,128)S(1)} %add_add_fusion.refs_0_), channel_id=1, source_target_pairs={{0,6},{2,0},{4,2},{6,4},{1,7},{3,1},{5,3},{7,5},{8,14},{10,8},{12,... | collective-permute-start | bytes 1572872 | tf_op jit(solution)/shard_map/P_R1/ppermute | solution.py:435
  42.5 23.1 %collective-permute-start.11 = (f32[512,256]{1,0:T(8,128)S(1)}, f32[512,256]{1,0:T(8,128)S(1)}, u32[]{:S(2)}, u32[]{:S(2)}) collective-permute-start(f32[512,256]{1,0:T(8,128)S(1)} %add_add_fusion.refs_0_), channel_id=1, source_target_pairs={{0,4},{2,6},{4,0},{6,2},{1,5},{3,7},{5,1},{7,3},{8,12},{10,14},{12... | collective-permute-start | bytes 1572872 | tf_op jit(solution)/shard_map/P_K1/ppermute | solution.py:435
  42.5 26.4 %collective-permute-start.10 = (f32[512,256]{1,0:T(8,128)S(1)}, f32[512,256]{1,0:T(8,128)S(1)}, u32[]{:S(2)}, u32[]{:S(2)}) collective-permute-start(f32[512,256]{1,0:T(8,128)S(1)} %add_add_fusion.refs_0_), channel_id=1, source_target_pairs={{0,2},{2,4},{4,6},{6,0},{1,3},{3,5},{5,7},{7,1},{8,10},{10,12},{12... | collective-permute-start | bytes 1572872 | tf_op jit(solution)/shard_map/P_L1/ppermute | solution.py:435
  48.2 20.7 %collective-permute-start.13 = (f32[2,256,256]{2,1,0:T(8,128)S(1)}, f32[2,256,256]{2,1,0:T(8,128)S(1)}, u32[]{:S(2)}, u32[]{:S(2)}) collective-permute-start(f32[2,256,256]{2,1,0:T(8,128)S(1)} %get-tuple-element.117), channel_id=1, source_target_pairs={{0,16},{1,65},{2,18},{3,67},{4,20},{5,69},{6,22},{7,71},{8,24},{9,... | collective-permute-start | bytes 1572872 | tf_op jit(solution)/shard_map/P_H0/ppermute | solution.py:466
  49.2 19.7 %collective-permute-start.14 = (f32[2,256,256]{2,1,0:T(8,128)S(1)}, f32[2,256,256]{2,1,0:T(8,128)S(1)}, u32[]{:S(2)}, u32[]{:S(2)}) collective-permute-start(f32[2,256,256]{2,1,0:T(8,128)S(1)} %get-tuple-element.118), channel_id=1, source_target_pairs={{0,48},{1,73},{2,50},{3,75},{4,52},{5,77},{6,54},{7,79},{8,56},{9,... | collective-permute-start | bytes 1572872 | tf_op jit(solution)/shard_map/P_H0/ppermute | solution.py:466
  69.1 4.2 %collective-permute-start.15 = (f32[2048,256]{1,0:T(8,128)S(1)}, f32[2048,256]{1,0:T(8,128)S(1)}, u32[]{:S(2)}, u32[]{:S(2)}) collective-permute-start(f32[2048,256]{1,0:T(8,128)S(1)} %pack_1.1.refs_0_), channel_id=1, source_target_pairs={{0,1},{1,0},{2,3},{3,2},{4,5},{5,4},{6,7},{7,6},{8,9},{9,8},{10,11... | collective-permute-start | bytes 6291464 | tf_op jit(solution)/shard_map/P_S1/ppermute | solution.py:440
  69.3 16.2 %collective-permute-start.16 = (f32[4,256,256]{2,1,0:T(8,128)S(1)}, f32[4,256,256]{2,1,0:T(8,128)S(1)}, u32[]{:S(2)}, u32[]{:S(2)}) collective-permute-start(f32[4,256,256]{2,1,0:T(8,128)S(1)} %add_dynamic-update-slice_fusion.3), channel_id=1, source_target_pairs={{0,16},{1,65},{2,18},{3,67},{4,20},{5,69},{6,22},{7,71},{8,24},{9,... | collective-permute-start | bytes 3145736 | tf_op jit(solution)/shard_map/P_F0/ppermute | solution.py:466
  69.8 15.7 %collective-permute-start.17 = (f32[4,256,256]{2,1,0:T(8,128)S(1)}, f32[4,256,256]{2,1,0:T(8,128)S(1)}, u32[]{:S(2)}, u32[]{:S(2)}) collective-permute-start(f32[4,256,256]{2,1,0:T(8,128)S(1)} %add_dynamic-update-slice_fusion.2), channel_id=1, source_target_pairs={{0,48},{1,73},{2,50},{3,75},{4,52},{5,77},{6,54},{7,79},{8,56},{9,... | collective-permute-start | bytes 3145736 | tf_op jit(solution)/shard_map/P_F0/ppermute | solution.py:466
  85.5 10.1 %collective-permute-start.23 = (f32[2,256,256]{2,1,0:T(8,128)S(1)}, f32[2,256,256]{2,1,0:T(8,128)S(1)}, u32[]{:S(2)}, u32[]{:S(2)}) collective-permute-start(f32[2,256,256]{2,1,0:T(8,128)S(1)} %get-tuple-element.136), channel_id=1, source_target_pairs={{0,48},{1,73},{2,50},{3,75},{4,52},{5,77},{6,54},{7,79},{8,56},{9,... | collective-permute-start | bytes 1572872 | tf_op jit(solution)/shard_map/P_H1/ppermute | solution.py:466
  88.9 10.6 %collective-permute-start.21 = (f32[2,256,256]{2,1,0:T(8,128)S(1)}, f32[2,256,256]{2,1,0:T(8,128)S(1)}, u32[]{:S(2)}, u32[]{:S(2)}) collective-permute-start(f32[2,256,256]{2,1,0:T(8,128)S(1)} %get-tuple-element.134), channel_id=1, source_target_pairs={{0,16},{1,65},{2,18},{3,67},{4,20},{5,69},{6,22},{7,71},{8,24},{9,... | collective-permute-start | bytes 1572872 | tf_op jit(solution)/shard_map/P_H1/ppermute | solution.py:466
  95.8 21.7 %collective-permute-start.24 = (f32[4,256,256]{2,1,0:T(8,128)S(1)}, f32[4,256,256]{2,1,0:T(8,128)S(1)}, u32[]{:S(2)}, u32[]{:S(2)}) collective-permute-start(f32[4,256,256]{2,1,0:T(8,128)S(1)} %add_dynamic-update-slice_fusion), channel_id=1, source_target_pairs={{0,48},{1,73},{2,50},{3,75},{4,52},{5,77},{6,54},{7,79},{8,56},{9,... | collective-permute-start | bytes 3145736 | tf_op jit(solution)/shard_map/P_F1/ppermute | solution.py:466
  99.7 21.7 %collective-permute-start.22 = (f32[4,256,256]{2,1,0:T(8,128)S(1)}, f32[4,256,256]{2,1,0:T(8,128)S(1)}, u32[]{:S(2)}, u32[]{:S(2)}) collective-permute-start(f32[4,256,256]{2,1,0:T(8,128)S(1)} %add_dynamic-update-slice_fusion.1), channel_id=1, source_target_pairs={{0,16},{1,65},{2,18},{3,67},{4,20},{5,69},{6,22},{7,71},{8,24},{9,... | collective-permute-start | bytes 3145736 | tf_op jit(solution)/shard_map/P_F1/ppermute | solution.py:466
  99.9 25.4 %collective-permute-start.20 = (f32[256,256]{1,0:T(8,128)S(1)}, f32[256,256]{1,0:T(8,128)S(1)}, u32[]{:S(2)}, u32[]{:S(2)}) collective-permute-start(f32[256,256]{1,0:T(8,128)S(1)} %get-tuple-element.143), channel_id=1, source_target_pairs={{0,72},{1,49},{2,74},{3,51},{4,76},{5,53},{6,78},{7,55},{8,64},{9,... | collective-permute-start | bytes 786440 | tf_op jit(solution)/shard_map/P_G0/ppermute | solution.py:466
  103.7 22.6 %collective-permute-start.19 = (f32[256,256]{1,0:T(8,128)S(1)}, f32[256,256]{1,0:T(8,128)S(1)}, u32[]{:S(2)}, u32[]{:S(2)}) collective-permute-start(f32[256,256]{1,0:T(8,128)S(1)} %get-tuple-element.144), channel_id=1, source_target_pairs={{0,8},{1,33},{2,10},{3,35},{4,12},{5,37},{6,14},{7,39},{8,0},{9,41... | collective-permute-start | bytes 786440 | tf_op jit(solution)/shard_map/P_G0/ppermute | solution.py:466
  103.8 22.5 %collective-permute-start.18 = (f32[256,256]{1,0:T(8,128)S(1)}, f32[256,256]{1,0:T(8,128)S(1)}, u32[]{:S(2)}, u32[]{:S(2)}) collective-permute-start(f32[256,256]{1,0:T(8,128)S(1)} %get-tuple-element.145), channel_id=1, source_target_pairs={{0,64},{1,17},{2,66},{3,19},{4,68},{5,21},{6,70},{7,23},{8,72},{9,... | collective-permute-start | bytes 786440 | tf_op jit(solution)/shard_map/P_G0/ppermute | solution.py:466
  121.6 10.5 %collective-permute-start.27 = (f32[256,256]{1,0:T(8,128)S(1)}, f32[256,256]{1,0:T(8,128)S(1)}, u32[]{:S(2)}, u32[]{:S(2)}) collective-permute-start(f32[256,256]{1,0:T(8,128)S(1)} %get-tuple-element.139), channel_id=1, source_target_pairs={{0,72},{1,49},{2,74},{3,51},{4,76},{5,53},{6,78},{7,55},{8,64},{9,... | collective-permute-start | bytes 786440 | tf_op jit(solution)/shard_map/P_G1/ppermute | solution.py:466
  125.3 8.0 %collective-permute-start.26 = (f32[256,256]{1,0:T(8,128)S(1)}, f32[256,256]{1,0:T(8,128)S(1)}, u32[]{:S(2)}, u32[]{:S(2)}) collective-permute-start(f32[256,256]{1,0:T(8,128)S(1)} %get-tuple-element.140), channel_id=1, source_target_pairs={{0,8},{1,33},{2,10},{3,35},{4,12},{5,37},{6,14},{7,39},{8,0},{9,41... | collective-permute-start | bytes 786440 | tf_op jit(solution)/shard_map/P_G1/ppermute | solution.py:466
  125.4 10.4 %collective-permute-start.25 = (f32[256,256]{1,0:T(8,128)S(1)}, f32[256,256]{1,0:T(8,128)S(1)}, u32[]{:S(2)}, u32[]{:S(2)}) collective-permute-start(f32[256,256]{1,0:T(8,128)S(1)} %get-tuple-element.141), channel_id=1, source_target_pairs={{0,64},{1,17},{2,66},{3,19},{4,68},{5,21},{6,70},{7,23},{8,72},{9,... | collective-permute-start | bytes 786440 | tf_op jit(solution)/shard_map/P_G1/ppermute | solution.py:466

commit v10 on v9

--- a/solution.py
+++ b/solution.py
@@ -13,14 +13,12 @@
 COL = ("x", "core")
 SIZES = (2, 4, 2, 4, 2)
 CHUNKS = 2
-COST = (40 << 30, 40 << 30)
 CLUSTER = 512
 HALF = 128
 WIDE = 2 * HALF
 PAD = 128
 NEAR = 8
 FAR = 4
-VMEM_LIMIT = 60 << 20
 SCOPED = 10 << 20
 
 ANY = pl.BlockSpec(memory_space=pl.ANY)
@@ -371,7 +369,7 @@
             pltpu.SemaphoreType.DMA((FAR,)),
         ],
         compiler_params=pltpu.CompilerParams(vmem_limit_bytes=SCOPED),
-        cost_estimate=pl.CostEstimate(flops=COST[index], bytes_accessed=1, transcendentals=0),
+        cost_estimate=pl.CostEstimate(flops=40 << 30, bytes_accessed=1, transcendentals=0),
     )(table, *held, *blocks)
 
 
@@ -436,27 +434,27 @@
 
     def both_cores(parts, index):
         mine = pack(parts, index)
-        with jax.named_scope(f"P_S{index}"):
+        with jax.named_scope(f"other_core_{index}"):
             return mine, lax.ppermute(mine, "core", swap)
 
     middle = CLUSTER // 2
     blocks_a, done_a = prepare_near(table, near_z, 0, NEAR // 2)
     upper, lower = own_0[:middle], own_0[middle:]
-    upper = upper + (across_dir(upper, "P_ZU") + done_a[0, 0])
+    upper = upper + (across_dir(upper, "dir_upper") + done_a[0, 0])
     blocks_b, done_b = prepare_near(table, near_z, NEAR // 2, NEAR // 2)
     upper, lower = lax.optimization_barrier((upper, lower))
-    left_u, right_u = step(upper, 1, "P_LU"), step(upper, 3, "P_RU")
-    lower = lower + (across_dir(lower, "P_ZL") + done_b[0, 0])
+    left_u, right_u = step(upper, 1, "left_upper"), step(upper, 3, "right_upper")
+    lower = lower + (across_dir(lower, "dir_lower") + done_b[0, 0])
     own_1, lower, left_u, right_u = lax.optimization_barrier((own_1, lower, left_u, right_u))
-    left_l, right_l = step(lower, 1, "P_LL"), step(lower, 3, "P_RL")
-    came_1 = across_dir(own_1, "P_Z1")
+    left_l, right_l = step(lower, 1, "left_lower"), step(lower, 3, "right_lower")
+    came_1 = across_dir(own_1, "dir_second")
     right_l, table_far = lax.optimization_barrier((right_l, table))
     blocks_u, blocks_v, done_far = prepare_far(table_far, far_ut, far_vt)
-    upper_0, lower_0 = step(left_u, 1, "P_A0"), step(right_l, 3, "P_B0")
+    upper_0, lower_0 = step(left_u, 1, "pass_upper"), step(right_l, 3, "pass_lower")
     own_1 = own_1 + (came_1 + done_far[0, 0])
     own_1, upper_0, lower_0 = lax.optimization_barrier((own_1, upper_0, lower_0))
-    left_1, right_1 = step(own_1, 1, "P_L1"), step(own_1, 3, "P_R1")
-    across_1 = step(own_1, 2, "P_K1")
+    left_1, right_1 = step(own_1, 1, "left_second"), step(own_1, 3, "right_second")
+    across_1 = step(own_1, 2, "across_second")
     held_0 = both_cores([upper, lower, left_u, left_l, upper_0, lower_0, right_u, right_l], 0)
     blocks = (blocks_a, blocks_b, blocks_u, blocks_v)
 
@@ -466,15 +464,15 @@
             return lax.ppermute(part, AXES, turn)
 
     def first_step(upper, lower, index):
-        return go(upper, first_turn[0], f"P_H{index}"), go(lower, first_turn[2], f"P_H{index}")
+        return go(upper, first_turn[0], f"ring_first_{index}"), go(lower, first_turn[2], f"ring_first_{index}")
 
     def second_step(ahead, behind, came, index):
         ahead, behind = ahead.at[:2].add(came[0]), behind.at[2:].add(came[1])
-        return go(ahead, first_turn[0], f"P_F{index}"), go(behind, first_turn[2], f"P_F{index}")
+        return go(ahead, first_turn[0], f"ring_second_{index}"), go(behind, first_turn[2], f"ring_second_{index}")
 
     def other_ring(mine, came, index):
         mine, *away = [mine[k] + came[0][k] + came[1][k] for k in range(4)]
-        return mine, [go(part, turn, f"P_G{index}") for part, turn in zip(away, second_turn)]
+        return mine, [go(part, turn, f"other_ring_{index}") for part, turn in zip(away, second_turn)]
 
     mine, ahead, upper_0, lower_0, behind, done_0 = apply_blocks(table, held_0, blocks, 0)
     came_0 = first_step(upper_0, lower_0, 0)

time: 137 us -> 138 us (level)
  starting transfers between devices: 39.4 us -> 41.9 us
    ppermute x9, starting transfers between devices: 11.1 us -> 12.5 us  [step(): return lax.ppermute(part, 'x', [(i, (i + k) % 4) for i in range(4)])]
  transfers between devices with their start and end apart: 28 -> 28, of which waited for: 17 -> 16; matrix products, arithmetic and copies ran while one was open for 3% -> 3% of each run, Pallas kernels for 11% -> 11%
where the time goes in v10:
time: 138 us
  waiting for transfers between devices  72.3 us (52%)
  starting transfers between devices  41.9 us (30%)
  Pallas kernels  19 us (14%)
  other arithmetic  3.03 us (2%)
  local copies, waits for them, and re-layouts  1.66 us (1%)
    ppermute x14, waiting for transfers between devices, go(): return lax.ppermute(part, AXES, turn)  39.6 us
    ppermute x9, waiting for transfers between devices, step(): return lax.ppermute(part, 'x', [(i, (i + k) % 4) for i in range(4)])  28.2 us
    ppermute x14, starting transfers between devices, go(): return lax.ppermute(part, AXES, turn)  24.8 us
    ppermute x9, starting transfers between devices, step(): return lax.ppermute(part, 'x', [(i, (i + k) % 4) for i in range(4)])  12.5 us
    pallas_call x2, Pallas kernels, apply_blocks(): pl.pallas_call(apply_kernel, name=f'apply_{index}', in_specs=[SMEM] + [AN...  8.45 us
    ppermute x3, starting transfers between devices, across_dir(): return lax.ppermute(part, 'dir', swap)  4.39 us
    pallas_call x2, Pallas kernels, prepare_near(): pl.pallas_call(functools.partial(prepare_near_kernel, first), name=f'prep...  4.1 us
    ppermute x3, waiting for transfers between devices, across_dir(): return lax.ppermute(part, 'dir', swap)  3.97 us
  transfers between devices with their start and end apart: 28, of which 16 were waited for; matrix products, arithmetic and copies ran while one was open for 3% of the time, Pallas kernels for 11%

profile of v10, /device:TPU:0, one launch (start us, length us, event | category | flops | bytes accessed | tf_op | source)
XLA Modules:
  0.0 138.1 jit_solution(16608367134838463808)
XLA Ops:
  0.0 3.0 %rhs.5 = (f32[512,256]{1,0:T(8,128)S(1)}, f32[512,256]{1,0:T(8,128)S(1)}) custom-call(bf16[1024,512]{1,0:T(8,128)(2,1)} %cot_ref.1, bf16[2,512,1024]{2,1,0:T(8,128)(2,1)} %rad_ref.1), custom_call_target="tpu_custom_call" | custom-call | flops 1073741824 | bytes 4194304 | tf_op jit(solution)/shard_map/rhs/pallas_call | solution.py:88
  3.1 2.1 %collective-permute-start = (f32[256,256]{1,0:T(8,128)S(1)}, f32[256,256]{1,0:T(8,128)S(1)}, u32[]{:S(2)}, u32[]{:S(2)}) collective-permute-start(f32[256,256]{1,0:T(8,128)S(1)} %slice.199), channel_id=1, source_target_pairs={{0,64},{64,0},{1,65},{65,1},{2,66},{66,2},{3,67},{67,3},{4,68},{68... | collective-permute-start | bytes 786440 | tf_op jit(solution)/shard_map/dir_upper/ppermute | solution.py:429
  5.3 3.5 %prepare_near_0.1 = (bf16[4,512,2048]{2,1,0:T(8,128)(2,1)S(1)}, f32[8,128]{1,0:T(8,128)S(1)}) custom-call(s32[48]{0:T(128)S(1)} %concatenate.11.table, f32[2,8,512,512]{3,2,1,0:T(8,128)} %z_ref.3), custom_call_target="tpu_custom_call" | custom-call | flops 268435456 | bytes 8388608 | tf_op jit(solution)/shard_map/prepare_near_0/pallas_call | solution.py:137
  8.9 0.5 slice.200
  9.4 2.1 %collective-permute-done = f32[256,256]{1,0:T(8,128)S(1)} collective-permute-done((f32[256,256]{1,0:T(8,128)S(1)}, f32[256,256]{1,0:T(8,128)S(1)}, u32[]{:S(2)}, u32[]{:S(2)}) %collective-permute-start) | collective-permute-done | bytes 262176 | tf_op jit(solution)/shard_map/dir_upper/ppermute | solution.py:429
  11.5 0.7 fusion.11
  12.2 1.8 %collective-permute-start.1 = (f32[256,256]{1,0:T(8,128)S(1)}, f32[256,256]{1,0:T(8,128)S(1)}, u32[]{:S(2)}, u32[]{:S(2)}) collective-permute-start(f32[256,256]{1,0:T(8,128)S(1)} %get-tuple-element.100), channel_id=1, source_target_pairs={{0,64},{64,0},{1,65},{65,1},{2,66},{66,2},{3,67},{67,3},{4,68},{68... | collective-permute-start | bytes 786440 | tf_op jit(solution)/shard_map/dir_lower/ppermute | solution.py:429
  14.0 2.8 %collective-permute-start.3 = (f32[256,256]{1,0:T(8,128)S(1)}, f32[256,256]{1,0:T(8,128)S(1)}, u32[]{:S(2)}, u32[]{:S(2)}) collective-permute-start(f32[256,256]{1,0:T(8,128)S(1)} %get-tuple-element.98.refs_0_), channel_id=1, source_target_pairs={{0,6},{2,0},{4,2},{6,4},{1,7},{3,1},{5,3},{7,5},{8,14},{10,8},{12,... | collective-permute-start | bytes 786440 | tf_op jit(solution)/shard_map/right_upper/ppermute | solution.py:433
  16.8 0.6 prepare_near_4.1
  17.3 0.5 slice.202
  17.9 1.9 %collective-permute-done.1 = f32[256,256]{1,0:T(8,128)S(1)} collective-permute-done((f32[256,256]{1,0:T(8,128)S(1)}, f32[256,256]{1,0:T(8,128)S(1)}, u32[]{:S(2)}, u32[]{:S(2)}) %collective-permute-start.1) | collective-permute-done | bytes 262176 | tf_op jit(solution)/shard_map/dir_lower/ppermute | solution.py:429
  19.7 0.7 add_add_fusion.1.refs_1_
  20.4 0.8 collective-permute-done.3.refs_6_
  21.2 3.4 %collective-permute-done.2.refs_2_ = f32[256,256]{1,0:T(8,128)S(1)} collective-permute-done((f32[256,256]{1,0:T(8,128)S(1)}, f32[256,256]{1,0:T(8,128)S(1)}, u32[]{:S(2)}, u32[]{:S(2)}) %collective-permute-start.2) | collective-permute-done | bytes 262176 | tf_op jit(solution)/shard_map/left_upper/ppermute | solution.py:433
  24.6 0.5 collective-permute-start.5
  25.1 1.8 %collective-permute-start.6 = (f32[256,256]{1,0:T(8,128)S(1)}, f32[256,256]{1,0:T(8,128)S(1)}, u32[]{:S(2)}, u32[]{:S(2)}) collective-permute-start(f32[256,256]{1,0:T(8,128)S(1)} %add_add_fusion.1.refs_1_), channel_id=1, source_target_pairs={{0,6},{2,0},{4,2},{6,4},{1,7},{3,1},{5,3},{7,5},{8,14},{10,8},{12,... | collective-permute-start | bytes 786440 | tf_op jit(solution)/shard_map/right_lower/ppermute | solution.py:433
  26.8 0.2 collective-permute-start.4
  27.1 5.4 %collective-permute-done.6.refs_7_ = f32[256,256]{1,0:T(8,128)S(1)} collective-permute-done((f32[256,256]{1,0:T(8,128)S(1)}, f32[256,256]{1,0:T(8,128)S(1)}, u32[]{:S(2)}, u32[]{:S(2)}) %collective-permute-start.6) | collective-permute-done | bytes 262176 | tf_op jit(solution)/shard_map/right_lower/ppermute | solution.py:433
  32.5 3.0 %collective-permute-start.8 = (f32[256,256]{1,0:T(8,128)S(1)}, f32[256,256]{1,0:T(8,128)S(1)}, u32[]{:S(2)}, u32[]{:S(2)}) collective-permute-start(f32[256,256]{1,0:T(8,128)S(1)} %collective-permute-done.6.refs_7_), channel_id=1, source_target_pairs={{0,6},{2,0},{4,2},{6,4},{1,7},{3,1},{5,3},{7,5},{8,14},{10,8},{12,... | collective-permute-start | bytes 786440 | tf_op jit(solution)/shard_map/pass_lower/ppermute | solution.py:433
  35.5 2.0 %prepare_far.1 = (bf16[4,128,2048]{2,1,0:T(8,128)(2,1)S(1)}, bf16[4,512,512]{2,1,0:T(8,128)(2,1)S(1)}, f32[8,128]{1,0:T(8,128)S(1)}) custom-call(s32[48]{0:T(128)S(1)} %concatenate.11.table, f32[2,4,96,512]{3,2,1,0:T(8,128)} %u_ref.1, f32[2,4,96,512]{3,2,1,0:T(8,128)} %v_ref.1), custom_call_target="tpu_custom_call" | custom-call | flops 268435456 | bytes 4194304 | tf_op jit(solution)/shard_map/prepare_far/pallas_call | solution.py:190
  37.5 0.5 slice.203
  38.0 0.7 add_add_fusion.refs_0_
  38.8 0.6 collective-permute-done.8.refs_5_
  39.8 3.8 %collective-permute-start.12 = (f32[512,256]{1,0:T(8,128)S(1)}, f32[512,256]{1,0:T(8,128)S(1)}, u32[]{:S(2)}, u32[]{:S(2)}) collective-permute-start(f32[512,256]{1,0:T(8,128)S(1)} %add_add_fusion.refs_0_), channel_id=1, source_target_pairs={{0,6},{2,0},{4,2},{6,4},{1,7},{3,1},{5,3},{7,5},{8,14},{10,8},{12,... | collective-permute-start | bytes 1572872 | tf_op jit(solution)/shard_map/right_second/ppermute | solution.py:433
  43.5 0.9 collective-permute-start.10
  44.5 4.2 %apply_0.1 = (f32[4,256,256]{2,1,0:T(8,128)S(1)}, f32[4,256,256]{2,1,0:T(8,128)S(1)}, f32[2,256,256]{2,1,0:T(8,128)S(1)}, f32[2,256,256]{2,1,0:T(8,128)S(1)}, f3...) custom-call(s32[48]{0:T(128)S(1)} %concatenate.11.table, f32[2048,256]{1,0:T(8,128)S(1)} %pack_0.1.refs_0_, ...), custom_call_target="tpu_custom_call" | custom-call | flops 42949672960 | bytes 1 | tf_op jit(solution)/shard_map/apply_0/pallas_call | solution.py:359
  48.7 1.3 collective-permute-start.13
  50.0 2.0 %collective-permute-start.14 = (f32[2,256,256]{2,1,0:T(8,128)S(1)}, f32[2,256,256]{2,1,0:T(8,128)S(1)}, u32[]{:S(2)}, u32[]{:S(2)}) collective-permute-start(f32[2,256,256]{2,1,0:T(8,128)S(1)} %get-tuple-element.118), channel_id=1, source_target_pairs={{0,48},{1,73},{2,50},{3,75},{4,52},{5,77},{6,54},{7,79},{8,56},{9,... | collective-permute-start | bytes 1572872 | tf_op jit(solution)/shard_map/ring_first_0/ppermute | solution.py:464
  52.0 14.6 %collective-permute-done.12.refs_3_ = f32[512,256]{1,0:T(8,128)S(1)} collective-permute-done((f32[512,256]{1,0:T(8,128)S(1)}, f32[512,256]{1,0:T(8,128)S(1)}, u32[]{:S(2)}, u32[]{:S(2)}) %collective-permute-start.12) | collective-permute-done | bytes 524320 | tf_op jit(solution)/shard_map/right_second/ppermute | solution.py:433
  66.5 3.4 %collective-permute-done.10.refs_1_ = f32[512,256]{1,0:T(8,128)S(1)} collective-permute-done((f32[512,256]{1,0:T(8,128)S(1)}, f32[512,256]{1,0:T(8,128)S(1)}, u32[]{:S(2)}, u32[]{:S(2)}) %collective-permute-start.10) | collective-permute-done | bytes 524320 | tf_op jit(solution)/shard_map/left_second/ppermute | solution.py:433
  70.4 0.5 collective-permute-start.16
  71.1 2.8 %collective-permute-start.17 = (f32[4,256,256]{2,1,0:T(8,128)S(1)}, f32[4,256,256]{2,1,0:T(8,128)S(1)}, u32[]{:S(2)}, u32[]{:S(2)}) collective-permute-start(f32[4,256,256]{2,1,0:T(8,128)S(1)} %add_dynamic-update-slice_fusion.2), channel_id=1, source_target_pairs={{0,48},{1,73},{2,50},{3,75},{4,52},{5,77},{6,54},{7,79},{8,56},{9,... | collective-permute-start | bytes 3145736 | tf_op jit(solution)/shard_map/ring_second_0/ppermute | solution.py:464
  73.9 0.5 collective-permute-done.15.refs_1_
  74.4 4.2 %apply_1.1 = (f32[4,256,256]{2,1,0:T(8,128)S(1)}, f32[4,256,256]{2,1,0:T(8,128)S(1)}, f32[2,256,256]{2,1,0:T(8,128)S(1)}, f32[2,256,256]{2,1,0:T(8,128)S(1)}, f3...) custom-call(s32[48]{0:T(128)S(1)} %concatenate.11.table, f32[2048,256]{1,0:T(8,128)S(1)} %pack_1.1.refs_0_, ...), custom_call_target="tpu_custom_call" | custom-call | flops 42949672960 | bytes 1 | tf_op jit(solution)/shard_map/apply_1/pallas_call | solution.py:359
  78.6 7.8 %collective-permute-done.16 = f32[4,256,256]{2,1,0:T(8,128)S(1)} collective-permute-done((f32[4,256,256]{2,1,0:T(8,128)S(1)}, f32[4,256,256]{2,1,0:T(8,128)S(1)}, u32[]{:S(2)}, u32[]{:S(2)}) %collective-permute-start.16) | collective-permute-done | bytes 1048608 | tf_op jit(solution)/shard_map/ring_second_0/ppermute | solution.py:464
  86.5 3.4 %collective-permute-start.23 = (f32[2,256,256]{2,1,0:T(8,128)S(1)}, f32[2,256,256]{2,1,0:T(8,128)S(1)}, u32[]{:S(2)}, u32[]{:S(2)}) collective-permute-start(f32[2,256,256]{2,1,0:T(8,128)S(1)} %get-tuple-element.136), channel_id=1, source_target_pairs={{0,48},{1,73},{2,50},{3,75},{4,52},{5,77},{6,54},{7,79},{8,56},{9,... | collective-permute-start | bytes 1572872 | tf_op jit(solution)/shard_map/ring_first_1/ppermute | solution.py:464
  89.9 6.7 %collective-permute-done.23 = f32[2,256,256]{2,1,0:T(8,128)S(1)} collective-permute-done((f32[2,256,256]{2,1,0:T(8,128)S(1)}, f32[2,256,256]{2,1,0:T(8,128)S(1)}, u32[]{:S(2)}, u32[]{:S(2)}) %collective-permute-start.23) | collective-permute-done | bytes 524320 | tf_op jit(solution)/shard_map/ring_first_1/ppermute | solution.py:464
  96.7 3.8 %collective-permute-start.24 = (f32[4,256,256]{2,1,0:T(8,128)S(1)}, f32[4,256,256]{2,1,0:T(8,128)S(1)}, u32[]{:S(2)}, u32[]{:S(2)}) collective-permute-start(f32[4,256,256]{2,1,0:T(8,128)S(1)} %add_dynamic-update-slice_fusion), channel_id=1, source_target_pairs={{0,48},{1,73},{2,50},{3,75},{4,52},{5,77},{6,54},{7,79},{8,56},{9,... | collective-permute-start | bytes 3145736 | tf_op jit(solution)/shard_map/ring_second_1/ppermute | solution.py:464
  100.9 4.2 %collective-permute-start.20 = (f32[256,256]{1,0:T(8,128)S(1)}, f32[256,256]{1,0:T(8,128)S(1)}, u32[]{:S(2)}, u32[]{:S(2)}) collective-permute-start(f32[256,256]{1,0:T(8,128)S(1)} %get-tuple-element.143), channel_id=1, source_target_pairs={{0,72},{1,49},{2,74},{3,51},{4,76},{5,53},{6,78},{7,55},{8,64},{9,... | collective-permute-start | bytes 786440 | tf_op jit(solution)/shard_map/other_ring_0/ppermute | solution.py:464
  105.1 1.3 collective-permute-start.18
  106.3 12.1 %collective-permute-done.24 = f32[4,256,256]{2,1,0:T(8,128)S(1)} collective-permute-done((f32[4,256,256]{2,1,0:T(8,128)S(1)}, f32[4,256,256]{2,1,0:T(8,128)S(1)}, u32[]{:S(2)}, u32[]{:S(2)}) %collective-permute-start.24) | collective-permute-done | bytes 1048608 | tf_op jit(solution)/shard_map/ring_second_1/ppermute | solution.py:464
  118.4 3.9 %collective-permute-done.22 = f32[4,256,256]{2,1,0:T(8,128)S(1)} collective-permute-done((f32[4,256,256]{2,1,0:T(8,128)S(1)}, f32[4,256,256]{2,1,0:T(8,128)S(1)}, u32[]{:S(2)}, u32[]{:S(2)}) %collective-permute-start.22) | collective-permute-done | bytes 1048608 | tf_op jit(solution)/shard_map/ring_second_1/ppermute | solution.py:464
  122.5 4.2 %collective-permute-start.27 = (f32[256,256]{1,0:T(8,128)S(1)}, f32[256,256]{1,0:T(8,128)S(1)}, u32[]{:S(2)}, u32[]{:S(2)}) collective-permute-start(f32[256,256]{1,0:T(8,128)S(1)} %get-tuple-element.139), channel_id=1, source_target_pairs={{0,72},{1,49},{2,74},{3,51},{4,76},{5,53},{6,78},{7,55},{8,64},{9,... | collective-permute-start | bytes 786440 | tf_op jit(solution)/shard_map/other_ring_1/ppermute | solution.py:464
  126.7 1.3 collective-permute-start.25
  128.0 5.4 %collective-permute-done.27.refs_7_ = f32[256,256]{1,0:T(8,128)S(1)} collective-permute-done((f32[256,256]{1,0:T(8,128)S(1)}, f32[256,256]{1,0:T(8,128)S(1)}, u32[]{:S(2)}, u32[]{:S(2)}) %collective-permute-start.27) | collective-permute-done | bytes 262176 | tf_op jit(solution)/shard_map/other_ring_1/ppermute | solution.py:464
  133.4 1.3 collective-permute-done.26.refs_6_
  134.7 2.4 %collective-permute-done.25.refs_5_ = f32[256,256]{1,0:T(8,128)S(1)} collective-permute-done((f32[256,256]{1,0:T(8,128)S(1)}, f32[256,256]{1,0:T(8,128)S(1)}, u32[]{:S(2)}, u32[]{:S(2)}) %collective-permute-start.25) | collective-permute-done | bytes 262176 | tf_op jit(solution)/shard_map/other_ring_1/ppermute | solution.py:464
  137.1 1.0 finish.1
  (42 shorter events, 1.8 us)
Async XLA Ops:
  0.0 5.2 %copy-start = (s32[8,2]{0,1:T(2,128)S(1)}, s32[8,2]{0,1:T(2,128)}, u32[]{:S(2)}) copy-start(s32[8,2]{0,1:T(2,128)} %param.20) | copy-start | bytes 196
  0.0 5.2 %copy-start.1 = (s32[4,2]{0,1:T(2,128)S(1)}, s32[4,2]{0,1:T(2,128)}, u32[]{:S(2)}) copy-start(s32[4,2]{0,1:T(2,128)} %param.23) | copy-start | bytes 100
  0.0 5.2 %copy-start.2 = (s32[1,2]{1,0:T(1,128)S(1)}, s32[1,2]{1,0:T(1,128)}, u32[]{:S(2)}) copy-start(s32[1,2]{1,0:T(1,128)} %param.25) | copy-start | bytes 28
  0.0 5.2 %copy-start.3 = (s32[4]{0:T(128)S(1)}, s32[4]{0:T(128)}, u32[]{:S(2)}) copy-start(s32[4]{0:T(128)} %param.24) | copy-start | bytes 52
  3.1 8.4 %collective-permute-start = (f32[256,256]{1,0:T(8,128)S(1)}, f32[256,256]{1,0:T(8,128)S(1)}, u32[]{:S(2)}, u32[]{:S(2)}) collective-permute-start(f32[256,256]{1,0:T(8,128)S(1)} %slice.199), channel_id=1, source_target_pairs={{0,64},{64,0},{1,65},{65,1},{2,66},{66,2},{3,67},{67,3},{4,68},{68... | collective-permute-start | bytes 786440 | tf_op jit(solution)/shard_map/dir_upper/ppermute | solution.py:429
  12.2 7.6 %collective-permute-start.1 = (f32[256,256]{1,0:T(8,128)S(1)}, f32[256,256]{1,0:T(8,128)S(1)}, u32[]{:S(2)}, u32[]{:S(2)}) collective-permute-start(f32[256,256]{1,0:T(8,128)S(1)} %get-tuple-element.100), channel_id=1, source_target_pairs={{0,64},{64,0},{1,65},{65,1},{2,66},{66,2},{3,67},{67,3},{4,68},{68... | collective-permute-start | bytes 786440 | tf_op jit(solution)/shard_map/dir_lower/ppermute | solution.py:429
  14.0 7.2 %collective-permute-start.3 = (f32[256,256]{1,0:T(8,128)S(1)}, f32[256,256]{1,0:T(8,128)S(1)}, u32[]{:S(2)}, u32[]{:S(2)}) collective-permute-start(f32[256,256]{1,0:T(8,128)S(1)} %get-tuple-element.98.refs_0_), channel_id=1, source_target_pairs={{0,6},{2,0},{4,2},{6,4},{1,7},{3,1},{5,3},{7,5},{8,14},{10,8},{12,... | collective-permute-start | bytes 786440 | tf_op jit(solution)/shard_map/right_upper/ppermute | solution.py:433
  16.8 7.8 %collective-permute-start.2 = (f32[256,256]{1,0:T(8,128)S(1)}, f32[256,256]{1,0:T(8,128)S(1)}, u32[]{:S(2)}, u32[]{:S(2)}) collective-permute-start(f32[256,256]{1,0:T(8,128)S(1)} %get-tuple-element.98.refs_0_), channel_id=1, source_target_pairs={{0,2},{2,4},{4,6},{6,0},{1,3},{3,5},{5,7},{7,1},{8,10},{10,12},{12... | collective-permute-start | bytes 786440 | tf_op jit(solution)/shard_map/left_upper/ppermute | solution.py:433
  24.6 13.5 %collective-permute-start.5 = (f32[512,256]{1,0:T(8,128)S(1)}, f32[512,256]{1,0:T(8,128)S(1)}, u32[]{:S(2)}, u32[]{:S(2)}) collective-permute-start(f32[512,256]{1,0:T(8,128)S(1)} %get-tuple-element.104), channel_id=1, source_target_pairs={{0,64},{64,0},{1,65},{65,1},{2,66},{66,2},{3,67},{67,3},{4,68},{68... | collective-permute-start | bytes 1572872 | tf_op jit(solution)/shard_map/dir_second/ppermute | solution.py:429
  25.1 7.5 %collective-permute-start.6 = (f32[256,256]{1,0:T(8,128)S(1)}, f32[256,256]{1,0:T(8,128)S(1)}, u32[]{:S(2)}, u32[]{:S(2)}) collective-permute-start(f32[256,256]{1,0:T(8,128)S(1)} %add_add_fusion.1.refs_1_), channel_id=1, source_target_pairs={{0,6},{2,0},{4,2},{6,4},{1,7},{3,1},{5,3},{7,5},{8,14},{10,8},{12,... | collective-permute-start | bytes 786440 | tf_op jit(solution)/shard_map/right_lower/ppermute | solution.py:433
  26.8 12.6 %collective-permute-start.4 = (f32[256,256]{1,0:T(8,128)S(1)}, f32[256,256]{1,0:T(8,128)S(1)}, u32[]{:S(2)}, u32[]{:S(2)}) collective-permute-start(f32[256,256]{1,0:T(8,128)S(1)} %add_add_fusion.1.refs_1_), channel_id=1, source_target_pairs={{0,2},{2,4},{4,6},{6,0},{1,3},{3,5},{5,7},{7,1},{8,10},{10,12},{12... | collective-permute-start | bytes 786440 | tf_op jit(solution)/shard_map/left_lower/ppermute | solution.py:433
  27.1 11.7 %collective-permute-start.7 = (f32[256,256]{1,0:T(8,128)S(1)}, f32[256,256]{1,0:T(8,128)S(1)}, u32[]{:S(2)}, u32[]{:S(2)}) collective-permute-start(f32[256,256]{1,0:T(8,128)S(1)} %collective-permute-done.2.refs_2_), channel_id=1, source_target_pairs={{0,2},{2,4},{4,6},{6,0},{1,3},{3,5},{5,7},{7,1},{8,10},{10,12},{12... | collective-permute-start | bytes 786440 | tf_op jit(solution)/shard_map/pass_upper/ppermute | solution.py:433
  32.5 6.9 %collective-permute-start.8 = (f32[256,256]{1,0:T(8,128)S(1)}, f32[256,256]{1,0:T(8,128)S(1)}, u32[]{:S(2)}, u32[]{:S(2)}) collective-permute-start(f32[256,256]{1,0:T(8,128)S(1)} %collective-permute-done.6.refs_7_), channel_id=1, source_target_pairs={{0,6},{2,0},{4,2},{6,4},{1,7},{3,1},{5,3},{7,5},{8,14},{10,8},{12,... | collective-permute-start | bytes 786440 | tf_op jit(solution)/shard_map/pass_lower/ppermute | solution.py:433
  39.7 4.8 %collective-permute-start.9 = (f32[2048,256]{1,0:T(8,128)S(1)}, f32[2048,256]{1,0:T(8,128)S(1)}, u32[]{:S(2)}, u32[]{:S(2)}) collective-permute-start(f32[2048,256]{1,0:T(8,128)S(1)} %pack_0.1.refs_0_), channel_id=1, source_target_pairs={{0,1},{1,0},{2,3},{3,2},{4,5},{5,4},{6,7},{7,6},{8,9},{9,8},{10,11... | collective-permute-start | bytes 6291464 | tf_op jit(solution)/shard_map/other_core_0/ppermute | solution.py:438
  39.8 26.8 %collective-permute-start.12 = (f32[512,256]{1,0:T(8,128)S(1)}, f32[512,256]{1,0:T(8,128)S(1)}, u32[]{:S(2)}, u32[]{:S(2)}) collective-permute-start(f32[512,256]{1,0:T(8,128)S(1)} %add_add_fusion.refs_0_), channel_id=1, source_target_pairs={{0,6},{2,0},{4,2},{6,4},{1,7},{3,1},{5,3},{7,5},{8,14},{10,8},{12,... | collective-permute-start | bytes 1572872 | tf_op jit(solution)/shard_map/right_second/ppermute | solution.py:433
  43.5 23.0 %collective-permute-start.11 = (f32[512,256]{1,0:T(8,128)S(1)}, f32[512,256]{1,0:T(8,128)S(1)}, u32[]{:S(2)}, u32[]{:S(2)}) collective-permute-start(f32[512,256]{1,0:T(8,128)S(1)} %add_add_fusion.refs_0_), channel_id=1, source_target_pairs={{0,4},{2,6},{4,0},{6,2},{1,5},{3,7},{5,1},{7,3},{8,12},{10,14},{12... | collective-permute-start | bytes 1572872 | tf_op jit(solution)/shard_map/across_second/ppermute | solution.py:433
  43.5 26.4 %collective-permute-start.10 = (f32[512,256]{1,0:T(8,128)S(1)}, f32[512,256]{1,0:T(8,128)S(1)}, u32[]{:S(2)}, u32[]{:S(2)}) collective-permute-start(f32[512,256]{1,0:T(8,128)S(1)} %add_add_fusion.refs_0_), channel_id=1, source_target_pairs={{0,2},{2,4},{4,6},{6,0},{1,3},{3,5},{5,7},{7,1},{8,10},{10,12},{12... | collective-permute-start | bytes 1572872 | tf_op jit(solution)/shard_map/left_second/ppermute | solution.py:433
  48.7 21.3 %collective-permute-start.13 = (f32[2,256,256]{2,1,0:T(8,128)S(1)}, f32[2,256,256]{2,1,0:T(8,128)S(1)}, u32[]{:S(2)}, u32[]{:S(2)}) collective-permute-start(f32[2,256,256]{2,1,0:T(8,128)S(1)} %get-tuple-element.117), channel_id=1, source_target_pairs={{0,16},{1,65},{2,18},{3,67},{4,20},{5,69},{6,22},{7,71},{8,24},{9,... | collective-permute-start | bytes 1572872 | tf_op jit(solution)/shard_map/ring_first_0/ppermute | solution.py:464
  50.0 20.0 %collective-permute-start.14 = (f32[2,256,256]{2,1,0:T(8,128)S(1)}, f32[2,256,256]{2,1,0:T(8,128)S(1)}, u32[]{:S(2)}, u32[]{:S(2)}) collective-permute-start(f32[2,256,256]{2,1,0:T(8,128)S(1)} %get-tuple-element.118), channel_id=1, source_target_pairs={{0,48},{1,73},{2,50},{3,75},{4,52},{5,77},{6,54},{7,79},{8,56},{9,... | collective-permute-start | bytes 1572872 | tf_op jit(solution)/shard_map/ring_first_0/ppermute | solution.py:464
  70.2 4.2 %collective-permute-start.15 = (f32[2048,256]{1,0:T(8,128)S(1)}, f32[2048,256]{1,0:T(8,128)S(1)}, u32[]{:S(2)}, u32[]{:S(2)}) collective-permute-start(f32[2048,256]{1,0:T(8,128)S(1)} %pack_1.1.refs_0_), channel_id=1, source_target_pairs={{0,1},{1,0},{2,3},{3,2},{4,5},{5,4},{6,7},{7,6},{8,9},{9,8},{10,11... | collective-permute-start | bytes 6291464 | tf_op jit(solution)/shard_map/other_core_1/ppermute | solution.py:438
  70.4 16.1 %collective-permute-start.16 = (f32[4,256,256]{2,1,0:T(8,128)S(1)}, f32[4,256,256]{2,1,0:T(8,128)S(1)}, u32[]{:S(2)}, u32[]{:S(2)}) collective-permute-start(f32[4,256,256]{2,1,0:T(8,128)S(1)} %add_dynamic-update-slice_fusion.3), channel_id=1, source_target_pairs={{0,16},{1,65},{2,18},{3,67},{4,20},{5,69},{6,22},{7,71},{8,24},{9,... | collective-permute-start | bytes 3145736 | tf_op jit(solution)/shard_map/ring_second_0/ppermute | solution.py:464
  71.1 15.4 %collective-permute-start.17 = (f32[4,256,256]{2,1,0:T(8,128)S(1)}, f32[4,256,256]{2,1,0:T(8,128)S(1)}, u32[]{:S(2)}, u32[]{:S(2)}) collective-permute-start(f32[4,256,256]{2,1,0:T(8,128)S(1)} %add_dynamic-update-slice_fusion.2), channel_id=1, source_target_pairs={{0,48},{1,73},{2,50},{3,75},{4,52},{5,77},{6,54},{7,79},{8,56},{9,... | collective-permute-start | bytes 3145736 | tf_op jit(solution)/shard_map/ring_second_0/ppermute | solution.py:464
  86.5 10.1 %collective-permute-start.23 = (f32[2,256,256]{2,1,0:T(8,128)S(1)}, f32[2,256,256]{2,1,0:T(8,128)S(1)}, u32[]{:S(2)}, u32[]{:S(2)}) collective-permute-start(f32[2,256,256]{2,1,0:T(8,128)S(1)} %get-tuple-element.136), channel_id=1, source_target_pairs={{0,48},{1,73},{2,50},{3,75},{4,52},{5,77},{6,54},{7,79},{8,56},{9,... | collective-permute-start | bytes 1572872 | tf_op jit(solution)/shard_map/ring_first_1/ppermute | solution.py:464
  89.9 10.6 %collective-permute-start.21 = (f32[2,256,256]{2,1,0:T(8,128)S(1)}, f32[2,256,256]{2,1,0:T(8,128)S(1)}, u32[]{:S(2)}, u32[]{:S(2)}) collective-permute-start(f32[2,256,256]{2,1,0:T(8,128)S(1)} %get-tuple-element.134), channel_id=1, source_target_pairs={{0,16},{1,65},{2,18},{3,67},{4,20},{5,69},{6,22},{7,71},{8,24},{9,... | collective-permute-start | bytes 1572872 | tf_op jit(solution)/shard_map/ring_first_1/ppermute | solution.py:464
  96.7 21.7 %collective-permute-start.24 = (f32[4,256,256]{2,1,0:T(8,128)S(1)}, f32[4,256,256]{2,1,0:T(8,128)S(1)}, u32[]{:S(2)}, u32[]{:S(2)}) collective-permute-start(f32[4,256,256]{2,1,0:T(8,128)S(1)} %add_dynamic-update-slice_fusion), channel_id=1, source_target_pairs={{0,48},{1,73},{2,50},{3,75},{4,52},{5,77},{6,54},{7,79},{8,56},{9,... | collective-permute-start | bytes 3145736 | tf_op jit(solution)/shard_map/ring_second_1/ppermute | solution.py:464
  100.6 21.7 %collective-permute-start.22 = (f32[4,256,256]{2,1,0:T(8,128)S(1)}, f32[4,256,256]{2,1,0:T(8,128)S(1)}, u32[]{:S(2)}, u32[]{:S(2)}) collective-permute-start(f32[4,256,256]{2,1,0:T(8,128)S(1)} %add_dynamic-update-slice_fusion.1), channel_id=1, source_target_pairs={{0,16},{1,65},{2,18},{3,67},{4,20},{5,69},{6,22},{7,71},{8,24},{9,... | collective-permute-start | bytes 3145736 | tf_op jit(solution)/shard_map/ring_second_1/ppermute | solution.py:464
  100.9 25.8 %collective-permute-start.20 = (f32[256,256]{1,0:T(8,128)S(1)}, f32[256,256]{1,0:T(8,128)S(1)}, u32[]{:S(2)}, u32[]{:S(2)}) collective-permute-start(f32[256,256]{1,0:T(8,128)S(1)} %get-tuple-element.143), channel_id=1, source_target_pairs={{0,72},{1,49},{2,74},{3,51},{4,76},{5,53},{6,78},{7,55},{8,64},{9,... | collective-permute-start | bytes 786440 | tf_op jit(solution)/shard_map/other_ring_0/ppermute | solution.py:464
  105.1 22.9 %collective-permute-start.19 = (f32[256,256]{1,0:T(8,128)S(1)}, f32[256,256]{1,0:T(8,128)S(1)}, u32[]{:S(2)}, u32[]{:S(2)}) collective-permute-start(f32[256,256]{1,0:T(8,128)S(1)} %get-tuple-element.144), channel_id=1, source_target_pairs={{0,8},{1,33},{2,10},{3,35},{4,12},{5,37},{6,14},{7,39},{8,0},{9,41... | collective-permute-start | bytes 786440 | tf_op jit(solution)/shard_map/other_ring_0/ppermute | solution.py:464
  105.1 22.9 %collective-permute-start.18 = (f32[256,256]{1,0:T(8,128)S(1)}, f32[256,256]{1,0:T(8,128)S(1)}, u32[]{:S(2)}, u32[]{:S(2)}) collective-permute-start(f32[256,256]{1,0:T(8,128)S(1)} %get-tuple-element.145), channel_id=1, source_target_pairs={{0,64},{1,17},{2,66},{3,19},{4,68},{5,21},{6,70},{7,23},{8,72},{9,... | collective-permute-start | bytes 786440 | tf_op jit(solution)/shard_map/other_ring_0/ppermute | solution.py:464
  122.5 10.9 %collective-permute-start.27 = (f32[256,256]{1,0:T(8,128)S(1)}, f32[256,256]{1,0:T(8,128)S(1)}, u32[]{:S(2)}, u32[]{:S(2)}) collective-permute-start(f32[256,256]{1,0:T(8,128)S(1)} %get-tuple-element.139), channel_id=1, source_target_pairs={{0,72},{1,49},{2,74},{3,51},{4,76},{5,53},{6,78},{7,55},{8,64},{9,... | collective-permute-start | bytes 786440 | tf_op jit(solution)/shard_map/other_ring_1/ppermute | solution.py:464
  126.7 8.0 %collective-permute-start.26 = (f32[256,256]{1,0:T(8,128)S(1)}, f32[256,256]{1,0:T(8,128)S(1)}, u32[]{:S(2)}, u32[]{:S(2)}) collective-permute-start(f32[256,256]{1,0:T(8,128)S(1)} %get-tuple-element.140), channel_id=1, source_target_pairs={{0,8},{1,33},{2,10},{3,35},{4,12},{5,37},{6,14},{7,39},{8,0},{9,41... | collective-permute-start | bytes 786440 | tf_op jit(solution)/shard_map/other_ring_1/ppermute | solution.py:464
  126.7 10.4 %collective-permute-start.25 = (f32[256,256]{1,0:T(8,128)S(1)}, f32[256,256]{1,0:T(8,128)S(1)}, u32[]{:S(2)}, u32[]{:S(2)}) collective-permute-start(f32[256,256]{1,0:T(8,128)S(1)} %get-tuple-element.141), channel_id=1, source_target_pairs={{0,64},{1,17},{2,66},{3,19},{4,68},{5,21},{6,70},{7,23},{8,72},{9,... | collective-permute-start | bytes 786440 | tf_op jit(solution)/shard_map/other_ring_1/ppermute | solution.py:464
